TPU v7x, 256 devices: a whole 4x4x8 slice. The times are simulated.
256 devices in a mesh: dp: 8 (over x, core), clique: 32 (over y, z).
Axes of the slice: x: 4, y: 4, z: 8, core: 2. Of those that a mesh axis runs over, the one named last changes fastest.
Arguments:
- table_rows: int32 [33, 524288], P(None, 'dp'), may hold values from 0 to 255
- attribute_order: int32 [33], replicated, may hold values from 0 to 32, each once
- log_potential: float32 [32, 256, 256], P('clique'), may hold values from -4 to 18
- measure_noise: float32 [32, 256, 256], P('clique'), may hold values from -24 to 24
Outputs:
- updated_potentials: float32 [32, 256, 256], P('clique')
- beliefs: float32 [32, 256, 256], P('clique')
Inputs may be any that keep to these rules, and one draw needn't show every extreme that they name: `attribute_order`: each of the 33 attributes appears once.
All inputs are finite; a program needn't handle non-finite values.
Results may differ from a plain program's by a relative error of at most 0.0003.
Values sent between devices are 32-bit elements; how exact they have to be, the bound alone decides.
No kernel may reach another device: no remote copies, remote signals or barrier semaphores. Data moves between devices by JAX's collectives and lax.ppermute only.
A program may use at most 128 MiB of HBM per device.

v0:
```python
import math

import jax
import jax.numpy as jnp
from jax import lax
from jax.sharding import PartitionSpec as P

HIGH = lax.Precision.HIGHEST
step_size = 0.25


def prefix(value, axis, join, neutral, backward):
    count, mine = (lax.axis_size(axis), lax.axis_index(axis))
    pieces = lax.all_gather(value, axis)
    if backward:
        pieces = pieces[::-1]
        mine = count - 1 - mine
    running = jnp.full_like(value, 0) + jnp.asarray(neutral, value.dtype)

    def turn(position, running):
        longer = join(running, pieces[position])
        return jnp.where(position < mine, longer, running)

    return lax.fori_loop(0, count - 1, turn, running)


def rescale_matrix(matrix):
    return matrix / jnp.mean(matrix)


def rescale_vector(vector):
    return vector / jnp.sum(vector)


def chain_product(kernels):
    product = rescale_matrix(kernels[0])
    return product


def local_messages(first_in, last_in):
    forward = [rescale_vector(first_in)]
    backward = [rescale_vector(last_in)]
    return (jnp.stack(forward), jnp.stack(backward))


def clique_marginals(potential):
    kernels = jnp.exp(potential)
    domain_size = kernels.shape[1]
    product = chain_product(kernels)

    def joined_forward(earlier, later):
        return rescale_matrix(jnp.dot(earlier, later, precision=HIGH))

    def joined_backward(earlier, later):
        return rescale_matrix(jnp.dot(later, earlier, precision=HIGH))

    identity_matrix = jnp.eye(domain_size, dtype=jnp.float32)
    before = prefix(product, "clique", joined_forward, identity_matrix, False)
    after = prefix(product, "clique", joined_backward, identity_matrix, True)
    first_in = jnp.sum(before, axis=0)
    last_in = jnp.sum(after, axis=1)
    forward, backward = local_messages(first_in, last_in)
    joint = forward[:, :, None] * kernels * backward[:, None, :]
    total = jnp.sum(joint, axis=(1, 2), keepdims=True)
    return joint * (domain_size * domain_size) / total


def clique_counts(table_rows, chosen, domain_size):
    rows_total = table_rows.shape[1]
    block_rows = math.gcd(rows_total, 4096)
    columns = jnp.take(table_rows, chosen, axis=0)
    levels = jnp.arange(domain_size, dtype=jnp.int32)
    cliques_here = chosen.shape[0] - 1

    def add_block(number, totals):
        window = lax.dynamic_slice_in_dim(columns, number * block_rows, block_rows, 1)
        onehot = (window[:, :, None] == levels).astype(jnp.bfloat16)
        return totals + jnp.einsum(
            "jra,jrb->jab", onehot[:-1], onehot[1:], preferred_element_type=jnp.float32
        )

    empty = jnp.zeros((cliques_here, domain_size, domain_size), jnp.float32)
    return lax.fori_loop(0, rows_total // block_rows, add_block, empty)


def per_device(table_rows, attribute_order, log_potential, measure_noise):
    cliques_here = log_potential.shape[0]
    domain_size = log_potential.shape[1]
    start_at = lax.axis_index("clique") * cliques_here
    chosen = lax.dynamic_slice_in_dim(attribute_order, start_at, cliques_here + 1)
    first_beliefs = clique_marginals(log_potential)
    partial_counts = clique_counts(table_rows, chosen, domain_size)
    counts = lax.psum(partial_counts, "dp")
    total_rows = table_rows.shape[1] * lax.axis_size("dp")
    measured = (counts + measure_noise) * (domain_size * domain_size / total_rows)
    potential = log_potential
    potential = potential - step_size * (first_beliefs - measured)
    return (potential, first_beliefs)


def solution(mesh):
    in_specs = (P(None, "dp"), P(), P("clique", None, None), P("clique", None, None))
    out_specs = (P("clique", None, None), P("clique", None, None))
    return jax.shard_map(
        per_device, mesh=mesh, in_specs=in_specs, out_specs=out_specs, check_vma=False
    )
```

profile of v0, /device:TPU:1, one launch (start us, length us, event | category | flops | bytes accessed | tf_op | source)
XLA Modules:
  0.0 307.5 jit_solution(10314902839621671484)
XLA Ops:
  12.9 5.1 %gather_fusion = s32[2,65536]{1,0:T(2,128)S(1)} fusion(s32[33,65536]{1,0:T(8,128)} %param.10, s32[1024]{0:T(1024)S(1)} %pad_clamp_fusion), kind=kCustom, calls=%fused_computation | custom fusion | bytes 1048584 | tf_op jit(solution)/shard_map/jit(_take)/gather | solution.py:71
  18.3 50.2 %while.42 = (s32[]{:T(128)}, f32[1,256,256]{2,1,0:T(8,128)S(1)}, s32[2,65536]{1,0:T(2,128)S(1)}, s32[]{:T(128)}, s32[]{:T(128)}, /*index=5*/s32[]{:T(128)}, s32[]{:T(128)}) while((s32[]{:T(128)}, f32[1,256,256]{2,1,0:T(8,128)S(1)}, s32[2,65536]{1,0:T(2,128)S(1)}, s32[]{:T(128)}, s32[]{:T(128)}, /*index=5*/s32[]{:T(128)}, ...), condition=%wide.region_13.14_spmd.clone, body=%wide.region_12.13_spmd.clone.sunk | while | flops 539099136 | bytes 4817041 | solution.py:83
  69.4 44.9 %all-gather.2.cloned.1.call-done = f32[32,256,256]{2,1,0:T(8,128)} async-done(((f32[1,256,256]{2,1,0:T(8,128)}), f32[32,256,256]{2,1,0:T(8,128)}) %all-gather.2.cloned.1.call-update) | async-done | bytes 8388624 | tf_op jit(solution)/shard_map/all_gather | solution.py:14
  114.3 89.3 %while.40 = (s32[]{:T(128)}, f32[256,256]{0,1:T(8,128)S(1)}, s32[]{:T(128)}, f32[32,256,256]{2,1,0:T(8,128)}, s32[]{:T(128)}, /*index=5*/f32[]{:T(128)}) while((s32[]{:T(128)}, f32[256,256]{0,1:T(8,128)S(1)}, s32[]{:T(128)}, f32[32,256,256]{2,1,0:T(8,128)}, s32[]{:T(128)}, /*index=5*/f32[]{:T(128)}) %tuple.101), condition=%wide.region_3.4_spmd, body=%wide.region_1.3_spmd.sunk | while | flops 201523200 | bytes 1572975 | solution.py:24
  114.3 2.1 fusion.27
  117.2 2.2 fusion.27
  120.0 2.2 fusion.27
  122.9 2.2 fusion.27
  125.8 2.2 fusion.27
  128.7 2.2 fusion.27
  131.6 2.2 fusion.27
  134.5 2.2 fusion.27
  137.3 2.2 fusion.27
  140.2 2.2 fusion.27
  143.1 2.2 fusion.27
  146.0 2.2 fusion.27
  148.9 2.2 fusion.27
  151.7 2.2 fusion.27
  154.6 2.2 fusion.27
  157.5 2.2 fusion.27
  160.4 2.2 fusion.27
  163.3 2.2 fusion.27
  166.1 2.2 fusion.27
  169.0 2.2 fusion.27
  171.9 2.2 fusion.27
  174.8 2.2 fusion.27
  177.7 2.2 fusion.27
  180.6 2.2 fusion.27
  183.4 2.2 fusion.27
  186.3 2.2 fusion.27
  189.2 2.2 fusion.27
  192.1 2.2 fusion.27
  195.0 2.2 fusion.27
  197.8 2.2 fusion.27
  200.7 2.2 fusion.27
  204.3 7.5 %rev.3 = f32[32,256,256]{2,1,0:T(8,128)} reverse(f32[32,256,256]{2,1,0:T(8,128)} %get-tuple-element.437), dimensions={0} | reverse | bytes 16777216 | tf_op jit(solution)/shard_map/rev | solution.py:16
  211.8 82.8 %while.41 = (s32[]{:T(128)}, f32[256,256]{1,0:T(8,128)S(1)}, s32[]{:T(128)}, f32[32,256,256]{2,1,0:T(8,128)}, s32[]{:T(128)}, /*index=5*/f32[]{:T(128)}) while((s32[]{:T(128)}, f32[256,256]{1,0:T(8,128)S(1)}, s32[]{:T(128)}, f32[32,256,256]{2,1,0:T(8,128)}, s32[]{:T(128)}, /*index=5*/f32[]{:T(128)}) %tuple.98), condition=%wide.region_8.9_spmd, body=%wide.region_6.0_spmd.sunk | while | flops 201523200 | bytes 1572975 | solution.py:24
  211.8 2.0 fusion.29
  217.2 1.9 fusion.29
  219.9 1.9 fusion.29
  227.9 1.9 fusion.29
  235.9 1.9 fusion.29
  243.9 1.9 fusion.29
  251.9 1.9 fusion.29
  259.9 1.9 fusion.29
  267.9 1.9 fusion.29
  270.6 1.9 fusion.29
  297.4 2.6 multiply_subtract_fusion
  (154 shorter events, 102.1 us)
Async XLA Ops:
  8.0 106.3 %all-gather.2.cloned.1.call-start = ((), (), s32[]{:S(2)}) async-start(), calls=%async_computation | async-start | bytes 8650752 | tf_op jit(solution)/shard_map/all_gather | solution.py:14
  12.0 285.4 %all-reduce.2.cloned.1.call-start = ((), (), s32[]{:S(2)}) async-start(), calls=%async_computation.1 | async-start | bytes 524288 | tf_op jit(solution)/shard_map/psum | solution.py:93
  68.5 0.7 copy-start.2
  204.3 92.3 %copy-start = (f32[1,256,256]{2,1,0:T(8,128)S(1)}, f32[1,256,256]{2,1,0:T(8,128)}, u32[]{:S(2)}) copy-start(f32[1,256,256]{2,1,0:T(8,128)} %param.12) | copy-start | bytes 786436
  211.8 85.6 %copy-start.1 = (f32[1,256,256]{2,1,0:T(8,128)S(1)}, f32[1,256,256]{2,1,0:T(8,128)}, u32[]{:S(2)}) copy-start(f32[1,256,256]{2,1,0:T(8,128)} %param.13) | copy-start | bytes 786436
Sparse Core Ops, SparseCore 0:
  12.3 101.8 all-gather.1
Sparse Core Ops, SparseCore 1:
  69.3 67.5 all-reduce.1
where the time goes:
time: 310 us; the launch traced here: 307 us
  matrix products  153 us (49%)
  waiting for transfers between devices  44.9 us (14%)
  loops' own time  42.8 us (14%)
  other arithmetic  36.4 us (12%)
  between operations  16.2 us (5%)
  local copies, waits for them, and re-layouts  13.6 us (4%)
    dot_general x31, matrix products, joined_forward(): return rescale_matrix(jnp.dot(earlier, later, precision=HIGH))  66.8 us
    dot_general x31, matrix products, joined_backward(): return rescale_matrix(jnp.dot(later, earlier, precision=HIGH))  60.1 us
    all_gather x1, waiting for transfers between devices, prefix(): pieces = lax.all_gather(value, axis)  44.9 us
    another operation x2, loops' own time, prefix(): return lax.fori_loop(0, count - 1, turn, running)  42.1 us
    dot_general x16, matrix products, add_block(): jnp.einsum('jra,jrb->jab', onehot[:-1], onehot[1:], preferred_element_typ...  26.4 us
    eq x16, other arithmetic, add_block(): onehot = (window[:, :, None] == levels).astype(jnp.bfloat16)  22.9 us
    rev x1, local copies, waits for them, and re-layouts, prefix(): pieces = pieces[::-1]  7.51 us
  transfers between devices with their start and end apart: 2, of which 1 were waited for; matrix products, arithmetic and copies ran while one was open for 64% of the time, Pallas kernels for 0%

commit v1 on v0

v1 whole, which is shorter than its diff:
```python
import functools

import jax
import jax.numpy as jnp
from jax import lax
from jax.experimental import pallas as pl
from jax.experimental.pallas import tpu as pltpu
from jax.sharding import PartitionSpec as P

step_size = 0.25
shift = 7.0
Y, Z, QUAD = 4, 8, 4
VMEM_LIMIT = 50 << 20


def place():
    dp, clique = (lax.axis_index("dp"), lax.axis_index("clique"))
    return (lax.rem(dp, 2), lax.div(clique, Z), lax.rem(clique, Z))


def along_clique(where):
    return [(y * Z + z, where(y, z)[0] * Z + where(y, z)[1]) for y in range(Y) for z in range(Z)]


def along_dp(where):
    return [(2 * x + c, 2 * where(x, c)[0] + where(x, c)[1]) for x in range(4) for c in range(2)]


def other_core(value):
    return lax.ppermute(value, "dp", along_dp(lambda x, c: (x, 1 - c)))


def in_quad(z, step):
    return z // QUAD * QUAD + (z + step) % QUAD


def split(value):
    high = value.astype(jnp.bfloat16)
    low = (value - high.astype(jnp.float32)).astype(jnp.bfloat16)
    return (high, low)


def product(left, right):
    left_high, left_low = split(left)
    right_high, right_low = split(right)
    dot = functools.partial(jnp.dot, preferred_element_type=jnp.float32)
    return dot(left_high, right_high) + (dot(left_high, right_low) + dot(left_low, right_high))


def diagonal(size):
    rows = lax.broadcasted_iota(jnp.int32, (size, size), 0)
    return rows == lax.broadcasted_iota(jnp.int32, (size, size), 1)


def as_column(row, eye):
    return jnp.sum(jnp.where(eye, row, 0.0), axis=1, keepdims=True)


def as_row(column, eye):
    return jnp.sum(jnp.where(eye, column, 0.0), axis=0, keepdims=True)


def row_times(row, matrix, eye):
    moved = jnp.sum(as_column(row, eye) * matrix, axis=0, keepdims=True)
    return moved / jnp.sum(moved, axis=1, keepdims=True)


def times_row(matrix, row, eye):
    moved = as_row(jnp.sum(matrix * row, axis=1, keepdims=True), eye)
    return moved / jnp.sum(moved, axis=1, keepdims=True)


def half_kernel(potential_ref, half_ref):
    core, _, _ = place()
    half = half_ref.shape[0]
    half_ref[...] = jnp.exp(potential_ref[pl.ds(core * half, half), :] - shift)


def put_halves(stack_ref, slot, mine_ref, theirs_ref, core):
    half = mine_ref.shape[0]
    stack_ref[slot, pl.ds(core * half, half), :] = mine_ref[...]
    stack_ref[slot, pl.ds((1 - core) * half, half), :] = theirs_ref[...]


def quad_kernel(potential_ref, a1, a2, a3, b1, b2, b3, quad_ref, product_ref, half_ref):
    core, _, z = place()
    mine = lax.rem(z, QUAD)
    half, size = half_ref.shape
    quad_ref[mine] = jnp.exp(potential_ref[...] - shift)
    for step, (own, sibling) in enumerate(((a1, b1), (a2, b2), (a3, b3)), 1):
        put_halves(quad_ref, lax.rem(mine + QUAD - step, QUAD), own, sibling, core)
    scale = 1.0 / size
    left = product(quad_ref[0], quad_ref[1]) * scale
    right = product(quad_ref[2], quad_ref[3]) * scale
    product_ref[...] = product(left, right) * scale
    half_ref[...] = product_ref[pl.ds(core * half, half), :]


def block_kernel(product_ref, a1, a2, a3, b1, b2, b3, block_ref, message_ref):
    core, y, z = place()
    mine = 2 * lax.rem(y, 2) + lax.div(z, QUAD)
    size = product_ref.shape[0]
    block_ref[mine] = product_ref[...]
    for flip, (own, sibling) in enumerate(((a1, b1), (a2, b2), (a3, b3)), 1):
        put_halves(block_ref, mine ^ flip, own, sibling, core)
    eye = diagonal(size)
    ones = jnp.ones((1, size), jnp.float32)

    @pl.when(y < 2)
    def _():
        row = ones
        for position in range(4):
            row = row_times(row, block_ref[position], eye)
        message_ref[...] = jnp.broadcast_to(row, message_ref.shape)

    @pl.when(y >= 2)
    def _():
        row = ones
        for position in range(4):
            row = times_row(block_ref[3 - position], row, eye)
        message_ref[...] = jnp.broadcast_to(row, message_ref.shape)


def final_kernel(
    scale, potential_ref, noise_ref, quad_ref, block_ref, message_ref, mine_ref, theirs_ref,
    updated_ref, beliefs_ref, counts_ref
):
    core, y, z = place()
    size = potential_ref.shape[0]
    half = mine_ref.shape[0]
    counts_ref[pl.ds(core * half, half), :] = mine_ref[...]
    counts_ref[pl.ds((1 - core) * half, half), :] = theirs_ref[...]
    eye = diagonal(size)
    ones = jnp.ones((1, size), jnp.float32)
    arrived = message_ref[0:1, :]
    in_block = 2 * lax.rem(y, 2) + lax.div(z, QUAD)
    mine = lax.rem(z, QUAD)
    forward = jnp.where(y >= 2, arrived, ones)
    backward = jnp.where(y >= 2, ones, arrived)
    forward = lax.fori_loop(
        0, in_block, lambda i, row: row_times(row, block_ref[i], eye), forward
    )
    forward = lax.fori_loop(0, mine, lambda i, row: row_times(row, quad_ref[i], eye), forward)
    backward = lax.fori_loop(
        0, 3 - in_block, lambda i, row: times_row(block_ref[3 - i], row, eye), backward
    )
    backward = lax.fori_loop(
        0, 3 - mine, lambda i, row: times_row(quad_ref[3 - i], row, eye), backward
    )
    joint = as_column(forward, eye) * quad_ref[mine] * backward
    total = jnp.sum(jnp.sum(joint, axis=0, keepdims=True), axis=1, keepdims=True)
    beliefs = joint * (size * size / total)
    beliefs_ref[...] = beliefs
    measured = (counts_ref[...] + noise_ref[...]) * scale
    updated_ref[...] = potential_ref[...] - step_size * (beliefs - measured)


def count_kernel(part, order_ref, left_ref, right_ref, mine_ref, theirs_ref, total_ref):
    core, y, z = place()
    clique = y * Z + z
    half, size = mine_ref.shape
    step = pl.program_id(0)

    @pl.when(step == 0)
    def _():
        total_ref[...] = jnp.zeros_like(total_ref)

    levels = lax.broadcasted_iota(jnp.int32, (size, part), 0).astype(jnp.bfloat16)
    one = jnp.ones((size, part), jnp.bfloat16)
    zero = jnp.zeros((size, part), jnp.bfloat16)

    def onehot(ref, attribute, begin):
        values = ref[pl.ds(lax.rem(attribute, 8), 1), begin : begin + part]
        values = values.astype(jnp.float32).astype(jnp.bfloat16)
        return jnp.where(values == levels, one, zero).astype(jnp.float8_e4m3fn)

    total = total_ref[...]
    for begin in range(0, left_ref.shape[1], part):
        total = total + lax.dot_general(
            onehot(left_ref, order_ref[clique], begin),
            onehot(right_ref, order_ref[clique + 1], begin),
            (((1,), (1,)), ((), ())),
            preferred_element_type=jnp.float32,
        )
    total_ref[...] = total

    @pl.when(step == pl.num_programs(0) - 1)
    def _():
        mine_ref[...] = total_ref[pl.ds(core * half, half), :]
        theirs_ref[...] = total_ref[pl.ds((1 - core) * half, half), :]


def shape(*dims):
    return jax.ShapeDtypeStruct(dims, jnp.float32)


PARAMS = pltpu.CompilerParams(vmem_limit_bytes=VMEM_LIMIT)


def count_halves(order, table_rows, size):
    window, part = 16384, 8192

    def rows_of(offset):
        def block(step, order_ref):
            return (lax.div(order_ref[lax.axis_index("clique") + offset], 8), step)

        return pl.BlockSpec((8, window), block)

    half = pl.BlockSpec((size // 2, size), lambda step, order_ref: (0, 0))
    return pl.pallas_call(
        functools.partial(count_kernel, part),
        out_shape=(shape(size // 2, size), shape(size // 2, size)),
        grid_spec=pltpu.PrefetchScalarGridSpec(
            num_scalar_prefetch=1,
            grid=(table_rows.shape[1] // window,),
            in_specs=[rows_of(0), rows_of(1)],
            out_specs=(half, half),
            scratch_shapes=[pltpu.VMEM((size, size), jnp.float32)],
        ),
        compiler_params=PARAMS,
        name="counts",
    )(order, table_rows, table_rows)


def per_device(table_rows, attribute_order, log_potential, measure_noise):
    size = log_potential.shape[1]
    potential = log_potential[0]
    call = functools.partial(pl.pallas_call, compiler_params=PARAMS)
    half = call(half_kernel, out_shape=shape(size // 2, size), name="half")(potential)
    quads = [
        lax.ppermute(half, "clique", along_clique(lambda y, z, s=s: (y, in_quad(z, s))))
        for s in (1, 2, 3)
    ]
    mine, theirs = count_halves(attribute_order, table_rows, size)
    sibling_quads = [other_core(value) for value in quads]
    quad, quad_product, half_product = call(
        quad_kernel,
        out_shape=(shape(QUAD, size, size), shape(size, size), shape(size // 2, size)),
        name="quad",
    )(potential, *quads, *sibling_quads)
    moves = (
        lambda y, z: (y, Z - 1 - z),
        lambda y, z: (y ^ 1, z),
        lambda y, z: (y ^ 1, Z - 1 - z),
    )
    blocks = [lax.ppermute(half_product, "clique", along_clique(move)) for move in moves]
    chip_counts = mine + other_core(theirs)
    spread = [
        lax.ppermute(chip_counts, "dp", along_dp(lambda x, c, s=s: ((x + s) % 4, c)))
        for s in (1, 2, 3)
    ]
    sibling_blocks = [other_core(value) for value in blocks]
    block, message = call(
        block_kernel, out_shape=(shape(4, size, size), shape(8, size)), name="block"
    )(quad_product, *blocks, *sibling_blocks)
    message = lax.ppermute(message, "clique", along_clique(lambda y, z: (y ^ 2, z)))
    counts = chip_counts + spread[0] + spread[1] + spread[2]
    sibling_counts = other_core(counts)
    total_rows = table_rows.shape[1] * lax.axis_size("dp")
    updated, beliefs = call(
        functools.partial(final_kernel, size * size / total_rows),
        out_shape=(shape(size, size), shape(size, size)),
        scratch_shapes=[pltpu.VMEM((size, size), jnp.float32)],
        name="final",
    )(potential, measure_noise[0], quad, block, message, counts, sibling_counts)
    return (updated[None], beliefs[None])


def solution(mesh):
    in_specs = (P(None, "dp"), P(), P("clique", None, None), P("clique", None, None))
    out_specs = (P("clique", None, None), P("clique", None, None))
    return jax.shard_map(
        per_device, mesh=mesh, in_specs=in_specs, out_specs=out_specs, check_vma=False
    )
```

time: 310 us -> 48.7 us (0.16)
  matrix products: 153 us -> 0 us
  loops' own time: 42.8 us -> 0 us
  waiting for transfers between devices: 44.9 us -> 7.29 us
  other arithmetic: 36.4 us -> 0.06 us
  starting transfers between devices: 0.08 us -> 26.2 us
  between operations: 16.2 us -> 0.72 us
  Pallas kernels: 0 us -> 12.7 us
  local copies, waits for them, and re-layouts: 13.6 us -> 1.61 us
    dot_general x78 -> x0, matrix products: 153 us -> none  [the longest x31 66.8 us: joined_forward(): return rescale_matrix(jnp.dot(earlier, later, precision=HIGH))]
    all_gather x1 -> x0, waiting for transfers between devices: 44.9 us -> none  [prefix(): pieces = lax.all_gather(value, axis)]
    another operation x3 -> x0, loops' own time: 42.8 us -> none  [the longest x2 42.1 us: prefix(): return lax.fori_loop(0, count - 1, turn, running)]
    ppermute x0 -> x18, starting transfers between devices: none -> 26.2 us  [the longest x8 8.37 us: other_core(): return lax.ppermute(value, 'dp', along_dp(lambda x, c: (x, 1 - c)))]
    eq x16 -> x0, other arithmetic: 22.9 us -> none  [add_block(): onehot = (window[:, :, None] == levels).astype(jnp.bfloat16)]
    pallas_call x0 -> x5, Pallas kernels: none -> 12.7 us  [the longest x1 8.6 us: count_halves(): pl.pallas_call(functools.partial(count_kernel, part), out_shape=(shape(si...]
    rev x1 -> x0, local copies, waits for them, and re-layouts: 7.51 us -> none  [prefix(): pieces = pieces[::-1]]
    ppermute x0 -> x18, waiting for transfers between devices: none -> 7.29 us  [the longest x3 4.73 us: per_device(): lax.ppermute(half_product, 'clique', along_clique(move))]
  transfers between devices with their start and end apart: 2 -> 18, of which waited for: 1 -> 5; matrix products, arithmetic and copies ran while one was open for 64% -> 0% of each run, Pallas kernels for 0% -> 21%
where the time goes in v1:
time: 48.7 us; the launch traced here: 48.6 us
  starting transfers between devices  26.2 us (54%)
  Pallas kernels  12.7 us (26%)
  waiting for transfers between devices  7.29 us (15%)
  local copies, waits for them, and re-layouts  1.61 us (3%)
  between operations  0.72 us (1%)
    pallas_call x1, Pallas kernels, count_halves(): pl.pallas_call(functools.partial(count_kernel, part), out_shape=(shape(si...  8.6 us
    ppermute x8, starting transfers between devices, other_core(): return lax.ppermute(value, 'dp', along_dp(lambda x, c: (x, 1 - c)))  8.37 us
    ppermute x3, starting transfers between devices, per_device(): lax.ppermute(half, 'clique', along_clique(lambda y, z, s=s: (y, in_quad(z...  6.26 us
    ppermute x3, waiting for transfers between devices, per_device(): lax.ppermute(half_product, 'clique', along_clique(move))  4.73 us
    ppermute x3, starting transfers between devices, per_device(): lax.ppermute(half_product, 'clique', along_clique(move))  4.54 us
    ppermute x3, starting transfers between devices, per_device(): lax.ppermute(chip_counts, 'dp', along_dp(lambda x, c, s=s: ((x + s) % 4,...  4.36 us
    ppermute x1, starting transfers between devices, per_device(): lax.ppermute(message, 'clique', along_clique(lambda y, z: (y ^ 2, z)))  2.66 us
    pallas_call x1, Pallas kernels, per_device(): call(functools.partial(final_kernel, size * size / total_rows), out_shape...  2.26 us
  transfers between devices with their start and end apart: 18, of which 5 were waited for; matrix products, arithmetic and copies ran while one was open for 0% of the time, Pallas kernels for 21%

profile of v1, /device:TPU:1, one launch (start us, length us, event | category | flops | bytes accessed | tf_op | source)
XLA Modules:
  0.0 48.6 jit_solution(1392891169558335462)
XLA Ops:
  0.6 0.0 copy-start
  0.6 0.9 %copy-done = f32[1,256,256]{2,1,0:T(8,128)S(1)} copy-done((f32[1,256,256]{2,1,0:T(8,128)S(1)}, f32[1,256,256]{2,1,0:T(8,128)}, u32[]{:S(2)}) %copy-start) | copy-done | bytes 262168
  1.6 0.0 copy-start.1
  1.6 0.0 copy-start.2
  1.6 2.5 %collective-permute-start = (f32[128,256]{1,0:T(8,128)S(1)}, f32[128,256]{1,0:T(8,128)S(1)}, u32[]{:S(2)}, u32[]{:S(2)}) collective-permute-start(f32[128,256]{1,0:T(8,128)S(1)} %half.1), channel_id=1, source_target_pairs={{0,1},{1,2},{2,3},{3,0},{4,5},{5,6},{6,7},{7,4},{8,9},{9,10},{10,1... | collective-permute-start | bytes 393224 | tf_op jit(solution)/shard_map/ppermute | solution.py:231
  4.2 3.0 %collective-permute-start.1 = (f32[128,256]{1,0:T(8,128)S(1)}, f32[128,256]{1,0:T(8,128)S(1)}, u32[]{:S(2)}, u32[]{:S(2)}) collective-permute-start(f32[128,256]{1,0:T(8,128)S(1)} %half.1), channel_id=1, source_target_pairs={{0,2},{1,3},{2,0},{3,1},{4,6},{5,7},{6,4},{7,5},{8,10},{9,11},{10,... | collective-permute-start | bytes 393224 | tf_op jit(solution)/shard_map/ppermute | solution.py:231
  7.2 0.7 %collective-permute-start.2 = (f32[128,256]{1,0:T(8,128)S(1)}, f32[128,256]{1,0:T(8,128)S(1)}, u32[]{:S(2)}, u32[]{:S(2)}) collective-permute-start(f32[128,256]{1,0:T(8,128)S(1)} %half.1), channel_id=1, source_target_pairs={{0,3},{1,0},{2,1},{3,2},{4,7},{5,4},{6,5},{7,6},{8,11},{9,8},{10,9... | collective-permute-start | bytes 393224 | tf_op jit(solution)/shard_map/ppermute | solution.py:231
  7.9 0.0 copy-start.3
  7.9 0.7 %copy-done.3 = s32[33]{0:T(128)S(1)} copy-done((s32[33]{0:T(128)S(1)}, s32[33]{0:T(128)}, u32[]{:S(2)}) %copy-start.3) | copy-done | bytes 156
  8.6 8.6 %counts.1 = (f32[128,256]{1,0:T(8,128)S(1)}, f32[128,256]{1,0:T(8,128)S(1)}) custom-call(s32[33]{0:T(128)S(1)} %copy-done.3, s32[33,65536]{1,0:T(8,128)} %right_ref.1, s32[33,65536]{1,0:T(8,128)} %right_ref.1), custom_call_target="tpu_custom_call" | custom-call | tf_op jit(solution)/shard_map/counts/pallas_call | solution.py:210
  17.2 1.6 %collective-permute-start.13 = (f32[128,256]{1,0:T(8,128)S(1)}, f32[128,256]{1,0:T(8,128)S(1)}, u32[]{:S(2)}, u32[]{:S(2)}) collective-permute-start(f32[128,256]{1,0:T(8,128)S(1)} %get-tuple-element.17), channel_id=1, source_target_pairs={{0,32},{32,0},{64,96},{96,64},{128,160},{160,128},{192,224},{224,1... | collective-permute-start | bytes 393224 | tf_op jit(solution)/shard_map/ppermute | solution.py:30
  18.8 0.0 collective-permute-done.a1
  18.8 0.1 collective-permute-start.3
  18.9 0.0 collective-permute-done.1.a2
  18.9 0.4 collective-permute-start.4
  19.3 0.0 collective-permute-done.2.a3
  19.3 0.1 collective-permute-start.5
  19.4 0.4 collective-permute-done.13
  19.8 2.6 %collective-permute-start.16 = (f32[128,256]{1,0:T(8,128)S(1)}, f32[128,256]{1,0:T(8,128)S(1)}, u32[]{:S(2)}, u32[]{:S(2)}) collective-permute-start(f32[128,256]{1,0:T(8,128)S(1)} %add.12), channel_id=1, source_target_pairs={{0,192},{32,224},{64,0},{96,32},{128,64},{160,96},{192,128},{224,1... | collective-permute-start | bytes 393224 | tf_op jit(solution)/shard_map/ppermute | solution.py:249
  22.3 0.0 collective-permute-done.3.b1
  22.3 0.0 collective-permute-done.4.b2
  22.3 0.0 collective-permute-done.5.b3
  22.3 0.0 copy-done.1
  22.4 1.0 %quad.1 = (f32[4,256,256]{2,1,0:T(8,128)S(1)}, f32[256,256]{1,0:T(8,128)S(1)}, f32[128,256]{1,0:T(8,128)S(1)}) custom-call(f32[256,256]{1,0:T(8,128)S(1)} %bitcast.5, f32[128,256]{1,0:T(8,128)S(1)} %collective-permute-done.a1, f32[128,256]{1,0:T(8,128)S(1)} %collective-permute-done.1.a2, f32[128,256]{1,0:T(8,128)S(1)} %collective-permute-done.2.a3, ...), custom_call_target="tpu_custom_call" | custom-call | tf_op jit(solution)/shard_map/quad/pallas_call | solution.py:236
  23.3 3.2 %collective-permute-start.6 = (f32[128,256]{1,0:T(8,128)S(1)}, f32[128,256]{1,0:T(8,128)S(1)}, u32[]{:S(2)}, u32[]{:S(2)}) collective-permute-start(f32[128,256]{1,0:T(8,128)S(1)} %get-tuple-element.13), channel_id=1, source_target_pairs={{0,7},{1,6},{2,5},{3,4},{4,3},{5,2},{6,1},{7,0},{8,15},{9,14},{10,... | collective-permute-start | bytes 393224 | tf_op jit(solution)/shard_map/ppermute | solution.py:246
  26.6 1.3 %collective-permute-start.7 = (f32[128,256]{1,0:T(8,128)S(1)}, f32[128,256]{1,0:T(8,128)S(1)}, u32[]{:S(2)}, u32[]{:S(2)}) collective-permute-start(f32[128,256]{1,0:T(8,128)S(1)} %get-tuple-element.13), channel_id=1, source_target_pairs={{0,8},{1,9},{2,10},{3,11},{4,12},{5,13},{6,14},{7,15},{8,0},{9,1},... | collective-permute-start | bytes 393224 | tf_op jit(solution)/shard_map/ppermute | solution.py:246
  27.9 0.0 collective-permute-start.8
  27.9 1.5 %collective-permute-start.15 = (f32[128,256]{1,0:T(8,128)S(1)}, f32[128,256]{1,0:T(8,128)S(1)}, u32[]{:S(2)}, u32[]{:S(2)}) collective-permute-start(f32[128,256]{1,0:T(8,128)S(1)} %add.12), channel_id=1, source_target_pairs={{0,128},{32,160},{64,192},{96,224},{128,0},{160,32},{192,64},{224,... | collective-permute-start | bytes 393224 | tf_op jit(solution)/shard_map/ppermute | solution.py:249
  29.4 0.0 collective-permute-done.16
  29.4 0.3 collective-permute-start.14
  29.7 2.8 %collective-permute-done.6.a1 = f32[128,256]{1,0:T(8,128)S(1)} collective-permute-done((f32[128,256]{1,0:T(8,128)S(1)}, f32[128,256]{1,0:T(8,128)S(1)}, u32[]{:S(2)}, u32[]{:S(2)}) %collective-permute-start.6) | collective-permute-done | bytes 131104 | tf_op jit(solution)/shard_map/ppermute | solution.py:246
  32.5 4.7 %collective-permute-start.9 = (f32[128,256]{1,0:T(8,128)S(1)}, f32[128,256]{1,0:T(8,128)S(1)}, u32[]{:S(2)}, u32[]{:S(2)}) collective-permute-start(f32[128,256]{1,0:T(8,128)S(1)} %collective-permute-done.6.a1), channel_id=1, source_target_pairs={{0,32},{32,0},{64,96},{96,64},{128,160},{160,128},{192,224},{224,1... | collective-permute-start | bytes 393224 | tf_op jit(solution)/shard_map/ppermute | solution.py:30
  37.2 0.0 collective-permute-done.7.a2
  37.2 0.0 collective-permute-start.10
  37.2 1.9 %collective-permute-done.8.a3 = f32[128,256]{1,0:T(8,128)S(1)} collective-permute-done((f32[128,256]{1,0:T(8,128)S(1)}, f32[128,256]{1,0:T(8,128)S(1)}, u32[]{:S(2)}, u32[]{:S(2)}) %collective-permute-start.8) | collective-permute-done | bytes 131104 | tf_op jit(solution)/shard_map/ppermute | solution.py:246
  39.1 1.4 %collective-permute-start.11 = (f32[128,256]{1,0:T(8,128)S(1)}, f32[128,256]{1,0:T(8,128)S(1)}, u32[]{:S(2)}, u32[]{:S(2)}) collective-permute-start(f32[128,256]{1,0:T(8,128)S(1)} %collective-permute-done.8.a3), channel_id=1, source_target_pairs={{0,32},{32,0},{64,96},{96,64},{128,160},{160,128},{192,224},{224,1... | collective-permute-start | bytes 393224 | tf_op jit(solution)/shard_map/ppermute | solution.py:30
  40.5 0.0 collective-permute-done.15
  40.5 0.0 collective-permute-done.14
  40.5 0.1 collective-permute-start.17
  40.6 0.0 collective-permute-done.9.b1
  40.6 0.0 collective-permute-done.10.b2
  40.6 0.8 %collective-permute-done.11.b3 = f32[128,256]{1,0:T(8,128)S(1)} collective-permute-done((f32[128,256]{1,0:T(8,128)S(1)}, f32[128,256]{1,0:T(8,128)S(1)}, u32[]{:S(2)}, u32[]{:S(2)}) %collective-permute-start.11) | collective-permute-done | bytes 131104 | tf_op jit(solution)/shard_map/ppermute | solution.py:30
  41.4 0.9 %block.1 = (f32[4,256,256]{2,1,0:T(8,128)S(1)}, f32[8,256]{1,0:T(8,128)S(1)}) custom-call(f32[256,256]{1,0:T(8,128)S(1)} %get-tuple-element.12.product_ref, f32[128,256]{1,0:T(8,128)S(1)} %collective-permute-done.6.a1, f32[128,256]{1,0:T(8,128)S(1)} %collective-permute-done.7.a2, f32[128,256]{1,0:T(8,128)S(1)} %collective-permute-done.8.a3, ...), custom_call_target="tpu_custom_call" | custom-call | tf_op jit(solution)/shard_map/block/pallas_call | solution.py:253
  42.3 2.7 %collective-permute-start.12 = (f32[8,256]{1,0:T(8,128)S(1)}, f32[8,256]{1,0:T(8,128)S(1)}, u32[]{:S(2)}, u32[]{:S(2)}) collective-permute-start(f32[8,256]{1,0:T(8,128)S(1)} %get-tuple-element.15), channel_id=1, source_target_pairs={{0,16},{1,17},{2,18},{3,19},{4,20},{5,21},{6,22},{7,23},{8,24},{9,... | collective-permute-start | bytes 24584 | tf_op jit(solution)/shard_map/ppermute | solution.py:256
  45.0 0.0 collective-permute-done.17.theirs_ref
  45.0 1.4 %collective-permute-done.12.message_ref = f32[8,256]{1,0:T(8,128)S(1)} collective-permute-done((f32[8,256]{1,0:T(8,128)S(1)}, f32[8,256]{1,0:T(8,128)S(1)}, u32[]{:S(2)}, u32[]{:S(2)}) %collective-permute-start.12) | collective-permute-done | bytes 8224 | tf_op jit(solution)/shard_map/ppermute | solution.py:256
  46.3 0.0 copy-done.2
  46.3 2.3 %final.1 = (f32[256,256]{1,0:T(8,128)}, f32[256,256]{1,0:T(8,128)}) custom-call(f32[256,256]{1,0:T(8,128)S(1)} %bitcast.6, f32[256,256]{1,0:T(8,128)S(1)} %bitcast.7, f32[4,256,256]{2,1,0:T(8,128)S(1)} %get-tuple-element.11.quad_ref, f32[4,256,256]{2,1,0:T(8,128)S(1)} %get-tuple-element.14.block_ref, f32[8,256]{1,0:T(8,128)S(1)} %collective-permute-done.12.message_ref, ...), custom_call_target="tpu_custom_call" | custom-call | tf_op jit(solution)/shard_map/final/pallas_call | solution.py:260
  (3 shorter events, 0.1 us)
Async XLA Ops:
  0.6 1.0 %copy-start = (f32[1,256,256]{2,1,0:T(8,128)S(1)}, f32[1,256,256]{2,1,0:T(8,128)}, u32[]{:S(2)}) copy-start(f32[1,256,256]{2,1,0:T(8,128)} %param.6) | copy-start | bytes 786436
  1.6 20.7 %copy-start.1 = (f32[1,256,256]{2,1,0:T(8,128)S(1)}, f32[1,256,256]{2,1,0:T(8,128)}, u32[]{:S(2)}) copy-start(f32[1,256,256]{2,1,0:T(8,128)} %param.6) | copy-start | bytes 786436
  1.6 44.7 %copy-start.2 = (f32[1,256,256]{2,1,0:T(8,128)S(1)}, f32[1,256,256]{2,1,0:T(8,128)}, u32[]{:S(2)}) copy-start(f32[1,256,256]{2,1,0:T(8,128)} %param.7) | copy-start | bytes 786436
  1.6 17.1 %collective-permute-start = (f32[128,256]{1,0:T(8,128)S(1)}, f32[128,256]{1,0:T(8,128)S(1)}, u32[]{:S(2)}, u32[]{:S(2)}) collective-permute-start(f32[128,256]{1,0:T(8,128)S(1)} %half.1), channel_id=1, source_target_pairs={{0,1},{1,2},{2,3},{3,0},{4,5},{5,6},{6,7},{7,4},{8,9},{9,10},{10,1... | collective-permute-start | bytes 393224 | tf_op jit(solution)/shard_map/ppermute | solution.py:231
  4.2 14.7 %collective-permute-start.1 = (f32[128,256]{1,0:T(8,128)S(1)}, f32[128,256]{1,0:T(8,128)S(1)}, u32[]{:S(2)}, u32[]{:S(2)}) collective-permute-start(f32[128,256]{1,0:T(8,128)S(1)} %half.1), channel_id=1, source_target_pairs={{0,2},{1,3},{2,0},{3,1},{4,6},{5,7},{6,4},{7,5},{8,10},{9,11},{10,... | collective-permute-start | bytes 393224 | tf_op jit(solution)/shard_map/ppermute | solution.py:231
  7.2 12.1 %collective-permute-start.2 = (f32[128,256]{1,0:T(8,128)S(1)}, f32[128,256]{1,0:T(8,128)S(1)}, u32[]{:S(2)}, u32[]{:S(2)}) collective-permute-start(f32[128,256]{1,0:T(8,128)S(1)} %half.1), channel_id=1, source_target_pairs={{0,3},{1,0},{2,1},{3,2},{4,7},{5,4},{6,5},{7,6},{8,11},{9,8},{10,9... | collective-permute-start | bytes 393224 | tf_op jit(solution)/shard_map/ppermute | solution.py:231
  7.9 0.7 %copy-start.3 = (s32[33]{0:T(128)S(1)}, s32[33]{0:T(128)}, u32[]{:S(2)}) copy-start(s32[33]{0:T(128)} %order_ref.1) | copy-start | bytes 400
  17.2 2.6 %collective-permute-start.13 = (f32[128,256]{1,0:T(8,128)S(1)}, f32[128,256]{1,0:T(8,128)S(1)}, u32[]{:S(2)}, u32[]{:S(2)}) collective-permute-start(f32[128,256]{1,0:T(8,128)S(1)} %get-tuple-element.17), channel_id=1, source_target_pairs={{0,32},{32,0},{64,96},{96,64},{128,160},{160,128},{192,224},{224,1... | collective-permute-start | bytes 393224 | tf_op jit(solution)/shard_map/ppermute | solution.py:30
  18.8 3.6 %collective-permute-start.3 = (f32[128,256]{1,0:T(8,128)S(1)}, f32[128,256]{1,0:T(8,128)S(1)}, u32[]{:S(2)}, u32[]{:S(2)}) collective-permute-start(f32[128,256]{1,0:T(8,128)S(1)} %collective-permute-done.a1), channel_id=1, source_target_pairs={{0,32},{32,0},{64,96},{96,64},{128,160},{160,128},{192,224},{224,1... | collective-permute-start | bytes 393224 | tf_op jit(solution)/shard_map/ppermute | solution.py:30
  18.9 3.5 %collective-permute-start.4 = (f32[128,256]{1,0:T(8,128)S(1)}, f32[128,256]{1,0:T(8,128)S(1)}, u32[]{:S(2)}, u32[]{:S(2)}) collective-permute-start(f32[128,256]{1,0:T(8,128)S(1)} %collective-permute-done.1.a2), channel_id=1, source_target_pairs={{0,32},{32,0},{64,96},{96,64},{128,160},{160,128},{192,224},{224,1... | collective-permute-start | bytes 393224 | tf_op jit(solution)/shard_map/ppermute | solution.py:30
  19.3 3.1 %collective-permute-start.5 = (f32[128,256]{1,0:T(8,128)S(1)}, f32[128,256]{1,0:T(8,128)S(1)}, u32[]{:S(2)}, u32[]{:S(2)}) collective-permute-start(f32[128,256]{1,0:T(8,128)S(1)} %collective-permute-done.2.a3), channel_id=1, source_target_pairs={{0,32},{32,0},{64,96},{96,64},{128,160},{160,128},{192,224},{224,1... | collective-permute-start | bytes 393224 | tf_op jit(solution)/shard_map/ppermute | solution.py:30
  19.8 9.6 %collective-permute-start.16 = (f32[128,256]{1,0:T(8,128)S(1)}, f32[128,256]{1,0:T(8,128)S(1)}, u32[]{:S(2)}, u32[]{:S(2)}) collective-permute-start(f32[128,256]{1,0:T(8,128)S(1)} %add.12), channel_id=1, source_target_pairs={{0,192},{32,224},{64,0},{96,32},{128,64},{160,96},{192,128},{224,1... | collective-permute-start | bytes 393224 | tf_op jit(solution)/shard_map/ppermute | solution.py:249
  23.3 9.1 %collective-permute-start.6 = (f32[128,256]{1,0:T(8,128)S(1)}, f32[128,256]{1,0:T(8,128)S(1)}, u32[]{:S(2)}, u32[]{:S(2)}) collective-permute-start(f32[128,256]{1,0:T(8,128)S(1)} %get-tuple-element.13), channel_id=1, source_target_pairs={{0,7},{1,6},{2,5},{3,4},{4,3},{5,2},{6,1},{7,0},{8,15},{9,14},{10,... | collective-permute-start | bytes 393224 | tf_op jit(solution)/shard_map/ppermute | solution.py:246
  26.6 10.6 %collective-permute-start.7 = (f32[128,256]{1,0:T(8,128)S(1)}, f32[128,256]{1,0:T(8,128)S(1)}, u32[]{:S(2)}, u32[]{:S(2)}) collective-permute-start(f32[128,256]{1,0:T(8,128)S(1)} %get-tuple-element.13), channel_id=1, source_target_pairs={{0,8},{1,9},{2,10},{3,11},{4,12},{5,13},{6,14},{7,15},{8,0},{9,1},... | collective-permute-start | bytes 393224 | tf_op jit(solution)/shard_map/ppermute | solution.py:246
  27.9 11.2 %collective-permute-start.8 = (f32[128,256]{1,0:T(8,128)S(1)}, f32[128,256]{1,0:T(8,128)S(1)}, u32[]{:S(2)}, u32[]{:S(2)}) collective-permute-start(f32[128,256]{1,0:T(8,128)S(1)} %get-tuple-element.13), channel_id=1, source_target_pairs={{0,15},{1,14},{2,13},{3,12},{4,11},{5,10},{6,9},{7,8},{8,7},{9,6},... | collective-permute-start | bytes 393224 | tf_op jit(solution)/shard_map/ppermute | solution.py:246
  27.9 12.6 %collective-permute-start.15 = (f32[128,256]{1,0:T(8,128)S(1)}, f32[128,256]{1,0:T(8,128)S(1)}, u32[]{:S(2)}, u32[]{:S(2)}) collective-permute-start(f32[128,256]{1,0:T(8,128)S(1)} %add.12), channel_id=1, source_target_pairs={{0,128},{32,160},{64,192},{96,224},{128,0},{160,32},{192,64},{224,... | collective-permute-start | bytes 393224 | tf_op jit(solution)/shard_map/ppermute | solution.py:249
  29.4 11.1 %collective-permute-start.14 = (f32[128,256]{1,0:T(8,128)S(1)}, f32[128,256]{1,0:T(8,128)S(1)}, u32[]{:S(2)}, u32[]{:S(2)}) collective-permute-start(f32[128,256]{1,0:T(8,128)S(1)} %add.12), channel_id=1, source_target_pairs={{0,64},{32,96},{64,128},{96,160},{128,192},{160,224},{192,0},{224,... | collective-permute-start | bytes 393224 | tf_op jit(solution)/shard_map/ppermute | solution.py:249
  32.5 8.1 %collective-permute-start.9 = (f32[128,256]{1,0:T(8,128)S(1)}, f32[128,256]{1,0:T(8,128)S(1)}, u32[]{:S(2)}, u32[]{:S(2)}) collective-permute-start(f32[128,256]{1,0:T(8,128)S(1)} %collective-permute-done.6.a1), channel_id=1, source_target_pairs={{0,32},{32,0},{64,96},{96,64},{128,160},{160,128},{192,224},{224,1... | collective-permute-start | bytes 393224 | tf_op jit(solution)/shard_map/ppermute | solution.py:30
  37.2 3.5 %collective-permute-start.10 = (f32[128,256]{1,0:T(8,128)S(1)}, f32[128,256]{1,0:T(8,128)S(1)}, u32[]{:S(2)}, u32[]{:S(2)}) collective-permute-start(f32[128,256]{1,0:T(8,128)S(1)} %collective-permute-done.7.a2), channel_id=1, source_target_pairs={{0,32},{32,0},{64,96},{96,64},{128,160},{160,128},{192,224},{224,1... | collective-permute-start | bytes 393224 | tf_op jit(solution)/shard_map/ppermute | solution.py:30
  39.1 2.3 %collective-permute-start.11 = (f32[128,256]{1,0:T(8,128)S(1)}, f32[128,256]{1,0:T(8,128)S(1)}, u32[]{:S(2)}, u32[]{:S(2)}) collective-permute-start(f32[128,256]{1,0:T(8,128)S(1)} %collective-permute-done.8.a3), channel_id=1, source_target_pairs={{0,32},{32,0},{64,96},{96,64},{128,160},{160,128},{192,224},{224,1... | collective-permute-start | bytes 393224 | tf_op jit(solution)/shard_map/ppermute | solution.py:30
  40.5 4.5 %collective-permute-start.17 = (f32[128,256]{1,0:T(8,128)S(1)}, f32[128,256]{1,0:T(8,128)S(1)}, u32[]{:S(2)}, u32[]{:S(2)}) collective-permute-start(f32[128,256]{1,0:T(8,128)S(1)} %add_add_fusion.mine_ref), channel_id=1, source_target_pairs={{0,32},{32,0},{64,96},{96,64},{128,160},{160,128},{192,224},{224,1... | collective-permute-start | bytes 393224 | tf_op jit(solution)/shard_map/ppermute | solution.py:30
  42.3 4.0 %collective-permute-start.12 = (f32[8,256]{1,0:T(8,128)S(1)}, f32[8,256]{1,0:T(8,128)S(1)}, u32[]{:S(2)}, u32[]{:S(2)}) collective-permute-start(f32[8,256]{1,0:T(8,128)S(1)} %get-tuple-element.15), channel_id=1, source_target_pairs={{0,16},{1,17},{2,18},{3,19},{4,20},{5,21},{6,22},{7,23},{8,24},{9,... | collective-permute-start | bytes 24584 | tf_op jit(solution)/shard_map/ppermute | solution.py:256

commit v2 on v1

v2 whole, which is shorter than its diff:
```python
import functools

import jax
import jax.numpy as jnp
from jax import lax
from jax.experimental import pallas as pl
from jax.experimental.pallas import tpu as pltpu
from jax.sharding import PartitionSpec as P

step_size = 0.25
shift = 7.0
Y, Z, QUAD = 4, 8, 4
VMEM_LIMIT = 50 << 20


def place():
    dp, clique = (lax.axis_index("dp"), lax.axis_index("clique"))
    return (lax.rem(dp, 2), lax.div(clique, Z), lax.rem(clique, Z))


def along_clique(where):
    return [(y * Z + z, where(y, z)[0] * Z + where(y, z)[1]) for y in range(Y) for z in range(Z)]


def along_dp(where):
    return [(2 * x + c, 2 * where(x, c)[0] + where(x, c)[1]) for x in range(4) for c in range(2)]


def other_core(value):
    return lax.ppermute(value, "dp", along_dp(lambda x, c: (x, 1 - c)))


def in_quad(z, step):
    return z // QUAD * QUAD + (z + step) % QUAD


def split(value):
    high = value.astype(jnp.bfloat16)
    low = (value - high.astype(jnp.float32)).astype(jnp.bfloat16)
    return (high, low)


def product(left, right):
    left_high, left_low = split(left)
    right_high, right_low = split(right)
    dot = functools.partial(jnp.dot, preferred_element_type=jnp.float32)
    return dot(left_high, right_high) + (dot(left_high, right_low) + dot(left_low, right_high))


def diagonal(size):
    rows = lax.broadcasted_iota(jnp.int32, (size, size), 0)
    return rows == lax.broadcasted_iota(jnp.int32, (size, size), 1)


def as_column(row, eye):
    return jnp.sum(jnp.where(eye, row, 0.0), axis=1, keepdims=True)


def as_row(column, eye):
    return jnp.sum(jnp.where(eye, column, 0.0), axis=0, keepdims=True)


def row_times(row, matrix, eye):
    moved = jnp.sum(as_column(row, eye) * matrix, axis=0, keepdims=True)
    return moved / jnp.sum(moved, axis=1, keepdims=True)


def times_row(matrix, row, eye):
    moved = as_row(jnp.sum(matrix * row, axis=1, keepdims=True), eye)
    return moved / jnp.sum(moved, axis=1, keepdims=True)


def half_kernel(order_ref, potential_ref, order_out_ref, half_ref, copied_ref, semaphore):
    core, _, _ = place()
    half = half_ref.shape[0]
    copy = pltpu.make_async_copy(
        potential_ref.at[pl.ds(core * half, half), :], copied_ref, semaphore
    )
    copy.start()
    order_out_ref[...] = order_ref[...]
    copy.wait()
    half_ref[...] = jnp.exp(copied_ref[...] - shift)


def put_halves(stack_ref, slot, mine_ref, theirs_ref, core):
    half = mine_ref.shape[0]
    stack_ref[slot, pl.ds(core * half, half), :] = mine_ref[...]
    stack_ref[slot, pl.ds((1 - core) * half, half), :] = theirs_ref[...]


def quad_kernel(potential_ref, a1, a2, a3, b1, b2, b3, quad_ref, product_ref, half_ref):
    core, _, z = place()
    mine = lax.rem(z, QUAD)
    half, size = half_ref.shape
    quad_ref[mine] = jnp.exp(potential_ref[...] - shift)
    for step, (own, sibling) in enumerate(((a1, b1), (a2, b2), (a3, b3)), 1):
        put_halves(quad_ref, lax.rem(mine + QUAD - step, QUAD), own, sibling, core)
    scale = 1.0 / size
    left = product(quad_ref[0], quad_ref[1]) * scale
    right = product(quad_ref[2], quad_ref[3]) * scale
    whole = product(left, right) * scale
    largest = jnp.max(jnp.max(whole, axis=0, keepdims=True), axis=1, keepdims=True)
    product_ref[...] = whole / largest
    half_ref[...] = product_ref[pl.ds(core * half, half), :]


def octet_kernel(product_ref, own_ref, sibling_ref, other_ref, half_ref):
    core, _, z = place()
    half = half_ref.shape[0]
    rows = pl.ds(core * half, half)
    other_ref[rows, :] = own_ref[...]
    other_ref[pl.ds((1 - core) * half, half), :] = sibling_ref[...]

    @pl.when(z < QUAD)
    def _():
        half_ref[...] = product(product_ref[rows, :], other_ref[...])

    @pl.when(z >= QUAD)
    def _():
        half_ref[...] = product(other_ref[rows, :], product_ref[...])


def final_kernel(
    scale, potential_ref, noise_ref, quad_ref, other_ref, a1, a2, a3, b1, b2, b3, mine_ref, theirs_ref,
    updated_ref, beliefs_ref, octet_ref
):
    core, y, z = place()
    size = potential_ref.shape[0]
    half = mine_ref.shape[0]
    for step, (own, sibling) in enumerate(((a1, b1), (a2, b2), (a3, b3)), 1):
        put_halves(octet_ref, lax.rem(y + Y - step, Y), own, sibling, core)
    eye = diagonal(size)
    ones = jnp.ones((1, size), jnp.float32)
    later_quad = lax.div(z, QUAD)
    mine = lax.rem(z, QUAD)
    forward = lax.fori_loop(0, y, lambda i, row: row_times(row, octet_ref[i], eye), ones)
    forward = lax.fori_loop(
        0, later_quad, lambda i, row: row_times(row, other_ref[...], eye), forward
    )
    forward = lax.fori_loop(0, mine, lambda i, row: row_times(row, quad_ref[i], eye), forward)
    backward = lax.fori_loop(
        0, Y - 1 - y, lambda i, row: times_row(octet_ref[Y - 1 - i], row, eye), ones
    )
    backward = lax.fori_loop(
        0, 1 - later_quad, lambda i, row: times_row(other_ref[...], row, eye), backward
    )
    backward = lax.fori_loop(
        0, 3 - mine, lambda i, row: times_row(quad_ref[3 - i], row, eye), backward
    )
    joint = as_column(forward, eye) * quad_ref[mine] * backward
    total = jnp.sum(jnp.sum(joint, axis=0, keepdims=True), axis=1, keepdims=True)
    beliefs_ref[...] = joint * (size * size / total)
    for place_at, counts_ref in ((core, mine_ref), (1 - core, theirs_ref)):
        rows = pl.ds(place_at * half, half)
        measured = (counts_ref[...] + noise_ref[rows, :]) * scale
        updated_ref[rows, :] = potential_ref[rows, :] - step_size * (beliefs_ref[rows, :] - measured)


def count_kernel(part, order_ref, left_ref, right_ref, *refs):
    _, y, z = place()
    clique = y * Z + z
    step = pl.program_id(0)
    total_ref = refs[-1]
    size = total_ref.shape[0]

    @pl.when(step == 0)
    def _():
        total_ref[...] = refs[0][...] if len(refs) > 2 else jnp.zeros_like(total_ref)

    levels = lax.broadcasted_iota(jnp.int32, (size, part), 0).astype(jnp.bfloat16)
    one = jnp.ones((size, part), jnp.bfloat16)
    zero = jnp.zeros((size, part), jnp.bfloat16)

    def onehot(ref, attribute, begin):
        values = ref[pl.ds(lax.rem(attribute, 8), 1), begin : begin + part]
        values = values.astype(jnp.float32).astype(jnp.bfloat16)
        return jnp.where(values == levels, one, zero).astype(jnp.float8_e4m3fn)

    total = total_ref[...]
    for begin in range(0, left_ref.shape[1], part):
        total = total + lax.dot_general(
            onehot(left_ref, order_ref[clique], begin),
            onehot(right_ref, order_ref[clique + 1], begin),
            (((1,), (1,)), ((), ())),
            preferred_element_type=jnp.float32,
        )
    total_ref[...] = total

    if len(refs) > 2:

        @pl.when(step == pl.num_programs(0) - 1)
        def _():
            core, _, _ = place()
            mine_ref, theirs_ref = refs[1:3]
            half = size // 2
            mine_ref[...] = total_ref[pl.ds(core * half, half), :]
            theirs_ref[...] = total_ref[pl.ds((1 - core) * half, half), :]


def shape(*dims):
    return jax.ShapeDtypeStruct(dims, jnp.float32)


PARAMS = pltpu.CompilerParams(vmem_limit_bytes=VMEM_LIMIT)


def count_rows(order, table_rows, size, first, last, window, part, earlier=None):
    def rows_of(offset):
        def block(step, order_ref):
            return (lax.div(order_ref[lax.axis_index("clique") + offset], 8), first + step)

        return pl.BlockSpec((8, window), block)

    half = pl.BlockSpec((size // 2, size), lambda step, order_ref: (0, 0))
    whole = pl.BlockSpec((size, size), lambda step, order_ref: (0, 0))
    resumed = earlier is not None
    return pl.pallas_call(
        functools.partial(count_kernel, part),
        out_shape=(shape(size // 2, size),) * 2 if resumed else shape(size, size),
        grid_spec=pltpu.PrefetchScalarGridSpec(
            num_scalar_prefetch=1,
            grid=(last - first,),
            in_specs=[rows_of(0), rows_of(1)] + [whole] * resumed,
            out_specs=(half, half) if resumed else whole,
            scratch_shapes=[pltpu.VMEM((size, size), jnp.float32)] * resumed,
        ),
        compiler_params=PARAMS,
        name="counts",
    )(order, table_rows, table_rows, *((earlier,) if resumed else ()))


def per_device(table_rows, attribute_order, log_potential, measure_noise):
    size = log_potential.shape[1]
    potential = log_potential[0]
    call = functools.partial(pl.pallas_call, compiler_params=PARAMS)
    vmem = pl.BlockSpec(memory_space=pltpu.VMEM)
    order, half = call(
        half_kernel,
        in_specs=[vmem, pl.BlockSpec(memory_space=pl.ANY)],
        out_specs=(vmem, vmem),
        out_shape=(jax.ShapeDtypeStruct(attribute_order.shape, jnp.int32), shape(size // 2, size)),
        scratch_shapes=[pltpu.VMEM((size // 2, size), jnp.float32), pltpu.SemaphoreType.DMA],
        name="half",
    )(attribute_order, potential)
    quads = [
        lax.ppermute(half, "clique", along_clique(lambda y, z, s=s: (y, in_quad(z, s))))
        for s in (1, 2, 3)
    ]
    window, part = 16384, 8192
    windows = table_rows.shape[1] // window
    first_part = windows // 2
    early = count_rows(order, table_rows, size, 0, first_part, window, part)
    quads, early = lax.optimization_barrier((quads, early))
    sibling_quads = [other_core(value) for value in quads]
    quad, quad_product, half_product = call(
        quad_kernel,
        out_shape=(shape(QUAD, size, size), shape(size, size), shape(size // 2, size)),
        name="quad",
    )(potential, *quads, *sibling_quads)
    other = lax.ppermute(half_product, "clique", along_clique(lambda y, z: (y, Z - 1 - z)))
    early, quad_product = lax.optimization_barrier((early, quad_product))
    mine, theirs = count_rows(
        order, table_rows, size, first_part, windows, window, part, early
    )
    other, mine, theirs = lax.optimization_barrier((other, mine, theirs))
    sibling_other = other_core(other)
    other_product, half_octet = call(
        octet_kernel, out_shape=(shape(size, size), shape(size // 2, size)), name="octet"
    )(quad_product, other, sibling_other)
    octets = [
        lax.ppermute(half_octet, "clique", along_clique(lambda y, z, s=s: ((y + s) % Y, z)))
        for s in (1, 2, 3)
    ]
    chip_counts = mine + other_core(theirs)
    chip_counts, other_product = lax.optimization_barrier((chip_counts, other_product))
    spread = [
        lax.ppermute(chip_counts, "dp", along_dp(lambda x, c, s=s: ((x + s) % 4, c)))
        for s in (1, 2, 3)
    ]
    sibling_octets = [other_core(value) for value in octets]
    counts = chip_counts + spread[0] + spread[1] + spread[2]
    sibling_counts = other_core(counts)
    total_rows = table_rows.shape[1] * lax.axis_size("dp")
    updated, beliefs = call(
        functools.partial(final_kernel, size * size / total_rows),
        out_shape=(shape(size, size), shape(size, size)),
        scratch_shapes=[pltpu.VMEM((Y, size, size), jnp.float32)],
        name="final",
    )(
        potential, measure_noise[0], quad, other_product, *octets, *sibling_octets,
        counts, sibling_counts,
    )
    return (updated[None], beliefs[None])


def solution(mesh):
    in_specs = (P(None, "dp"), P(), P("clique", None, None), P("clique", None, None))
    out_specs = (P("clique", None, None), P("clique", None, None))
    return jax.shard_map(
        per_device, mesh=mesh, in_specs=in_specs, out_specs=out_specs, check_vma=False
    )
```

time: 48.7 us -> 54.4 us (1.12)
  waiting for transfers between devices: 7.29 us -> 13.7 us
  starting transfers between devices: 26.2 us -> 23.8 us
  Pallas kernels: 12.7 us -> 14.3 us
    ppermute x3, waiting for transfers between devices: 0.01 us -> 5.44 us  [per_device(): lax.ppermute(half, 'clique', along_clique(lambda y, z, s=s: (y, in_quad(z...]
    ppermute x4, waiting for transfers between devices: 6.09 us -> 0.66 us  [the longest x3 0.66 us: per_device(): lax.ppermute(half_octet, 'clique', along_clique(lambda y, z, s=s: ((y + s...]
    ppermute x3, waiting for transfers between devices: 0.01 us -> 4.23 us  [per_device(): lax.ppermute(chip_counts, 'dp', along_dp(lambda x, c, s=s: ((x + s) % 4,...]
    ppermute x8 -> x9, waiting for transfers between devices: 1.19 us -> 3.33 us  [other_core(): return lax.ppermute(value, 'dp', along_dp(lambda x, c: (x, 1 - c)))]
    pallas_call x3 -> x4, Pallas kernels: 9.5 us -> 10.8 us  [the longest x2 10.4 us: count_rows(): pl.pallas_call(functools.partial(count_kernel, part), out_shape=(shape(si...]
    ppermute x8 -> x9, starting transfers between devices: 8.37 us -> 7.55 us  [other_core(): return lax.ppermute(value, 'dp', along_dp(lambda x, c: (x, 1 - c)))]
    ppermute x3, starting transfers between devices: 4.36 us -> 3.68 us  [per_device(): lax.ppermute(chip_counts, 'dp', along_dp(lambda x, c, s=s: ((x + s) % 4,...]
    ppermute x3, starting transfers between devices: 6.26 us -> 5.63 us  [per_device(): lax.ppermute(half, 'clique', along_clique(lambda y, z, s=s: (y, in_quad(z...]
  transfers between devices with their start and end apart: 18 -> 19, of which waited for: 5 -> 10; matrix products, arithmetic and copies ran while one was open for 0% -> 0% of each run, Pallas kernels for 21% -> 19%
where the time goes in v2:
time: 54.4 us; the launch traced here: 54.2 us
  starting transfers between devices  23.8 us (44%)
  Pallas kernels  14.3 us (26%)
  waiting for transfers between devices  13.7 us (25%)
  local copies, waits for them, and re-layouts  1.61 us (3%)
  between operations  0.72 us (1%)
    pallas_call x2, Pallas kernels, count_rows(): pl.pallas_call(functools.partial(count_kernel, part), out_shape=(shape(si...  10.4 us
    ppermute x9, starting transfers between devices, other_core(): return lax.ppermute(value, 'dp', along_dp(lambda x, c: (x, 1 - c)))  7.55 us
    ppermute x3, starting transfers between devices, per_device(): lax.ppermute(half, 'clique', along_clique(lambda y, z, s=s: (y, in_quad(z...  5.63 us
    ppermute x3, waiting for transfers between devices, per_device(): lax.ppermute(half, 'clique', along_clique(lambda y, z, s=s: (y, in_quad(z...  5.44 us
    ppermute x3, starting transfers between devices, per_device(): lax.ppermute(half_octet, 'clique', along_clique(lambda y, z, s=s: ((y + s...  4.38 us
    ppermute x3, waiting for transfers between devices, per_device(): lax.ppermute(chip_counts, 'dp', along_dp(lambda x, c, s=s: ((x + s) % 4,...  4.23 us
    ppermute x3, starting transfers between devices, per_device(): lax.ppermute(chip_counts, 'dp', along_dp(lambda x, c, s=s: ((x + s) % 4,...  3.68 us
    ppermute x9, waiting for transfers between devices, other_core(): return lax.ppermute(value, 'dp', along_dp(lambda x, c: (x, 1 - c)))  3.33 us
  transfers between devices with their start and end apart: 19, of which 10 were waited for; matrix products, arithmetic and copies ran while one was open for 0% of the time, Pallas kernels for 19%

profile of v2, /device:TPU:1, one launch (start us, length us, event | category | flops | bytes accessed | tf_op | source)
XLA Modules:
  0.0 54.2 jit_solution(9778747822217310393)
XLA Ops:
  0.6 0.0 copy-start
  0.6 0.9 %copy-done = f32[1,256,256]{2,1,0:T(8,128)S(1)} copy-done((f32[1,256,256]{2,1,0:T(8,128)S(1)}, f32[1,256,256]{2,1,0:T(8,128)}, u32[]{:S(2)}) %copy-start) | copy-done | bytes 262168
  1.6 0.7 %copy-done.3 = s32[33]{0:T(128)S(1)} copy-done((s32[33]{0:T(128)S(1)}, s32[33]{0:T(128)}, u32[]{:S(2)}) %copy-start.3) | copy-done | bytes 156
  2.2 0.2 half.1
  2.4 5.3 %collective-permute-start.2 = (f32[128,256]{1,0:T(8,128)S(1)}, f32[128,256]{1,0:T(8,128)S(1)}, u32[]{:S(2)}, u32[]{:S(2)}) collective-permute-start(f32[128,256]{1,0:T(8,128)S(1)} %get-tuple-element.24), channel_id=1, source_target_pairs={{0,3},{1,0},{2,1},{3,2},{4,7},{5,4},{6,5},{7,6},{8,11},{9,8},{10,9... | collective-permute-start | bytes 393224 | tf_op jit(solution)/shard_map/ppermute | solution.py:246
  7.7 0.0 collective-permute-start.1
  7.7 0.4 collective-permute-start
  8.1 5.2 %counts.2.refs_0_ = f32[256,256]{1,0:T(8,128)S(1)} custom-call(s32[33]{0:T(128)S(1)} %get-tuple-element.25.order_ref, s32[33,65536]{1,0:T(8,128)} %right_ref.3, s32[33,65536]{1,0:T(8,128)} %right_ref.3), custom_call_target="tpu_custom_call" | custom-call | tf_op jit(solution)/shard_map/counts/pallas_call | solution.py:217
  13.2 0.0 collective-permute-done.2.a3
  13.3 5.4 %collective-permute-done.1.a2 = f32[128,256]{1,0:T(8,128)S(1)} collective-permute-done((f32[128,256]{1,0:T(8,128)S(1)}, f32[128,256]{1,0:T(8,128)S(1)}, u32[]{:S(2)}, u32[]{:S(2)}) %collective-permute-start.1) | collective-permute-done | bytes 131104 | tf_op jit(solution)/shard_map/ppermute | solution.py:246
  18.7 0.0 collective-permute-done.a1
  18.7 1.2 %collective-permute-start.3 = (f32[128,256]{1,0:T(8,128)S(1)}, f32[128,256]{1,0:T(8,128)S(1)}, u32[]{:S(2)}, u32[]{:S(2)}) collective-permute-start(f32[128,256]{1,0:T(8,128)S(1)} %collective-permute-done.a1), channel_id=1, source_target_pairs={{0,32},{32,0},{64,96},{96,64},{128,160},{160,128},{192,224},{224,1... | collective-permute-start | bytes 393224 | tf_op jit(solution)/shard_map/ppermute | solution.py:30
  19.8 0.0 collective-permute-start.4
  19.9 0.5 collective-permute-start.5
  20.4 0.5 collective-permute-done.3.b1
  20.8 0.4 collective-permute-done.4.b2
  21.2 0.2 collective-permute-done.5.b3
  21.4 1.0 %quad.1 = (f32[4,256,256]{2,1,0:T(8,128)S(1)}, f32[256,256]{1,0:T(8,128)S(1)}, f32[128,256]{1,0:T(8,128)S(1)}) custom-call(f32[256,256]{1,0:T(8,128)S(1)} %bitcast.5, f32[128,256]{1,0:T(8,128)S(1)} %collective-permute-done.a1, f32[128,256]{1,0:T(8,128)S(1)} %collective-permute-done.1.a2, f32[128,256]{1,0:T(8,128)S(1)} %collective-permute-done.2.a3, ...), custom_call_target="tpu_custom_call" | custom-call | tf_op jit(solution)/shard_map/quad/pallas_call | solution.py:255
  22.4 2.6 %collective-permute-start.6 = (f32[128,256]{1,0:T(8,128)S(1)}, f32[128,256]{1,0:T(8,128)S(1)}, u32[]{:S(2)}, u32[]{:S(2)}) collective-permute-start(f32[128,256]{1,0:T(8,128)S(1)} %get-tuple-element.30), channel_id=1, source_target_pairs={{0,7},{1,6},{2,5},{3,4},{4,3},{5,2},{6,1},{7,0},{8,15},{9,14},{10,... | collective-permute-start | bytes 393224 | tf_op jit(solution)/shard_map/ppermute | solution.py:260
  25.0 5.2 %counts.3 = (f32[128,256]{1,0:T(8,128)S(1)}, f32[128,256]{1,0:T(8,128)S(1)}) custom-call(s32[33]{0:T(128)S(1)} %get-tuple-element.25.order_ref, s32[33,65536]{1,0:T(8,128)} %right_ref.3, s32[33,65536]{1,0:T(8,128)} %right_ref.3, f32[256,256]{1,0:T(8,128)S(1)} %counts.2.refs_0_), custom_call_target="tpu_custom_call" | custom-call | tf_op jit(solution)/shard_map/counts/pallas_call | solution.py:217
  30.2 0.0 collective-permute-done.6.own_ref
  30.2 2.2 %collective-permute-start.7 = (f32[128,256]{1,0:T(8,128)S(1)}, f32[128,256]{1,0:T(8,128)S(1)}, u32[]{:S(2)}, u32[]{:S(2)}) collective-permute-start(f32[128,256]{1,0:T(8,128)S(1)} %get-tuple-element.37), channel_id=1, source_target_pairs={{0,32},{32,0},{64,96},{96,64},{128,160},{160,128},{192,224},{224,1... | collective-permute-start | bytes 393224 | tf_op jit(solution)/shard_map/ppermute | solution.py:30
  32.4 0.0 collective-permute-start.8
  32.4 1.0 %collective-permute-done.7 = f32[128,256]{1,0:T(8,128)S(1)} collective-permute-done((f32[128,256]{1,0:T(8,128)S(1)}, f32[128,256]{1,0:T(8,128)S(1)}, u32[]{:S(2)}, u32[]{:S(2)}) %collective-permute-start.7) | collective-permute-done | bytes 131104 | tf_op jit(solution)/shard_map/ppermute | solution.py:30
  33.5 0.3 collective-permute-done.8.sibling_ref
  33.8 0.2 octet.1
  34.1 2.6 %collective-permute-start.17 = (f32[128,256]{1,0:T(8,128)S(1)}, f32[128,256]{1,0:T(8,128)S(1)}, u32[]{:S(2)}, u32[]{:S(2)}) collective-permute-start(f32[128,256]{1,0:T(8,128)S(1)} %add.12), channel_id=1, source_target_pairs={{0,192},{32,224},{64,0},{96,32},{128,64},{160,96},{192,128},{224,1... | collective-permute-start | bytes 393224 | tf_op jit(solution)/shard_map/ppermute | solution.py:277
  36.6 0.5 collective-permute-start.16
  37.1 0.6 %collective-permute-start.15 = (f32[128,256]{1,0:T(8,128)S(1)}, f32[128,256]{1,0:T(8,128)S(1)}, u32[]{:S(2)}, u32[]{:S(2)}) collective-permute-start(f32[128,256]{1,0:T(8,128)S(1)} %add.12), channel_id=1, source_target_pairs={{0,64},{32,96},{64,128},{96,160},{128,192},{160,224},{192,0},{224,... | collective-permute-start | bytes 393224 | tf_op jit(solution)/shard_map/ppermute | solution.py:277
  37.7 2.7 %collective-permute-start.11 = (f32[128,256]{1,0:T(8,128)S(1)}, f32[128,256]{1,0:T(8,128)S(1)}, u32[]{:S(2)}, u32[]{:S(2)}) collective-permute-start(f32[128,256]{1,0:T(8,128)S(1)} %get-tuple-element.42), channel_id=1, source_target_pairs={{0,24},{1,25},{2,26},{3,27},{4,28},{5,29},{6,30},{7,31},{8,0},{9,1... | collective-permute-start | bytes 393224 | tf_op jit(solution)/shard_map/ppermute | solution.py:271
  40.5 0.3 collective-permute-start.10
  40.8 1.2 %collective-permute-done.17 = f32[128,256]{1,0:T(8,128)S(1)} collective-permute-done((f32[128,256]{1,0:T(8,128)S(1)}, f32[128,256]{1,0:T(8,128)S(1)}, u32[]{:S(2)}, u32[]{:S(2)}) %collective-permute-start.17) | collective-permute-done | bytes 131104 | tf_op jit(solution)/shard_map/ppermute | solution.py:277
  42.0 1.3 %collective-permute-start.9 = (f32[128,256]{1,0:T(8,128)S(1)}, f32[128,256]{1,0:T(8,128)S(1)}, u32[]{:S(2)}, u32[]{:S(2)}) collective-permute-start(f32[128,256]{1,0:T(8,128)S(1)} %get-tuple-element.42), channel_id=1, source_target_pairs={{0,8},{1,9},{2,10},{3,11},{4,12},{5,13},{6,14},{7,15},{8,16},{9,17... | collective-permute-start | bytes 393224 | tf_op jit(solution)/shard_map/ppermute | solution.py:271
  43.3 0.0 collective-permute-done.16
  43.3 3.0 %collective-permute-done.15 = f32[128,256]{1,0:T(8,128)S(1)} collective-permute-done((f32[128,256]{1,0:T(8,128)S(1)}, f32[128,256]{1,0:T(8,128)S(1)}, u32[]{:S(2)}, u32[]{:S(2)}) %collective-permute-start.15) | collective-permute-done | bytes 131104 | tf_op jit(solution)/shard_map/ppermute | solution.py:277
  46.4 0.6 %collective-permute-start.18 = (f32[128,256]{1,0:T(8,128)S(1)}, f32[128,256]{1,0:T(8,128)S(1)}, u32[]{:S(2)}, u32[]{:S(2)}) collective-permute-start(f32[128,256]{1,0:T(8,128)S(1)} %add_add_fusion.mine_ref), channel_id=1, source_target_pairs={{0,32},{32,0},{64,96},{96,64},{128,160},{160,128},{192,224},{224,1... | collective-permute-start | bytes 393224 | tf_op jit(solution)/shard_map/ppermute | solution.py:30
  47.0 0.0 collective-permute-done.11.a3
  47.0 0.1 collective-permute-start.14
  47.1 0.0 collective-permute-done.10.a2
  47.1 1.9 %collective-permute-start.13 = (f32[128,256]{1,0:T(8,128)S(1)}, f32[128,256]{1,0:T(8,128)S(1)}, u32[]{:S(2)}, u32[]{:S(2)}) collective-permute-start(f32[128,256]{1,0:T(8,128)S(1)} %collective-permute-done.10.a2), channel_id=1, source_target_pairs={{0,32},{32,0},{64,96},{96,64},{128,160},{160,128},{192,224},{224,1... | collective-permute-start | bytes 393224 | tf_op jit(solution)/shard_map/ppermute | solution.py:30
  49.0 0.7 %collective-permute-done.9.a1 = f32[128,256]{1,0:T(8,128)S(1)} collective-permute-done((f32[128,256]{1,0:T(8,128)S(1)}, f32[128,256]{1,0:T(8,128)S(1)}, u32[]{:S(2)}, u32[]{:S(2)}) %collective-permute-start.9) | collective-permute-done | bytes 131104 | tf_op jit(solution)/shard_map/ppermute | solution.py:271
  49.7 1.0 %collective-permute-start.12 = (f32[128,256]{1,0:T(8,128)S(1)}, f32[128,256]{1,0:T(8,128)S(1)}, u32[]{:S(2)}, u32[]{:S(2)}) collective-permute-start(f32[128,256]{1,0:T(8,128)S(1)} %collective-permute-done.9.a1), channel_id=1, source_target_pairs={{0,32},{32,0},{64,96},{96,64},{128,160},{160,128},{192,224},{224,1... | collective-permute-start | bytes 393224 | tf_op jit(solution)/shard_map/ppermute | solution.py:30
  50.7 0.0 collective-permute-done.18.theirs_ref
  50.7 0.0 collective-permute-done.14.b3
  50.7 0.0 collective-permute-done.13.b2
  50.7 1.0 %collective-permute-done.12.b1 = f32[128,256]{1,0:T(8,128)S(1)} collective-permute-done((f32[128,256]{1,0:T(8,128)S(1)}, f32[128,256]{1,0:T(8,128)S(1)}, u32[]{:S(2)}, u32[]{:S(2)}) %collective-permute-start.12) | collective-permute-done | bytes 131104 | tf_op jit(solution)/shard_map/ppermute | solution.py:30
  51.7 0.0 copy-done.2
  51.7 2.5 %final.1 = (f32[256,256]{1,0:T(8,128)}, f32[256,256]{1,0:T(8,128)}) custom-call(f32[256,256]{1,0:T(8,128)S(1)} %bitcast.6, f32[256,256]{1,0:T(8,128)S(1)} %bitcast.7, f32[4,256,256]{2,1,0:T(8,128)S(1)} %get-tuple-element.29.quad_ref, f32[256,256]{1,0:T(8,128)S(1)} %get-tuple-element.41.other_ref, f32[128,256]{1,0:T(8,128)S(1)} %collective-permute-done.9.a1, ...), custom_call_target="tpu_custom_call" | custom-call | tf_op jit(solution)/shard_map/final/pallas_call | solution.py:284
  (6 shorter events, 0.1 us)
Async XLA Ops:
  0.6 1.0 %copy-start = (f32[1,256,256]{2,1,0:T(8,128)S(1)}, f32[1,256,256]{2,1,0:T(8,128)}, u32[]{:S(2)}) copy-start(f32[1,256,256]{2,1,0:T(8,128)} %param.6) | copy-start | bytes 786436
  1.6 0.7 %copy-start.3 = (s32[33]{0:T(128)S(1)}, s32[33]{0:T(128)}, u32[]{:S(2)}) copy-start(s32[33]{0:T(128)} %order_ref.1) | copy-start | bytes 400
  2.4 10.8 %collective-permute-start.2 = (f32[128,256]{1,0:T(8,128)S(1)}, f32[128,256]{1,0:T(8,128)S(1)}, u32[]{:S(2)}, u32[]{:S(2)}) collective-permute-start(f32[128,256]{1,0:T(8,128)S(1)} %get-tuple-element.24), channel_id=1, source_target_pairs={{0,3},{1,0},{2,1},{3,2},{4,7},{5,4},{6,5},{7,6},{8,11},{9,8},{10,9... | collective-permute-start | bytes 393224 | tf_op jit(solution)/shard_map/ppermute | solution.py:246
  7.7 11.0 %collective-permute-start.1 = (f32[128,256]{1,0:T(8,128)S(1)}, f32[128,256]{1,0:T(8,128)S(1)}, u32[]{:S(2)}, u32[]{:S(2)}) collective-permute-start(f32[128,256]{1,0:T(8,128)S(1)} %get-tuple-element.24), channel_id=1, source_target_pairs={{0,2},{1,3},{2,0},{3,1},{4,6},{5,7},{6,4},{7,5},{8,10},{9,11},{10,... | collective-permute-start | bytes 393224 | tf_op jit(solution)/shard_map/ppermute | solution.py:246
  7.7 11.0 %collective-permute-start = (f32[128,256]{1,0:T(8,128)S(1)}, f32[128,256]{1,0:T(8,128)S(1)}, u32[]{:S(2)}, u32[]{:S(2)}) collective-permute-start(f32[128,256]{1,0:T(8,128)S(1)} %get-tuple-element.24), channel_id=1, source_target_pairs={{0,1},{1,2},{2,3},{3,0},{4,5},{5,6},{6,7},{7,4},{8,9},{9,10},{10,1... | collective-permute-start | bytes 393224 | tf_op jit(solution)/shard_map/ppermute | solution.py:246
  8.1 13.3 %copy-start.1 = (f32[1,256,256]{2,1,0:T(8,128)S(1)}, f32[1,256,256]{2,1,0:T(8,128)}, u32[]{:S(2)}) copy-start(f32[1,256,256]{2,1,0:T(8,128)} %param.6) | copy-start | bytes 786436
  18.7 2.1 %collective-permute-start.3 = (f32[128,256]{1,0:T(8,128)S(1)}, f32[128,256]{1,0:T(8,128)S(1)}, u32[]{:S(2)}, u32[]{:S(2)}) collective-permute-start(f32[128,256]{1,0:T(8,128)S(1)} %collective-permute-done.a1), channel_id=1, source_target_pairs={{0,32},{32,0},{64,96},{96,64},{128,160},{160,128},{192,224},{224,1... | collective-permute-start | bytes 393224 | tf_op jit(solution)/shard_map/ppermute | solution.py:30
  19.8 1.3 %collective-permute-start.4 = (f32[128,256]{1,0:T(8,128)S(1)}, f32[128,256]{1,0:T(8,128)S(1)}, u32[]{:S(2)}, u32[]{:S(2)}) collective-permute-start(f32[128,256]{1,0:T(8,128)S(1)} %collective-permute-done.1.a2), channel_id=1, source_target_pairs={{0,32},{32,0},{64,96},{96,64},{128,160},{160,128},{192,224},{224,1... | collective-permute-start | bytes 393224 | tf_op jit(solution)/shard_map/ppermute | solution.py:30
  19.9 1.5 %collective-permute-start.5 = (f32[128,256]{1,0:T(8,128)S(1)}, f32[128,256]{1,0:T(8,128)S(1)}, u32[]{:S(2)}, u32[]{:S(2)}) collective-permute-start(f32[128,256]{1,0:T(8,128)S(1)} %collective-permute-done.2.a3), channel_id=1, source_target_pairs={{0,32},{32,0},{64,96},{96,64},{128,160},{160,128},{192,224},{224,1... | collective-permute-start | bytes 393224 | tf_op jit(solution)/shard_map/ppermute | solution.py:30
  22.4 7.8 %collective-permute-start.6 = (f32[128,256]{1,0:T(8,128)S(1)}, f32[128,256]{1,0:T(8,128)S(1)}, u32[]{:S(2)}, u32[]{:S(2)}) collective-permute-start(f32[128,256]{1,0:T(8,128)S(1)} %get-tuple-element.30), channel_id=1, source_target_pairs={{0,7},{1,6},{2,5},{3,4},{4,3},{5,2},{6,1},{7,0},{8,15},{9,14},{10,... | collective-permute-start | bytes 393224 | tf_op jit(solution)/shard_map/ppermute | solution.py:260
  25.0 26.7 %copy-start.2 = (f32[1,256,256]{2,1,0:T(8,128)S(1)}, f32[1,256,256]{2,1,0:T(8,128)}, u32[]{:S(2)}) copy-start(f32[1,256,256]{2,1,0:T(8,128)} %param.7) | copy-start | bytes 786436
  30.2 3.2 %collective-permute-start.7 = (f32[128,256]{1,0:T(8,128)S(1)}, f32[128,256]{1,0:T(8,128)S(1)}, u32[]{:S(2)}, u32[]{:S(2)}) collective-permute-start(f32[128,256]{1,0:T(8,128)S(1)} %get-tuple-element.37), channel_id=1, source_target_pairs={{0,32},{32,0},{64,96},{96,64},{128,160},{160,128},{192,224},{224,1... | collective-permute-start | bytes 393224 | tf_op jit(solution)/shard_map/ppermute | solution.py:30
  32.4 1.3 %collective-permute-start.8 = (f32[128,256]{1,0:T(8,128)S(1)}, f32[128,256]{1,0:T(8,128)S(1)}, u32[]{:S(2)}, u32[]{:S(2)}) collective-permute-start(f32[128,256]{1,0:T(8,128)S(1)} %collective-permute-done.6.own_ref), channel_id=1, source_target_pairs={{0,32},{32,0},{64,96},{96,64},{128,160},{160,128},{192,224},{224,1... | collective-permute-start | bytes 393224 | tf_op jit(solution)/shard_map/ppermute | solution.py:30
  34.1 7.9 %collective-permute-start.17 = (f32[128,256]{1,0:T(8,128)S(1)}, f32[128,256]{1,0:T(8,128)S(1)}, u32[]{:S(2)}, u32[]{:S(2)}) collective-permute-start(f32[128,256]{1,0:T(8,128)S(1)} %add.12), channel_id=1, source_target_pairs={{0,192},{32,224},{64,0},{96,32},{128,64},{160,96},{192,128},{224,1... | collective-permute-start | bytes 393224 | tf_op jit(solution)/shard_map/ppermute | solution.py:277
  36.6 6.7 %collective-permute-start.16 = (f32[128,256]{1,0:T(8,128)S(1)}, f32[128,256]{1,0:T(8,128)S(1)}, u32[]{:S(2)}, u32[]{:S(2)}) collective-permute-start(f32[128,256]{1,0:T(8,128)S(1)} %add.12), channel_id=1, source_target_pairs={{0,128},{32,160},{64,192},{96,224},{128,0},{160,32},{192,64},{224,... | collective-permute-start | bytes 393224 | tf_op jit(solution)/shard_map/ppermute | solution.py:277
  37.1 9.2 %collective-permute-start.15 = (f32[128,256]{1,0:T(8,128)S(1)}, f32[128,256]{1,0:T(8,128)S(1)}, u32[]{:S(2)}, u32[]{:S(2)}) collective-permute-start(f32[128,256]{1,0:T(8,128)S(1)} %add.12), channel_id=1, source_target_pairs={{0,64},{32,96},{64,128},{96,160},{128,192},{160,224},{192,0},{224,... | collective-permute-start | bytes 393224 | tf_op jit(solution)/shard_map/ppermute | solution.py:277
  37.7 9.2 %collective-permute-start.11 = (f32[128,256]{1,0:T(8,128)S(1)}, f32[128,256]{1,0:T(8,128)S(1)}, u32[]{:S(2)}, u32[]{:S(2)}) collective-permute-start(f32[128,256]{1,0:T(8,128)S(1)} %get-tuple-element.42), channel_id=1, source_target_pairs={{0,24},{1,25},{2,26},{3,27},{4,28},{5,29},{6,30},{7,31},{8,0},{9,1... | collective-permute-start | bytes 393224 | tf_op jit(solution)/shard_map/ppermute | solution.py:271
  40.5 6.6 %collective-permute-start.10 = (f32[128,256]{1,0:T(8,128)S(1)}, f32[128,256]{1,0:T(8,128)S(1)}, u32[]{:S(2)}, u32[]{:S(2)}) collective-permute-start(f32[128,256]{1,0:T(8,128)S(1)} %get-tuple-element.42), channel_id=1, source_target_pairs={{0,16},{1,17},{2,18},{3,19},{4,20},{5,21},{6,22},{7,23},{8,24},{9,... | collective-permute-start | bytes 393224 | tf_op jit(solution)/shard_map/ppermute | solution.py:271
  42.0 7.7 %collective-permute-start.9 = (f32[128,256]{1,0:T(8,128)S(1)}, f32[128,256]{1,0:T(8,128)S(1)}, u32[]{:S(2)}, u32[]{:S(2)}) collective-permute-start(f32[128,256]{1,0:T(8,128)S(1)} %get-tuple-element.42), channel_id=1, source_target_pairs={{0,8},{1,9},{2,10},{3,11},{4,12},{5,13},{6,14},{7,15},{8,16},{9,17... | collective-permute-start | bytes 393224 | tf_op jit(solution)/shard_map/ppermute | solution.py:271
  46.4 4.3 %collective-permute-start.18 = (f32[128,256]{1,0:T(8,128)S(1)}, f32[128,256]{1,0:T(8,128)S(1)}, u32[]{:S(2)}, u32[]{:S(2)}) collective-permute-start(f32[128,256]{1,0:T(8,128)S(1)} %add_add_fusion.mine_ref), channel_id=1, source_target_pairs={{0,32},{32,0},{64,96},{96,64},{128,160},{160,128},{192,224},{224,1... | collective-permute-start | bytes 393224 | tf_op jit(solution)/shard_map/ppermute | solution.py:30
  47.0 3.7 %collective-permute-start.14 = (f32[128,256]{1,0:T(8,128)S(1)}, f32[128,256]{1,0:T(8,128)S(1)}, u32[]{:S(2)}, u32[]{:S(2)}) collective-permute-start(f32[128,256]{1,0:T(8,128)S(1)} %collective-permute-done.11.a3), channel_id=1, source_target_pairs={{0,32},{32,0},{64,96},{96,64},{128,160},{160,128},{192,224},{224,1... | collective-permute-start | bytes 393224 | tf_op jit(solution)/shard_map/ppermute | solution.py:30
  47.1 3.6 %collective-permute-start.13 = (f32[128,256]{1,0:T(8,128)S(1)}, f32[128,256]{1,0:T(8,128)S(1)}, u32[]{:S(2)}, u32[]{:S(2)}) collective-permute-start(f32[128,256]{1,0:T(8,128)S(1)} %collective-permute-done.10.a2), channel_id=1, source_target_pairs={{0,32},{32,0},{64,96},{96,64},{128,160},{160,128},{192,224},{224,1... | collective-permute-start | bytes 393224 | tf_op jit(solution)/shard_map/ppermute | solution.py:30
  49.7 2.0 %collective-permute-start.12 = (f32[128,256]{1,0:T(8,128)S(1)}, f32[128,256]{1,0:T(8,128)S(1)}, u32[]{:S(2)}, u32[]{:S(2)}) collective-permute-start(f32[128,256]{1,0:T(8,128)S(1)} %collective-permute-done.9.a1), channel_id=1, source_target_pairs={{0,32},{32,0},{64,96},{96,64},{128,160},{160,128},{192,224},{224,1... | collective-permute-start | bytes 393224 | tf_op jit(solution)/shard_map/ppermute | solution.py:30

commit v3 on v2

v3 whole, which is shorter than its diff:
```python
import functools

import jax
import jax.numpy as jnp
from jax import lax
from jax.experimental import pallas as pl
from jax.experimental.pallas import tpu as pltpu
from jax.sharding import PartitionSpec as P

step_size = 0.25
shift = 7.0
Y, Z, QUAD = 4, 8, 4
VMEM_LIMIT = 50 << 20


def place():
    dp, clique = (lax.axis_index("dp"), lax.axis_index("clique"))
    return (lax.rem(dp, 2), lax.div(clique, Z), lax.rem(clique, Z))


def along_clique(where):
    return [(y * Z + z, where(y, z)[0] * Z + where(y, z)[1]) for y in range(Y) for z in range(Z)]


def along_dp(where):
    return [(2 * x + c, 2 * where(x, c)[0] + where(x, c)[1]) for x in range(4) for c in range(2)]


def other_core(value):
    return lax.ppermute(value, "dp", along_dp(lambda x, c: (x, 1 - c)))


def in_quad(z, step):
    return z // QUAD * QUAD + (z + step) % QUAD


def split(value):
    high = value.astype(jnp.bfloat16)
    low = (value - high.astype(jnp.float32)).astype(jnp.bfloat16)
    return (high, low)


def product(left, right):
    left_high, left_low = split(left)
    right_high, right_low = split(right)
    dot = functools.partial(jnp.dot, preferred_element_type=jnp.float32)
    return dot(left_high, right_high) + (dot(left_high, right_low) + dot(left_low, right_high))


def diagonal(size):
    rows = lax.broadcasted_iota(jnp.int32, (size, size), 0)
    return rows == lax.broadcasted_iota(jnp.int32, (size, size), 1)


def as_column(row, eye):
    return jnp.sum(jnp.where(eye, row, 0.0), axis=1, keepdims=True)


def as_row(column, eye):
    return jnp.sum(jnp.where(eye, column, 0.0), axis=0, keepdims=True)


def row_times(row, matrix, eye):
    column = as_column(row, eye) / jnp.sum(row, axis=1, keepdims=True)
    return jnp.sum(column * matrix, axis=0, keepdims=True)


def times_row(matrix, row, eye):
    column = jnp.sum(matrix * row, axis=1, keepdims=True)
    return as_row(column, eye) / jnp.sum(column, axis=0, keepdims=True)


def read_kernel(order_hbm, potential_hbm, order_ref, kernel_ref, half_ref, copied_ref, semaphores):
    core, _, _ = place()
    copies = (
        pltpu.make_async_copy(order_hbm, order_ref, semaphores.at[0]),
        pltpu.make_async_copy(potential_hbm, copied_ref, semaphores.at[1]),
    )
    for copy in copies:
        copy.start()
    for copy in copies:
        copy.wait()
    half = half_ref.shape[0]
    kernel_ref[...] = jnp.exp(copied_ref[...] - shift)
    half_ref[...] = kernel_ref[pl.ds(core * half, half), :]


def put_others(stack_ref, mine, near, near_sibling, far, far_sibling, core):
    count = stack_ref.shape[0]
    half = far.shape[0]
    before, after, across = (lax.rem(mine + count + move, count) for move in (-1, 1, 2))
    stack_ref[jnp.where(core == 0, before, after)] = near[...]
    stack_ref[jnp.where(core == 0, after, before)] = near_sibling[...]
    stack_ref[across, pl.ds(core * half, half), :] = far[...]
    stack_ref[across, pl.ds((1 - core) * half, half), :] = far_sibling[...]


def quad_kernel(kernel_ref, near, near_sibling, far, far_sibling, quad_ref, product_ref, half_ref):
    core, _, z = place()
    mine = lax.rem(z, QUAD)
    half, size = half_ref.shape
    quad_ref[mine] = kernel_ref[...]
    put_others(quad_ref, mine, near, near_sibling, far, far_sibling, core)
    scale = 1.0 / size
    left = product(quad_ref[0], quad_ref[1]) * scale
    right = product(quad_ref[2], quad_ref[3]) * scale
    whole = product(left, right) * scale
    largest = jnp.max(jnp.max(whole, axis=0, keepdims=True), axis=1, keepdims=True)
    product_ref[...] = whole / largest
    half_ref[...] = product_ref[pl.ds(core * half, half), :]


def octet_kernel(product_ref, own_ref, sibling_ref, other_ref, octet_ref, half_ref):
    core, _, z = place()
    half = half_ref.shape[0]
    rows = pl.ds(core * half, half)
    other_ref[rows, :] = own_ref[...]
    other_ref[pl.ds((1 - core) * half, half), :] = sibling_ref[...]

    @pl.when(z < QUAD)
    def _():
        octet_ref[...] = product(product_ref[...], other_ref[...])

    @pl.when(z >= QUAD)
    def _():
        octet_ref[...] = product(other_ref[...], product_ref[...])

    half_ref[...] = octet_ref[rows, :]


def chip_kernel(own_ref, sibling_ref, both_ref, half_ref):
    core, _, _ = place()
    half = half_ref.shape[0]
    both_ref[...] = own_ref[...] + sibling_ref[...]
    half_ref[...] = both_ref[pl.ds(core * half, half), :]


def join_kernel(near_ref, far_ref, sum_ref):
    core, _, _ = place()
    half = far_ref.shape[0]
    sum_ref[...] = near_ref[...]
    sum_ref[pl.ds(core * half, half), :] += far_ref[...]


def final_kernel(
    scale, potential_ref, noise_ref, quad_ref, other_ref, near, near_sibling, far, far_sibling,
    chip_ref, join_ref, sibling_join_ref, updated_ref, beliefs_ref, octet_ref
):
    core, y, z = place()
    size = potential_ref.shape[0]
    put_others(octet_ref, y, near, near_sibling, far, far_sibling, core)
    eye = diagonal(size)
    ones = jnp.ones((1, size), jnp.float32)
    later_quad = lax.div(z, QUAD)
    mine = lax.rem(z, QUAD)
    forward = lax.fori_loop(0, y, lambda i, row: row_times(row, octet_ref[i], eye), ones)
    forward = lax.fori_loop(
        0, later_quad, lambda i, row: row_times(row, other_ref[...], eye), forward
    )
    forward = lax.fori_loop(0, mine, lambda i, row: row_times(row, quad_ref[i], eye), forward)
    backward = lax.fori_loop(
        0, Y - 1 - y, lambda i, row: times_row(octet_ref[Y - 1 - i], row, eye), ones
    )
    backward = lax.fori_loop(
        0, 1 - later_quad, lambda i, row: times_row(other_ref[...], row, eye), backward
    )
    backward = lax.fori_loop(
        0, 3 - mine, lambda i, row: times_row(quad_ref[3 - i], row, eye), backward
    )
    column = as_column(forward, eye) / jnp.sum(forward, axis=1, keepdims=True)
    joint = column * quad_ref[mine] * backward
    total = jnp.sum(jnp.sum(joint, axis=0, keepdims=True), axis=1, keepdims=True)
    beliefs = joint * (size * size / total)
    beliefs_ref[...] = beliefs
    counts = chip_ref[...] + join_ref[...] + sibling_join_ref[...]
    measured = (counts + noise_ref[...]) * scale
    updated_ref[...] = potential_ref[...] - step_size * (beliefs - measured)


def count_kernel(part, order_ref, left_ref, right_ref, total_ref):
    _, y, z = place()
    clique = y * Z + z
    size = total_ref.shape[0]

    @pl.when(pl.program_id(0) == 0)
    def _():
        total_ref[...] = jnp.zeros_like(total_ref)

    levels = lax.broadcasted_iota(jnp.int32, (size, part), 0).astype(jnp.bfloat16)
    one = jnp.ones((size, part), jnp.bfloat16)
    zero = jnp.zeros((size, part), jnp.bfloat16)

    def onehot(ref, attribute, begin):
        values = ref[pl.ds(lax.rem(attribute, 8), 1), begin : begin + part]
        values = values.astype(jnp.float32).astype(jnp.bfloat16)
        return jnp.where(values == levels, one, zero).astype(jnp.float8_e4m3fn)

    total = total_ref[...]
    for begin in range(0, left_ref.shape[1], part):
        total = total + lax.dot_general(
            onehot(left_ref, order_ref[clique], begin),
            onehot(right_ref, order_ref[clique + 1], begin),
            (((1,), (1,)), ((), ())),
            preferred_element_type=jnp.float32,
        )
    total_ref[...] = total


def shape(*dims):
    return jax.ShapeDtypeStruct(dims, jnp.float32)


PARAMS = pltpu.CompilerParams(vmem_limit_bytes=VMEM_LIMIT)


def count_pairs(order, table_rows, size):
    window, part = 16384, 8192

    def rows_of(offset):
        def block(step, order_ref):
            return (lax.div(order_ref[lax.axis_index("clique") + offset], 8), step)

        return pl.BlockSpec((8, window), block)

    return pl.pallas_call(
        functools.partial(count_kernel, part),
        out_shape=shape(size, size),
        grid_spec=pltpu.PrefetchScalarGridSpec(
            num_scalar_prefetch=1,
            grid=(table_rows.shape[1] // window,),
            in_specs=[rows_of(0), rows_of(1)],
            out_specs=pl.BlockSpec((size, size), lambda step, order_ref: (0, 0)),
        ),
        compiler_params=PARAMS,
        name="counts",
    )(order, table_rows, table_rows)


def everywhere(move):
    pairs = []
    for x in range(4):
        for c in range(2):
            for y in range(Y):
                for z in range(Z):
                    to_x, to_y, to_z = move(x, c, y, z)
                    source = (2 * x + c) * Y * Z + y * Z + z
                    pairs.append((source, (2 * to_x + c) * Y * Z + to_y * Z + to_z))
    return pairs


def exchange(whole, half, step):
    axes = ("dp", "clique")
    near = lax.ppermute(whole, axes, everywhere(lambda x, c, y, z: step(x, y, z, 1 - 2 * c)))
    far = lax.ppermute(half, axes, everywhere(lambda x, c, y, z: step(x, y, z, 2)))
    return (near, far)


def per_device(table_rows, attribute_order, log_potential, measure_noise):
    size = log_potential.shape[1]
    potential = log_potential[0]
    call = functools.partial(pl.pallas_call, compiler_params=PARAMS)
    vmem = pl.BlockSpec(memory_space=pltpu.VMEM)
    hbm = pl.BlockSpec(memory_space=pltpu.HBM)
    whole, half = (shape(size, size), shape(size // 2, size))
    order, kernel, half_of_kernel = call(
        read_kernel,
        in_specs=[hbm, hbm],
        out_specs=(vmem, vmem, vmem),
        out_shape=(jax.ShapeDtypeStruct(attribute_order.shape, jnp.int32), whole, half),
        scratch_shapes=[pltpu.VMEM((size, size), jnp.float32), pltpu.SemaphoreType.DMA((2,))],
        name="read",
    )(
        pltpu.with_memory_space_constraint(attribute_order, pltpu.HBM),
        pltpu.with_memory_space_constraint(potential, pltpu.HBM),
    )
    near, far = exchange(
        kernel, half_of_kernel, lambda x, y, z, s: (x, y, z // QUAD * QUAD + (z + s) % QUAD)
    )
    counts = count_pairs(order, table_rows, size)
    near, far, counts = lax.optimization_barrier((near, far, counts))
    quad, quad_product, half_product = call(
        quad_kernel, out_shape=(shape(QUAD, size, size), whole, half), name="quad"
    )(kernel, near, other_core(near), far, other_core(far))
    other = lax.ppermute(half_product, "clique", along_clique(lambda y, z: (y, Z - 1 - z)))
    counts, quad_product = lax.optimization_barrier((counts, quad_product))
    chip_counts, half_counts = call(chip_kernel, out_shape=(whole, half), name="chip")(
        counts, other_core(counts)
    )
    near_counts, far_counts = exchange(
        chip_counts, half_counts, lambda x, y, z, s: ((x + s) % 4, y, z)
    )
    other, chip_counts = lax.optimization_barrier((other, chip_counts))
    other_product, octet, half_octet = call(
        octet_kernel, out_shape=(whole, whole, half), name="octet"
    )(quad_product, other, other_core(other))
    near, far = exchange(octet, half_octet, lambda x, y, z, s: (x, (y + s) % Y, z))
    joined = call(join_kernel, out_shape=whole, name="join")(near_counts, far_counts)
    total_rows = table_rows.shape[1] * lax.axis_size("dp")
    updated, beliefs = call(
        functools.partial(final_kernel, size * size / total_rows),
        out_shape=(whole, whole),
        scratch_shapes=[pltpu.VMEM((Y, size, size), jnp.float32)],
        name="final",
    )(
        potential, measure_noise[0], quad, other_product, near, other_core(near), far,
        other_core(far), chip_counts, joined, other_core(joined),
    )
    return (updated[None], beliefs[None])


def solution(mesh):
    in_specs = (P(None, "dp"), P(), P("clique", None, None), P("clique", None, None))
    out_specs = (P("clique", None, None), P("clique", None, None))
    return jax.shard_map(
        per_device, mesh=mesh, in_specs=in_specs, out_specs=out_specs, check_vma=False
    )
```

time: 54.4 us -> 50.3 us (0.925)
  starting transfers between devices: 23.8 us -> 20.1 us
  waiting for transfers between devices: 13.7 us -> 16 us
  local copies, waits for them, and re-layouts: 1.61 us -> 0.01 us
  Pallas kernels: 14.3 us -> 13.3 us
    ppermute x9 -> x7, starting transfers between devices: 7.55 us -> 1.83 us  [other_core(): return lax.ppermute(value, 'dp', along_dp(lambda x, c: (x, 1 - c)))]
    ppermute x1, waiting for transfers between devices: 0.01 us -> 5.51 us  [per_device(): lax.ppermute(half_product, 'clique', along_clique(lambda y, z: (y, Z - 1...]
    ppermute x1, starting transfers between devices: 2.57 us -> 6.17 us  [per_device(): lax.ppermute(half_product, 'clique', along_clique(lambda y, z: (y, Z - 1...]
    ppermute x9 -> x6, waiting for transfers between devices: 10.3 us -> 8.23 us  [the longest x3 7.86 us: exchange(): lax.ppermute(half, axes, everywhere(lambda x, c, y, z: step(x, y, z, 2)))]
    unnamed x8 -> x4, local copies, waits for them, and re-layouts: 1.61 us -> 0.01 us
    ppermute x9 -> x6, starting transfers between devices: 13.7 us -> 12.1 us  [the longest x3 10.5 us: exchange(): lax.ppermute(whole, axes, everywhere(lambda x, c, y, z: step(x, y, z, 1 -...]
    ppermute x9 -> x7, waiting for transfers between devices: 3.33 us -> 2.21 us  [other_core(): return lax.ppermute(value, 'dp', along_dp(lambda x, c: (x, 1 - c)))]
    pallas_call x5 -> x6, Pallas kernels: 11.8 us -> 11.3 us  [the longest x1 8.88 us: count_pairs(): pl.pallas_call(functools.partial(count_kernel, part), out_shape=shape(siz...]
  transfers between devices with their start and end apart: 19 -> 14, of which waited for: 10 -> 7; matrix products, arithmetic and copies ran while one was open for 0% -> 0% of each run, Pallas kernels for 19% -> 18%
where the time goes in v3:
time: 50.3 us; the launch traced here: 50.1 us
  starting transfers between devices  20.1 us (40%)
  waiting for transfers between devices  16 us (32%)
  Pallas kernels  13.3 us (26%)
  between operations  0.7 us (1%)
    ppermute x3, starting transfers between devices, exchange(): lax.ppermute(whole, axes, everywhere(lambda x, c, y, z: step(x, y, z, 1 -...  10.5 us
    pallas_call x1, Pallas kernels, count_pairs(): pl.pallas_call(functools.partial(count_kernel, part), out_shape=shape(siz...  8.88 us
    ppermute x3, waiting for transfers between devices, exchange(): lax.ppermute(half, axes, everywhere(lambda x, c, y, z: step(x, y, z, 2)))  7.86 us
    ppermute x1, starting transfers between devices, per_device(): lax.ppermute(half_product, 'clique', along_clique(lambda y, z: (y, Z - 1...  6.17 us
    ppermute x1, waiting for transfers between devices, per_device(): lax.ppermute(half_product, 'clique', along_clique(lambda y, z: (y, Z - 1...  5.51 us
    ppermute x7, waiting for transfers between devices, other_core(): return lax.ppermute(value, 'dp', along_dp(lambda x, c: (x, 1 - c)))  2.21 us
    pallas_call x1, Pallas kernels, per_device(): call(functools.partial(final_kernel, size * size / total_rows), out_shape...  2.01 us
    ppermute x7, starting transfers between devices, other_core(): return lax.ppermute(value, 'dp', along_dp(lambda x, c: (x, 1 - c)))  1.83 us
  transfers between devices with their start and end apart: 14, of which 7 were waited for; matrix products, arithmetic and copies ran while one was open for 0% of the time, Pallas kernels for 18%

profile of v3, /device:TPU:1, one launch (start us, length us, event | category | flops | bytes accessed | tf_op | source)
XLA Modules:
  0.0 50.1 jit_solution(9025476428182183721)
XLA Ops:
  0.6 1.1 %read.1 = (s32[33]{0:T(128)S(1)}, f32[256,256]{1,0:T(8,128)S(1)}, f32[128,256]{1,0:T(8,128)S(1)}) custom-call(s32[33]{0:T(128)} %order_hbm.1, f32[256,256]{1,0:T(8,128)} %bitcast.4), custom_call_target="tpu_custom_call" | custom-call | tf_op jit(solution)/shard_map/read/pallas_call | solution.py:265
  1.7 5.3 %collective-permute-start = (f32[256,256]{1,0:T(8,128)S(1)}, f32[256,256]{1,0:T(8,128)S(1)}, u32[]{:S(2)}, u32[]{:S(2)}) collective-permute-start(f32[256,256]{1,0:T(8,128)S(1)} %get-tuple-element.22.kernel_ref), channel_id=1, source_target_pairs={{0,1},{1,2},{2,3},{3,0},{4,5},{5,6},{6,7},{7,4},{8,9},{9,10},{10,1... | collective-permute-start | bytes 786440 | tf_op jit(solution)/shard_map/ppermute | solution.py:253
  6.9 0.0 collective-permute-start.1
  6.9 0.0 copy-start
  6.9 0.0 copy-start.1
  7.0 8.9 %counts.1.own_ref = f32[256,256]{1,0:T(8,128)S(1)} custom-call(s32[33]{0:T(128)S(1)} %get-tuple-element.24.order_ref, s32[33,65536]{1,0:T(8,128)} %right_ref.1, s32[33,65536]{1,0:T(8,128)} %right_ref.1), custom_call_target="tpu_custom_call" | custom-call | tf_op jit(solution)/shard_map/counts/pallas_call | solution.py:225
  15.8 1.9 %collective-permute-done.1.far = f32[128,256]{1,0:T(8,128)S(1)} collective-permute-done((f32[128,256]{1,0:T(8,128)S(1)}, f32[128,256]{1,0:T(8,128)S(1)}, u32[]{:S(2)}, u32[]{:S(2)}) %collective-permute-start.1) | collective-permute-done | bytes 131104 | tf_op jit(solution)/shard_map/ppermute | solution.py:254
  17.8 0.0 collective-permute-done.near
  17.8 0.1 collective-permute-start.2
  17.8 0.5 collective-permute-start.3
  18.3 1.2 %collective-permute-done.3.far_sibling = f32[128,256]{1,0:T(8,128)S(1)} collective-permute-done((f32[128,256]{1,0:T(8,128)S(1)}, f32[128,256]{1,0:T(8,128)S(1)}, u32[]{:S(2)}, u32[]{:S(2)}) %collective-permute-start.3) | collective-permute-done | bytes 131104 | tf_op jit(solution)/shard_map/ppermute | solution.py:30
  19.5 0.0 collective-permute-done.2.near_sibling
  19.5 1.0 %quad.1 = (f32[4,256,256]{2,1,0:T(8,128)S(1)}, f32[256,256]{1,0:T(8,128)S(1)}, f32[128,256]{1,0:T(8,128)S(1)}) custom-call(f32[256,256]{1,0:T(8,128)S(1)} %get-tuple-element.22.kernel_ref, f32[256,256]{1,0:T(8,128)S(1)} %collective-permute-done.near, f32[256,256]{1,0:T(8,128)S(1)} %collective-permute-done.2.near_sibling, ...), custom_call_target="tpu_custom_call" | custom-call | tf_op jit(solution)/shard_map/quad/pallas_call | solution.py:281
  20.5 0.2 collective-permute-start.5
  20.7 6.2 %collective-permute-start.4 = (f32[128,256]{1,0:T(8,128)S(1)}, f32[128,256]{1,0:T(8,128)S(1)}, u32[]{:S(2)}, u32[]{:S(2)}) collective-permute-start(f32[128,256]{1,0:T(8,128)S(1)} %get-tuple-element.31), channel_id=1, source_target_pairs={{0,7},{1,6},{2,5},{3,4},{4,3},{5,2},{6,1},{7,0},{8,15},{9,14},{10,... | collective-permute-start | bytes 393224 | tf_op jit(solution)/shard_map/ppermute | solution.py:284
  26.9 0.0 collective-permute-done.5.sibling_ref
  27.0 5.5 %collective-permute-done.4.own_ref = f32[128,256]{1,0:T(8,128)S(1)} collective-permute-done((f32[128,256]{1,0:T(8,128)S(1)}, f32[128,256]{1,0:T(8,128)S(1)}, u32[]{:S(2)}, u32[]{:S(2)}) %collective-permute-start.4) | collective-permute-done | bytes 131104 | tf_op jit(solution)/shard_map/ppermute | solution.py:284
  32.5 0.5 collective-permute-start.6
  32.9 2.5 %collective-permute-start.11 = (f32[256,256]{1,0:T(8,128)S(1)}, f32[256,256]{1,0:T(8,128)S(1)}, u32[]{:S(2)}, u32[]{:S(2)}) collective-permute-start(f32[256,256]{1,0:T(8,128)S(1)} %get-tuple-element.38.chip_ref), channel_id=1, source_target_pairs={{0,64},{1,65},{2,66},{3,67},{4,68},{5,69},{6,70},{7,71},{8,72},{9,... | collective-permute-start | bytes 786440 | tf_op jit(solution)/shard_map/ppermute | solution.py:253
  35.4 0.0 collective-permute-done.6.sibling_ref
  35.4 0.3 octet.1
  35.8 2.8 %collective-permute-start.7 = (f32[256,256]{1,0:T(8,128)S(1)}, f32[256,256]{1,0:T(8,128)S(1)}, u32[]{:S(2)}, u32[]{:S(2)}) collective-permute-start(f32[256,256]{1,0:T(8,128)S(1)} %get-tuple-element.36), channel_id=1, source_target_pairs={{0,8},{1,9},{2,10},{3,11},{4,12},{5,13},{6,14},{7,15},{8,16},{9,17... | collective-permute-start | bytes 786440 | tf_op jit(solution)/shard_map/ppermute | solution.py:253
  38.6 1.2 %collective-permute-start.12 = (f32[128,256]{1,0:T(8,128)S(1)}, f32[128,256]{1,0:T(8,128)S(1)}, u32[]{:S(2)}, u32[]{:S(2)}) collective-permute-start(f32[128,256]{1,0:T(8,128)S(1)} %get-tuple-element.39), channel_id=1, source_target_pairs={{0,128},{1,129},{2,130},{3,131},{4,132},{5,133},{6,134},{7,135},{8... | collective-permute-start | bytes 393224 | tf_op jit(solution)/shard_map/ppermute | solution.py:254
  39.8 0.3 collective-permute-start.9
  40.2 4.0 %collective-permute-done.12.far_ref = f32[128,256]{1,0:T(8,128)S(1)} collective-permute-done((f32[128,256]{1,0:T(8,128)S(1)}, f32[128,256]{1,0:T(8,128)S(1)}, u32[]{:S(2)}, u32[]{:S(2)}) %collective-permute-start.12) | collective-permute-done | bytes 131104 | tf_op jit(solution)/shard_map/ppermute | solution.py:254
  44.2 0.0 collective-permute-done.11.near_ref
  44.2 0.1 collective-permute-start.13
  44.3 0.4 collective-permute-done.7.near
  44.7 0.1 collective-permute-start.8
  44.8 1.9 %collective-permute-done.9.far = f32[128,256]{1,0:T(8,128)S(1)} collective-permute-done((f32[128,256]{1,0:T(8,128)S(1)}, f32[128,256]{1,0:T(8,128)S(1)}, u32[]{:S(2)}, u32[]{:S(2)}) %collective-permute-start.9) | collective-permute-done | bytes 131104 | tf_op jit(solution)/shard_map/ppermute | solution.py:254
  46.7 0.4 collective-permute-start.10
  47.1 1.0 %collective-permute-done.10.far_sibling = f32[128,256]{1,0:T(8,128)S(1)} collective-permute-done((f32[128,256]{1,0:T(8,128)S(1)}, f32[128,256]{1,0:T(8,128)S(1)}, u32[]{:S(2)}, u32[]{:S(2)}) %collective-permute-start.10) | collective-permute-done | bytes 131104 | tf_op jit(solution)/shard_map/ppermute | solution.py:30
  48.1 0.0 collective-permute-done.13.sibling_join_ref
  48.1 0.0 collective-permute-done.8.near_sibling
  48.1 0.0 copy-done
  48.1 0.0 copy-done.1
  48.1 2.0 %final.1 = (f32[256,256]{1,0:T(8,128)}, f32[256,256]{1,0:T(8,128)}) custom-call(f32[256,256]{1,0:T(8,128)S(1)} %bitcast.5, f32[256,256]{1,0:T(8,128)S(1)} %bitcast.6, f32[4,256,256]{2,1,0:T(8,128)S(1)} %get-tuple-element.27.quad_ref, f32[256,256]{1,0:T(8,128)S(1)} %get-tuple-element.35.other_ref, f32[256,256]{1,0:T(8,128)S(1)} %collective-permute-done.7.near, ...), custom_call_target="tpu_custom_call" | custom-call | tf_op jit(solution)/shard_map/final/pallas_call | solution.py:299
  (2 shorter events, 0.1 us)
Async XLA Ops:
  1.7 16.1 %collective-permute-start = (f32[256,256]{1,0:T(8,128)S(1)}, f32[256,256]{1,0:T(8,128)S(1)}, u32[]{:S(2)}, u32[]{:S(2)}) collective-permute-start(f32[256,256]{1,0:T(8,128)S(1)} %get-tuple-element.22.kernel_ref), channel_id=1, source_target_pairs={{0,1},{1,2},{2,3},{3,0},{4,5},{5,6},{6,7},{7,4},{8,9},{9,10},{10,1... | collective-permute-start | bytes 786440 | tf_op jit(solution)/shard_map/ppermute | solution.py:253
  6.9 10.8 %collective-permute-start.1 = (f32[128,256]{1,0:T(8,128)S(1)}, f32[128,256]{1,0:T(8,128)S(1)}, u32[]{:S(2)}, u32[]{:S(2)}) collective-permute-start(f32[128,256]{1,0:T(8,128)S(1)} %get-tuple-element.23), channel_id=1, source_target_pairs={{0,2},{1,3},{2,0},{3,1},{4,6},{5,7},{6,4},{7,5},{8,10},{9,11},{10,... | collective-permute-start | bytes 393224 | tf_op jit(solution)/shard_map/ppermute | solution.py:254
  6.9 41.2 %copy-start = (f32[1,256,256]{2,1,0:T(8,128)S(1)}, f32[1,256,256]{2,1,0:T(8,128)}, u32[]{:S(2)}) copy-start(f32[1,256,256]{2,1,0:T(8,128)} %param.6) | copy-start | bytes 786436
  6.9 41.2 %copy-start.1 = (f32[1,256,256]{2,1,0:T(8,128)S(1)}, f32[1,256,256]{2,1,0:T(8,128)}, u32[]{:S(2)}) copy-start(f32[1,256,256]{2,1,0:T(8,128)} %param.7) | copy-start | bytes 786436
  17.8 1.7 %collective-permute-start.2 = (f32[256,256]{1,0:T(8,128)S(1)}, f32[256,256]{1,0:T(8,128)S(1)}, u32[]{:S(2)}, u32[]{:S(2)}) collective-permute-start(f32[256,256]{1,0:T(8,128)S(1)} %collective-permute-done.near), channel_id=1, source_target_pairs={{0,32},{32,0},{64,96},{96,64},{128,160},{160,128},{192,224},{224,1... | collective-permute-start | bytes 786440 | tf_op jit(solution)/shard_map/ppermute | solution.py:30
  17.8 1.7 %collective-permute-start.3 = (f32[128,256]{1,0:T(8,128)S(1)}, f32[128,256]{1,0:T(8,128)S(1)}, u32[]{:S(2)}, u32[]{:S(2)}) collective-permute-start(f32[128,256]{1,0:T(8,128)S(1)} %collective-permute-done.1.far), channel_id=1, source_target_pairs={{0,32},{32,0},{64,96},{96,64},{128,160},{160,128},{192,224},{224,1... | collective-permute-start | bytes 393224 | tf_op jit(solution)/shard_map/ppermute | solution.py:30
  20.5 6.4 %collective-permute-start.5 = (f32[256,256]{1,0:T(8,128)S(1)}, f32[256,256]{1,0:T(8,128)S(1)}, u32[]{:S(2)}, u32[]{:S(2)}) collective-permute-start(f32[256,256]{1,0:T(8,128)S(1)} %counts.1.own_ref), channel_id=1, source_target_pairs={{0,32},{32,0},{64,96},{96,64},{128,160},{160,128},{192,224},{224,1... | collective-permute-start | bytes 786440 | tf_op jit(solution)/shard_map/ppermute | solution.py:30
  20.7 11.7 %collective-permute-start.4 = (f32[128,256]{1,0:T(8,128)S(1)}, f32[128,256]{1,0:T(8,128)S(1)}, u32[]{:S(2)}, u32[]{:S(2)}) collective-permute-start(f32[128,256]{1,0:T(8,128)S(1)} %get-tuple-element.31), channel_id=1, source_target_pairs={{0,7},{1,6},{2,5},{3,4},{4,3},{5,2},{6,1},{7,0},{8,15},{9,14},{10,... | collective-permute-start | bytes 393224 | tf_op jit(solution)/shard_map/ppermute | solution.py:284
  32.5 3.0 %collective-permute-start.6 = (f32[128,256]{1,0:T(8,128)S(1)}, f32[128,256]{1,0:T(8,128)S(1)}, u32[]{:S(2)}, u32[]{:S(2)}) collective-permute-start(f32[128,256]{1,0:T(8,128)S(1)} %collective-permute-done.4.own_ref), channel_id=1, source_target_pairs={{0,32},{32,0},{64,96},{96,64},{128,160},{160,128},{192,224},{224,1... | collective-permute-start | bytes 393224 | tf_op jit(solution)/shard_map/ppermute | solution.py:30
  32.9 11.2 %collective-permute-start.11 = (f32[256,256]{1,0:T(8,128)S(1)}, f32[256,256]{1,0:T(8,128)S(1)}, u32[]{:S(2)}, u32[]{:S(2)}) collective-permute-start(f32[256,256]{1,0:T(8,128)S(1)} %get-tuple-element.38.chip_ref), channel_id=1, source_target_pairs={{0,64},{1,65},{2,66},{3,67},{4,68},{5,69},{6,70},{7,71},{8,72},{9,... | collective-permute-start | bytes 786440 | tf_op jit(solution)/shard_map/ppermute | solution.py:253
  35.8 8.9 %collective-permute-start.7 = (f32[256,256]{1,0:T(8,128)S(1)}, f32[256,256]{1,0:T(8,128)S(1)}, u32[]{:S(2)}, u32[]{:S(2)}) collective-permute-start(f32[256,256]{1,0:T(8,128)S(1)} %get-tuple-element.36), channel_id=1, source_target_pairs={{0,8},{1,9},{2,10},{3,11},{4,12},{5,13},{6,14},{7,15},{8,16},{9,17... | collective-permute-start | bytes 786440 | tf_op jit(solution)/shard_map/ppermute | solution.py:253
  38.6 5.6 %collective-permute-start.12 = (f32[128,256]{1,0:T(8,128)S(1)}, f32[128,256]{1,0:T(8,128)S(1)}, u32[]{:S(2)}, u32[]{:S(2)}) collective-permute-start(f32[128,256]{1,0:T(8,128)S(1)} %get-tuple-element.39), channel_id=1, source_target_pairs={{0,128},{1,129},{2,130},{3,131},{4,132},{5,133},{6,134},{7,135},{8... | collective-permute-start | bytes 393224 | tf_op jit(solution)/shard_map/ppermute | solution.py:254
  39.8 6.9 %collective-permute-start.9 = (f32[128,256]{1,0:T(8,128)S(1)}, f32[128,256]{1,0:T(8,128)S(1)}, u32[]{:S(2)}, u32[]{:S(2)}) collective-permute-start(f32[128,256]{1,0:T(8,128)S(1)} %get-tuple-element.37), channel_id=1, source_target_pairs={{0,16},{1,17},{2,18},{3,19},{4,20},{5,21},{6,22},{7,23},{8,24},{9,... | collective-permute-start | bytes 393224 | tf_op jit(solution)/shard_map/ppermute | solution.py:254
  44.2 3.9 %collective-permute-start.13 = (f32[256,256]{1,0:T(8,128)S(1)}, f32[256,256]{1,0:T(8,128)S(1)}, u32[]{:S(2)}, u32[]{:S(2)}) collective-permute-start(f32[256,256]{1,0:T(8,128)S(1)} %join.1.join_ref), channel_id=1, source_target_pairs={{0,32},{32,0},{64,96},{96,64},{128,160},{160,128},{192,224},{224,1... | collective-permute-start | bytes 786440 | tf_op jit(solution)/shard_map/ppermute | solution.py:30
  44.7 3.4 %collective-permute-start.8 = (f32[256,256]{1,0:T(8,128)S(1)}, f32[256,256]{1,0:T(8,128)S(1)}, u32[]{:S(2)}, u32[]{:S(2)}) collective-permute-start(f32[256,256]{1,0:T(8,128)S(1)} %collective-permute-done.7.near), channel_id=1, source_target_pairs={{0,32},{32,0},{64,96},{96,64},{128,160},{160,128},{192,224},{224,1... | collective-permute-start | bytes 786440 | tf_op jit(solution)/shard_map/ppermute | solution.py:30
  46.7 1.4 %collective-permute-start.10 = (f32[128,256]{1,0:T(8,128)S(1)}, f32[128,256]{1,0:T(8,128)S(1)}, u32[]{:S(2)}, u32[]{:S(2)}) collective-permute-start(f32[128,256]{1,0:T(8,128)S(1)} %collective-permute-done.9.far), channel_id=1, source_target_pairs={{0,32},{32,0},{64,96},{96,64},{128,160},{160,128},{192,224},{224,1... | collective-permute-start | bytes 393224 | tf_op jit(solution)/shard_map/ppermute | solution.py:30

commit v4 on v3

--- a/solution.py
+++ b/solution.py
@@ -110,22 +110,72 @@
     half_ref[...] = product_ref[pl.ds(core * half, half), :]
 
 
-def octet_kernel(product_ref, own_ref, sibling_ref, other_ref, octet_ref, half_ref):
-    core, _, z = place()
-    half = half_ref.shape[0]
-    rows = pl.ds(core * half, half)
-    other_ref[rows, :] = own_ref[...]
-    other_ref[pl.ds((1 - core) * half, half), :] = sibling_ref[...]
-
-    @pl.when(z < QUAD)
-    def _():
-        octet_ref[...] = product(product_ref[...], other_ref[...])
-
-    @pl.when(z >= QUAD)
-    def _():
-        octet_ref[...] = product(other_ref[...], product_ref[...])
-
-    half_ref[...] = octet_ref[rows, :]
+def spots():
+    core, y, z = place()
+    return (core, y, 2 * lax.rem(y, 2) + lax.div(z, QUAD), lax.rem(z, QUAD))
+
+
+def block_kernel(product_ref, near, near_sibling, far, far_sibling, block_ref, message_ref):
+    core, y, mine, _ = spots()
+    size, half = (product_ref.shape[0], far.shape[0])
+    block_ref[mine] = product_ref[...]
+    block_ref[mine ^ (1 + core)] = near[...]
+    block_ref[mine ^ (2 - core)] = near_sibling[...]
+    block_ref[mine ^ 3, pl.ds(core * half, half), :] = far[...]
+    block_ref[mine ^ 3, pl.ds((1 - core) * half, half), :] = far_sibling[...]
+    eye = diagonal(size)
+    ones = jnp.ones((1, size), jnp.float32)
+
+    @pl.when(y < Y // 2)
+    def _():
+        row = ones
+        for position in range(4):
+            row = row_times(row, block_ref[position], eye)
+        message_ref[...] = jnp.broadcast_to(row, message_ref.shape)
+
+    @pl.when(y >= Y // 2)
+    def _():
+        row = ones
+        for position in range(4):
+            row = times_row(block_ref[3 - position], row, eye)
+        message_ref[...] = jnp.broadcast_to(row, message_ref.shape)
+
+
+def unit_product(left, right):
+    moved = product(left, right)
+    return moved / jnp.max(jnp.max(moved, axis=0, keepdims=True), axis=1, keepdims=True)
+
+
+def sides_kernel(quad_ref, block_ref, path_ref, known_ref):
+    _, y, in_block, mine = spots()
+    size = path_ref.shape[0]
+    eye = diagonal(size)
+    ones = jnp.ones((1, size), jnp.float32)
+    start = jnp.where(eye, 1.0, 0.0)
+
+    @pl.when(y >= Y // 2)
+    def _():
+        path = lax.fori_loop(0, in_block, lambda i, m: unit_product(m, block_ref[i]), start)
+        path_ref[...] = lax.fori_loop(0, mine, lambda i, m: unit_product(m, quad_ref[i]), path)
+        row = lax.fori_loop(
+            0, 3 - in_block, lambda i, row: times_row(block_ref[3 - i], row, eye), ones
+        )
+        row = lax.fori_loop(
+            0, QUAD - 1 - mine, lambda i, row: times_row(quad_ref[QUAD - 1 - i], row, eye), row
+        )
+        known_ref[...] = jnp.broadcast_to(row, known_ref.shape)
+
+    @pl.when(y < Y // 2)
+    def _():
+        path = lax.fori_loop(
+            0, 3 - in_block, lambda i, m: unit_product(block_ref[3 - i], m), start
+        )
+        path_ref[...] = lax.fori_loop(
+            0, QUAD - 1 - mine, lambda i, m: unit_product(quad_ref[QUAD - 1 - i], m), path
+        )
+        row = lax.fori_loop(0, in_block, lambda i, row: row_times(row, block_ref[i], eye), ones)
+        row = lax.fori_loop(0, mine, lambda i, row: row_times(row, quad_ref[i], eye), row)
+        known_ref[...] = jnp.broadcast_to(row, known_ref.shape)
 
 
 def chip_kernel(own_ref, sibling_ref, both_ref, half_ref):
@@ -143,32 +193,26 @@
 
 
 def final_kernel(
-    scale, potential_ref, noise_ref, quad_ref, other_ref, near, near_sibling, far, far_sibling,
-    chip_ref, join_ref, sibling_join_ref, updated_ref, beliefs_ref, octet_ref
+    scale, potential_ref, noise_ref, kernel_ref, path_ref, known_ref, message_ref, chip_ref,
+    join_ref, sibling_join_ref, updated_ref, beliefs_ref, column_ref, row_ref
 ):
-    core, y, z = place()
+    _, y, _, _ = spots()
     size = potential_ref.shape[0]
-    put_others(octet_ref, y, near, near_sibling, far, far_sibling, core)
     eye = diagonal(size)
-    ones = jnp.ones((1, size), jnp.float32)
-    later_quad = lax.div(z, QUAD)
-    mine = lax.rem(z, QUAD)
-    forward = lax.fori_loop(0, y, lambda i, row: row_times(row, octet_ref[i], eye), ones)
-    forward = lax.fori_loop(
-        0, later_quad, lambda i, row: row_times(row, other_ref[...], eye), forward
-    )
-    forward = lax.fori_loop(0, mine, lambda i, row: row_times(row, quad_ref[i], eye), forward)
-    backward = lax.fori_loop(
-        0, Y - 1 - y, lambda i, row: times_row(octet_ref[Y - 1 - i], row, eye), ones
-    )
-    backward = lax.fori_loop(
-        0, 1 - later_quad, lambda i, row: times_row(other_ref[...], row, eye), backward
-    )
-    backward = lax.fori_loop(
-        0, 3 - mine, lambda i, row: times_row(quad_ref[3 - i], row, eye), backward
-    )
-    column = as_column(forward, eye) / jnp.sum(forward, axis=1, keepdims=True)
-    joint = column * quad_ref[mine] * backward
+    known, message = (known_ref[0:1, :], message_ref[0:1, :])
+
+    @pl.when(y >= Y // 2)
+    def _():
+        forward = row_times(message, path_ref[...], eye)
+        column_ref[...] = as_column(forward, eye) / jnp.sum(forward, axis=1, keepdims=True)
+        row_ref[...] = known
+
+    @pl.when(y < Y // 2)
+    def _():
+        column_ref[...] = as_column(known, eye) / jnp.sum(known, axis=1, keepdims=True)
+        row_ref[...] = times_row(path_ref[...], message, eye)
+
+    joint = column_ref[...] * kernel_ref[...] * row_ref[...]
     total = jnp.sum(jnp.sum(joint, axis=0, keepdims=True), axis=1, keepdims=True)
     beliefs = joint * (size * size / total)
     beliefs_ref[...] = beliefs
@@ -248,11 +292,12 @@
     return pairs
 
 
-def exchange(whole, half, step):
+def exchange(whole, half, near_step, far_step):
     axes = ("dp", "clique")
-    near = lax.ppermute(whole, axes, everywhere(lambda x, c, y, z: step(x, y, z, 1 - 2 * c)))
-    far = lax.ppermute(half, axes, everywhere(lambda x, c, y, z: step(x, y, z, 2)))
-    return (near, far)
+    return (
+        lax.ppermute(whole, axes, everywhere(near_step)),
+        lax.ppermute(half, axes, everywhere(lambda x, c, y, z: far_step(x, y, z))),
+    )
 
 
 def per_device(table_rows, attribute_order, log_potential, measure_noise):
@@ -274,36 +319,53 @@
         pltpu.with_memory_space_constraint(potential, pltpu.HBM),
     )
     near, far = exchange(
-        kernel, half_of_kernel, lambda x, y, z, s: (x, y, z // QUAD * QUAD + (z + s) % QUAD)
+        kernel,
+        half_of_kernel,
+        lambda x, c, y, z: (x, y, z // QUAD * QUAD + (z + 1 - 2 * c) % QUAD),
+        lambda x, y, z: (x, y, z ^ 2),
     )
     counts = count_pairs(order, table_rows, size)
     near, far, counts = lax.optimization_barrier((near, far, counts))
     quad, quad_product, half_product = call(
         quad_kernel, out_shape=(shape(QUAD, size, size), whole, half), name="quad"
     )(kernel, near, other_core(near), far, other_core(far))
-    other = lax.ppermute(half_product, "clique", along_clique(lambda y, z: (y, Z - 1 - z)))
-    counts, quad_product = lax.optimization_barrier((counts, quad_product))
+    near, far = exchange(
+        quad_product,
+        half_product,
+        lambda x, c, y, z: (x, y ^ 1, z) if c else (x, y, Z - 1 - z),
+        lambda x, y, z: (x, y ^ 1, Z - 1 - z),
+    )
+    counts, quad = lax.optimization_barrier((counts, quad))
     chip_counts, half_counts = call(chip_kernel, out_shape=(whole, half), name="chip")(
         counts, other_core(counts)
     )
     near_counts, far_counts = exchange(
-        chip_counts, half_counts, lambda x, y, z, s: ((x + s) % 4, y, z)
-    )
-    other, chip_counts = lax.optimization_barrier((other, chip_counts))
-    other_product, octet, half_octet = call(
-        octet_kernel, out_shape=(whole, whole, half), name="octet"
-    )(quad_product, other, other_core(other))
-    near, far = exchange(octet, half_octet, lambda x, y, z, s: (x, (y + s) % Y, z))
+        chip_counts,
+        half_counts,
+        lambda x, c, y, z: ((x + 1 - 2 * c) % 4, y, z),
+        lambda x, y, z: (x ^ 2, y, z),
+    )
+    near, far, near_counts, far_counts = lax.optimization_barrier(
+        (near, far, near_counts, far_counts)
+    )
+    block, message = call(
+        block_kernel, out_shape=(shape(4, size, size), shape(8, size)), name="block"
+    )(quad_product, near, other_core(near), far, other_core(far))
     joined = call(join_kernel, out_shape=whole, name="join")(near_counts, far_counts)
+    arrived = lax.ppermute(message, "clique", along_clique(lambda y, z: (y ^ 2, z)))
+    path, known = call(sides_kernel, out_shape=(whole, shape(8, size)), name="sides")(quad, block)
     total_rows = table_rows.shape[1] * lax.axis_size("dp")
     updated, beliefs = call(
         functools.partial(final_kernel, size * size / total_rows),
         out_shape=(whole, whole),
-        scratch_shapes=[pltpu.VMEM((Y, size, size), jnp.float32)],
+        scratch_shapes=[
+            pltpu.VMEM((size, 1), jnp.float32),
+            pltpu.VMEM((1, size), jnp.float32),
+        ],
         name="final",
     )(
-        potential, measure_noise[0], quad, other_product, near, other_core(near), far,
-        other_core(far), chip_counts, joined, other_core(joined),
+        potential, measure_noise[0], kernel, path, known, arrived, chip_counts, joined,
+        other_core(joined),
     )
     return (updated[None], beliefs[None])
 

time: 50.3 us -> 48.8 us (0.970)
  waiting for transfers between devices: 16 us -> 11.1 us
  starting transfers between devices: 20.1 us -> 22 us
  Pallas kernels: 13.3 us -> 14.9 us
    ppermute x7, waiting for transfers between devices: 13.7 us -> 8.63 us  [the longest x3 8.62 us: exchange(): lax.ppermute(half, axes, everywhere(lambda x, c, y, z: far_step(x, y, z)))]
    pallas_call x1 -> x2, Pallas kernels: 0.32 us -> 3.05 us  [the longest x1 2.48 us: per_device(): call(sides_kernel, out_shape=(whole, shape(8, size)), name='sides')]
    ppermute x7, starting transfers between devices: 18.3 us -> 19.4 us  [the longest x3 9.38 us: exchange(): lax.ppermute(whole, axes, everywhere(near_step))]
    pallas_call x1, Pallas kernels: 2.01 us -> 1.18 us  [per_device(): call(functools.partial(final_kernel, size * size / total_rows), out_shape...]
    ppermute x7 -> x6, starting transfers between devices: 1.83 us -> 2.58 us  [other_core(): return lax.ppermute(value, 'dp', along_dp(lambda x, c: (x, 1 - c)))]
    ppermute x7 -> x6, waiting for transfers between devices: 2.21 us -> 2.43 us  [other_core(): return lax.ppermute(value, 'dp', along_dp(lambda x, c: (x, 1 - c)))]
  transfers between devices with their start and end apart: 14 -> 13, of which waited for: 7 -> 5; matrix products, arithmetic and copies ran while one was open for 0% -> 0% of each run, Pallas kernels for 18% -> 24%
where the time goes in v4:
time: 48.8 us; the launch traced here: 48.7 us
  starting transfers between devices  22 us (45%)
  Pallas kernels  14.9 us (31%)
  waiting for transfers between devices  11.1 us (23%)
  between operations  0.72 us (1%)
    ppermute x3, starting transfers between devices, exchange(): lax.ppermute(whole, axes, everywhere(near_step))  9.38 us
    ppermute x3, waiting for transfers between devices, exchange(): lax.ppermute(half, axes, everywhere(lambda x, c, y, z: far_step(x, y, z)))  8.62 us
    pallas_call x1, Pallas kernels, count_pairs(): pl.pallas_call(functools.partial(count_kernel, part), out_shape=shape(siz...  8.57 us
    ppermute x3, starting transfers between devices, exchange(): lax.ppermute(half, axes, everywhere(lambda x, c, y, z: far_step(x, y, z)))  7.29 us
    ppermute x1, starting transfers between devices, per_device(): lax.ppermute(message, 'clique', along_clique(lambda y, z: (y ^ 2, z)))  2.73 us
    ppermute x6, starting transfers between devices, other_core(): return lax.ppermute(value, 'dp', along_dp(lambda x, c: (x, 1 - c)))  2.58 us
    pallas_call x1, Pallas kernels, per_device(): call(sides_kernel, out_shape=(whole, shape(8, size)), name='sides')  2.48 us
    ppermute x6, waiting for transfers between devices, other_core(): return lax.ppermute(value, 'dp', along_dp(lambda x, c: (x, 1 - c)))  2.43 us
  transfers between devices with their start and end apart: 13, of which 5 were waited for; matrix products, arithmetic and copies ran while one was open for 0% of the time, Pallas kernels for 24%

profile of v4, /device:TPU:1, one launch (start us, length us, event | category | flops | bytes accessed | tf_op | source)
XLA Modules:
  0.0 48.7 jit_solution(8591544540158744456)
XLA Ops:
  0.6 1.1 %read.1 = (s32[33]{0:T(128)S(1)}, f32[256,256]{1,0:T(8,128)S(1)}, f32[128,256]{1,0:T(8,128)S(1)}) custom-call(s32[33]{0:T(128)} %order_hbm.1, f32[256,256]{1,0:T(8,128)} %bitcast.4), custom_call_target="tpu_custom_call" | custom-call | tf_op jit(solution)/shard_map/read/pallas_call | solution.py:310
  1.7 5.3 %collective-permute-start = (f32[256,256]{1,0:T(8,128)S(1)}, f32[256,256]{1,0:T(8,128)S(1)}, u32[]{:S(2)}, u32[]{:S(2)}) collective-permute-start(f32[256,256]{1,0:T(8,128)S(1)} %get-tuple-element.25.kernel_ref), channel_id=1, source_target_pairs={{0,1},{1,2},{2,3},{3,0},{4,5},{5,6},{6,7},{7,4},{8,9},{9,10},{10,1... | collective-permute-start | bytes 786440 | tf_op jit(solution)/shard_map/ppermute | solution.py:298
  6.9 0.0 collective-permute-start.1
  6.9 0.0 copy-start
  6.9 0.0 copy-start.1
  7.0 8.6 %counts.1.own_ref = f32[256,256]{1,0:T(8,128)S(1)} custom-call(s32[33]{0:T(128)S(1)} %get-tuple-element.27.order_ref, s32[33,65536]{1,0:T(8,128)} %right_ref.1, s32[33,65536]{1,0:T(8,128)} %right_ref.1), custom_call_target="tpu_custom_call" | custom-call | tf_op jit(solution)/shard_map/counts/pallas_call | solution.py:269
  15.5 2.2 %collective-permute-done.1.far = f32[128,256]{1,0:T(8,128)S(1)} collective-permute-done((f32[128,256]{1,0:T(8,128)S(1)}, f32[128,256]{1,0:T(8,128)S(1)}, u32[]{:S(2)}, u32[]{:S(2)}) %collective-permute-start.1) | collective-permute-done | bytes 131104 | tf_op jit(solution)/shard_map/ppermute | solution.py:299
  17.8 0.0 collective-permute-done.near
  17.8 0.1 collective-permute-start.2
  17.8 0.5 collective-permute-start.3
  18.3 1.2 %collective-permute-done.3.far_sibling = f32[128,256]{1,0:T(8,128)S(1)} collective-permute-done((f32[128,256]{1,0:T(8,128)S(1)}, f32[128,256]{1,0:T(8,128)S(1)}, u32[]{:S(2)}, u32[]{:S(2)}) %collective-permute-start.3) | collective-permute-done | bytes 131104 | tf_op jit(solution)/shard_map/ppermute | solution.py:30
  19.5 0.0 collective-permute-done.2.near_sibling
  19.5 1.0 %quad.1 = (f32[4,256,256]{2,1,0:T(8,128)S(1)}, f32[256,256]{1,0:T(8,128)S(1)}, f32[128,256]{1,0:T(8,128)S(1)}) custom-call(f32[256,256]{1,0:T(8,128)S(1)} %get-tuple-element.25.kernel_ref, f32[256,256]{1,0:T(8,128)S(1)} %collective-permute-done.near, f32[256,256]{1,0:T(8,128)S(1)} %collective-permute-done.2.near_sibling, ...), custom_call_target="tpu_custom_call" | custom-call | tf_op jit(solution)/shard_map/quad/pallas_call | solution.py:329
  20.5 0.2 collective-permute-start.6
  20.7 1.6 %collective-permute-start.4 = (f32[256,256]{1,0:T(8,128)S(1)}, f32[256,256]{1,0:T(8,128)S(1)}, u32[]{:S(2)}, u32[]{:S(2)}) collective-permute-start(f32[256,256]{1,0:T(8,128)S(1)} %get-tuple-element.33.product_ref), channel_id=1, source_target_pairs={{0,7},{1,6},{2,5},{3,4},{4,3},{5,2},{6,1},{7,0},{8,15},{9,14},{10,... | collective-permute-start | bytes 786440 | tf_op jit(solution)/shard_map/ppermute | solution.py:298
  22.3 0.0 collective-permute-done.6.sibling_ref
  22.4 2.6 %collective-permute-start.7 = (f32[256,256]{1,0:T(8,128)S(1)}, f32[256,256]{1,0:T(8,128)S(1)}, u32[]{:S(2)}, u32[]{:S(2)}) collective-permute-start(f32[256,256]{1,0:T(8,128)S(1)} %get-tuple-element.36.chip_ref), channel_id=1, source_target_pairs={{0,64},{1,65},{2,66},{3,67},{4,68},{5,69},{6,70},{7,71},{8,72},{9,... | collective-permute-start | bytes 786440 | tf_op jit(solution)/shard_map/ppermute | solution.py:298
  24.9 6.8 %collective-permute-start.5 = (f32[128,256]{1,0:T(8,128)S(1)}, f32[128,256]{1,0:T(8,128)S(1)}, u32[]{:S(2)}, u32[]{:S(2)}) collective-permute-start(f32[128,256]{1,0:T(8,128)S(1)} %get-tuple-element.34), channel_id=1, source_target_pairs={{0,15},{1,14},{2,13},{3,12},{4,11},{5,10},{6,9},{7,8},{8,7},{9,6},... | collective-permute-start | bytes 393224 | tf_op jit(solution)/shard_map/ppermute | solution.py:299
  31.7 0.5 %collective-permute-start.8 = (f32[128,256]{1,0:T(8,128)S(1)}, f32[128,256]{1,0:T(8,128)S(1)}, u32[]{:S(2)}, u32[]{:S(2)}) collective-permute-start(f32[128,256]{1,0:T(8,128)S(1)} %get-tuple-element.37), channel_id=1, source_target_pairs={{0,128},{1,129},{2,130},{3,131},{4,132},{5,133},{6,134},{7,135},{8... | collective-permute-start | bytes 393224 | tf_op jit(solution)/shard_map/ppermute | solution.py:299
  32.2 5.1 %collective-permute-done.5.far = f32[128,256]{1,0:T(8,128)S(1)} collective-permute-done((f32[128,256]{1,0:T(8,128)S(1)}, f32[128,256]{1,0:T(8,128)S(1)}, u32[]{:S(2)}, u32[]{:S(2)}) %collective-permute-start.5) | collective-permute-done | bytes 131104 | tf_op jit(solution)/shard_map/ppermute | solution.py:299
  37.3 0.0 collective-permute-done.4.near
  37.3 1.3 %collective-permute-done.8.far_ref = f32[128,256]{1,0:T(8,128)S(1)} collective-permute-done((f32[128,256]{1,0:T(8,128)S(1)}, f32[128,256]{1,0:T(8,128)S(1)}, u32[]{:S(2)}, u32[]{:S(2)}) %collective-permute-start.8) | collective-permute-done | bytes 131104 | tf_op jit(solution)/shard_map/ppermute | solution.py:299
  38.6 0.0 collective-permute-done.7.near_ref
  38.6 1.2 %collective-permute-start.9 = (f32[256,256]{1,0:T(8,128)S(1)}, f32[256,256]{1,0:T(8,128)S(1)}, u32[]{:S(2)}, u32[]{:S(2)}) collective-permute-start(f32[256,256]{1,0:T(8,128)S(1)} %collective-permute-done.4.near), channel_id=1, source_target_pairs={{0,32},{32,0},{64,96},{96,64},{128,160},{160,128},{192,224},{224,1... | collective-permute-start | bytes 786440 | tf_op jit(solution)/shard_map/ppermute | solution.py:30
  39.9 0.1 collective-permute-start.12
  40.0 0.5 %collective-permute-start.10 = (f32[128,256]{1,0:T(8,128)S(1)}, f32[128,256]{1,0:T(8,128)S(1)}, u32[]{:S(2)}, u32[]{:S(2)}) collective-permute-start(f32[128,256]{1,0:T(8,128)S(1)} %collective-permute-done.5.far), channel_id=1, source_target_pairs={{0,32},{32,0},{64,96},{96,64},{128,160},{160,128},{192,224},{224,1... | collective-permute-start | bytes 393224 | tf_op jit(solution)/shard_map/ppermute | solution.py:30
  40.5 1.2 %collective-permute-done.10.far_sibling = f32[128,256]{1,0:T(8,128)S(1)} collective-permute-done((f32[128,256]{1,0:T(8,128)S(1)}, f32[128,256]{1,0:T(8,128)S(1)}, u32[]{:S(2)}, u32[]{:S(2)}) %collective-permute-start.10) | collective-permute-done | bytes 131104 | tf_op jit(solution)/shard_map/ppermute | solution.py:30
  41.7 0.0 collective-permute-done.9.near_sibling
  41.7 0.6 %block.1 = (f32[4,256,256]{2,1,0:T(8,128)S(1)}, f32[8,256]{1,0:T(8,128)S(1)}) custom-call(f32[256,256]{1,0:T(8,128)S(1)} %get-tuple-element.33.product_ref, f32[256,256]{1,0:T(8,128)S(1)} %collective-permute-done.4.near, f32[256,256]{1,0:T(8,128)S(1)} %collective-permute-done.9.near_sibling, f32[128,256]{1,0:T(8,128)S(1)} %collective-permute-done.5.far, ...), custom_call_target="tpu_custom_call" | custom-call | tf_op jit(solution)/shard_map/block/pallas_call | solution.py:351
  42.3 2.7 %collective-permute-start.11 = (f32[8,256]{1,0:T(8,128)S(1)}, f32[8,256]{1,0:T(8,128)S(1)}, u32[]{:S(2)}, u32[]{:S(2)}) collective-permute-start(f32[8,256]{1,0:T(8,128)S(1)} %get-tuple-element.43), channel_id=1, source_target_pairs={{0,16},{1,17},{2,18},{3,19},{4,20},{5,21},{6,22},{7,23},{8,24},{9,... | collective-permute-start | bytes 24584 | tf_op jit(solution)/shard_map/ppermute | solution.py:355
  45.0 2.5 %sides.1 = (f32[256,256]{1,0:T(8,128)S(1)}, f32[8,256]{1,0:T(8,128)S(1)}) custom-call(f32[4,256,256]{2,1,0:T(8,128)S(1)} %get-tuple-element.32.quad_ref, f32[4,256,256]{2,1,0:T(8,128)S(1)} %get-tuple-element.40.block_ref), custom_call_target="tpu_custom_call" | custom-call | tf_op jit(solution)/shard_map/sides/pallas_call | solution.py:356
  47.5 0.0 collective-permute-done.12.sibling_join_ref
  47.5 0.0 collective-permute-done.11.message_ref
  47.5 0.0 copy-done
  47.5 0.0 copy-done.1
  47.5 1.2 %final.1 = (f32[256,256]{1,0:T(8,128)}, f32[256,256]{1,0:T(8,128)}) custom-call(f32[256,256]{1,0:T(8,128)S(1)} %bitcast.5, f32[256,256]{1,0:T(8,128)S(1)} %bitcast.6, f32[256,256]{1,0:T(8,128)S(1)} %get-tuple-element.25.kernel_ref, f32[256,256]{1,0:T(8,128)S(1)} %get-tuple-element.41.path_ref, f32[8,256]{1,0:T(8,128)S(1)} %get-tuple-element.42.known_ref, ...), custom_call_target="tpu_custom_call" | custom-call | tf_op jit(solution)/shard_map/final/pallas_call | solution.py:358
  (2 shorter events, 0.1 us)
Async XLA Ops:
  1.7 16.1 %collective-permute-start = (f32[256,256]{1,0:T(8,128)S(1)}, f32[256,256]{1,0:T(8,128)S(1)}, u32[]{:S(2)}, u32[]{:S(2)}) collective-permute-start(f32[256,256]{1,0:T(8,128)S(1)} %get-tuple-element.25.kernel_ref), channel_id=1, source_target_pairs={{0,1},{1,2},{2,3},{3,0},{4,5},{5,6},{6,7},{7,4},{8,9},{9,10},{10,1... | collective-permute-start | bytes 786440 | tf_op jit(solution)/shard_map/ppermute | solution.py:298
  6.9 10.8 %collective-permute-start.1 = (f32[128,256]{1,0:T(8,128)S(1)}, f32[128,256]{1,0:T(8,128)S(1)}, u32[]{:S(2)}, u32[]{:S(2)}) collective-permute-start(f32[128,256]{1,0:T(8,128)S(1)} %get-tuple-element.26), channel_id=1, source_target_pairs={{0,2},{1,3},{2,0},{3,1},{4,6},{5,7},{6,4},{7,5},{8,10},{9,11},{10,... | collective-permute-start | bytes 393224 | tf_op jit(solution)/shard_map/ppermute | solution.py:299
  6.9 40.6 %copy-start = (f32[1,256,256]{2,1,0:T(8,128)S(1)}, f32[1,256,256]{2,1,0:T(8,128)}, u32[]{:S(2)}) copy-start(f32[1,256,256]{2,1,0:T(8,128)} %param.6) | copy-start | bytes 786436
  6.9 40.6 %copy-start.1 = (f32[1,256,256]{2,1,0:T(8,128)S(1)}, f32[1,256,256]{2,1,0:T(8,128)}, u32[]{:S(2)}) copy-start(f32[1,256,256]{2,1,0:T(8,128)} %param.7) | copy-start | bytes 786436
  17.8 1.7 %collective-permute-start.2 = (f32[256,256]{1,0:T(8,128)S(1)}, f32[256,256]{1,0:T(8,128)S(1)}, u32[]{:S(2)}, u32[]{:S(2)}) collective-permute-start(f32[256,256]{1,0:T(8,128)S(1)} %collective-permute-done.near), channel_id=1, source_target_pairs={{0,32},{32,0},{64,96},{96,64},{128,160},{160,128},{192,224},{224,1... | collective-permute-start | bytes 786440 | tf_op jit(solution)/shard_map/ppermute | solution.py:30
  17.8 1.7 %collective-permute-start.3 = (f32[128,256]{1,0:T(8,128)S(1)}, f32[128,256]{1,0:T(8,128)S(1)}, u32[]{:S(2)}, u32[]{:S(2)}) collective-permute-start(f32[128,256]{1,0:T(8,128)S(1)} %collective-permute-done.1.far), channel_id=1, source_target_pairs={{0,32},{32,0},{64,96},{96,64},{128,160},{160,128},{192,224},{224,1... | collective-permute-start | bytes 393224 | tf_op jit(solution)/shard_map/ppermute | solution.py:30
  20.5 1.8 %collective-permute-start.6 = (f32[256,256]{1,0:T(8,128)S(1)}, f32[256,256]{1,0:T(8,128)S(1)}, u32[]{:S(2)}, u32[]{:S(2)}) collective-permute-start(f32[256,256]{1,0:T(8,128)S(1)} %counts.1.own_ref), channel_id=1, source_target_pairs={{0,32},{32,0},{64,96},{96,64},{128,160},{160,128},{192,224},{224,1... | collective-permute-start | bytes 786440 | tf_op jit(solution)/shard_map/ppermute | solution.py:30
  20.7 16.6 %collective-permute-start.4 = (f32[256,256]{1,0:T(8,128)S(1)}, f32[256,256]{1,0:T(8,128)S(1)}, u32[]{:S(2)}, u32[]{:S(2)}) collective-permute-start(f32[256,256]{1,0:T(8,128)S(1)} %get-tuple-element.33.product_ref), channel_id=1, source_target_pairs={{0,7},{1,6},{2,5},{3,4},{4,3},{5,2},{6,1},{7,0},{8,15},{9,14},{10,... | collective-permute-start | bytes 786440 | tf_op jit(solution)/shard_map/ppermute | solution.py:298
  22.4 16.2 %collective-permute-start.7 = (f32[256,256]{1,0:T(8,128)S(1)}, f32[256,256]{1,0:T(8,128)S(1)}, u32[]{:S(2)}, u32[]{:S(2)}) collective-permute-start(f32[256,256]{1,0:T(8,128)S(1)} %get-tuple-element.36.chip_ref), channel_id=1, source_target_pairs={{0,64},{1,65},{2,66},{3,67},{4,68},{5,69},{6,70},{7,71},{8,72},{9,... | collective-permute-start | bytes 786440 | tf_op jit(solution)/shard_map/ppermute | solution.py:298
  24.9 12.4 %collective-permute-start.5 = (f32[128,256]{1,0:T(8,128)S(1)}, f32[128,256]{1,0:T(8,128)S(1)}, u32[]{:S(2)}, u32[]{:S(2)}) collective-permute-start(f32[128,256]{1,0:T(8,128)S(1)} %get-tuple-element.34), channel_id=1, source_target_pairs={{0,15},{1,14},{2,13},{3,12},{4,11},{5,10},{6,9},{7,8},{8,7},{9,6},... | collective-permute-start | bytes 393224 | tf_op jit(solution)/shard_map/ppermute | solution.py:299
  31.7 6.9 %collective-permute-start.8 = (f32[128,256]{1,0:T(8,128)S(1)}, f32[128,256]{1,0:T(8,128)S(1)}, u32[]{:S(2)}, u32[]{:S(2)}) collective-permute-start(f32[128,256]{1,0:T(8,128)S(1)} %get-tuple-element.37), channel_id=1, source_target_pairs={{0,128},{1,129},{2,130},{3,131},{4,132},{5,133},{6,134},{7,135},{8... | collective-permute-start | bytes 393224 | tf_op jit(solution)/shard_map/ppermute | solution.py:299
  38.6 3.1 %collective-permute-start.9 = (f32[256,256]{1,0:T(8,128)S(1)}, f32[256,256]{1,0:T(8,128)S(1)}, u32[]{:S(2)}, u32[]{:S(2)}) collective-permute-start(f32[256,256]{1,0:T(8,128)S(1)} %collective-permute-done.4.near), channel_id=1, source_target_pairs={{0,32},{32,0},{64,96},{96,64},{128,160},{160,128},{192,224},{224,1... | collective-permute-start | bytes 786440 | tf_op jit(solution)/shard_map/ppermute | solution.py:30
  39.9 7.6 %collective-permute-start.12 = (f32[256,256]{1,0:T(8,128)S(1)}, f32[256,256]{1,0:T(8,128)S(1)}, u32[]{:S(2)}, u32[]{:S(2)}) collective-permute-start(f32[256,256]{1,0:T(8,128)S(1)} %join.1.join_ref), channel_id=1, source_target_pairs={{0,32},{32,0},{64,96},{96,64},{128,160},{160,128},{192,224},{224,1... | collective-permute-start | bytes 786440 | tf_op jit(solution)/shard_map/ppermute | solution.py:30
  40.0 1.7 %collective-permute-start.10 = (f32[128,256]{1,0:T(8,128)S(1)}, f32[128,256]{1,0:T(8,128)S(1)}, u32[]{:S(2)}, u32[]{:S(2)}) collective-permute-start(f32[128,256]{1,0:T(8,128)S(1)} %collective-permute-done.5.far), channel_id=1, source_target_pairs={{0,32},{32,0},{64,96},{96,64},{128,160},{160,128},{192,224},{224,1... | collective-permute-start | bytes 393224 | tf_op jit(solution)/shard_map/ppermute | solution.py:30
  42.3 5.2 %collective-permute-start.11 = (f32[8,256]{1,0:T(8,128)S(1)}, f32[8,256]{1,0:T(8,128)S(1)}, u32[]{:S(2)}, u32[]{:S(2)}) collective-permute-start(f32[8,256]{1,0:T(8,128)S(1)} %get-tuple-element.43), channel_id=1, source_target_pairs={{0,16},{1,17},{2,18},{3,19},{4,20},{5,21},{6,22},{7,23},{8,24},{9,... | collective-permute-start | bytes 24584 | tf_op jit(solution)/shard_map/ppermute | solution.py:355

commit v5 on v4

--- a/solution.py
+++ b/solution.py
@@ -345,12 +345,14 @@
         lambda x, c, y, z: ((x + 1 - 2 * c) % 4, y, z),
         lambda x, y, z: (x ^ 2, y, z),
     )
-    near, far, near_counts, far_counts = lax.optimization_barrier(
-        (near, far, near_counts, far_counts)
+    near, far, far_counts = lax.optimization_barrier((near, far, far_counts))
+    near_sibling, far_sibling = (other_core(near), other_core(far))
+    near_sibling, far_sibling, near_counts = lax.optimization_barrier(
+        (near_sibling, far_sibling, near_counts)
     )
     block, message = call(
         block_kernel, out_shape=(shape(4, size, size), shape(8, size)), name="block"
-    )(quad_product, near, other_core(near), far, other_core(far))
+    )(quad_product, near, near_sibling, far, far_sibling)
     joined = call(join_kernel, out_shape=whole, name="join")(near_counts, far_counts)
     arrived = lax.ppermute(message, "clique", along_clique(lambda y, z: (y ^ 2, z)))
     path, known = call(sides_kernel, out_shape=(whole, shape(8, size)), name="sides")(quad, block)

time: 48.8 us -> 48.7 us (level)
  waiting for transfers between devices: 11.1 us -> 9.14 us
  starting transfers between devices: 22 us -> 23.8 us
    ppermute x6, starting transfers between devices: 2.58 us -> 4.8 us  [other_core(): return lax.ppermute(value, 'dp', along_dp(lambda x, c: (x, 1 - c)))]
    ppermute x3, waiting for transfers between devices: 8.62 us -> 6.65 us  [exchange(): lax.ppermute(half, axes, everywhere(lambda x, c, y, z: far_step(x, y, z)))]
    ppermute x3, starting transfers between devices: 9.38 us -> 7.69 us  [exchange(): lax.ppermute(whole, axes, everywhere(near_step))]
    ppermute x3, starting transfers between devices: 7.29 us -> 8.61 us  [exchange(): lax.ppermute(half, axes, everywhere(lambda x, c, y, z: far_step(x, y, z)))]
  transfers between devices with their start and end apart: 13 -> 13, of which waited for: 5 -> 4; matrix products, arithmetic and copies ran while one was open for 0% -> 0% of each run, Pallas kernels for 24% -> 24%
where the time goes in v5:
time: 48.7 us; the launch traced here: 48.6 us
  starting transfers between devices  23.8 us (49%)
  Pallas kernels  14.9 us (31%)
  waiting for transfers between devices  9.14 us (19%)
  between operations  0.72 us (1%)
    ppermute x3, starting transfers between devices, exchange(): lax.ppermute(half, axes, everywhere(lambda x, c, y, z: far_step(x, y, z)))  8.61 us
    pallas_call x1, Pallas kernels, count_pairs(): pl.pallas_call(functools.partial(count_kernel, part), out_shape=shape(siz...  8.57 us
    ppermute x3, starting transfers between devices, exchange(): lax.ppermute(whole, axes, everywhere(near_step))  7.69 us
    ppermute x3, waiting for transfers between devices, exchange(): lax.ppermute(half, axes, everywhere(lambda x, c, y, z: far_step(x, y, z)))  6.65 us
    ppermute x6, starting transfers between devices, other_core(): return lax.ppermute(value, 'dp', along_dp(lambda x, c: (x, 1 - c)))  4.8 us
    ppermute x1, starting transfers between devices, per_device(): lax.ppermute(message, 'clique', along_clique(lambda y, z: (y ^ 2, z)))  2.73 us
    ppermute x6, waiting for transfers between devices, other_core(): return lax.ppermute(value, 'dp', along_dp(lambda x, c: (x, 1 - c)))  2.48 us
    pallas_call x1, Pallas kernels, per_device(): call(sides_kernel, out_shape=(whole, shape(8, size)), name='sides')  2.48 us
  transfers between devices with their start and end apart: 13, of which 4 were waited for; matrix products, arithmetic and copies ran while one was open for 0% of the time, Pallas kernels for 24%

profile of v5, /device:TPU:1, one launch (start us, length us, event | category | flops | bytes accessed | tf_op | source)
XLA Modules:
  0.0 48.6 jit_solution(5076527893971885682)
XLA Ops:
  0.6 1.1 %read.1 = (s32[33]{0:T(128)S(1)}, f32[256,256]{1,0:T(8,128)S(1)}, f32[128,256]{1,0:T(8,128)S(1)}) custom-call(s32[33]{0:T(128)} %order_hbm.1, f32[256,256]{1,0:T(8,128)} %bitcast.4), custom_call_target="tpu_custom_call" | custom-call | tf_op jit(solution)/shard_map/read/pallas_call | solution.py:310
  1.7 5.3 %collective-permute-start = (f32[256,256]{1,0:T(8,128)S(1)}, f32[256,256]{1,0:T(8,128)S(1)}, u32[]{:S(2)}, u32[]{:S(2)}) collective-permute-start(f32[256,256]{1,0:T(8,128)S(1)} %get-tuple-element.27.kernel_ref), channel_id=1, source_target_pairs={{0,1},{1,2},{2,3},{3,0},{4,5},{5,6},{6,7},{7,4},{8,9},{9,10},{10,1... | collective-permute-start | bytes 786440 | tf_op jit(solution)/shard_map/ppermute | solution.py:298
  6.9 0.0 collective-permute-start.1
  6.9 0.0 copy-start
  6.9 0.0 copy-start.1
  7.0 8.6 %counts.1.own_ref = f32[256,256]{1,0:T(8,128)S(1)} custom-call(s32[33]{0:T(128)S(1)} %get-tuple-element.29.order_ref, s32[33,65536]{1,0:T(8,128)} %right_ref.1, s32[33,65536]{1,0:T(8,128)} %right_ref.1), custom_call_target="tpu_custom_call" | custom-call | tf_op jit(solution)/shard_map/counts/pallas_call | solution.py:269
  15.5 2.2 %collective-permute-done.1.far = f32[128,256]{1,0:T(8,128)S(1)} collective-permute-done((f32[128,256]{1,0:T(8,128)S(1)}, f32[128,256]{1,0:T(8,128)S(1)}, u32[]{:S(2)}, u32[]{:S(2)}) %collective-permute-start.1) | collective-permute-done | bytes 131104 | tf_op jit(solution)/shard_map/ppermute | solution.py:299
  17.8 0.0 collective-permute-done.near
  17.8 0.1 collective-permute-start.2
  17.8 0.5 collective-permute-start.3
  18.3 1.2 %collective-permute-done.3.far_sibling = f32[128,256]{1,0:T(8,128)S(1)} collective-permute-done((f32[128,256]{1,0:T(8,128)S(1)}, f32[128,256]{1,0:T(8,128)S(1)}, u32[]{:S(2)}, u32[]{:S(2)}) %collective-permute-start.3) | collective-permute-done | bytes 131104 | tf_op jit(solution)/shard_map/ppermute | solution.py:30
  19.5 0.0 collective-permute-done.2.near_sibling
  19.5 1.0 %quad.1 = (f32[4,256,256]{2,1,0:T(8,128)S(1)}, f32[256,256]{1,0:T(8,128)S(1)}, f32[128,256]{1,0:T(8,128)S(1)}) custom-call(f32[256,256]{1,0:T(8,128)S(1)} %get-tuple-element.27.kernel_ref, f32[256,256]{1,0:T(8,128)S(1)} %collective-permute-done.near, f32[256,256]{1,0:T(8,128)S(1)} %collective-permute-done.2.near_sibling, ...), custom_call_target="tpu_custom_call" | custom-call | tf_op jit(solution)/shard_map/quad/pallas_call | solution.py:329
  20.5 0.2 collective-permute-start.6
  20.7 1.6 %collective-permute-start.4 = (f32[256,256]{1,0:T(8,128)S(1)}, f32[256,256]{1,0:T(8,128)S(1)}, u32[]{:S(2)}, u32[]{:S(2)}) collective-permute-start(f32[256,256]{1,0:T(8,128)S(1)} %get-tuple-element.35.product_ref), channel_id=1, source_target_pairs={{0,7},{1,6},{2,5},{3,4},{4,3},{5,2},{6,1},{7,0},{8,15},{9,14},{10,... | collective-permute-start | bytes 786440 | tf_op jit(solution)/shard_map/ppermute | solution.py:298
  22.3 5.8 %collective-permute-start.5 = (f32[128,256]{1,0:T(8,128)S(1)}, f32[128,256]{1,0:T(8,128)S(1)}, u32[]{:S(2)}, u32[]{:S(2)}) collective-permute-start(f32[128,256]{1,0:T(8,128)S(1)} %get-tuple-element.36), channel_id=1, source_target_pairs={{0,15},{1,14},{2,13},{3,12},{4,11},{5,10},{6,9},{7,8},{8,7},{9,6},... | collective-permute-start | bytes 393224 | tf_op jit(solution)/shard_map/ppermute | solution.py:299
  28.1 0.0 collective-permute-done.6.sibling_ref
  28.1 2.8 %collective-permute-start.7 = (f32[128,256]{1,0:T(8,128)S(1)}, f32[128,256]{1,0:T(8,128)S(1)}, u32[]{:S(2)}, u32[]{:S(2)}) collective-permute-start(f32[128,256]{1,0:T(8,128)S(1)} %get-tuple-element.38), channel_id=1, source_target_pairs={{0,128},{1,129},{2,130},{3,131},{4,132},{5,133},{6,134},{7,135},{8... | collective-permute-start | bytes 393224 | tf_op jit(solution)/shard_map/ppermute | solution.py:299
  31.0 0.9 %collective-permute-start.10 = (f32[256,256]{1,0:T(8,128)S(1)}, f32[256,256]{1,0:T(8,128)S(1)}, u32[]{:S(2)}, u32[]{:S(2)}) collective-permute-start(f32[256,256]{1,0:T(8,128)S(1)} %get-tuple-element.41.chip_ref), channel_id=1, source_target_pairs={{0,64},{1,65},{2,66},{3,67},{4,68},{5,69},{6,70},{7,71},{8,72},{9,... | collective-permute-start | bytes 786440 | tf_op jit(solution)/shard_map/ppermute | solution.py:298
  31.8 4.4 %collective-permute-done.5.far = f32[128,256]{1,0:T(8,128)S(1)} collective-permute-done((f32[128,256]{1,0:T(8,128)S(1)}, f32[128,256]{1,0:T(8,128)S(1)}, u32[]{:S(2)}, u32[]{:S(2)}) %collective-permute-start.5) | collective-permute-done | bytes 131104 | tf_op jit(solution)/shard_map/ppermute | solution.py:299
  36.2 0.0 collective-permute-done.4.near
  36.2 0.0 collective-permute-done.7.far_ref
  36.2 3.5 %collective-permute-start.8 = (f32[256,256]{1,0:T(8,128)S(1)}, f32[256,256]{1,0:T(8,128)S(1)}, u32[]{:S(2)}, u32[]{:S(2)}) collective-permute-start(f32[256,256]{1,0:T(8,128)S(1)} %collective-permute-done.4.near), channel_id=1, source_target_pairs={{0,32},{32,0},{64,96},{96,64},{128,160},{160,128},{192,224},{224,1... | collective-permute-start | bytes 786440 | tf_op jit(solution)/shard_map/ppermute | solution.py:30
  39.7 0.1 collective-permute-start.9
  39.8 1.3 %collective-permute-done.9.far_sibling = f32[128,256]{1,0:T(8,128)S(1)} collective-permute-done((f32[128,256]{1,0:T(8,128)S(1)}, f32[128,256]{1,0:T(8,128)S(1)}, u32[]{:S(2)}, u32[]{:S(2)}) %collective-permute-start.9) | collective-permute-done | bytes 131104 | tf_op jit(solution)/shard_map/ppermute | solution.py:30
  41.1 0.0 collective-permute-done.10.near_ref
  41.1 0.0 collective-permute-done.8.near_sibling
  41.1 0.5 collective-permute-start.12
  41.6 0.6 %block.1 = (f32[4,256,256]{2,1,0:T(8,128)S(1)}, f32[8,256]{1,0:T(8,128)S(1)}) custom-call(f32[256,256]{1,0:T(8,128)S(1)} %get-tuple-element.35.product_ref, f32[256,256]{1,0:T(8,128)S(1)} %collective-permute-done.4.near, f32[256,256]{1,0:T(8,128)S(1)} %collective-permute-done.8.near_sibling, f32[128,256]{1,0:T(8,128)S(1)} %collective-permute-done.5.far, ...), custom_call_target="tpu_custom_call" | custom-call | tf_op jit(solution)/shard_map/block/pallas_call | solution.py:353
  42.2 2.7 %collective-permute-start.11 = (f32[8,256]{1,0:T(8,128)S(1)}, f32[8,256]{1,0:T(8,128)S(1)}, u32[]{:S(2)}, u32[]{:S(2)}) collective-permute-start(f32[8,256]{1,0:T(8,128)S(1)} %get-tuple-element.47), channel_id=1, source_target_pairs={{0,16},{1,17},{2,18},{3,19},{4,20},{5,21},{6,22},{7,23},{8,24},{9,... | collective-permute-start | bytes 24584 | tf_op jit(solution)/shard_map/ppermute | solution.py:357
  44.9 2.5 %sides.1 = (f32[256,256]{1,0:T(8,128)S(1)}, f32[8,256]{1,0:T(8,128)S(1)}) custom-call(f32[4,256,256]{2,1,0:T(8,128)S(1)} %get-tuple-element.34.quad_ref, f32[4,256,256]{2,1,0:T(8,128)S(1)} %get-tuple-element.44.block_ref), custom_call_target="tpu_custom_call" | custom-call | tf_op jit(solution)/shard_map/sides/pallas_call | solution.py:358
  47.4 0.0 collective-permute-done.11.message_ref
  47.4 0.0 collective-permute-done.12.sibling_join_ref
  47.4 0.0 copy-done
  47.4 0.0 copy-done.1
  47.4 1.2 %final.1 = (f32[256,256]{1,0:T(8,128)}, f32[256,256]{1,0:T(8,128)}) custom-call(f32[256,256]{1,0:T(8,128)S(1)} %bitcast.5, f32[256,256]{1,0:T(8,128)S(1)} %bitcast.6, f32[256,256]{1,0:T(8,128)S(1)} %get-tuple-element.27.kernel_ref, f32[256,256]{1,0:T(8,128)S(1)} %get-tuple-element.45.path_ref, f32[8,256]{1,0:T(8,128)S(1)} %get-tuple-element.46.known_ref, ...), custom_call_target="tpu_custom_call" | custom-call | tf_op jit(solution)/shard_map/final/pallas_call | solution.py:360
  (2 shorter events, 0.1 us)
Async XLA Ops:
  1.7 16.1 %collective-permute-start = (f32[256,256]{1,0:T(8,128)S(1)}, f32[256,256]{1,0:T(8,128)S(1)}, u32[]{:S(2)}, u32[]{:S(2)}) collective-permute-start(f32[256,256]{1,0:T(8,128)S(1)} %get-tuple-element.27.kernel_ref), channel_id=1, source_target_pairs={{0,1},{1,2},{2,3},{3,0},{4,5},{5,6},{6,7},{7,4},{8,9},{9,10},{10,1... | collective-permute-start | bytes 786440 | tf_op jit(solution)/shard_map/ppermute | solution.py:298
  6.9 10.8 %collective-permute-start.1 = (f32[128,256]{1,0:T(8,128)S(1)}, f32[128,256]{1,0:T(8,128)S(1)}, u32[]{:S(2)}, u32[]{:S(2)}) collective-permute-start(f32[128,256]{1,0:T(8,128)S(1)} %get-tuple-element.28), channel_id=1, source_target_pairs={{0,2},{1,3},{2,0},{3,1},{4,6},{5,7},{6,4},{7,5},{8,10},{9,11},{10,... | collective-permute-start | bytes 393224 | tf_op jit(solution)/shard_map/ppermute | solution.py:299
  6.9 40.5 %copy-start = (f32[1,256,256]{2,1,0:T(8,128)S(1)}, f32[1,256,256]{2,1,0:T(8,128)}, u32[]{:S(2)}) copy-start(f32[1,256,256]{2,1,0:T(8,128)} %param.6) | copy-start | bytes 786436
  6.9 40.5 %copy-start.1 = (f32[1,256,256]{2,1,0:T(8,128)S(1)}, f32[1,256,256]{2,1,0:T(8,128)}, u32[]{:S(2)}) copy-start(f32[1,256,256]{2,1,0:T(8,128)} %param.7) | copy-start | bytes 786436
  17.8 1.7 %collective-permute-start.2 = (f32[256,256]{1,0:T(8,128)S(1)}, f32[256,256]{1,0:T(8,128)S(1)}, u32[]{:S(2)}, u32[]{:S(2)}) collective-permute-start(f32[256,256]{1,0:T(8,128)S(1)} %collective-permute-done.near), channel_id=1, source_target_pairs={{0,32},{32,0},{64,96},{96,64},{128,160},{160,128},{192,224},{224,1... | collective-permute-start | bytes 786440 | tf_op jit(solution)/shard_map/ppermute | solution.py:30
  17.8 1.7 %collective-permute-start.3 = (f32[128,256]{1,0:T(8,128)S(1)}, f32[128,256]{1,0:T(8,128)S(1)}, u32[]{:S(2)}, u32[]{:S(2)}) collective-permute-start(f32[128,256]{1,0:T(8,128)S(1)} %collective-permute-done.1.far), channel_id=1, source_target_pairs={{0,32},{32,0},{64,96},{96,64},{128,160},{160,128},{192,224},{224,1... | collective-permute-start | bytes 393224 | tf_op jit(solution)/shard_map/ppermute | solution.py:30
  20.5 7.6 %collective-permute-start.6 = (f32[256,256]{1,0:T(8,128)S(1)}, f32[256,256]{1,0:T(8,128)S(1)}, u32[]{:S(2)}, u32[]{:S(2)}) collective-permute-start(f32[256,256]{1,0:T(8,128)S(1)} %counts.1.own_ref), channel_id=1, source_target_pairs={{0,32},{32,0},{64,96},{96,64},{128,160},{160,128},{192,224},{224,1... | collective-permute-start | bytes 786440 | tf_op jit(solution)/shard_map/ppermute | solution.py:30
  20.7 15.5 %collective-permute-start.4 = (f32[256,256]{1,0:T(8,128)S(1)}, f32[256,256]{1,0:T(8,128)S(1)}, u32[]{:S(2)}, u32[]{:S(2)}) collective-permute-start(f32[256,256]{1,0:T(8,128)S(1)} %get-tuple-element.35.product_ref), channel_id=1, source_target_pairs={{0,7},{1,6},{2,5},{3,4},{4,3},{5,2},{6,1},{7,0},{8,15},{9,14},{10,... | collective-permute-start | bytes 786440 | tf_op jit(solution)/shard_map/ppermute | solution.py:298
  22.3 13.9 %collective-permute-start.5 = (f32[128,256]{1,0:T(8,128)S(1)}, f32[128,256]{1,0:T(8,128)S(1)}, u32[]{:S(2)}, u32[]{:S(2)}) collective-permute-start(f32[128,256]{1,0:T(8,128)S(1)} %get-tuple-element.36), channel_id=1, source_target_pairs={{0,15},{1,14},{2,13},{3,12},{4,11},{5,10},{6,9},{7,8},{8,7},{9,6},... | collective-permute-start | bytes 393224 | tf_op jit(solution)/shard_map/ppermute | solution.py:299
  28.1 8.1 %collective-permute-start.7 = (f32[128,256]{1,0:T(8,128)S(1)}, f32[128,256]{1,0:T(8,128)S(1)}, u32[]{:S(2)}, u32[]{:S(2)}) collective-permute-start(f32[128,256]{1,0:T(8,128)S(1)} %get-tuple-element.38), channel_id=1, source_target_pairs={{0,128},{1,129},{2,130},{3,131},{4,132},{5,133},{6,134},{7,135},{8... | collective-permute-start | bytes 393224 | tf_op jit(solution)/shard_map/ppermute | solution.py:299
  31.0 10.1 %collective-permute-start.10 = (f32[256,256]{1,0:T(8,128)S(1)}, f32[256,256]{1,0:T(8,128)S(1)}, u32[]{:S(2)}, u32[]{:S(2)}) collective-permute-start(f32[256,256]{1,0:T(8,128)S(1)} %get-tuple-element.41.chip_ref), channel_id=1, source_target_pairs={{0,64},{1,65},{2,66},{3,67},{4,68},{5,69},{6,70},{7,71},{8,72},{9,... | collective-permute-start | bytes 786440 | tf_op jit(solution)/shard_map/ppermute | solution.py:298
  36.2 4.9 %collective-permute-start.8 = (f32[256,256]{1,0:T(8,128)S(1)}, f32[256,256]{1,0:T(8,128)S(1)}, u32[]{:S(2)}, u32[]{:S(2)}) collective-permute-start(f32[256,256]{1,0:T(8,128)S(1)} %collective-permute-done.4.near), channel_id=1, source_target_pairs={{0,32},{32,0},{64,96},{96,64},{128,160},{160,128},{192,224},{224,1... | collective-permute-start | bytes 786440 | tf_op jit(solution)/shard_map/ppermute | solution.py:30
  39.7 1.3 %collective-permute-start.9 = (f32[128,256]{1,0:T(8,128)S(1)}, f32[128,256]{1,0:T(8,128)S(1)}, u32[]{:S(2)}, u32[]{:S(2)}) collective-permute-start(f32[128,256]{1,0:T(8,128)S(1)} %collective-permute-done.5.far), channel_id=1, source_target_pairs={{0,32},{32,0},{64,96},{96,64},{128,160},{160,128},{192,224},{224,1... | collective-permute-start | bytes 393224 | tf_op jit(solution)/shard_map/ppermute | solution.py:30
  41.1 6.3 %collective-permute-start.12 = (f32[256,256]{1,0:T(8,128)S(1)}, f32[256,256]{1,0:T(8,128)S(1)}, u32[]{:S(2)}, u32[]{:S(2)}) collective-permute-start(f32[256,256]{1,0:T(8,128)S(1)} %join.1.join_ref), channel_id=1, source_target_pairs={{0,32},{32,0},{64,96},{96,64},{128,160},{160,128},{192,224},{224,1... | collective-permute-start | bytes 786440 | tf_op jit(solution)/shard_map/ppermute | solution.py:30
  42.2 5.2 %collective-permute-start.11 = (f32[8,256]{1,0:T(8,128)S(1)}, f32[8,256]{1,0:T(8,128)S(1)}, u32[]{:S(2)}, u32[]{:S(2)}) collective-permute-start(f32[8,256]{1,0:T(8,128)S(1)} %get-tuple-element.47), channel_id=1, source_target_pairs={{0,16},{1,17},{2,18},{3,19},{4,20},{5,21},{6,22},{7,23},{8,24},{9,... | collective-permute-start | bytes 24584 | tf_op jit(solution)/shard_map/ppermute | solution.py:357

commit v6 on v3

--- a/solution.py
+++ b/solution.py
@@ -9,7 +9,7 @@
 
 step_size = 0.25
 shift = 7.0
-Y, Z, QUAD = 4, 8, 4
+Y, Z, QUAD, QUADS = 4, 8, 4, 8
 VMEM_LIMIT = 50 << 20
 
 
@@ -95,10 +95,10 @@
     stack_ref[across, pl.ds((1 - core) * half, half), :] = far_sibling[...]
 
 
-def quad_kernel(kernel_ref, near, near_sibling, far, far_sibling, quad_ref, product_ref, half_ref):
+def quad_kernel(kernel_ref, near, near_sibling, far, far_sibling, quad_ref, product_ref):
     core, _, z = place()
     mine = lax.rem(z, QUAD)
-    half, size = half_ref.shape
+    size = product_ref.shape[0]
     quad_ref[mine] = kernel_ref[...]
     put_others(quad_ref, mine, near, near_sibling, far, far_sibling, core)
     scale = 1.0 / size
@@ -107,25 +107,45 @@
     whole = product(left, right) * scale
     largest = jnp.max(jnp.max(whole, axis=0, keepdims=True), axis=1, keepdims=True)
     product_ref[...] = whole / largest
-    half_ref[...] = product_ref[pl.ds(core * half, half), :]
-
-
-def octet_kernel(product_ref, own_ref, sibling_ref, other_ref, octet_ref, half_ref):
-    core, _, z = place()
-    half = half_ref.shape[0]
-    rows = pl.ds(core * half, half)
-    other_ref[rows, :] = own_ref[...]
-    other_ref[pl.ds((1 - core) * half, half), :] = sibling_ref[...]
-
-    @pl.when(z < QUAD)
+
+
+def spots():
+    _, y, z = place()
+    return (y * (Z // QUAD) + lax.div(z, QUAD), lax.rem(z, QUAD))
+
+
+def hop_kernel(hop, product_ref, *refs):
+    here, _ = spots()
+    message_ref = refs[-1]
+    size = product_ref.shape[0]
+    eye = diagonal(size)
+
+    def arrived():
+        return refs[0][0:1, :] if len(refs) > 1 else jnp.ones((1, size), jnp.float32)
+
+    @pl.when(here == hop - 1)
     def _():
-        octet_ref[...] = product(product_ref[...], other_ref[...])
-
-    @pl.when(z >= QUAD)
+        row = row_times(arrived(), product_ref[...], eye)
+        message_ref[...] = jnp.broadcast_to(row, message_ref.shape)
+
+    @pl.when(here == QUADS - hop)
     def _():
-        octet_ref[...] = product(other_ref[...], product_ref[...])
-
-    half_ref[...] = octet_ref[rows, :]
+        row = times_row(product_ref[...], arrived(), eye)
+        message_ref[...] = jnp.broadcast_to(row, message_ref.shape)
+
+
+def hop_pairs(hop):
+    def quad_at(index, x, c, z):
+        y, half = divmod(index, Z // QUAD)
+        return (2 * x + c) * Y * Z + y * Z + (z if half == 0 else Z - 1 - z)
+
+    pairs = []
+    for x in range(4):
+        for c in range(2):
+            for z in range(QUAD):
+                for source, target in ((hop - 1, hop), (QUADS - hop, QUADS - 1 - hop)):
+                    pairs.append((quad_at(source, x, c, z), quad_at(target, x, c, z)))
+    return pairs
 
 
 def chip_kernel(own_ref, sibling_ref, both_ref, half_ref):
@@ -142,30 +162,23 @@
     sum_ref[pl.ds(core * half, half), :] += far_ref[...]
 
 
-def final_kernel(
-    scale, potential_ref, noise_ref, quad_ref, other_ref, near, near_sibling, far, far_sibling,
-    chip_ref, join_ref, sibling_join_ref, updated_ref, beliefs_ref, octet_ref
-):
-    core, y, z = place()
+def final_kernel(scale, potential_ref, noise_ref, quad_ref, chip_ref, join_ref, sibling_join_ref, *refs):
+    messages, (updated_ref, beliefs_ref, carried_ref) = (refs[:-3], refs[-3:])
+    here, mine = spots()
     size = potential_ref.shape[0]
-    put_others(octet_ref, y, near, near_sibling, far, far_sibling, core)
+    ones = jnp.ones((1, size), jnp.float32)
+    carried_ref[0] = ones
+    for hop, message_ref in enumerate(messages, 1):
+        carried_ref[hop] = message_ref[0:1, :]
     eye = diagonal(size)
-    ones = jnp.ones((1, size), jnp.float32)
-    later_quad = lax.div(z, QUAD)
-    mine = lax.rem(z, QUAD)
-    forward = lax.fori_loop(0, y, lambda i, row: row_times(row, octet_ref[i], eye), ones)
     forward = lax.fori_loop(
-        0, later_quad, lambda i, row: row_times(row, other_ref[...], eye), forward
-    )
-    forward = lax.fori_loop(0, mine, lambda i, row: row_times(row, quad_ref[i], eye), forward)
+        0, mine, lambda i, row: row_times(row, quad_ref[i], eye), carried_ref[here]
+    )
     backward = lax.fori_loop(
-        0, Y - 1 - y, lambda i, row: times_row(octet_ref[Y - 1 - i], row, eye), ones
-    )
-    backward = lax.fori_loop(
-        0, 1 - later_quad, lambda i, row: times_row(other_ref[...], row, eye), backward
-    )
-    backward = lax.fori_loop(
-        0, 3 - mine, lambda i, row: times_row(quad_ref[3 - i], row, eye), backward
+        0,
+        QUAD - 1 - mine,
+        lambda i, row: times_row(quad_ref[QUAD - 1 - i], row, eye),
+        carried_ref[QUADS - 1 - here],
     )
     column = as_column(forward, eye) / jnp.sum(forward, axis=1, keepdims=True)
     joint = column * quad_ref[mine] * backward
@@ -248,11 +261,12 @@
     return pairs
 
 
-def exchange(whole, half, step):
+def exchange(whole, half, near_step, far_step):
     axes = ("dp", "clique")
-    near = lax.ppermute(whole, axes, everywhere(lambda x, c, y, z: step(x, y, z, 1 - 2 * c)))
-    far = lax.ppermute(half, axes, everywhere(lambda x, c, y, z: step(x, y, z, 2)))
-    return (near, far)
+    return (
+        lax.ppermute(whole, axes, everywhere(near_step)),
+        lax.ppermute(half, axes, everywhere(lambda x, c, y, z: far_step(x, y, z))),
+    )
 
 
 def per_device(table_rows, attribute_order, log_potential, measure_noise):
@@ -274,36 +288,49 @@
         pltpu.with_memory_space_constraint(potential, pltpu.HBM),
     )
     near, far = exchange(
-        kernel, half_of_kernel, lambda x, y, z, s: (x, y, z // QUAD * QUAD + (z + s) % QUAD)
+        kernel,
+        half_of_kernel,
+        lambda x, c, y, z: (x, y, z // QUAD * QUAD + (z + 1 - 2 * c) % QUAD),
+        lambda x, y, z: (x, y, z ^ 2),
     )
     counts = count_pairs(order, table_rows, size)
     near, far, counts = lax.optimization_barrier((near, far, counts))
-    quad, quad_product, half_product = call(
-        quad_kernel, out_shape=(shape(QUAD, size, size), whole, half), name="quad"
+    sibling_counts = other_core(counts)
+    quad, quad_product = call(
+        quad_kernel, out_shape=(shape(QUAD, size, size), whole), name="quad"
     )(kernel, near, other_core(near), far, other_core(far))
-    other = lax.ppermute(half_product, "clique", along_clique(lambda y, z: (y, Z - 1 - z)))
-    counts, quad_product = lax.optimization_barrier((counts, quad_product))
     chip_counts, half_counts = call(chip_kernel, out_shape=(whole, half), name="chip")(
-        counts, other_core(counts)
-    )
-    near_counts, far_counts = exchange(
-        chip_counts, half_counts, lambda x, y, z, s: ((x + s) % 4, y, z)
-    )
-    other, chip_counts = lax.optimization_barrier((other, chip_counts))
-    other_product, octet, half_octet = call(
-        octet_kernel, out_shape=(whole, whole, half), name="octet"
-    )(quad_product, other, other_core(other))
-    near, far = exchange(octet, half_octet, lambda x, y, z, s: (x, (y + s) % Y, z))
+        counts, sibling_counts
+    )
+    messages = []
+    for hop in range(1, QUADS):
+        message = call(
+            functools.partial(hop_kernel, hop), out_shape=shape(8, size), name="hop"
+        )(quad_product, *messages[-1:])
+        messages.append(lax.ppermute(message, ("dp", "clique"), hop_pairs(hop)))
+        if hop == 2:
+            messages[-1], chip_counts, half_counts = lax.optimization_barrier(
+                (messages[-1], chip_counts, half_counts)
+            )
+            near_counts, far_counts = exchange(
+                chip_counts,
+                half_counts,
+                lambda x, c, y, z: ((x + 1 - 2 * c) % 4, y, z),
+                lambda x, y, z: (x ^ 2, y, z),
+            )
+        if hop == 5:
+            messages[-1], near_counts, far_counts = lax.optimization_barrier(
+                (messages[-1], near_counts, far_counts)
+            )
     joined = call(join_kernel, out_shape=whole, name="join")(near_counts, far_counts)
     total_rows = table_rows.shape[1] * lax.axis_size("dp")
     updated, beliefs = call(
         functools.partial(final_kernel, size * size / total_rows),
         out_shape=(whole, whole),
-        scratch_shapes=[pltpu.VMEM((Y, size, size), jnp.float32)],
+        scratch_shapes=[pltpu.VMEM((QUADS, 1, size), jnp.float32)],
         name="final",
     )(
-        potential, measure_noise[0], quad, other_product, near, other_core(near), far,
-        other_core(far), chip_counts, joined, other_core(joined),
+        potential, measure_noise[0], quad, chip_counts, joined, other_core(joined), *messages
     )
     return (updated[None], beliefs[None])
 

time: 50.3 us -> 74.5 us (1.48)
  the two profiles are of different devices: /device:TPU:1 before, /device:TPU:32 now
where the time goes in v6:
time: 74.5 us; the launch traced here: 74.3 us
  waiting for transfers between devices  40.5 us (54%)
  starting transfers between devices  20.6 us (28%)
  Pallas kernels  12.4 us (17%)
  between operations  0.84 us (1%)
    ppermute x7, waiting for transfers between devices, per_device(): messages.append(lax.ppermute(message, ('dp', 'clique'), hop_pairs(hop)))  32.4 us
    ppermute x7, starting transfers between devices, per_device(): messages.append(lax.ppermute(message, ('dp', 'clique'), hop_pairs(hop)))  11.4 us
    pallas_call x1, Pallas kernels, count_pairs(): pl.pallas_call(functools.partial(count_kernel, part), out_shape=shape(siz...  8.57 us
    ppermute x2, waiting for transfers between devices, exchange(): lax.ppermute(half, axes, everywhere(lambda x, c, y, z: far_step(x, y, z)))  6.47 us
    ppermute x2, starting transfers between devices, exchange(): lax.ppermute(half, axes, everywhere(lambda x, c, y, z: far_step(x, y, z)))  5.02 us
    ppermute x2, starting transfers between devices, exchange(): lax.ppermute(whole, axes, everywhere(near_step))  3.56 us
    ppermute x4, waiting for transfers between devices, other_core(): return lax.ppermute(value, 'dp', along_dp(lambda x, c: (x, 1 - c)))  1.59 us
  transfers between devices with their start and end apart: 15, of which 5 were waited for; matrix products, arithmetic and copies ran while one was open for 0% of the time, Pallas kernels for 13%

profile of v6, /device:TPU:32, one launch (start us, length us, event | category | flops | bytes accessed | tf_op | source)
XLA Modules:
  0.0 74.3 jit_solution(5882628385121635185)
XLA Ops:
  0.6 1.1 %read.1 = (s32[33]{0:T(128)S(1)}, f32[256,256]{1,0:T(8,128)S(1)}, f32[128,256]{1,0:T(8,128)S(1)}) custom-call(s32[33]{0:T(128)} %order_hbm.1, f32[256,256]{1,0:T(8,128)} %bitcast.4), custom_call_target="tpu_custom_call" | custom-call | tf_op jit(solution)/shard_map/read/pallas_call | solution.py:279
  1.7 2.0 %collective-permute-start = (f32[256,256]{1,0:T(8,128)S(1)}, f32[256,256]{1,0:T(8,128)S(1)}, u32[]{:S(2)}, u32[]{:S(2)}) collective-permute-start(f32[256,256]{1,0:T(8,128)S(1)} %get-tuple-element.20.kernel_ref), channel_id=1, source_target_pairs={{0,1},{1,2},{2,3},{3,0},{4,5},{5,6},{6,7},{7,4},{8,9},{9,10},{10,1... | collective-permute-start | bytes 786440 | tf_op jit(solution)/shard_map/ppermute | solution.py:267
  3.7 2.3 %collective-permute-start.1 = (f32[128,256]{1,0:T(8,128)S(1)}, f32[128,256]{1,0:T(8,128)S(1)}, u32[]{:S(2)}, u32[]{:S(2)}) collective-permute-start(f32[128,256]{1,0:T(8,128)S(1)} %get-tuple-element.21), channel_id=1, source_target_pairs={{0,2},{1,3},{2,0},{3,1},{4,6},{5,7},{6,4},{7,5},{8,10},{9,11},{10,... | collective-permute-start | bytes 393224 | tf_op jit(solution)/shard_map/ppermute | solution.py:268
  6.0 0.0 copy-start
  6.0 0.0 copy-start.1
  6.0 8.6 %counts.1.own_ref = f32[256,256]{1,0:T(8,128)S(1)} custom-call(s32[33]{0:T(128)S(1)} %get-tuple-element.22.order_ref, s32[33,65536]{1,0:T(8,128)} %right_ref.1, s32[33,65536]{1,0:T(8,128)} %right_ref.1), custom_call_target="tpu_custom_call" | custom-call | tf_op jit(solution)/shard_map/counts/pallas_call | solution.py:238
  14.6 1.4 %collective-permute-done.1.far = f32[128,256]{1,0:T(8,128)S(1)} collective-permute-done((f32[128,256]{1,0:T(8,128)S(1)}, f32[128,256]{1,0:T(8,128)S(1)}, u32[]{:S(2)}, u32[]{:S(2)}) %collective-permute-start.1) | collective-permute-done | bytes 131104 | tf_op jit(solution)/shard_map/ppermute | solution.py:268
  16.0 0.0 collective-permute-done.near
  16.0 0.0 collective-permute-start.2
  16.0 0.5 collective-permute-start.6
  16.5 0.0 collective-permute-start.3
  16.5 1.6 %collective-permute-done.3.far_sibling = f32[128,256]{1,0:T(8,128)S(1)} collective-permute-done((f32[128,256]{1,0:T(8,128)S(1)}, f32[128,256]{1,0:T(8,128)S(1)}, u32[]{:S(2)}, u32[]{:S(2)}) %collective-permute-start.3) | collective-permute-done | bytes 131104 | tf_op jit(solution)/shard_map/ppermute | solution.py:30
  18.1 0.0 collective-permute-done.2.near_sibling
  18.1 1.0 %quad.1 = (f32[4,256,256]{2,1,0:T(8,128)S(1)}, f32[256,256]{1,0:T(8,128)S(1)}) custom-call(f32[256,256]{1,0:T(8,128)S(1)} %get-tuple-element.20.kernel_ref, f32[256,256]{1,0:T(8,128)S(1)} %collective-permute-done.near, f32[256,256]{1,0:T(8,128)S(1)} %collective-permute-done.2.near_sibling, f32[128,256]{1,0:T(8,128)S(1)} %collective-permute-done.1.far, ...), custom_call_target="tpu_custom_call" | custom-call | tf_op jit(solution)/shard_map/quad/pallas_call | solution.py:299
  19.1 0.1 hop.7
  19.2 6.8 %collective-permute-start.4 = (f32[8,256]{1,0:T(8,128)S(1)}, f32[8,256]{1,0:T(8,128)S(1)}, u32[]{:S(2)}, u32[]{:S(2)}) collective-permute-start(f32[8,256]{1,0:T(8,128)S(1)} %hop.7), channel_id=1, source_target_pairs={{0,7},{31,24},{1,6},{30,25},{2,5},{29,26},{3,4},{28,27},{32,39},{6... | collective-permute-start | bytes 24584 | tf_op jit(solution)/shard_map/ppermute | solution.py:310
  26.0 1.3 %collective-permute-done.4.refs_0_ = f32[8,256]{1,0:T(8,128)S(1)} collective-permute-done((f32[8,256]{1,0:T(8,128)S(1)}, f32[8,256]{1,0:T(8,128)S(1)}, u32[]{:S(2)}, u32[]{:S(2)}) %collective-permute-start.4) | collective-permute-done | bytes 8224 | tf_op jit(solution)/shard_map/ppermute | solution.py:310
  27.4 0.7 collective-permute-start.5
  28.1 0.0 collective-permute-done.6.sibling_ref
  28.2 0.0 collective-permute-done.5.refs_0_.refs_1_
  28.2 1.6 %collective-permute-start.10 = (f32[256,256]{1,0:T(8,128)S(1)}, f32[256,256]{1,0:T(8,128)S(1)}, u32[]{:S(2)}, u32[]{:S(2)}) collective-permute-start(f32[256,256]{1,0:T(8,128)S(1)} %get-tuple-element.30.chip_ref), channel_id=1, source_target_pairs={{0,64},{1,65},{2,66},{3,67},{4,68},{5,69},{6,70},{7,71},{8,72},{9,... | collective-permute-start | bytes 786440 | tf_op jit(solution)/shard_map/ppermute | solution.py:267
  29.7 2.7 %collective-permute-start.11 = (f32[128,256]{1,0:T(8,128)S(1)}, f32[128,256]{1,0:T(8,128)S(1)}, u32[]{:S(2)}, u32[]{:S(2)}) collective-permute-start(f32[128,256]{1,0:T(8,128)S(1)} %get-tuple-element.32), channel_id=1, source_target_pairs={{0,128},{1,129},{2,130},{3,131},{4,132},{5,133},{6,134},{7,135},{8... | collective-permute-start | bytes 393224 | tf_op jit(solution)/shard_map/ppermute | solution.py:268
  32.5 0.7 collective-permute-start.7
  33.2 0.0 collective-permute-done.7.refs_0_.refs_2_
  33.2 0.7 collective-permute-start.8
  33.9 0.0 collective-permute-done.8.refs_0_.refs_3_
  33.9 0.7 collective-permute-start.9
  34.6 0.0 collective-permute-done.9.refs_0_.refs_4_
  34.6 5.0 %collective-permute-done.11.far_ref = f32[128,256]{1,0:T(8,128)S(1)} collective-permute-done((f32[128,256]{1,0:T(8,128)S(1)}, f32[128,256]{1,0:T(8,128)S(1)}, u32[]{:S(2)}, u32[]{:S(2)}) %collective-permute-start.11) | collective-permute-done | bytes 131104 | tf_op jit(solution)/shard_map/ppermute | solution.py:268
  39.6 0.0 collective-permute-done.10.near_ref
  39.7 0.1 collective-permute-start.12
  39.8 0.7 collective-permute-start.13
  40.5 0.0 collective-permute-done.13.refs_0_.refs_5_
  40.5 1.3 %collective-permute-start.14 = (f32[8,256]{1,0:T(8,128)S(1)}, f32[8,256]{1,0:T(8,128)S(1)}, u32[]{:S(2)}, u32[]{:S(2)}) collective-permute-start(f32[8,256]{1,0:T(8,128)S(1)} %hop.13), channel_id=1, source_target_pairs={{24,31},{7,0},{25,30},{6,1},{26,29},{5,2},{27,28},{4,3},{56,63},{3... | collective-permute-start | bytes 24584 | tf_op jit(solution)/shard_map/ppermute | solution.py:310
  41.8 31.0 %collective-permute-done.14.refs_6_ = f32[8,256]{1,0:T(8,128)S(1)} collective-permute-done((f32[8,256]{1,0:T(8,128)S(1)}, f32[8,256]{1,0:T(8,128)S(1)}, u32[]{:S(2)}, u32[]{:S(2)}) %collective-permute-start.14) | collective-permute-done | bytes 8224 | tf_op jit(solution)/shard_map/ppermute | solution.py:310
  72.9 0.0 collective-permute-done.12.sibling_join_ref
  72.9 0.0 copy-done
  72.9 0.0 copy-done.1
  72.9 1.4 %final.1 = (f32[256,256]{1,0:T(8,128)}, f32[256,256]{1,0:T(8,128)}) custom-call(f32[256,256]{1,0:T(8,128)S(1)} %bitcast.5, f32[256,256]{1,0:T(8,128)S(1)} %bitcast.6, f32[4,256,256]{2,1,0:T(8,128)S(1)} %get-tuple-element.25.quad_ref, f32[256,256]{1,0:T(8,128)S(1)} %get-tuple-element.30.chip_ref, f32[256,256]{1,0:T(8,128)S(1)} %join.1.join_ref, ...), custom_call_target="tpu_custom_call" | custom-call | tf_op jit(solution)/shard_map/final/pallas_call | solution.py:327
  (8 shorter events, 0.2 us)
Async XLA Ops:
  1.7 14.3 %collective-permute-start = (f32[256,256]{1,0:T(8,128)S(1)}, f32[256,256]{1,0:T(8,128)S(1)}, u32[]{:S(2)}, u32[]{:S(2)}) collective-permute-start(f32[256,256]{1,0:T(8,128)S(1)} %get-tuple-element.20.kernel_ref), channel_id=1, source_target_pairs={{0,1},{1,2},{2,3},{3,0},{4,5},{5,6},{6,7},{7,4},{8,9},{9,10},{10,1... | collective-permute-start | bytes 786440 | tf_op jit(solution)/shard_map/ppermute | solution.py:267
  3.7 12.3 %collective-permute-start.1 = (f32[128,256]{1,0:T(8,128)S(1)}, f32[128,256]{1,0:T(8,128)S(1)}, u32[]{:S(2)}, u32[]{:S(2)}) collective-permute-start(f32[128,256]{1,0:T(8,128)S(1)} %get-tuple-element.21), channel_id=1, source_target_pairs={{0,2},{1,3},{2,0},{3,1},{4,6},{5,7},{6,4},{7,5},{8,10},{9,11},{10,... | collective-permute-start | bytes 393224 | tf_op jit(solution)/shard_map/ppermute | solution.py:268
  6.0 66.9 %copy-start = (f32[1,256,256]{2,1,0:T(8,128)S(1)}, f32[1,256,256]{2,1,0:T(8,128)}, u32[]{:S(2)}) copy-start(f32[1,256,256]{2,1,0:T(8,128)} %param.6) | copy-start | bytes 786436
  6.0 66.9 %copy-start.1 = (f32[1,256,256]{2,1,0:T(8,128)S(1)}, f32[1,256,256]{2,1,0:T(8,128)}, u32[]{:S(2)}) copy-start(f32[1,256,256]{2,1,0:T(8,128)} %param.7) | copy-start | bytes 786436
  16.0 2.1 %collective-permute-start.2 = (f32[256,256]{1,0:T(8,128)S(1)}, f32[256,256]{1,0:T(8,128)S(1)}, u32[]{:S(2)}, u32[]{:S(2)}) collective-permute-start(f32[256,256]{1,0:T(8,128)S(1)} %collective-permute-done.near), channel_id=1, source_target_pairs={{0,32},{32,0},{64,96},{96,64},{128,160},{160,128},{192,224},{224,1... | collective-permute-start | bytes 786440 | tf_op jit(solution)/shard_map/ppermute | solution.py:30
  16.0 12.1 %collective-permute-start.6 = (f32[256,256]{1,0:T(8,128)S(1)}, f32[256,256]{1,0:T(8,128)S(1)}, u32[]{:S(2)}, u32[]{:S(2)}) collective-permute-start(f32[256,256]{1,0:T(8,128)S(1)} %counts.1.own_ref), channel_id=1, source_target_pairs={{0,32},{32,0},{64,96},{96,64},{128,160},{160,128},{192,224},{224,1... | collective-permute-start | bytes 786440 | tf_op jit(solution)/shard_map/ppermute | solution.py:30
  16.5 1.6 %collective-permute-start.3 = (f32[128,256]{1,0:T(8,128)S(1)}, f32[128,256]{1,0:T(8,128)S(1)}, u32[]{:S(2)}, u32[]{:S(2)}) collective-permute-start(f32[128,256]{1,0:T(8,128)S(1)} %collective-permute-done.1.far), channel_id=1, source_target_pairs={{0,32},{32,0},{64,96},{96,64},{128,160},{160,128},{192,224},{224,1... | collective-permute-start | bytes 393224 | tf_op jit(solution)/shard_map/ppermute | solution.py:30
  19.2 8.2 %collective-permute-start.4 = (f32[8,256]{1,0:T(8,128)S(1)}, f32[8,256]{1,0:T(8,128)S(1)}, u32[]{:S(2)}, u32[]{:S(2)}) collective-permute-start(f32[8,256]{1,0:T(8,128)S(1)} %hop.7), channel_id=1, source_target_pairs={{0,7},{31,24},{1,6},{30,25},{2,5},{29,26},{3,4},{28,27},{32,39},{6... | collective-permute-start | bytes 24584 | tf_op jit(solution)/shard_map/ppermute | solution.py:310
  27.4 0.7 collective-permute-start.5
  28.2 11.5 %collective-permute-start.10 = (f32[256,256]{1,0:T(8,128)S(1)}, f32[256,256]{1,0:T(8,128)S(1)}, u32[]{:S(2)}, u32[]{:S(2)}) collective-permute-start(f32[256,256]{1,0:T(8,128)S(1)} %get-tuple-element.30.chip_ref), channel_id=1, source_target_pairs={{0,64},{1,65},{2,66},{3,67},{4,68},{5,69},{6,70},{7,71},{8,72},{9,... | collective-permute-start | bytes 786440 | tf_op jit(solution)/shard_map/ppermute | solution.py:267
  29.7 9.9 %collective-permute-start.11 = (f32[128,256]{1,0:T(8,128)S(1)}, f32[128,256]{1,0:T(8,128)S(1)}, u32[]{:S(2)}, u32[]{:S(2)}) collective-permute-start(f32[128,256]{1,0:T(8,128)S(1)} %get-tuple-element.32), channel_id=1, source_target_pairs={{0,128},{1,129},{2,130},{3,131},{4,132},{5,133},{6,134},{7,135},{8... | collective-permute-start | bytes 393224 | tf_op jit(solution)/shard_map/ppermute | solution.py:268
  32.5 0.7 collective-permute-start.7
  33.2 0.7 collective-permute-start.8
  33.9 0.7 collective-permute-start.9
  39.7 33.2 %collective-permute-start.12 = (f32[256,256]{1,0:T(8,128)S(1)}, f32[256,256]{1,0:T(8,128)S(1)}, u32[]{:S(2)}, u32[]{:S(2)}) collective-permute-start(f32[256,256]{1,0:T(8,128)S(1)} %join.1.join_ref), channel_id=1, source_target_pairs={{0,32},{32,0},{64,96},{96,64},{128,160},{160,128},{192,224},{224,1... | collective-permute-start | bytes 786440 | tf_op jit(solution)/shard_map/ppermute | solution.py:30
  39.8 0.7 collective-permute-start.13
  40.5 32.3 %collective-permute-start.14 = (f32[8,256]{1,0:T(8,128)S(1)}, f32[8,256]{1,0:T(8,128)S(1)}, u32[]{:S(2)}, u32[]{:S(2)}) collective-permute-start(f32[8,256]{1,0:T(8,128)S(1)} %hop.13), channel_id=1, source_target_pairs={{24,31},{7,0},{25,30},{6,1},{26,29},{5,2},{27,28},{4,3},{56,63},{3... | collective-permute-start | bytes 24584 | tf_op jit(solution)/shard_map/ppermute | solution.py:310

commit v7 on v4

--- a/solution.py
+++ b/solution.py
@@ -70,8 +70,7 @@
     return as_row(column, eye) / jnp.sum(column, axis=0, keepdims=True)
 
 
-def read_kernel(order_hbm, potential_hbm, order_ref, kernel_ref, half_ref, copied_ref, semaphores):
-    core, _, _ = place()
+def read_kernel(order_hbm, potential_hbm, order_ref, kernel_ref, copied_ref, semaphores):
     copies = (
         pltpu.make_async_copy(order_hbm, order_ref, semaphores.at[0]),
         pltpu.make_async_copy(potential_hbm, copied_ref, semaphores.at[1]),
@@ -80,34 +79,22 @@
         copy.start()
     for copy in copies:
         copy.wait()
-    half = half_ref.shape[0]
     kernel_ref[...] = jnp.exp(copied_ref[...] - shift)
-    half_ref[...] = kernel_ref[pl.ds(core * half, half), :]
-
-
-def put_others(stack_ref, mine, near, near_sibling, far, far_sibling, core):
-    count = stack_ref.shape[0]
-    half = far.shape[0]
-    before, after, across = (lax.rem(mine + count + move, count) for move in (-1, 1, 2))
-    stack_ref[jnp.where(core == 0, before, after)] = near[...]
-    stack_ref[jnp.where(core == 0, after, before)] = near_sibling[...]
-    stack_ref[across, pl.ds(core * half, half), :] = far[...]
-    stack_ref[across, pl.ds((1 - core) * half, half), :] = far_sibling[...]
-
-
-def quad_kernel(kernel_ref, near, near_sibling, far, far_sibling, quad_ref, product_ref, half_ref):
-    core, _, z = place()
+
+
+def quad_kernel(kernel_ref, first, second, third, quad_ref, product_ref):
+    _, _, z = place()
     mine = lax.rem(z, QUAD)
-    half, size = half_ref.shape
+    size = product_ref.shape[0]
     quad_ref[mine] = kernel_ref[...]
-    put_others(quad_ref, mine, near, near_sibling, far, far_sibling, core)
+    for step, arrived in enumerate((first, second, third), 1):
+        quad_ref[lax.rem(mine + QUAD - step, QUAD)] = arrived[...]
     scale = 1.0 / size
     left = product(quad_ref[0], quad_ref[1]) * scale
     right = product(quad_ref[2], quad_ref[3]) * scale
     whole = product(left, right) * scale
     largest = jnp.max(jnp.max(whole, axis=0, keepdims=True), axis=1, keepdims=True)
     product_ref[...] = whole / largest
-    half_ref[...] = product_ref[pl.ds(core * half, half), :]
 
 
 def spots():
@@ -115,14 +102,12 @@
     return (core, y, 2 * lax.rem(y, 2) + lax.div(z, QUAD), lax.rem(z, QUAD))
 
 
-def block_kernel(product_ref, near, near_sibling, far, far_sibling, block_ref, message_ref):
-    core, y, mine, _ = spots()
-    size, half = (product_ref.shape[0], far.shape[0])
+def block_kernel(product_ref, first, second, third, block_ref, message_ref):
+    _, y, mine, _ = spots()
+    size = product_ref.shape[0]
     block_ref[mine] = product_ref[...]
-    block_ref[mine ^ (1 + core)] = near[...]
-    block_ref[mine ^ (2 - core)] = near_sibling[...]
-    block_ref[mine ^ 3, pl.ds(core * half, half), :] = far[...]
-    block_ref[mine ^ 3, pl.ds((1 - core) * half, half), :] = far_sibling[...]
+    for flip, arrived in enumerate((first, second, third), 1):
+        block_ref[mine ^ flip] = arrived[...]
     eye = diagonal(size)
     ones = jnp.ones((1, size), jnp.float32)
 
@@ -178,45 +163,40 @@
         known_ref[...] = jnp.broadcast_to(row, known_ref.shape)
 
 
-def chip_kernel(own_ref, sibling_ref, both_ref, half_ref):
-    core, _, _ = place()
-    half = half_ref.shape[0]
-    both_ref[...] = own_ref[...] + sibling_ref[...]
-    half_ref[...] = both_ref[pl.ds(core * half, half), :]
-
-
-def join_kernel(near_ref, far_ref, sum_ref):
-    core, _, _ = place()
-    half = far_ref.shape[0]
-    sum_ref[...] = near_ref[...]
-    sum_ref[pl.ds(core * half, half), :] += far_ref[...]
+def vectors_kernel(path_ref, known_ref, message_ref, vectors_ref):
+    _, y, _, _ = spots()
+    size = path_ref.shape[0]
+    eye = diagonal(size)
+    known, message = (known_ref[0:1, :], message_ref[0:1, :])
+
+    @pl.when(y >= Y // 2)
+    def _():
+        vectors_ref[0:1, :] = row_times(message, path_ref[...], eye)
+        vectors_ref[1:2, :] = known
+
+    @pl.when(y < Y // 2)
+    def _():
+        vectors_ref[0:1, :] = known
+        vectors_ref[1:2, :] = times_row(path_ref[...], message, eye)
+
+    vectors_ref[2:, :] = jnp.zeros((vectors_ref.shape[0] - 2, size), jnp.float32)
 
 
 def final_kernel(
-    scale, potential_ref, noise_ref, kernel_ref, path_ref, known_ref, message_ref, chip_ref,
-    join_ref, sibling_join_ref, updated_ref, beliefs_ref, column_ref, row_ref
+    scale, potential_ref, noise_ref, vectors_ref, sibling_vectors_ref, counts_ref, sibling_counts_ref,
+    updated_ref, beliefs_ref
 ):
-    _, y, _, _ = spots()
+    core, _, _, _ = spots()
     size = potential_ref.shape[0]
     eye = diagonal(size)
-    known, message = (known_ref[0:1, :], message_ref[0:1, :])
-
-    @pl.when(y >= Y // 2)
-    def _():
-        forward = row_times(message, path_ref[...], eye)
-        column_ref[...] = as_column(forward, eye) / jnp.sum(forward, axis=1, keepdims=True)
-        row_ref[...] = known
-
-    @pl.when(y < Y // 2)
-    def _():
-        column_ref[...] = as_column(known, eye) / jnp.sum(known, axis=1, keepdims=True)
-        row_ref[...] = times_row(path_ref[...], message, eye)
-
-    joint = column_ref[...] * kernel_ref[...] * row_ref[...]
+    vectors = jnp.where(core == 0, vectors_ref[...], sibling_vectors_ref[...])
+    forward, backward = (vectors[0:1, :], vectors[1:2, :])
+    column = as_column(forward, eye) / jnp.sum(forward, axis=1, keepdims=True)
+    joint = column * jnp.exp(potential_ref[...] - shift) * backward
     total = jnp.sum(jnp.sum(joint, axis=0, keepdims=True), axis=1, keepdims=True)
     beliefs = joint * (size * size / total)
     beliefs_ref[...] = beliefs
-    counts = chip_ref[...] + join_ref[...] + sibling_join_ref[...]
+    counts = jnp.where(core == 0, sibling_counts_ref[...], counts_ref[...])
     measured = (counts + noise_ref[...]) * scale
     updated_ref[...] = potential_ref[...] - step_size * (beliefs - measured)
 
@@ -280,24 +260,16 @@
     )(order, table_rows, table_rows)
 
 
-def everywhere(move):
+def on_core(value, mover, move):
     pairs = []
     for x in range(4):
         for c in range(2):
             for y in range(Y):
                 for z in range(Z):
-                    to_x, to_y, to_z = move(x, c, y, z)
+                    to_x, to_y, to_z = move(x, y, z) if c == mover else (x, y, z)
                     source = (2 * x + c) * Y * Z + y * Z + z
                     pairs.append((source, (2 * to_x + c) * Y * Z + to_y * Z + to_z))
-    return pairs
-
-
-def exchange(whole, half, near_step, far_step):
-    axes = ("dp", "clique")
-    return (
-        lax.ppermute(whole, axes, everywhere(near_step)),
-        lax.ppermute(half, axes, everywhere(lambda x, c, y, z: far_step(x, y, z))),
-    )
+    return lax.ppermute(value, ("dp", "clique"), pairs)
 
 
 def per_device(table_rows, attribute_order, log_potential, measure_noise):
@@ -306,67 +278,55 @@
     call = functools.partial(pl.pallas_call, compiler_params=PARAMS)
     vmem = pl.BlockSpec(memory_space=pltpu.VMEM)
     hbm = pl.BlockSpec(memory_space=pltpu.HBM)
-    whole, half = (shape(size, size), shape(size // 2, size))
-    order, kernel, half_of_kernel = call(
+    whole = shape(size, size)
+    order, kernel = call(
         read_kernel,
         in_specs=[hbm, hbm],
-        out_specs=(vmem, vmem, vmem),
-        out_shape=(jax.ShapeDtypeStruct(attribute_order.shape, jnp.int32), whole, half),
+        out_specs=(vmem, vmem),
+        out_shape=(jax.ShapeDtypeStruct(attribute_order.shape, jnp.int32), whole),
         scratch_shapes=[pltpu.VMEM((size, size), jnp.float32), pltpu.SemaphoreType.DMA((2,))],
         name="read",
     )(
         pltpu.with_memory_space_constraint(attribute_order, pltpu.HBM),
         pltpu.with_memory_space_constraint(potential, pltpu.HBM),
     )
-    near, far = exchange(
-        kernel,
-        half_of_kernel,
-        lambda x, c, y, z: (x, y, z // QUAD * QUAD + (z + 1 - 2 * c) % QUAD),
-        lambda x, y, z: (x, y, z ^ 2),
-    )
+    quads = [
+        on_core(kernel, 0, lambda x, y, z, s=s: (x, y, z // QUAD * QUAD + (z + s) % QUAD))
+        for s in (1, 2, 3)
+    ]
     counts = count_pairs(order, table_rows, size)
-    near, far, counts = lax.optimization_barrier((near, far, counts))
-    quad, quad_product, half_product = call(
-        quad_kernel, out_shape=(shape(QUAD, size, size), whole, half), name="quad"
-    )(kernel, near, other_core(near), far, other_core(far))
-    near, far = exchange(
-        quad_product,
-        half_product,
-        lambda x, c, y, z: (x, y ^ 1, z) if c else (x, y, Z - 1 - z),
-        lambda x, y, z: (x, y ^ 1, Z - 1 - z),
-    )
+    quads, counts = lax.optimization_barrier((quads, counts))
+    quad, quad_product = call(
+        quad_kernel, out_shape=(shape(QUAD, size, size), whole), name="quad"
+    )(kernel, *quads)
+    blocks = [
+        on_core(quad_product, 0, move)
+        for move in (
+            lambda x, y, z: (x, y, Z - 1 - z),
+            lambda x, y, z: (x, y ^ 1, z),
+            lambda x, y, z: (x, y ^ 1, Z - 1 - z),
+        )
+    ]
     counts, quad = lax.optimization_barrier((counts, quad))
-    chip_counts, half_counts = call(chip_kernel, out_shape=(whole, half), name="chip")(
-        counts, other_core(counts)
-    )
-    near_counts, far_counts = exchange(
-        chip_counts,
-        half_counts,
-        lambda x, c, y, z: ((x + 1 - 2 * c) % 4, y, z),
-        lambda x, y, z: (x ^ 2, y, z),
-    )
-    near, far, near_counts, far_counts = lax.optimization_barrier(
-        (near, far, near_counts, far_counts)
-    )
+    chip_counts = counts + other_core(counts)
+    spread = [
+        on_core(chip_counts, 1, lambda x, y, z, s=s: ((x + s) % 4, y, z)) for s in (1, 2, 3)
+    ]
+    counts = chip_counts + spread[0] + spread[1] + spread[2]
     block, message = call(
         block_kernel, out_shape=(shape(4, size, size), shape(8, size)), name="block"
-    )(quad_product, near, other_core(near), far, other_core(far))
-    joined = call(join_kernel, out_shape=whole, name="join")(near_counts, far_counts)
-    arrived = lax.ppermute(message, "clique", along_clique(lambda y, z: (y ^ 2, z)))
+    )(quad_product, *blocks)
+    arrived = on_core(message, 0, lambda x, y, z: (x, y ^ 2, z))
     path, known = call(sides_kernel, out_shape=(whole, shape(8, size)), name="sides")(quad, block)
+    arrived, path, counts = lax.optimization_barrier((arrived, path, counts))
+    sibling_counts = other_core(counts)
+    vectors = call(vectors_kernel, out_shape=shape(8, size), name="vectors")(path, known, arrived)
     total_rows = table_rows.shape[1] * lax.axis_size("dp")
     updated, beliefs = call(
         functools.partial(final_kernel, size * size / total_rows),
         out_shape=(whole, whole),
-        scratch_shapes=[
-            pltpu.VMEM((size, 1), jnp.float32),
-            pltpu.VMEM((1, size), jnp.float32),
-        ],
         name="final",
-    )(
-        potential, measure_noise[0], kernel, path, known, arrived, chip_counts, joined,
-        other_core(joined),
-    )
+    )(potential, measure_noise[0], vectors, other_core(vectors), counts, sibling_counts)
     return (updated[None], beliefs[None])
 
 

time: 48.8 us -> 57.7 us (1.18)
  starting transfers between devices: 22 us -> 37.3 us
  waiting for transfers between devices: 11.1 us -> 4.17 us
    ppermute x6 -> x3, starting transfers between devices: 2.58 us -> 23.5 us  [other_core(): return lax.ppermute(value, 'dp', along_dp(lambda x, c: (x, 1 - c)))]
    ppermute x7 -> x10, waiting for transfers between devices: 8.63 us -> 3.01 us  [on_core(): return lax.ppermute(value, ('dp', 'clique'), pairs)]
    ppermute x7 -> x10, starting transfers between devices: 19.4 us -> 13.8 us  [on_core(): return lax.ppermute(value, ('dp', 'clique'), pairs)]
    ppermute x6 -> x3, waiting for transfers between devices: 2.43 us -> 1.16 us  [other_core(): return lax.ppermute(value, 'dp', along_dp(lambda x, c: (x, 1 - c)))]
    pallas_call x4 -> x3, Pallas kernels: 2.13 us -> 2.17 us  [the longest x1 1.03 us: per_device(): call(read_kernel, in_specs=[hbm, hbm], out_specs=(vmem, vmem), out_shape=...]
  transfers between devices with their start and end apart: 13 -> 13, of which waited for: 5 -> 2; matrix products, arithmetic and copies ran while one was open for 0% -> 0% of each run, Pallas kernels for 24% -> 21%
where the time goes in v7:
time: 57.7 us; the launch traced here: 57.3 us
  starting transfers between devices  37.3 us (65%)
  Pallas kernels  14.8 us (26%)
  waiting for transfers between devices  4.17 us (7%)
  between operations  0.86 us (1%)
    ppermute x3, starting transfers between devices, other_core(): return lax.ppermute(value, 'dp', along_dp(lambda x, c: (x, 1 - c)))  23.5 us
    ppermute x10, starting transfers between devices, on_core(): return lax.ppermute(value, ('dp', 'clique'), pairs)  13.8 us
    pallas_call x1, Pallas kernels, count_pairs(): pl.pallas_call(functools.partial(count_kernel, part), out_shape=shape(siz...  8.58 us
    ppermute x10, waiting for transfers between devices, on_core(): return lax.ppermute(value, ('dp', 'clique'), pairs)  3.01 us
    pallas_call x1, Pallas kernels, per_device(): call(sides_kernel, out_shape=(whole, shape(8, size)), name='sides')  2.48 us
    ppermute x3, waiting for transfers between devices, other_core(): return lax.ppermute(value, 'dp', along_dp(lambda x, c: (x, 1 - c)))  1.16 us
  transfers between devices with their start and end apart: 13, of which 2 were waited for; matrix products, arithmetic and copies ran while one was open for 0% of the time, Pallas kernels for 21%

profile of v7, /device:TPU:1, one launch (start us, length us, event | category | flops | bytes accessed | tf_op | source)
XLA Modules:
  0.0 57.3 jit_solution(5548868769028913578)
XLA Ops:
  0.6 1.0 %read.1 = (s32[33]{0:T(128)S(1)}, f32[256,256]{1,0:T(8,128)S(1)}) custom-call(s32[33]{0:T(128)} %order_hbm.1, f32[256,256]{1,0:T(8,128)} %bitcast.4), custom_call_target="tpu_custom_call" | custom-call | tf_op jit(solution)/shard_map/read/pallas_call | solution.py:282
  1.7 0.7 %collective-permute-start.2 = (f32[256,256]{1,0:T(8,128)S(1)}, f32[256,256]{1,0:T(8,128)S(1)}, u32[]{:S(2)}, u32[]{:S(2)}) collective-permute-start(f32[256,256]{1,0:T(8,128)S(1)} %get-tuple-element.21.kernel_ref), channel_id=1, source_target_pairs={{0,3},{1,0},{2,1},{3,2},{4,7},{5,4},{6,5},{7,6},{8,11},{9,8},{10,9... | collective-permute-start | bytes 786440 | tf_op jit(solution)/shard_map/ppermute | solution.py:272
  2.3 0.7 %collective-permute-start.1 = (f32[256,256]{1,0:T(8,128)S(1)}, f32[256,256]{1,0:T(8,128)S(1)}, u32[]{:S(2)}, u32[]{:S(2)}) collective-permute-start(f32[256,256]{1,0:T(8,128)S(1)} %get-tuple-element.21.kernel_ref), channel_id=1, source_target_pairs={{0,2},{1,3},{2,0},{3,1},{4,6},{5,7},{6,4},{7,5},{8,10},{9,11},{10,... | collective-permute-start | bytes 786440 | tf_op jit(solution)/shard_map/ppermute | solution.py:272
  3.0 0.7 %collective-permute-start = (f32[256,256]{1,0:T(8,128)S(1)}, f32[256,256]{1,0:T(8,128)S(1)}, u32[]{:S(2)}, u32[]{:S(2)}) collective-permute-start(f32[256,256]{1,0:T(8,128)S(1)} %get-tuple-element.21.kernel_ref), channel_id=1, source_target_pairs={{0,1},{1,2},{2,3},{3,0},{4,5},{5,6},{6,7},{7,4},{8,9},{9,10},{10,1... | collective-permute-start | bytes 786440 | tf_op jit(solution)/shard_map/ppermute | solution.py:272
  3.7 0.0 copy-start
  3.7 0.0 copy-start.1
  3.7 8.6 %counts.1 = f32[256,256]{1,0:T(8,128)S(1)} custom-call(s32[33]{0:T(128)S(1)} %get-tuple-element.22.order_ref, s32[33,65536]{1,0:T(8,128)} %right_ref.1, s32[33,65536]{1,0:T(8,128)} %right_ref.1), custom_call_target="tpu_custom_call" | custom-call | tf_op jit(solution)/shard_map/counts/pallas_call | solution.py:249
  12.3 0.0 collective-permute-done.2.third
  12.3 0.0 collective-permute-done.1.second
  12.4 0.0 collective-permute-done.first
  12.4 1.0 %quad.1 = (f32[4,256,256]{2,1,0:T(8,128)S(1)}, f32[256,256]{1,0:T(8,128)S(1)}) custom-call(f32[256,256]{1,0:T(8,128)S(1)} %get-tuple-element.21.kernel_ref, f32[256,256]{1,0:T(8,128)S(1)} %collective-permute-done.first, f32[256,256]{1,0:T(8,128)S(1)} %collective-permute-done.1.second, f32[256,256]{1,0:T(8,128)S(1)} %collective-permute-done.2.third), custom_call_target="tpu_custom_call" | custom-call | tf_op jit(solution)/shard_map/quad/pallas_call | solution.py:299
  13.4 10.8 %collective-permute-start.7 = (f32[256,256]{1,0:T(8,128)S(1)}, f32[256,256]{1,0:T(8,128)S(1)}, u32[]{:S(2)}, u32[]{:S(2)}) collective-permute-start(f32[256,256]{1,0:T(8,128)S(1)} %counts.1), channel_id=1, source_target_pairs={{0,32},{32,0},{64,96},{96,64},{128,160},{160,128},{192,224},{224,1... | collective-permute-start | bytes 786440 | tf_op jit(solution)/shard_map/ppermute | solution.py:30
  24.2 0.7 %collective-permute-start.5 = (f32[256,256]{1,0:T(8,128)S(1)}, f32[256,256]{1,0:T(8,128)S(1)}, u32[]{:S(2)}, u32[]{:S(2)}) collective-permute-start(f32[256,256]{1,0:T(8,128)S(1)} %get-tuple-element.26.product_ref), channel_id=1, source_target_pairs={{0,15},{1,14},{2,13},{3,12},{4,11},{5,10},{6,9},{7,8},{8,7},{9,6},... | collective-permute-start | bytes 786440 | tf_op jit(solution)/shard_map/ppermute | solution.py:272
  24.9 0.7 %collective-permute-start.4 = (f32[256,256]{1,0:T(8,128)S(1)}, f32[256,256]{1,0:T(8,128)S(1)}, u32[]{:S(2)}, u32[]{:S(2)}) collective-permute-start(f32[256,256]{1,0:T(8,128)S(1)} %get-tuple-element.26.product_ref), channel_id=1, source_target_pairs={{0,8},{1,9},{2,10},{3,11},{4,12},{5,13},{6,14},{7,15},{8,0},{9,1},... | collective-permute-start | bytes 786440 | tf_op jit(solution)/shard_map/ppermute | solution.py:272
  25.5 0.7 %collective-permute-start.3 = (f32[256,256]{1,0:T(8,128)S(1)}, f32[256,256]{1,0:T(8,128)S(1)}, u32[]{:S(2)}, u32[]{:S(2)}) collective-permute-start(f32[256,256]{1,0:T(8,128)S(1)} %get-tuple-element.26.product_ref), channel_id=1, source_target_pairs={{0,7},{1,6},{2,5},{3,4},{4,3},{5,2},{6,1},{7,0},{8,15},{9,14},{10,... | collective-permute-start | bytes 786440 | tf_op jit(solution)/shard_map/ppermute | solution.py:272
  26.2 0.0 collective-permute-done.7
  26.3 4.2 %collective-permute-start.10 = (f32[256,256]{1,0:T(8,128)S(1)}, f32[256,256]{1,0:T(8,128)S(1)}, u32[]{:S(2)}, u32[]{:S(2)}) collective-permute-start(f32[256,256]{1,0:T(8,128)S(1)} %add.12), channel_id=1, source_target_pairs={{0,0},{1,1},{2,2},{3,3},{4,4},{5,5},{6,6},{7,7},{8,8},{9,9},{10,10... | collective-permute-start | bytes 786440 | tf_op jit(solution)/shard_map/ppermute | solution.py:272
  30.5 2.4 %collective-permute-start.9 = (f32[256,256]{1,0:T(8,128)S(1)}, f32[256,256]{1,0:T(8,128)S(1)}, u32[]{:S(2)}, u32[]{:S(2)}) collective-permute-start(f32[256,256]{1,0:T(8,128)S(1)} %add.12), channel_id=1, source_target_pairs={{0,0},{1,1},{2,2},{3,3},{4,4},{5,5},{6,6},{7,7},{8,8},{9,9},{10,10... | collective-permute-start | bytes 786440 | tf_op jit(solution)/shard_map/ppermute | solution.py:272
  32.9 0.0 collective-permute-done.5.third
  32.9 2.5 %collective-permute-start.8 = (f32[256,256]{1,0:T(8,128)S(1)}, f32[256,256]{1,0:T(8,128)S(1)}, u32[]{:S(2)}, u32[]{:S(2)}) collective-permute-start(f32[256,256]{1,0:T(8,128)S(1)} %add.12), channel_id=1, source_target_pairs={{0,0},{1,1},{2,2},{3,3},{4,4},{5,5},{6,6},{7,7},{8,8},{9,9},{10,10... | collective-permute-start | bytes 786440 | tf_op jit(solution)/shard_map/ppermute | solution.py:272
  35.4 0.0 collective-permute-done.4.second
  35.4 0.0 collective-permute-done.3.first
  35.4 0.6 block.1
  36.0 0.7 %collective-permute-start.6 = (f32[8,256]{1,0:T(8,128)S(1)}, f32[8,256]{1,0:T(8,128)S(1)}, u32[]{:S(2)}, u32[]{:S(2)}) collective-permute-start(f32[8,256]{1,0:T(8,128)S(1)} %get-tuple-element.27), channel_id=1, source_target_pairs={{0,16},{1,17},{2,18},{3,19},{4,20},{5,21},{6,22},{7,23},{8,24},{9,... | collective-permute-start | bytes 24584 | tf_op jit(solution)/shard_map/ppermute | solution.py:272
  36.7 2.5 %sides.1 = (f32[256,256]{1,0:T(8,128)S(1)}, f32[8,256]{1,0:T(8,128)S(1)}) custom-call(f32[4,256,256]{2,1,0:T(8,128)S(1)} %get-tuple-element.30.quad_ref, f32[4,256,256]{2,1,0:T(8,128)S(1)} %get-tuple-element.31.block_ref), custom_call_target="tpu_custom_call" | custom-call | tf_op jit(solution)/shard_map/sides/pallas_call | solution.py:320
  39.2 0.0 collective-permute-done.10
  39.2 0.0 collective-permute-done.9
  39.2 3.0 %collective-permute-done.8 = f32[256,256]{1,0:T(8,128)S(1)} collective-permute-done((f32[256,256]{1,0:T(8,128)S(1)}, f32[256,256]{1,0:T(8,128)S(1)}, u32[]{:S(2)}, u32[]{:S(2)}) %collective-permute-start.8) | collective-permute-done | bytes 262176 | tf_op jit(solution)/shard_map/ppermute | solution.py:272
  42.2 0.1 add_add_fusion.counts_ref
  42.3 0.0 collective-permute-done.6.message_ref
  42.3 12.6 %collective-permute-start.12 = (f32[256,256]{1,0:T(8,128)S(1)}, f32[256,256]{1,0:T(8,128)S(1)}, u32[]{:S(2)}, u32[]{:S(2)}) collective-permute-start(f32[256,256]{1,0:T(8,128)S(1)} %add_add_fusion.counts_ref), channel_id=1, source_target_pairs={{0,32},{32,0},{64,96},{96,64},{128,160},{160,128},{192,224},{224,1... | collective-permute-start | bytes 786440 | tf_op jit(solution)/shard_map/ppermute | solution.py:30
  54.9 0.1 vectors.1.vectors_ref
  55.0 0.1 collective-permute-start.11
  55.1 1.2 %collective-permute-done.11.sibling_vectors_ref = f32[8,256]{1,0:T(8,128)S(1)} collective-permute-done((f32[8,256]{1,0:T(8,128)S(1)}, f32[8,256]{1,0:T(8,128)S(1)}, u32[]{:S(2)}, u32[]{:S(2)}) %collective-permute-start.11) | collective-permute-done | bytes 8224 | tf_op jit(solution)/shard_map/ppermute | solution.py:30
  56.3 0.0 collective-permute-done.12.sibling_counts_ref
  56.3 0.0 copy-done
  56.3 0.0 copy-done.1
  56.3 1.0 %final.1 = (f32[256,256]{1,0:T(8,128)}, f32[256,256]{1,0:T(8,128)}) custom-call(f32[256,256]{1,0:T(8,128)S(1)} %bitcast.5, f32[256,256]{1,0:T(8,128)S(1)} %bitcast.6, f32[8,256]{1,0:T(8,128)S(1)} %vectors.1.vectors_ref, f32[8,256]{1,0:T(8,128)S(1)} %collective-permute-done.11.sibling_vectors_ref, f32[256,256]{1,0:T(8,128)S(1)} %add_add_fusion.counts_ref, ...), custom_call_target="tpu_custom_call" | custom-call | tf_op jit(solution)/shard_map/final/pallas_call | solution.py:325
  (1 shorter events, 0.0 us)
Async XLA Ops:
  1.7 10.7 %collective-permute-start.2 = (f32[256,256]{1,0:T(8,128)S(1)}, f32[256,256]{1,0:T(8,128)S(1)}, u32[]{:S(2)}, u32[]{:S(2)}) collective-permute-start(f32[256,256]{1,0:T(8,128)S(1)} %get-tuple-element.21.kernel_ref), channel_id=1, source_target_pairs={{0,3},{1,0},{2,1},{3,2},{4,7},{5,4},{6,5},{7,6},{8,11},{9,8},{10,9... | collective-permute-start | bytes 786440 | tf_op jit(solution)/shard_map/ppermute | solution.py:272
  2.3 10.0 %collective-permute-start.1 = (f32[256,256]{1,0:T(8,128)S(1)}, f32[256,256]{1,0:T(8,128)S(1)}, u32[]{:S(2)}, u32[]{:S(2)}) collective-permute-start(f32[256,256]{1,0:T(8,128)S(1)} %get-tuple-element.21.kernel_ref), channel_id=1, source_target_pairs={{0,2},{1,3},{2,0},{3,1},{4,6},{5,7},{6,4},{7,5},{8,10},{9,11},{10,... | collective-permute-start | bytes 786440 | tf_op jit(solution)/shard_map/ppermute | solution.py:272
  3.0 9.3 %collective-permute-start = (f32[256,256]{1,0:T(8,128)S(1)}, f32[256,256]{1,0:T(8,128)S(1)}, u32[]{:S(2)}, u32[]{:S(2)}) collective-permute-start(f32[256,256]{1,0:T(8,128)S(1)} %get-tuple-element.21.kernel_ref), channel_id=1, source_target_pairs={{0,1},{1,2},{2,3},{3,0},{4,5},{5,6},{6,7},{7,4},{8,9},{9,10},{10,1... | collective-permute-start | bytes 786440 | tf_op jit(solution)/shard_map/ppermute | solution.py:272
  3.7 52.6 %copy-start = (f32[1,256,256]{2,1,0:T(8,128)S(1)}, f32[1,256,256]{2,1,0:T(8,128)}, u32[]{:S(2)}) copy-start(f32[1,256,256]{2,1,0:T(8,128)} %param.6) | copy-start | bytes 786436
  3.7 52.6 %copy-start.1 = (f32[1,256,256]{2,1,0:T(8,128)S(1)}, f32[1,256,256]{2,1,0:T(8,128)}, u32[]{:S(2)}) copy-start(f32[1,256,256]{2,1,0:T(8,128)} %param.7) | copy-start | bytes 786436
  13.4 12.8 %collective-permute-start.7 = (f32[256,256]{1,0:T(8,128)S(1)}, f32[256,256]{1,0:T(8,128)S(1)}, u32[]{:S(2)}, u32[]{:S(2)}) collective-permute-start(f32[256,256]{1,0:T(8,128)S(1)} %counts.1), channel_id=1, source_target_pairs={{0,32},{32,0},{64,96},{96,64},{128,160},{160,128},{192,224},{224,1... | collective-permute-start | bytes 786440 | tf_op jit(solution)/shard_map/ppermute | solution.py:30
  24.2 8.7 %collective-permute-start.5 = (f32[256,256]{1,0:T(8,128)S(1)}, f32[256,256]{1,0:T(8,128)S(1)}, u32[]{:S(2)}, u32[]{:S(2)}) collective-permute-start(f32[256,256]{1,0:T(8,128)S(1)} %get-tuple-element.26.product_ref), channel_id=1, source_target_pairs={{0,15},{1,14},{2,13},{3,12},{4,11},{5,10},{6,9},{7,8},{8,7},{9,6},... | collective-permute-start | bytes 786440 | tf_op jit(solution)/shard_map/ppermute | solution.py:272
  24.9 10.6 %collective-permute-start.4 = (f32[256,256]{1,0:T(8,128)S(1)}, f32[256,256]{1,0:T(8,128)S(1)}, u32[]{:S(2)}, u32[]{:S(2)}) collective-permute-start(f32[256,256]{1,0:T(8,128)S(1)} %get-tuple-element.26.product_ref), channel_id=1, source_target_pairs={{0,8},{1,9},{2,10},{3,11},{4,12},{5,13},{6,14},{7,15},{8,0},{9,1},... | collective-permute-start | bytes 786440 | tf_op jit(solution)/shard_map/ppermute | solution.py:272
  25.5 9.9 %collective-permute-start.3 = (f32[256,256]{1,0:T(8,128)S(1)}, f32[256,256]{1,0:T(8,128)S(1)}, u32[]{:S(2)}, u32[]{:S(2)}) collective-permute-start(f32[256,256]{1,0:T(8,128)S(1)} %get-tuple-element.26.product_ref), channel_id=1, source_target_pairs={{0,7},{1,6},{2,5},{3,4},{4,3},{5,2},{6,1},{7,0},{8,15},{9,14},{10,... | collective-permute-start | bytes 786440 | tf_op jit(solution)/shard_map/ppermute | solution.py:272
  26.3 12.9 %collective-permute-start.10 = (f32[256,256]{1,0:T(8,128)S(1)}, f32[256,256]{1,0:T(8,128)S(1)}, u32[]{:S(2)}, u32[]{:S(2)}) collective-permute-start(f32[256,256]{1,0:T(8,128)S(1)} %add.12), channel_id=1, source_target_pairs={{0,0},{1,1},{2,2},{3,3},{4,4},{5,5},{6,6},{7,7},{8,8},{9,9},{10,10... | collective-permute-start | bytes 786440 | tf_op jit(solution)/shard_map/ppermute | solution.py:272
  30.5 8.7 %collective-permute-start.9 = (f32[256,256]{1,0:T(8,128)S(1)}, f32[256,256]{1,0:T(8,128)S(1)}, u32[]{:S(2)}, u32[]{:S(2)}) collective-permute-start(f32[256,256]{1,0:T(8,128)S(1)} %add.12), channel_id=1, source_target_pairs={{0,0},{1,1},{2,2},{3,3},{4,4},{5,5},{6,6},{7,7},{8,8},{9,9},{10,10... | collective-permute-start | bytes 786440 | tf_op jit(solution)/shard_map/ppermute | solution.py:272
  32.9 9.3 %collective-permute-start.8 = (f32[256,256]{1,0:T(8,128)S(1)}, f32[256,256]{1,0:T(8,128)S(1)}, u32[]{:S(2)}, u32[]{:S(2)}) collective-permute-start(f32[256,256]{1,0:T(8,128)S(1)} %add.12), channel_id=1, source_target_pairs={{0,0},{1,1},{2,2},{3,3},{4,4},{5,5},{6,6},{7,7},{8,8},{9,9},{10,10... | collective-permute-start | bytes 786440 | tf_op jit(solution)/shard_map/ppermute | solution.py:272
  36.0 6.2 %collective-permute-start.6 = (f32[8,256]{1,0:T(8,128)S(1)}, f32[8,256]{1,0:T(8,128)S(1)}, u32[]{:S(2)}, u32[]{:S(2)}) collective-permute-start(f32[8,256]{1,0:T(8,128)S(1)} %get-tuple-element.27), channel_id=1, source_target_pairs={{0,16},{1,17},{2,18},{3,19},{4,20},{5,21},{6,22},{7,23},{8,24},{9,... | collective-permute-start | bytes 24584 | tf_op jit(solution)/shard_map/ppermute | solution.py:272
  42.3 14.0 %collective-permute-start.12 = (f32[256,256]{1,0:T(8,128)S(1)}, f32[256,256]{1,0:T(8,128)S(1)}, u32[]{:S(2)}, u32[]{:S(2)}) collective-permute-start(f32[256,256]{1,0:T(8,128)S(1)} %add_add_fusion.counts_ref), channel_id=1, source_target_pairs={{0,32},{32,0},{64,96},{96,64},{128,160},{160,128},{192,224},{224,1... | collective-permute-start | bytes 786440 | tf_op jit(solution)/shard_map/ppermute | solution.py:30
  55.0 1.3 %collective-permute-start.11 = (f32[8,256]{1,0:T(8,128)S(1)}, f32[8,256]{1,0:T(8,128)S(1)}, u32[]{:S(2)}, u32[]{:S(2)}) collective-permute-start(f32[8,256]{1,0:T(8,128)S(1)} %vectors.1.vectors_ref), channel_id=1, source_target_pairs={{0,32},{32,0},{64,96},{96,64},{128,160},{160,128},{192,224},{224,1... | collective-permute-start | bytes 24584 | tf_op jit(solution)/shard_map/ppermute | solution.py:30

commit v8 on v3

--- a/solution.py
+++ b/solution.py
@@ -85,22 +85,19 @@
     half_ref[...] = kernel_ref[pl.ds(core * half, half), :]
 
 
-def put_others(stack_ref, mine, near, near_sibling, far, far_sibling, core):
-    count = stack_ref.shape[0]
-    half = far.shape[0]
-    before, after, across = (lax.rem(mine + count + move, count) for move in (-1, 1, 2))
-    stack_ref[jnp.where(core == 0, before, after)] = near[...]
-    stack_ref[jnp.where(core == 0, after, before)] = near_sibling[...]
-    stack_ref[across, pl.ds(core * half, half), :] = far[...]
-    stack_ref[across, pl.ds((1 - core) * half, half), :] = far_sibling[...]
-
-
-def quad_kernel(kernel_ref, near, near_sibling, far, far_sibling, quad_ref, product_ref, half_ref):
+def put_halves(stack_ref, slot, own, sibling, core):
+    half = own.shape[0]
+    stack_ref[slot, pl.ds(core * half, half), :] = own[...]
+    stack_ref[slot, pl.ds((1 - core) * half, half), :] = sibling[...]
+
+
+def quad_kernel(kernel_ref, a1, a2, a3, b1, b2, b3, quad_ref, product_ref, half_ref):
     core, _, z = place()
     mine = lax.rem(z, QUAD)
     half, size = half_ref.shape
     quad_ref[mine] = kernel_ref[...]
-    put_others(quad_ref, mine, near, near_sibling, far, far_sibling, core)
+    for step, (own, sibling) in enumerate(((a1, b1), (a2, b2), (a3, b3)), 1):
+        put_halves(quad_ref, lax.rem(mine + QUAD - step, QUAD), own, sibling, core)
     scale = 1.0 / size
     left = product(quad_ref[0], quad_ref[1]) * scale
     right = product(quad_ref[2], quad_ref[3]) * scale
@@ -110,7 +107,33 @@
     half_ref[...] = product_ref[pl.ds(core * half, half), :]
 
 
-def octet_kernel(product_ref, own_ref, sibling_ref, other_ref, octet_ref, half_ref):
+def unit_product(left, right):
+    moved = product(left, right)
+    return moved / jnp.max(jnp.max(moved, axis=0, keepdims=True), axis=1, keepdims=True)
+
+
+def paths_kernel(quad_ref, other_ref, before_ref, after_ref):
+    _, _, z = place()
+    later_quad, mine = (lax.div(z, QUAD), lax.rem(z, QUAD))
+    size = before_ref.shape[0]
+    unit = jnp.where(diagonal(size), 1.0, 0.0)
+    other = other_ref[...]
+    before_ref[...] = lax.fori_loop(
+        0, mine, lambda i, m: unit_product(m, quad_ref[i]), jnp.where(later_quad == 1, other, unit)
+    )
+    after_ref[...] = lax.fori_loop(
+        0,
+        QUAD - 1 - mine,
+        lambda i, m: unit_product(m, quad_ref[mine + 1 + i]),
+        unit,
+    )
+
+    @pl.when(later_quad == 0)
+    def _():
+        after_ref[...] = unit_product(after_ref[...], other)
+
+
+def octet_kernel(product_ref, own_ref, sibling_ref, other_ref, half_ref):
     core, _, z = place()
     half = half_ref.shape[0]
     rows = pl.ds(core * half, half)
@@ -119,13 +142,11 @@
 
     @pl.when(z < QUAD)
     def _():
-        octet_ref[...] = product(product_ref[...], other_ref[...])
+        half_ref[...] = product(product_ref[rows, :], other_ref[...])
 
     @pl.when(z >= QUAD)
     def _():
-        octet_ref[...] = product(other_ref[...], product_ref[...])
-
-    half_ref[...] = octet_ref[rows, :]
+        half_ref[...] = product(other_ref[rows, :], product_ref[...])
 
 
 def chip_kernel(own_ref, sibling_ref, both_ref, half_ref):
@@ -143,32 +164,23 @@
 
 
 def final_kernel(
-    scale, potential_ref, noise_ref, quad_ref, other_ref, near, near_sibling, far, far_sibling,
+    scale, potential_ref, noise_ref, kernel_ref, before_ref, after_ref, a1, a2, a3, b1, b2, b3,
     chip_ref, join_ref, sibling_join_ref, updated_ref, beliefs_ref, octet_ref
 ):
-    core, y, z = place()
+    core, y, _ = place()
     size = potential_ref.shape[0]
-    put_others(octet_ref, y, near, near_sibling, far, far_sibling, core)
+    for step, (own, sibling) in enumerate(((a1, b1), (a2, b2), (a3, b3)), 1):
+        put_halves(octet_ref, lax.rem(y + Y - step, Y), own, sibling, core)
     eye = diagonal(size)
     ones = jnp.ones((1, size), jnp.float32)
-    later_quad = lax.div(z, QUAD)
-    mine = lax.rem(z, QUAD)
     forward = lax.fori_loop(0, y, lambda i, row: row_times(row, octet_ref[i], eye), ones)
-    forward = lax.fori_loop(
-        0, later_quad, lambda i, row: row_times(row, other_ref[...], eye), forward
-    )
-    forward = lax.fori_loop(0, mine, lambda i, row: row_times(row, quad_ref[i], eye), forward)
+    forward = row_times(forward, before_ref[...], eye)
     backward = lax.fori_loop(
         0, Y - 1 - y, lambda i, row: times_row(octet_ref[Y - 1 - i], row, eye), ones
     )
-    backward = lax.fori_loop(
-        0, 1 - later_quad, lambda i, row: times_row(other_ref[...], row, eye), backward
-    )
-    backward = lax.fori_loop(
-        0, 3 - mine, lambda i, row: times_row(quad_ref[3 - i], row, eye), backward
-    )
+    backward = times_row(after_ref[...], backward, eye)
     column = as_column(forward, eye) / jnp.sum(forward, axis=1, keepdims=True)
-    joint = column * quad_ref[mine] * backward
+    joint = column * kernel_ref[...] * backward
     total = jnp.sum(jnp.sum(joint, axis=0, keepdims=True), axis=1, keepdims=True)
     beliefs = joint * (size * size / total)
     beliefs_ref[...] = beliefs
@@ -273,28 +285,36 @@
         pltpu.with_memory_space_constraint(attribute_order, pltpu.HBM),
         pltpu.with_memory_space_constraint(potential, pltpu.HBM),
     )
-    near, far = exchange(
-        kernel, half_of_kernel, lambda x, y, z, s: (x, y, z // QUAD * QUAD + (z + s) % QUAD)
-    )
+    quads = [
+        lax.ppermute(half_of_kernel, "clique", along_clique(lambda y, z, s=s: (y, in_quad(z, s))))
+        for s in (1, 2, 3)
+    ]
     counts = count_pairs(order, table_rows, size)
-    near, far, counts = lax.optimization_barrier((near, far, counts))
+    quads, counts = lax.optimization_barrier((quads, counts))
     quad, quad_product, half_product = call(
         quad_kernel, out_shape=(shape(QUAD, size, size), whole, half), name="quad"
-    )(kernel, near, other_core(near), far, other_core(far))
+    )(kernel, *quads, *[other_core(value) for value in quads])
     other = lax.ppermute(half_product, "clique", along_clique(lambda y, z: (y, Z - 1 - z)))
-    counts, quad_product = lax.optimization_barrier((counts, quad_product))
+    counts, quad = lax.optimization_barrier((counts, quad))
     chip_counts, half_counts = call(chip_kernel, out_shape=(whole, half), name="chip")(
         counts, other_core(counts)
     )
     near_counts, far_counts = exchange(
         chip_counts, half_counts, lambda x, y, z, s: ((x + s) % 4, y, z)
     )
-    other, chip_counts = lax.optimization_barrier((other, chip_counts))
-    other_product, octet, half_octet = call(
-        octet_kernel, out_shape=(whole, whole, half), name="octet"
-    )(quad_product, other, other_core(other))
-    near, far = exchange(octet, half_octet, lambda x, y, z, s: (x, (y + s) % Y, z))
+    other, far_counts = lax.optimization_barrier((other, far_counts))
+    sibling_other = other_core(other)
+    sibling_other, near_counts = lax.optimization_barrier((sibling_other, near_counts))
+    other_product, half_octet = call(octet_kernel, out_shape=(whole, half), name="octet")(
+        quad_product, other, sibling_other
+    )
+    octets = [
+        lax.ppermute(half_octet, "clique", along_clique(lambda y, z, s=s: ((y + s) % Y, z)))
+        for s in (1, 2, 3)
+    ]
+    before, after = call(paths_kernel, out_shape=(whole, whole), name="paths")(quad, other_product)
     joined = call(join_kernel, out_shape=whole, name="join")(near_counts, far_counts)
+    octets, before, joined = lax.optimization_barrier((octets, before, joined))
     total_rows = table_rows.shape[1] * lax.axis_size("dp")
     updated, beliefs = call(
         functools.partial(final_kernel, size * size / total_rows),
@@ -302,8 +322,8 @@
         scratch_shapes=[pltpu.VMEM((Y, size, size), jnp.float32)],
         name="final",
     )(
-        potential, measure_noise[0], quad, other_product, near, other_core(near), far,
-        other_core(far), chip_counts, joined, other_core(joined),
+        potential, measure_noise[0], kernel, before, after, *octets,
+        *[other_core(value) for value in octets], chip_counts, joined, other_core(joined),
     )
     return (updated[None], beliefs[None])
 

time: 50.3 us -> 52.8 us (1.050); the launches traced: 50.1 us -> 51.8 us
  Pallas kernels: 13.3 us -> 14.8 us
  starting transfers between devices: 20.1 us -> 20.9 us
  waiting for transfers between devices: 16 us -> 15.4 us
    ppermute x3 -> x1, starting transfers between devices: 10.5 us -> 0.86 us  [exchange(): lax.ppermute(whole, axes, everywhere(lambda x, c, y, z: step(x, y, z, 1 -...]
    ppermute x0 -> x6, starting transfers between devices: none -> 9.49 us  [the longest x3 5.63 us: per_device(): lax.ppermute(half_of_kernel, 'clique', along_clique(lambda y, z, s=s: (y,...]
    ppermute x3 -> x1, waiting for transfers between devices: 7.86 us -> 0.01 us  [exchange(): lax.ppermute(half, axes, everywhere(lambda x, c, y, z: step(x, y, z, 2)))]
    ppermute x0 -> x6, waiting for transfers between devices: none -> 7.8 us  [the longest x3 6.08 us: per_device(): lax.ppermute(half_octet, 'clique', along_clique(lambda y, z, s=s: ((y + s...]
    ppermute x1, starting transfers between devices: 6.17 us -> 2.79 us  [per_device(): lax.ppermute(half_product, 'clique', along_clique(lambda y, z: (y, Z - 1...]
    ppermute x7 -> x9, starting transfers between devices: 1.83 us -> 4.97 us  [other_core(): return lax.ppermute(value, 'dp', along_dp(lambda x, c: (x, 1 - c)))]
    ppermute x1, waiting for transfers between devices: 5.51 us -> 2.67 us  [per_device(): lax.ppermute(half_product, 'clique', along_clique(lambda y, z: (y, Z - 1...]
    ppermute x3 -> x1, waiting for transfers between devices: 0.37 us -> 2.5 us  [exchange(): lax.ppermute(whole, axes, everywhere(lambda x, c, y, z: step(x, y, z, 1 -...]
  transfers between devices with their start and end apart: 14 -> 18, of which waited for: 7 -> 12; matrix products, arithmetic and copies ran while one was open for 0% -> 0% of each run, Pallas kernels for 18% -> 21%
where the time goes in v8:
time: 52.8 us; the launch traced here: 51.8 us
  starting transfers between devices  20.9 us (40%)
  waiting for transfers between devices  15.4 us (29%)
  Pallas kernels  14.8 us (28%)
  between operations  0.71 us (1%)
    pallas_call x1, Pallas kernels, count_pairs(): pl.pallas_call(functools.partial(count_kernel, part), out_shape=shape(siz...  8.9 us
    ppermute x3, waiting for transfers between devices, per_device(): lax.ppermute(half_octet, 'clique', along_clique(lambda y, z, s=s: ((y + s...  6.08 us
    ppermute x3, starting transfers between devices, per_device(): lax.ppermute(half_of_kernel, 'clique', along_clique(lambda y, z, s=s: (y,...  5.63 us
    ppermute x9, starting transfers between devices, other_core(): return lax.ppermute(value, 'dp', along_dp(lambda x, c: (x, 1 - c)))  4.97 us
    ppermute x3, starting transfers between devices, per_device(): lax.ppermute(half_octet, 'clique', along_clique(lambda y, z, s=s: ((y + s...  3.85 us
    ppermute x1, starting transfers between devices, exchange(): lax.ppermute(half, axes, everywhere(lambda x, c, y, z: step(x, y, z, 2)))  2.83 us
    ppermute x1, starting transfers between devices, per_device(): lax.ppermute(half_product, 'clique', along_clique(lambda y, z: (y, Z - 1...  2.79 us
    ppermute x1, waiting for transfers between devices, per_device(): lax.ppermute(half_product, 'clique', along_clique(lambda y, z: (y, Z - 1...  2.67 us
  transfers between devices with their start and end apart: 18, of which 12 were waited for; matrix products, arithmetic and copies ran while one was open for 0% of the time, Pallas kernels for 21%

profile of v8, /device:TPU:1, one launch (start us, length us, event | category | flops | bytes accessed | tf_op | source)
XLA Modules:
  0.0 51.8 jit_solution(13549992850389520055)
XLA Ops:
  0.6 1.1 %read.1 = (s32[33]{0:T(128)S(1)}, f32[256,256]{1,0:T(8,128)S(1)}, f32[128,256]{1,0:T(8,128)S(1)}) custom-call(s32[33]{0:T(128)} %order_hbm.1, f32[256,256]{1,0:T(8,128)} %bitcast.4), custom_call_target="tpu_custom_call" | custom-call | tf_op jit(solution)/shard_map/read/pallas_call | solution.py:277
  1.7 5.3 %collective-permute-start.2 = (f32[128,256]{1,0:T(8,128)S(1)}, f32[128,256]{1,0:T(8,128)S(1)}, u32[]{:S(2)}, u32[]{:S(2)}) collective-permute-start(f32[128,256]{1,0:T(8,128)S(1)} %get-tuple-element.32), channel_id=1, source_target_pairs={{0,3},{1,0},{2,1},{3,2},{4,7},{5,4},{6,5},{7,6},{8,11},{9,8},{10,9... | collective-permute-start | bytes 393224 | tf_op jit(solution)/shard_map/ppermute | solution.py:289
  6.9 0.0 collective-permute-start.1
  6.9 0.4 collective-permute-start
  7.3 0.0 copy-start
  7.3 0.0 copy-start.1
  7.3 8.9 %counts.1.own_ref = f32[256,256]{1,0:T(8,128)S(1)} custom-call(s32[33]{0:T(128)S(1)} %get-tuple-element.33.order_ref, s32[33,65536]{1,0:T(8,128)} %right_ref.1, s32[33,65536]{1,0:T(8,128)} %right_ref.1), custom_call_target="tpu_custom_call" | custom-call | tf_op jit(solution)/shard_map/counts/pallas_call | solution.py:237
  16.2 0.0 collective-permute-done.2.a3
  16.2 1.7 %collective-permute-done.1.a2 = f32[128,256]{1,0:T(8,128)S(1)} collective-permute-done((f32[128,256]{1,0:T(8,128)S(1)}, f32[128,256]{1,0:T(8,128)S(1)}, u32[]{:S(2)}, u32[]{:S(2)}) %collective-permute-start.1) | collective-permute-done | bytes 131104 | tf_op jit(solution)/shard_map/ppermute | solution.py:289
  18.0 0.0 collective-permute-done.a1
  18.0 1.2 %collective-permute-start.3 = (f32[128,256]{1,0:T(8,128)S(1)}, f32[128,256]{1,0:T(8,128)S(1)}, u32[]{:S(2)}, u32[]{:S(2)}) collective-permute-start(f32[128,256]{1,0:T(8,128)S(1)} %collective-permute-done.a1), channel_id=1, source_target_pairs={{0,32},{32,0},{64,96},{96,64},{128,160},{160,128},{192,224},{224,1... | collective-permute-start | bytes 393224 | tf_op jit(solution)/shard_map/ppermute | solution.py:30
  19.1 0.0 collective-permute-start.4
  19.1 0.5 collective-permute-start.5
  19.6 0.5 collective-permute-done.3.b1
  20.1 0.4 collective-permute-done.4.b2
  20.5 0.2 collective-permute-done.5.b3
  20.7 1.0 %quad.1 = (f32[4,256,256]{2,1,0:T(8,128)S(1)}, f32[256,256]{1,0:T(8,128)S(1)}, f32[128,256]{1,0:T(8,128)S(1)}) custom-call(f32[256,256]{1,0:T(8,128)S(1)} %get-tuple-element.31.kernel_ref, f32[128,256]{1,0:T(8,128)S(1)} %collective-permute-done.a1, f32[128,256]{1,0:T(8,128)S(1)} %collective-permute-done.1.a2, f32[128,256]{1,0:T(8,128)S(1)} %collective-permute-done.2.a3, ...), custom_call_target="tpu_custom_call" | custom-call | tf_op jit(solution)/shard_map/quad/pallas_call | solution.py:294
  21.7 0.4 collective-permute-start.7
  22.1 2.8 %collective-permute-start.6 = (f32[128,256]{1,0:T(8,128)S(1)}, f32[128,256]{1,0:T(8,128)S(1)}, u32[]{:S(2)}, u32[]{:S(2)}) collective-permute-start(f32[128,256]{1,0:T(8,128)S(1)} %get-tuple-element.38), channel_id=1, source_target_pairs={{0,7},{1,6},{2,5},{3,4},{4,3},{5,2},{6,1},{7,0},{8,15},{9,14},{10,... | collective-permute-start | bytes 393224 | tf_op jit(solution)/shard_map/ppermute | solution.py:297
  24.9 0.0 collective-permute-done.7.sibling_ref
  24.9 2.8 %collective-permute-start.8 = (f32[128,256]{1,0:T(8,128)S(1)}, f32[128,256]{1,0:T(8,128)S(1)}, u32[]{:S(2)}, u32[]{:S(2)}) collective-permute-start(f32[128,256]{1,0:T(8,128)S(1)} %get-tuple-element.42), channel_id=1, source_target_pairs={{0,128},{1,129},{2,130},{3,131},{4,132},{5,133},{6,134},{7,135},{8... | collective-permute-start | bytes 393224 | tf_op jit(solution)/shard_map/ppermute | solution.py:266
  27.8 0.9 %collective-permute-start.10 = (f32[256,256]{1,0:T(8,128)S(1)}, f32[256,256]{1,0:T(8,128)S(1)}, u32[]{:S(2)}, u32[]{:S(2)}) collective-permute-start(f32[256,256]{1,0:T(8,128)S(1)} %get-tuple-element.44.chip_ref), channel_id=1, source_target_pairs={{0,64},{1,65},{2,66},{3,67},{4,68},{5,69},{6,70},{7,71},{8,72},{9,... | collective-permute-start | bytes 786440 | tf_op jit(solution)/shard_map/ppermute | solution.py:265
  28.6 2.7 %collective-permute-done.6.own_ref = f32[128,256]{1,0:T(8,128)S(1)} collective-permute-done((f32[128,256]{1,0:T(8,128)S(1)}, f32[128,256]{1,0:T(8,128)S(1)}, u32[]{:S(2)}, u32[]{:S(2)}) %collective-permute-start.6) | collective-permute-done | bytes 131104 | tf_op jit(solution)/shard_map/ppermute | solution.py:297
  31.3 0.0 collective-permute-done.8.far_ref
  31.3 1.1 %collective-permute-start.9 = (f32[128,256]{1,0:T(8,128)S(1)}, f32[128,256]{1,0:T(8,128)S(1)}, u32[]{:S(2)}, u32[]{:S(2)}) collective-permute-start(f32[128,256]{1,0:T(8,128)S(1)} %collective-permute-done.6.own_ref), channel_id=1, source_target_pairs={{0,32},{32,0},{64,96},{96,64},{128,160},{160,128},{192,224},{224,1... | collective-permute-start | bytes 393224 | tf_op jit(solution)/shard_map/ppermute | solution.py:30
  32.4 2.5 %collective-permute-done.10.near_ref = f32[256,256]{1,0:T(8,128)S(1)} collective-permute-done((f32[256,256]{1,0:T(8,128)S(1)}, f32[256,256]{1,0:T(8,128)S(1)}, u32[]{:S(2)}, u32[]{:S(2)}) %collective-permute-start.10) | collective-permute-done | bytes 262176 | tf_op jit(solution)/shard_map/ppermute | solution.py:265
  34.9 0.0 collective-permute-done.9.sibling_ref
  34.9 0.3 octet.1
  35.2 3.1 %collective-permute-start.13 = (f32[128,256]{1,0:T(8,128)S(1)}, f32[128,256]{1,0:T(8,128)S(1)}, u32[]{:S(2)}, u32[]{:S(2)}) collective-permute-start(f32[128,256]{1,0:T(8,128)S(1)} %get-tuple-element.46), channel_id=1, source_target_pairs={{0,24},{1,25},{2,26},{3,27},{4,28},{5,29},{6,30},{7,31},{8,0},{9,1... | collective-permute-start | bytes 393224 | tf_op jit(solution)/shard_map/ppermute | solution.py:312
  38.3 0.0 collective-permute-start.12
  38.3 0.7 %collective-permute-start.11 = (f32[128,256]{1,0:T(8,128)S(1)}, f32[128,256]{1,0:T(8,128)S(1)}, u32[]{:S(2)}, u32[]{:S(2)}) collective-permute-start(f32[128,256]{1,0:T(8,128)S(1)} %get-tuple-element.46), channel_id=1, source_target_pairs={{0,8},{1,9},{2,10},{3,11},{4,12},{5,13},{6,14},{7,15},{8,16},{9,17... | collective-permute-start | bytes 393224 | tf_op jit(solution)/shard_map/ppermute | solution.py:312
  39.0 1.9 %paths.1 = (f32[256,256]{1,0:T(8,128)S(1)}, f32[256,256]{1,0:T(8,128)S(1)}) custom-call(f32[4,256,256]{2,1,0:T(8,128)S(1)} %get-tuple-element.47.quad_ref, f32[256,256]{1,0:T(8,128)S(1)} %get-tuple-element.48.other_ref), custom_call_target="tpu_custom_call" | custom-call | tf_op jit(solution)/shard_map/paths/pallas_call | solution.py:315
  41.0 2.2 %collective-permute-done.13.a3 = f32[128,256]{1,0:T(8,128)S(1)} collective-permute-done((f32[128,256]{1,0:T(8,128)S(1)}, f32[128,256]{1,0:T(8,128)S(1)}, u32[]{:S(2)}, u32[]{:S(2)}) %collective-permute-start.13) | collective-permute-done | bytes 131104 | tf_op jit(solution)/shard_map/ppermute | solution.py:312
  43.2 0.5 %collective-permute-done.12.a2 = f32[128,256]{1,0:T(8,128)S(1)} collective-permute-done((f32[128,256]{1,0:T(8,128)S(1)}, f32[128,256]{1,0:T(8,128)S(1)}, u32[]{:S(2)}, u32[]{:S(2)}) %collective-permute-start.12) | collective-permute-done | bytes 131104 | tf_op jit(solution)/shard_map/ppermute | solution.py:312
  43.7 3.3 %collective-permute-done.11.a1 = f32[128,256]{1,0:T(8,128)S(1)} collective-permute-done((f32[128,256]{1,0:T(8,128)S(1)}, f32[128,256]{1,0:T(8,128)S(1)}, u32[]{:S(2)}, u32[]{:S(2)}) %collective-permute-start.11) | collective-permute-done | bytes 131104 | tf_op jit(solution)/shard_map/ppermute | solution.py:312
  47.0 1.2 %collective-permute-start.17 = (f32[256,256]{1,0:T(8,128)S(1)}, f32[256,256]{1,0:T(8,128)S(1)}, u32[]{:S(2)}, u32[]{:S(2)}) collective-permute-start(f32[256,256]{1,0:T(8,128)S(1)} %join.1.join_ref), channel_id=1, source_target_pairs={{0,32},{32,0},{64,96},{96,64},{128,160},{160,128},{192,224},{224,1... | collective-permute-start | bytes 786440 | tf_op jit(solution)/shard_map/ppermute | solution.py:30
  48.3 0.0 collective-permute-start.14
  48.3 0.5 collective-permute-start.15
  48.8 0.0 collective-permute-start.16
  48.8 0.8 %collective-permute-done.14.b1 = f32[128,256]{1,0:T(8,128)S(1)} collective-permute-done((f32[128,256]{1,0:T(8,128)S(1)}, f32[128,256]{1,0:T(8,128)S(1)}, u32[]{:S(2)}, u32[]{:S(2)}) %collective-permute-start.14) | collective-permute-done | bytes 131104 | tf_op jit(solution)/shard_map/ppermute | solution.py:30
  49.6 0.2 collective-permute-done.15.b2
  49.8 0.3 collective-permute-done.16.b3
  50.1 0.0 collective-permute-done.17.sibling_join_ref
  50.1 0.0 copy-done
  50.1 0.0 copy-done.1
  50.2 1.6 %final.1 = (f32[256,256]{1,0:T(8,128)}, f32[256,256]{1,0:T(8,128)}) custom-call(f32[256,256]{1,0:T(8,128)S(1)} %bitcast.5, f32[256,256]{1,0:T(8,128)S(1)} %bitcast.6, f32[256,256]{1,0:T(8,128)S(1)} %get-tuple-element.31.kernel_ref, f32[256,256]{1,0:T(8,128)S(1)} %get-tuple-element.52.before_ref, f32[256,256]{1,0:T(8,128)S(1)} %get-tuple-element.53.after_ref, ...), custom_call_target="tpu_custom_call" | custom-call | tf_op jit(solution)/shard_map/final/pallas_call | solution.py:319
  (2 shorter events, 0.1 us)
Async XLA Ops:
  1.7 14.5 %collective-permute-start.2 = (f32[128,256]{1,0:T(8,128)S(1)}, f32[128,256]{1,0:T(8,128)S(1)}, u32[]{:S(2)}, u32[]{:S(2)}) collective-permute-start(f32[128,256]{1,0:T(8,128)S(1)} %get-tuple-element.32), channel_id=1, source_target_pairs={{0,3},{1,0},{2,1},{3,2},{4,7},{5,4},{6,5},{7,6},{8,11},{9,8},{10,9... | collective-permute-start | bytes 393224 | tf_op jit(solution)/shard_map/ppermute | solution.py:289
  6.9 11.0 %collective-permute-start.1 = (f32[128,256]{1,0:T(8,128)S(1)}, f32[128,256]{1,0:T(8,128)S(1)}, u32[]{:S(2)}, u32[]{:S(2)}) collective-permute-start(f32[128,256]{1,0:T(8,128)S(1)} %get-tuple-element.32), channel_id=1, source_target_pairs={{0,2},{1,3},{2,0},{3,1},{4,6},{5,7},{6,4},{7,5},{8,10},{9,11},{10,... | collective-permute-start | bytes 393224 | tf_op jit(solution)/shard_map/ppermute | solution.py:289
  6.9 11.0 %collective-permute-start = (f32[128,256]{1,0:T(8,128)S(1)}, f32[128,256]{1,0:T(8,128)S(1)}, u32[]{:S(2)}, u32[]{:S(2)}) collective-permute-start(f32[128,256]{1,0:T(8,128)S(1)} %get-tuple-element.32), channel_id=1, source_target_pairs={{0,1},{1,2},{2,3},{3,0},{4,5},{5,6},{6,7},{7,4},{8,9},{9,10},{10,1... | collective-permute-start | bytes 393224 | tf_op jit(solution)/shard_map/ppermute | solution.py:289
  7.3 42.8 %copy-start = (f32[1,256,256]{2,1,0:T(8,128)S(1)}, f32[1,256,256]{2,1,0:T(8,128)}, u32[]{:S(2)}) copy-start(f32[1,256,256]{2,1,0:T(8,128)} %param.6) | copy-start | bytes 786436
  7.3 42.8 %copy-start.1 = (f32[1,256,256]{2,1,0:T(8,128)S(1)}, f32[1,256,256]{2,1,0:T(8,128)}, u32[]{:S(2)}) copy-start(f32[1,256,256]{2,1,0:T(8,128)} %param.7) | copy-start | bytes 786436
  18.0 2.1 %collective-permute-start.3 = (f32[128,256]{1,0:T(8,128)S(1)}, f32[128,256]{1,0:T(8,128)S(1)}, u32[]{:S(2)}, u32[]{:S(2)}) collective-permute-start(f32[128,256]{1,0:T(8,128)S(1)} %collective-permute-done.a1), channel_id=1, source_target_pairs={{0,32},{32,0},{64,96},{96,64},{128,160},{160,128},{192,224},{224,1... | collective-permute-start | bytes 393224 | tf_op jit(solution)/shard_map/ppermute | solution.py:30
  19.1 1.3 %collective-permute-start.4 = (f32[128,256]{1,0:T(8,128)S(1)}, f32[128,256]{1,0:T(8,128)S(1)}, u32[]{:S(2)}, u32[]{:S(2)}) collective-permute-start(f32[128,256]{1,0:T(8,128)S(1)} %collective-permute-done.1.a2), channel_id=1, source_target_pairs={{0,32},{32,0},{64,96},{96,64},{128,160},{160,128},{192,224},{224,1... | collective-permute-start | bytes 393224 | tf_op jit(solution)/shard_map/ppermute | solution.py:30
  19.1 1.5 %collective-permute-start.5 = (f32[128,256]{1,0:T(8,128)S(1)}, f32[128,256]{1,0:T(8,128)S(1)}, u32[]{:S(2)}, u32[]{:S(2)}) collective-permute-start(f32[128,256]{1,0:T(8,128)S(1)} %collective-permute-done.2.a3), channel_id=1, source_target_pairs={{0,32},{32,0},{64,96},{96,64},{128,160},{160,128},{192,224},{224,1... | collective-permute-start | bytes 393224 | tf_op jit(solution)/shard_map/ppermute | solution.py:30
  21.7 3.2 %collective-permute-start.7 = (f32[256,256]{1,0:T(8,128)S(1)}, f32[256,256]{1,0:T(8,128)S(1)}, u32[]{:S(2)}, u32[]{:S(2)}) collective-permute-start(f32[256,256]{1,0:T(8,128)S(1)} %counts.1.own_ref), channel_id=1, source_target_pairs={{0,32},{32,0},{64,96},{96,64},{128,160},{160,128},{192,224},{224,1... | collective-permute-start | bytes 786440 | tf_op jit(solution)/shard_map/ppermute | solution.py:30
  22.1 9.2 %collective-permute-start.6 = (f32[128,256]{1,0:T(8,128)S(1)}, f32[128,256]{1,0:T(8,128)S(1)}, u32[]{:S(2)}, u32[]{:S(2)}) collective-permute-start(f32[128,256]{1,0:T(8,128)S(1)} %get-tuple-element.38), channel_id=1, source_target_pairs={{0,7},{1,6},{2,5},{3,4},{4,3},{5,2},{6,1},{7,0},{8,15},{9,14},{10,... | collective-permute-start | bytes 393224 | tf_op jit(solution)/shard_map/ppermute | solution.py:297
  24.9 6.4 %collective-permute-start.8 = (f32[128,256]{1,0:T(8,128)S(1)}, f32[128,256]{1,0:T(8,128)S(1)}, u32[]{:S(2)}, u32[]{:S(2)}) collective-permute-start(f32[128,256]{1,0:T(8,128)S(1)} %get-tuple-element.42), channel_id=1, source_target_pairs={{0,128},{1,129},{2,130},{3,131},{4,132},{5,133},{6,134},{7,135},{8... | collective-permute-start | bytes 393224 | tf_op jit(solution)/shard_map/ppermute | solution.py:266
  27.8 7.2 %collective-permute-start.10 = (f32[256,256]{1,0:T(8,128)S(1)}, f32[256,256]{1,0:T(8,128)S(1)}, u32[]{:S(2)}, u32[]{:S(2)}) collective-permute-start(f32[256,256]{1,0:T(8,128)S(1)} %get-tuple-element.44.chip_ref), channel_id=1, source_target_pairs={{0,64},{1,65},{2,66},{3,67},{4,68},{5,69},{6,70},{7,71},{8,72},{9,... | collective-permute-start | bytes 786440 | tf_op jit(solution)/shard_map/ppermute | solution.py:265
  31.3 3.6 %collective-permute-start.9 = (f32[128,256]{1,0:T(8,128)S(1)}, f32[128,256]{1,0:T(8,128)S(1)}, u32[]{:S(2)}, u32[]{:S(2)}) collective-permute-start(f32[128,256]{1,0:T(8,128)S(1)} %collective-permute-done.6.own_ref), channel_id=1, source_target_pairs={{0,32},{32,0},{64,96},{96,64},{128,160},{160,128},{192,224},{224,1... | collective-permute-start | bytes 393224 | tf_op jit(solution)/shard_map/ppermute | solution.py:30
  35.2 8.0 %collective-permute-start.13 = (f32[128,256]{1,0:T(8,128)S(1)}, f32[128,256]{1,0:T(8,128)S(1)}, u32[]{:S(2)}, u32[]{:S(2)}) collective-permute-start(f32[128,256]{1,0:T(8,128)S(1)} %get-tuple-element.46), channel_id=1, source_target_pairs={{0,24},{1,25},{2,26},{3,27},{4,28},{5,29},{6,30},{7,31},{8,0},{9,1... | collective-permute-start | bytes 393224 | tf_op jit(solution)/shard_map/ppermute | solution.py:312
  38.3 5.4 %collective-permute-start.12 = (f32[128,256]{1,0:T(8,128)S(1)}, f32[128,256]{1,0:T(8,128)S(1)}, u32[]{:S(2)}, u32[]{:S(2)}) collective-permute-start(f32[128,256]{1,0:T(8,128)S(1)} %get-tuple-element.46), channel_id=1, source_target_pairs={{0,16},{1,17},{2,18},{3,19},{4,20},{5,21},{6,22},{7,23},{8,24},{9,... | collective-permute-start | bytes 393224 | tf_op jit(solution)/shard_map/ppermute | solution.py:312
  38.3 8.7 %collective-permute-start.11 = (f32[128,256]{1,0:T(8,128)S(1)}, f32[128,256]{1,0:T(8,128)S(1)}, u32[]{:S(2)}, u32[]{:S(2)}) collective-permute-start(f32[128,256]{1,0:T(8,128)S(1)} %get-tuple-element.46), channel_id=1, source_target_pairs={{0,8},{1,9},{2,10},{3,11},{4,12},{5,13},{6,14},{7,15},{8,16},{9,17... | collective-permute-start | bytes 393224 | tf_op jit(solution)/shard_map/ppermute | solution.py:312
  47.0 3.1 %collective-permute-start.17 = (f32[256,256]{1,0:T(8,128)S(1)}, f32[256,256]{1,0:T(8,128)S(1)}, u32[]{:S(2)}, u32[]{:S(2)}) collective-permute-start(f32[256,256]{1,0:T(8,128)S(1)} %join.1.join_ref), channel_id=1, source_target_pairs={{0,32},{32,0},{64,96},{96,64},{128,160},{160,128},{192,224},{224,1... | collective-permute-start | bytes 786440 | tf_op jit(solution)/shard_map/ppermute | solution.py:30
  48.3 1.3 %collective-permute-start.14 = (f32[128,256]{1,0:T(8,128)S(1)}, f32[128,256]{1,0:T(8,128)S(1)}, u32[]{:S(2)}, u32[]{:S(2)}) collective-permute-start(f32[128,256]{1,0:T(8,128)S(1)} %collective-permute-done.11.a1), channel_id=1, source_target_pairs={{0,32},{32,0},{64,96},{96,64},{128,160},{160,128},{192,224},{224,1... | collective-permute-start | bytes 393224 | tf_op jit(solution)/shard_map/ppermute | solution.py:30
  48.3 1.5 %collective-permute-start.15 = (f32[128,256]{1,0:T(8,128)S(1)}, f32[128,256]{1,0:T(8,128)S(1)}, u32[]{:S(2)}, u32[]{:S(2)}) collective-permute-start(f32[128,256]{1,0:T(8,128)S(1)} %collective-permute-done.12.a2), channel_id=1, source_target_pairs={{0,32},{32,0},{64,96},{96,64},{128,160},{160,128},{192,224},{224,1... | collective-permute-start | bytes 393224 | tf_op jit(solution)/shard_map/ppermute | solution.py:30
  48.8 1.3 %collective-permute-start.16 = (f32[128,256]{1,0:T(8,128)S(1)}, f32[128,256]{1,0:T(8,128)S(1)}, u32[]{:S(2)}, u32[]{:S(2)}) collective-permute-start(f32[128,256]{1,0:T(8,128)S(1)} %collective-permute-done.13.a3), channel_id=1, source_target_pairs={{0,32},{32,0},{64,96},{96,64},{128,160},{160,128},{192,224},{224,1... | collective-permute-start | bytes 393224 | tf_op jit(solution)/shard_map/ppermute | solution.py:30

commit v9 on v5

--- a/solution.py
+++ b/solution.py
@@ -86,11 +86,10 @@
 
 
 def put_others(stack_ref, mine, near, near_sibling, far, far_sibling, core):
-    count = stack_ref.shape[0]
     half = far.shape[0]
-    before, after, across = (lax.rem(mine + count + move, count) for move in (-1, 1, 2))
-    stack_ref[jnp.where(core == 0, before, after)] = near[...]
-    stack_ref[jnp.where(core == 0, after, before)] = near_sibling[...]
+    across = mine ^ 2
+    stack_ref[mine ^ (1 + 2 * core)] = near[...]
+    stack_ref[mine ^ (3 - 2 * core)] = near_sibling[...]
     stack_ref[across, pl.ds(core * half, half), :] = far[...]
     stack_ref[across, pl.ds((1 - core) * half, half), :] = far_sibling[...]
 
@@ -321,7 +320,7 @@
     near, far = exchange(
         kernel,
         half_of_kernel,
-        lambda x, c, y, z: (x, y, z // QUAD * QUAD + (z + 1 - 2 * c) % QUAD),
+        lambda x, c, y, z: (x, y, z ^ (1 + 2 * c)),
         lambda x, y, z: (x, y, z ^ 2),
     )
     counts = count_pairs(order, table_rows, size)
@@ -332,8 +331,8 @@
     near, far = exchange(
         quad_product,
         half_product,
-        lambda x, c, y, z: (x, y ^ 1, z) if c else (x, y, Z - 1 - z),
-        lambda x, y, z: (x, y ^ 1, Z - 1 - z),
+        lambda x, c, y, z: (x, y ^ 1, z) if c else (x, y, z ^ 6),
+        lambda x, y, z: (x, y ^ 1, z ^ 6),
     )
     counts, quad = lax.optimization_barrier((counts, quad))
     chip_counts, half_counts = call(chip_kernel, out_shape=(whole, half), name="chip")(
@@ -342,7 +341,7 @@
     near_counts, far_counts = exchange(
         chip_counts,
         half_counts,
-        lambda x, c, y, z: ((x + 1 - 2 * c) % 4, y, z),
+        lambda x, c, y, z: (x ^ (1 + 2 * c), y, z),
         lambda x, y, z: (x ^ 2, y, z),
     )
     near, far, far_counts = lax.optimization_barrier((near, far, far_counts))

time: 48.7 us -> 46.5 us (0.955)
  starting transfers between devices: 23.8 us -> 20.9 us
  waiting for transfers between devices: 9.14 us -> 9.73 us
    ppermute x3, starting transfers between devices: 8.61 us -> 6.31 us  [exchange(): lax.ppermute(half, axes, everywhere(lambda x, c, y, z: far_step(x, y, z)))]
    ppermute x6, starting transfers between devices: 4.8 us -> 4.11 us  [other_core(): return lax.ppermute(value, 'dp', along_dp(lambda x, c: (x, 1 - c)))]
    ppermute x3, waiting for transfers between devices: 6.65 us -> 7.24 us  [exchange(): lax.ppermute(half, axes, everywhere(lambda x, c, y, z: far_step(x, y, z)))]
  transfers between devices with their start and end apart: 13 -> 13, of which waited for: 4 -> 4; matrix products, arithmetic and copies ran while one was open for 0% -> 0% of each run, Pallas kernels for 24% -> 25%
where the time goes in v9:
time: 46.5 us; the launch traced here: 46.2 us
  starting transfers between devices  20.9 us (45%)
  Pallas kernels  14.9 us (32%)
  waiting for transfers between devices  9.73 us (21%)
  between operations  0.72 us (2%)
    pallas_call x1, Pallas kernels, count_pairs(): pl.pallas_call(functools.partial(count_kernel, part), out_shape=shape(siz...  8.57 us
    ppermute x3, starting transfers between devices, exchange(): lax.ppermute(whole, axes, everywhere(near_step))  7.42 us
    ppermute x3, waiting for transfers between devices, exchange(): lax.ppermute(half, axes, everywhere(lambda x, c, y, z: far_step(x, y, z)))  7.24 us
    ppermute x3, starting transfers between devices, exchange(): lax.ppermute(half, axes, everywhere(lambda x, c, y, z: far_step(x, y, z)))  6.31 us
    ppermute x6, starting transfers between devices, other_core(): return lax.ppermute(value, 'dp', along_dp(lambda x, c: (x, 1 - c)))  4.11 us
    ppermute x1, starting transfers between devices, per_device(): lax.ppermute(message, 'clique', along_clique(lambda y, z: (y ^ 2, z)))  3.02 us
    ppermute x6, waiting for transfers between devices, other_core(): return lax.ppermute(value, 'dp', along_dp(lambda x, c: (x, 1 - c)))  2.48 us
    pallas_call x1, Pallas kernels, per_device(): call(sides_kernel, out_shape=(whole, shape(8, size)), name='sides')  2.48 us
  transfers between devices with their start and end apart: 13, of which 4 were waited for; matrix products, arithmetic and copies ran while one was open for 0% of the time, Pallas kernels for 25%

profile of v9, /device:TPU:1, one launch (start us, length us, event | category | flops | bytes accessed | tf_op | source)
XLA Modules:
  0.0 46.2 jit_solution(1516394245261765369)
XLA Ops:
  0.6 1.1 %read.1 = (s32[33]{0:T(128)S(1)}, f32[256,256]{1,0:T(8,128)S(1)}, f32[128,256]{1,0:T(8,128)S(1)}) custom-call(s32[33]{0:T(128)} %order_hbm.1, f32[256,256]{1,0:T(8,128)} %bitcast.4), custom_call_target="tpu_custom_call" | custom-call | tf_op jit(solution)/shard_map/read/pallas_call | solution.py:309
  1.7 5.3 %collective-permute-start = (f32[256,256]{1,0:T(8,128)S(1)}, f32[256,256]{1,0:T(8,128)S(1)}, u32[]{:S(2)}, u32[]{:S(2)}) collective-permute-start(f32[256,256]{1,0:T(8,128)S(1)} %get-tuple-element.27.kernel_ref), channel_id=1, source_target_pairs={{0,1},{1,0},{2,3},{3,2},{4,5},{5,4},{6,7},{7,6},{8,9},{9,8},{10,11... | collective-permute-start | bytes 786440 | tf_op jit(solution)/shard_map/ppermute | solution.py:297
  7.0 0.0 collective-permute-start.1
  7.0 0.0 copy-start
  7.0 0.0 copy-start.1
  7.0 8.6 %counts.1.own_ref = f32[256,256]{1,0:T(8,128)S(1)} custom-call(s32[33]{0:T(128)S(1)} %get-tuple-element.29.order_ref, s32[33,65536]{1,0:T(8,128)} %right_ref.1, s32[33,65536]{1,0:T(8,128)} %right_ref.1), custom_call_target="tpu_custom_call" | custom-call | tf_op jit(solution)/shard_map/counts/pallas_call | solution.py:268
  15.5 2.2 %collective-permute-done.1.far = f32[128,256]{1,0:T(8,128)S(1)} collective-permute-done((f32[128,256]{1,0:T(8,128)S(1)}, f32[128,256]{1,0:T(8,128)S(1)}, u32[]{:S(2)}, u32[]{:S(2)}) %collective-permute-start.1) | collective-permute-done | bytes 131104 | tf_op jit(solution)/shard_map/ppermute | solution.py:298
  17.8 0.0 collective-permute-done.near
  17.8 0.0 collective-permute-start.2
  17.8 0.5 %collective-permute-start.3 = (f32[128,256]{1,0:T(8,128)S(1)}, f32[128,256]{1,0:T(8,128)S(1)}, u32[]{:S(2)}, u32[]{:S(2)}) collective-permute-start(f32[128,256]{1,0:T(8,128)S(1)} %collective-permute-done.1.far), channel_id=1, source_target_pairs={{0,32},{32,0},{64,96},{96,64},{128,160},{160,128},{192,224},{224,1... | collective-permute-start | bytes 393224 | tf_op jit(solution)/shard_map/ppermute | solution.py:30
  18.3 1.2 %collective-permute-done.3.far_sibling = f32[128,256]{1,0:T(8,128)S(1)} collective-permute-done((f32[128,256]{1,0:T(8,128)S(1)}, f32[128,256]{1,0:T(8,128)S(1)}, u32[]{:S(2)}, u32[]{:S(2)}) %collective-permute-start.3) | collective-permute-done | bytes 131104 | tf_op jit(solution)/shard_map/ppermute | solution.py:30
  19.5 0.0 collective-permute-done.2.near_sibling
  19.5 1.0 %quad.1 = (f32[4,256,256]{2,1,0:T(8,128)S(1)}, f32[256,256]{1,0:T(8,128)S(1)}, f32[128,256]{1,0:T(8,128)S(1)}) custom-call(f32[256,256]{1,0:T(8,128)S(1)} %get-tuple-element.27.kernel_ref, f32[256,256]{1,0:T(8,128)S(1)} %collective-permute-done.near, f32[256,256]{1,0:T(8,128)S(1)} %collective-permute-done.2.near_sibling, ...), custom_call_target="tpu_custom_call" | custom-call | tf_op jit(solution)/shard_map/quad/pallas_call | solution.py:328
  20.5 0.2 collective-permute-start.6
  20.7 1.3 %collective-permute-start.4 = (f32[256,256]{1,0:T(8,128)S(1)}, f32[256,256]{1,0:T(8,128)S(1)}, u32[]{:S(2)}, u32[]{:S(2)}) collective-permute-start(f32[256,256]{1,0:T(8,128)S(1)} %get-tuple-element.35.product_ref), channel_id=1, source_target_pairs={{0,6},{1,7},{2,4},{3,5},{4,2},{5,3},{6,0},{7,1},{8,14},{9,15},{10,... | collective-permute-start | bytes 786440 | tf_op jit(solution)/shard_map/ppermute | solution.py:297
  22.0 3.5 %collective-permute-start.5 = (f32[128,256]{1,0:T(8,128)S(1)}, f32[128,256]{1,0:T(8,128)S(1)}, u32[]{:S(2)}, u32[]{:S(2)}) collective-permute-start(f32[128,256]{1,0:T(8,128)S(1)} %get-tuple-element.36), channel_id=1, source_target_pairs={{0,14},{1,15},{2,12},{3,13},{4,10},{5,11},{6,8},{7,9},{8,6},{9,7},... | collective-permute-start | bytes 393224 | tf_op jit(solution)/shard_map/ppermute | solution.py:298
  25.5 0.0 collective-permute-done.6.sibling_ref
  25.6 2.8 %collective-permute-start.7 = (f32[128,256]{1,0:T(8,128)S(1)}, f32[128,256]{1,0:T(8,128)S(1)}, u32[]{:S(2)}, u32[]{:S(2)}) collective-permute-start(f32[128,256]{1,0:T(8,128)S(1)} %get-tuple-element.38), channel_id=1, source_target_pairs={{0,128},{1,129},{2,130},{3,131},{4,132},{5,133},{6,134},{7,135},{8... | collective-permute-start | bytes 393224 | tf_op jit(solution)/shard_map/ppermute | solution.py:298
  28.4 0.9 %collective-permute-start.10 = (f32[256,256]{1,0:T(8,128)S(1)}, f32[256,256]{1,0:T(8,128)S(1)}, u32[]{:S(2)}, u32[]{:S(2)}) collective-permute-start(f32[256,256]{1,0:T(8,128)S(1)} %get-tuple-element.41.chip_ref), channel_id=1, source_target_pairs={{0,64},{1,65},{2,66},{3,67},{4,68},{5,69},{6,70},{7,71},{8,72},{9,... | collective-permute-start | bytes 786440 | tf_op jit(solution)/shard_map/ppermute | solution.py:297
  29.3 5.0 %collective-permute-done.5.far = f32[128,256]{1,0:T(8,128)S(1)} collective-permute-done((f32[128,256]{1,0:T(8,128)S(1)}, f32[128,256]{1,0:T(8,128)S(1)}, u32[]{:S(2)}, u32[]{:S(2)}) %collective-permute-start.5) | collective-permute-done | bytes 131104 | tf_op jit(solution)/shard_map/ppermute | solution.py:298
  34.3 0.0 collective-permute-done.4.near
  34.3 0.0 collective-permute-done.7.far_ref
  34.3 2.8 %collective-permute-start.8 = (f32[256,256]{1,0:T(8,128)S(1)}, f32[256,256]{1,0:T(8,128)S(1)}, u32[]{:S(2)}, u32[]{:S(2)}) collective-permute-start(f32[256,256]{1,0:T(8,128)S(1)} %collective-permute-done.4.near), channel_id=1, source_target_pairs={{0,32},{32,0},{64,96},{96,64},{128,160},{160,128},{192,224},{224,1... | collective-permute-start | bytes 786440 | tf_op jit(solution)/shard_map/ppermute | solution.py:30
  37.1 0.1 collective-permute-start.9
  37.2 1.3 %collective-permute-done.9.far_sibling = f32[128,256]{1,0:T(8,128)S(1)} collective-permute-done((f32[128,256]{1,0:T(8,128)S(1)}, f32[128,256]{1,0:T(8,128)S(1)}, u32[]{:S(2)}, u32[]{:S(2)}) %collective-permute-start.9) | collective-permute-done | bytes 131104 | tf_op jit(solution)/shard_map/ppermute | solution.py:30
  38.4 0.0 collective-permute-done.10.near_ref
  38.4 0.0 collective-permute-done.8.near_sibling
  38.5 0.5 collective-permute-start.12
  38.9 0.6 %block.1 = (f32[4,256,256]{2,1,0:T(8,128)S(1)}, f32[8,256]{1,0:T(8,128)S(1)}) custom-call(f32[256,256]{1,0:T(8,128)S(1)} %get-tuple-element.35.product_ref, f32[256,256]{1,0:T(8,128)S(1)} %collective-permute-done.4.near, f32[256,256]{1,0:T(8,128)S(1)} %collective-permute-done.8.near_sibling, f32[128,256]{1,0:T(8,128)S(1)} %collective-permute-done.5.far, ...), custom_call_target="tpu_custom_call" | custom-call | tf_op jit(solution)/shard_map/block/pallas_call | solution.py:352
  39.5 3.0 %collective-permute-start.11 = (f32[8,256]{1,0:T(8,128)S(1)}, f32[8,256]{1,0:T(8,128)S(1)}, u32[]{:S(2)}, u32[]{:S(2)}) collective-permute-start(f32[8,256]{1,0:T(8,128)S(1)} %get-tuple-element.47), channel_id=1, source_target_pairs={{0,16},{1,17},{2,18},{3,19},{4,20},{5,21},{6,22},{7,23},{8,24},{9,... | collective-permute-start | bytes 24584 | tf_op jit(solution)/shard_map/ppermute | solution.py:356
  42.5 2.5 %sides.1 = (f32[256,256]{1,0:T(8,128)S(1)}, f32[8,256]{1,0:T(8,128)S(1)}) custom-call(f32[4,256,256]{2,1,0:T(8,128)S(1)} %get-tuple-element.34.quad_ref, f32[4,256,256]{2,1,0:T(8,128)S(1)} %get-tuple-element.44.block_ref), custom_call_target="tpu_custom_call" | custom-call | tf_op jit(solution)/shard_map/sides/pallas_call | solution.py:357
  45.0 0.0 collective-permute-done.11.message_ref
  45.0 0.0 collective-permute-done.12.sibling_join_ref
  45.0 0.0 copy-done
  45.1 0.0 copy-done.1
  45.1 1.2 %final.1 = (f32[256,256]{1,0:T(8,128)}, f32[256,256]{1,0:T(8,128)}) custom-call(f32[256,256]{1,0:T(8,128)S(1)} %bitcast.5, f32[256,256]{1,0:T(8,128)S(1)} %bitcast.6, f32[256,256]{1,0:T(8,128)S(1)} %get-tuple-element.27.kernel_ref, f32[256,256]{1,0:T(8,128)S(1)} %get-tuple-element.45.path_ref, f32[8,256]{1,0:T(8,128)S(1)} %get-tuple-element.46.known_ref, ...), custom_call_target="tpu_custom_call" | custom-call | tf_op jit(solution)/shard_map/final/pallas_call | solution.py:359
  (2 shorter events, 0.1 us)
Async XLA Ops:
  1.7 16.1 %collective-permute-start = (f32[256,256]{1,0:T(8,128)S(1)}, f32[256,256]{1,0:T(8,128)S(1)}, u32[]{:S(2)}, u32[]{:S(2)}) collective-permute-start(f32[256,256]{1,0:T(8,128)S(1)} %get-tuple-element.27.kernel_ref), channel_id=1, source_target_pairs={{0,1},{1,0},{2,3},{3,2},{4,5},{5,4},{6,7},{7,6},{8,9},{9,8},{10,11... | collective-permute-start | bytes 786440 | tf_op jit(solution)/shard_map/ppermute | solution.py:297
  7.0 10.8 %collective-permute-start.1 = (f32[128,256]{1,0:T(8,128)S(1)}, f32[128,256]{1,0:T(8,128)S(1)}, u32[]{:S(2)}, u32[]{:S(2)}) collective-permute-start(f32[128,256]{1,0:T(8,128)S(1)} %get-tuple-element.28), channel_id=1, source_target_pairs={{0,2},{1,3},{2,0},{3,1},{4,6},{5,7},{6,4},{7,5},{8,10},{9,11},{10,... | collective-permute-start | bytes 393224 | tf_op jit(solution)/shard_map/ppermute | solution.py:298
  7.0 38.1 %copy-start = (f32[1,256,256]{2,1,0:T(8,128)S(1)}, f32[1,256,256]{2,1,0:T(8,128)}, u32[]{:S(2)}) copy-start(f32[1,256,256]{2,1,0:T(8,128)} %param.6) | copy-start | bytes 786436
  7.0 38.1 %copy-start.1 = (f32[1,256,256]{2,1,0:T(8,128)S(1)}, f32[1,256,256]{2,1,0:T(8,128)}, u32[]{:S(2)}) copy-start(f32[1,256,256]{2,1,0:T(8,128)} %param.7) | copy-start | bytes 786436
  17.8 1.7 %collective-permute-start.2 = (f32[256,256]{1,0:T(8,128)S(1)}, f32[256,256]{1,0:T(8,128)S(1)}, u32[]{:S(2)}, u32[]{:S(2)}) collective-permute-start(f32[256,256]{1,0:T(8,128)S(1)} %collective-permute-done.near), channel_id=1, source_target_pairs={{0,32},{32,0},{64,96},{96,64},{128,160},{160,128},{192,224},{224,1... | collective-permute-start | bytes 786440 | tf_op jit(solution)/shard_map/ppermute | solution.py:30
  17.8 1.7 %collective-permute-start.3 = (f32[128,256]{1,0:T(8,128)S(1)}, f32[128,256]{1,0:T(8,128)S(1)}, u32[]{:S(2)}, u32[]{:S(2)}) collective-permute-start(f32[128,256]{1,0:T(8,128)S(1)} %collective-permute-done.1.far), channel_id=1, source_target_pairs={{0,32},{32,0},{64,96},{96,64},{128,160},{160,128},{192,224},{224,1... | collective-permute-start | bytes 393224 | tf_op jit(solution)/shard_map/ppermute | solution.py:30
  20.5 5.0 %collective-permute-start.6 = (f32[256,256]{1,0:T(8,128)S(1)}, f32[256,256]{1,0:T(8,128)S(1)}, u32[]{:S(2)}, u32[]{:S(2)}) collective-permute-start(f32[256,256]{1,0:T(8,128)S(1)} %counts.1.own_ref), channel_id=1, source_target_pairs={{0,32},{32,0},{64,96},{96,64},{128,160},{160,128},{192,224},{224,1... | collective-permute-start | bytes 786440 | tf_op jit(solution)/shard_map/ppermute | solution.py:30
  20.7 13.5 %collective-permute-start.4 = (f32[256,256]{1,0:T(8,128)S(1)}, f32[256,256]{1,0:T(8,128)S(1)}, u32[]{:S(2)}, u32[]{:S(2)}) collective-permute-start(f32[256,256]{1,0:T(8,128)S(1)} %get-tuple-element.35.product_ref), channel_id=1, source_target_pairs={{0,6},{1,7},{2,4},{3,5},{4,2},{5,3},{6,0},{7,1},{8,14},{9,15},{10,... | collective-permute-start | bytes 786440 | tf_op jit(solution)/shard_map/ppermute | solution.py:297
  22.0 12.2 %collective-permute-start.5 = (f32[128,256]{1,0:T(8,128)S(1)}, f32[128,256]{1,0:T(8,128)S(1)}, u32[]{:S(2)}, u32[]{:S(2)}) collective-permute-start(f32[128,256]{1,0:T(8,128)S(1)} %get-tuple-element.36), channel_id=1, source_target_pairs={{0,14},{1,15},{2,12},{3,13},{4,10},{5,11},{6,8},{7,9},{8,6},{9,7},... | collective-permute-start | bytes 393224 | tf_op jit(solution)/shard_map/ppermute | solution.py:298
  25.6 8.7 %collective-permute-start.7 = (f32[128,256]{1,0:T(8,128)S(1)}, f32[128,256]{1,0:T(8,128)S(1)}, u32[]{:S(2)}, u32[]{:S(2)}) collective-permute-start(f32[128,256]{1,0:T(8,128)S(1)} %get-tuple-element.38), channel_id=1, source_target_pairs={{0,128},{1,129},{2,130},{3,131},{4,132},{5,133},{6,134},{7,135},{8... | collective-permute-start | bytes 393224 | tf_op jit(solution)/shard_map/ppermute | solution.py:298
  28.4 10.0 %collective-permute-start.10 = (f32[256,256]{1,0:T(8,128)S(1)}, f32[256,256]{1,0:T(8,128)S(1)}, u32[]{:S(2)}, u32[]{:S(2)}) collective-permute-start(f32[256,256]{1,0:T(8,128)S(1)} %get-tuple-element.41.chip_ref), channel_id=1, source_target_pairs={{0,64},{1,65},{2,66},{3,67},{4,68},{5,69},{6,70},{7,71},{8,72},{9,... | collective-permute-start | bytes 786440 | tf_op jit(solution)/shard_map/ppermute | solution.py:297
  34.3 4.2 %collective-permute-start.8 = (f32[256,256]{1,0:T(8,128)S(1)}, f32[256,256]{1,0:T(8,128)S(1)}, u32[]{:S(2)}, u32[]{:S(2)}) collective-permute-start(f32[256,256]{1,0:T(8,128)S(1)} %collective-permute-done.4.near), channel_id=1, source_target_pairs={{0,32},{32,0},{64,96},{96,64},{128,160},{160,128},{192,224},{224,1... | collective-permute-start | bytes 786440 | tf_op jit(solution)/shard_map/ppermute | solution.py:30
  37.1 1.3 %collective-permute-start.9 = (f32[128,256]{1,0:T(8,128)S(1)}, f32[128,256]{1,0:T(8,128)S(1)}, u32[]{:S(2)}, u32[]{:S(2)}) collective-permute-start(f32[128,256]{1,0:T(8,128)S(1)} %collective-permute-done.5.far), channel_id=1, source_target_pairs={{0,32},{32,0},{64,96},{96,64},{128,160},{160,128},{192,224},{224,1... | collective-permute-start | bytes 393224 | tf_op jit(solution)/shard_map/ppermute | solution.py:30
  38.5 6.6 %collective-permute-start.12 = (f32[256,256]{1,0:T(8,128)S(1)}, f32[256,256]{1,0:T(8,128)S(1)}, u32[]{:S(2)}, u32[]{:S(2)}) collective-permute-start(f32[256,256]{1,0:T(8,128)S(1)} %join.1.join_ref), channel_id=1, source_target_pairs={{0,32},{32,0},{64,96},{96,64},{128,160},{160,128},{192,224},{224,1... | collective-permute-start | bytes 786440 | tf_op jit(solution)/shard_map/ppermute | solution.py:30
  39.5 5.5 %collective-permute-start.11 = (f32[8,256]{1,0:T(8,128)S(1)}, f32[8,256]{1,0:T(8,128)S(1)}, u32[]{:S(2)}, u32[]{:S(2)}) collective-permute-start(f32[8,256]{1,0:T(8,128)S(1)} %get-tuple-element.47), channel_id=1, source_target_pairs={{0,16},{1,17},{2,18},{3,19},{4,20},{5,21},{6,22},{7,23},{8,24},{9,... | collective-permute-start | bytes 24584 | tf_op jit(solution)/shard_map/ppermute | solution.py:356

commit v10 on v9

--- a/solution.py
+++ b/solution.py
@@ -94,10 +94,10 @@
     stack_ref[across, pl.ds((1 - core) * half, half), :] = far_sibling[...]
 
 
-def quad_kernel(kernel_ref, near, near_sibling, far, far_sibling, quad_ref, product_ref, half_ref):
+def quad_kernel(kernel_ref, near, near_sibling, far, far_sibling, quad_ref, product_ref):
     core, _, z = place()
     mine = lax.rem(z, QUAD)
-    half, size = half_ref.shape
+    size = product_ref.shape[0]
     quad_ref[mine] = kernel_ref[...]
     put_others(quad_ref, mine, near, near_sibling, far, far_sibling, core)
     scale = 1.0 / size
@@ -106,7 +106,6 @@
     whole = product(left, right) * scale
     largest = jnp.max(jnp.max(whole, axis=0, keepdims=True), axis=1, keepdims=True)
     product_ref[...] = whole / largest
-    half_ref[...] = product_ref[pl.ds(core * half, half), :]
 
 
 def spots():
@@ -175,6 +174,12 @@
         row = lax.fori_loop(0, in_block, lambda i, row: row_times(row, block_ref[i], eye), ones)
         row = lax.fori_loop(0, mine, lambda i, row: row_times(row, quad_ref[i], eye), row)
         known_ref[...] = jnp.broadcast_to(row, known_ref.shape)
+
+
+def relay_kernel(whole_ref, half_ref):
+    core, _, _ = place()
+    half = half_ref.shape[0]
+    half_ref[...] = whole_ref[pl.ds(core * half, half), :]
 
 
 def chip_kernel(own_ref, sibling_ref, both_ref, half_ref):
@@ -325,14 +330,14 @@
     )
     counts = count_pairs(order, table_rows, size)
     near, far, counts = lax.optimization_barrier((near, far, counts))
-    quad, quad_product, half_product = call(
-        quad_kernel, out_shape=(shape(QUAD, size, size), whole, half), name="quad"
+    quad, quad_product = call(
+        quad_kernel, out_shape=(shape(QUAD, size, size), whole), name="quad"
     )(kernel, near, other_core(near), far, other_core(far))
-    near, far = exchange(
+    axes = ("dp", "clique")
+    near = lax.ppermute(
         quad_product,
-        half_product,
-        lambda x, c, y, z: (x, y ^ 1, z) if c else (x, y, z ^ 6),
-        lambda x, y, z: (x, y ^ 1, z ^ 6),
+        axes,
+        everywhere(lambda x, c, y, z: (x, y ^ 1, z) if c else (x, y, z ^ 6)),
     )
     counts, quad = lax.optimization_barrier((counts, quad))
     chip_counts, half_counts = call(chip_kernel, out_shape=(whole, half), name="chip")(
@@ -344,11 +349,16 @@
         lambda x, c, y, z: (x ^ (1 + 2 * c), y, z),
         lambda x, y, z: (x ^ 2, y, z),
     )
-    near, far, far_counts = lax.optimization_barrier((near, far, far_counts))
-    near_sibling, far_sibling = (other_core(near), other_core(far))
-    near_sibling, far_sibling, near_counts = lax.optimization_barrier(
-        (near_sibling, far_sibling, near_counts)
-    )
+    near, far_counts = lax.optimization_barrier((near, far_counts))
+    half_near = call(relay_kernel, out_shape=half, name="relay")(near)
+    far = lax.ppermute(
+        half_near,
+        axes,
+        everywhere(lambda x, c, y, z: (x, y, z ^ 6) if c else (x, y ^ 1, z)),
+    )
+    near_sibling = other_core(near)
+    far, near_sibling, near_counts = lax.optimization_barrier((far, near_sibling, near_counts))
+    far_sibling = other_core(far)
     block, message = call(
         block_kernel, out_shape=(shape(4, size, size), shape(8, size)), name="block"
     )(quad_product, near, near_sibling, far, far_sibling)

time: 46.5 us -> 47.8 us (1.028)
  starting transfers between devices: 20.9 us -> 22.6 us
  waiting for transfers between devices: 9.73 us -> 9.17 us
    ppermute x0 -> x2, starting transfers between devices: none -> 5.66 us  [the longest x1 4.36 us: per_device(): lax.ppermute(half_near, axes, everywhere(lambda x, c, y, z: (x, y, z ^ 6)...]
    ppermute x3 -> x2, starting transfers between devices: 6.31 us -> 2.84 us  [exchange(): lax.ppermute(half, axes, everywhere(lambda x, c, y, z: far_step(x, y, z)))]
    ppermute x3 -> x2, waiting for transfers between devices: 7.24 us -> 3.88 us  [exchange(): lax.ppermute(half, axes, everywhere(lambda x, c, y, z: far_step(x, y, z)))]
    ppermute x0 -> x2, waiting for transfers between devices: none -> 2.75 us  [the longest x1 2.66 us: per_device(): lax.ppermute(half_near, axes, everywhere(lambda x, c, y, z: (x, y, z ^ 6)...]
    ppermute x3 -> x2, starting transfers between devices: 7.42 us -> 6.12 us  [exchange(): lax.ppermute(whole, axes, everywhere(near_step))]
    ppermute x6, starting transfers between devices: 4.11 us -> 4.92 us  [other_core(): return lax.ppermute(value, 'dp', along_dp(lambda x, c: (x, 1 - c)))]
    pallas_call x1 -> x2, Pallas kernels: 1 us -> 1 us  [the longest x1 0.99 us: per_device(): call(quad_kernel, out_shape=(shape(QUAD, size, size), whole), name='quad')]
  transfers between devices with their start and end apart: 13 -> 13, of which waited for: 4 -> 7; matrix products, arithmetic and copies ran while one was open for 0% -> 0% of each run, Pallas kernels for 25% -> 25%
where the time goes in v10:
time: 47.8 us; the launch traced here: 47.7 us
  starting transfers between devices  22.6 us (47%)
  Pallas kernels  15.2 us (32%)
  waiting for transfers between devices  9.17 us (19%)
  between operations  0.73 us (2%)
    pallas_call x1, Pallas kernels, count_pairs(): pl.pallas_call(functools.partial(count_kernel, part), out_shape=shape(siz...  8.86 us
    ppermute x2, starting transfers between devices, exchange(): lax.ppermute(whole, axes, everywhere(near_step))  6.12 us
    ppermute x6, starting transfers between devices, other_core(): return lax.ppermute(value, 'dp', along_dp(lambda x, c: (x, 1 - c)))  4.92 us
    ppermute x1, starting transfers between devices, per_device(): lax.ppermute(half_near, axes, everywhere(lambda x, c, y, z: (x, y, z ^ 6)...  4.36 us
    ppermute x2, waiting for transfers between devices, exchange(): lax.ppermute(half, axes, everywhere(lambda x, c, y, z: far_step(x, y, z)))  3.88 us
    ppermute x1, starting transfers between devices, per_device(): lax.ppermute(message, 'clique', along_clique(lambda y, z: (y ^ 2, z)))  3.02 us
    ppermute x2, starting transfers between devices, exchange(): lax.ppermute(half, axes, everywhere(lambda x, c, y, z: far_step(x, y, z)))  2.84 us
    ppermute x1, waiting for transfers between devices, per_device(): lax.ppermute(half_near, axes, everywhere(lambda x, c, y, z: (x, y, z ^ 6)...  2.66 us
  transfers between devices with their start and end apart: 13, of which 7 were waited for; matrix products, arithmetic and copies ran while one was open for 0% of the time, Pallas kernels for 25%

profile of v10, /device:TPU:1, one launch (start us, length us, event | category | flops | bytes accessed | tf_op | source)
XLA Modules:
  0.0 47.7 jit_solution(4949564954353900826)
XLA Ops:
  0.6 1.1 %read.1 = (s32[33]{0:T(128)S(1)}, f32[256,256]{1,0:T(8,128)S(1)}, f32[128,256]{1,0:T(8,128)S(1)}) custom-call(s32[33]{0:T(128)} %order_hbm.1, f32[256,256]{1,0:T(8,128)} %bitcast.4), custom_call_target="tpu_custom_call" | custom-call | tf_op jit(solution)/shard_map/read/pallas_call | solution.py:314
  1.7 5.3 %collective-permute-start = (f32[256,256]{1,0:T(8,128)S(1)}, f32[256,256]{1,0:T(8,128)S(1)}, u32[]{:S(2)}, u32[]{:S(2)}) collective-permute-start(f32[256,256]{1,0:T(8,128)S(1)} %get-tuple-element.25.kernel_ref), channel_id=1, source_target_pairs={{0,1},{1,0},{2,3},{3,2},{4,5},{5,4},{6,7},{7,6},{8,9},{9,8},{10,11... | collective-permute-start | bytes 786440 | tf_op jit(solution)/shard_map/ppermute | solution.py:302
  7.0 0.0 collective-permute-start.1
  7.0 0.0 copy-start
  7.0 0.0 copy-start.1
  7.0 8.9 %counts.1.own_ref = f32[256,256]{1,0:T(8,128)S(1)} custom-call(s32[33]{0:T(128)S(1)} %get-tuple-element.27.order_ref, s32[33,65536]{1,0:T(8,128)} %right_ref.1, s32[33,65536]{1,0:T(8,128)} %right_ref.1), custom_call_target="tpu_custom_call" | custom-call | tf_op jit(solution)/shard_map/counts/pallas_call | solution.py:273
  15.8 2.0 %collective-permute-done.1.far = f32[128,256]{1,0:T(8,128)S(1)} collective-permute-done((f32[128,256]{1,0:T(8,128)S(1)}, f32[128,256]{1,0:T(8,128)S(1)}, u32[]{:S(2)}, u32[]{:S(2)}) %collective-permute-start.1) | collective-permute-done | bytes 131104 | tf_op jit(solution)/shard_map/ppermute | solution.py:303
  17.8 0.0 collective-permute-done.near
  17.8 0.0 collective-permute-start.2
  17.8 0.5 %collective-permute-start.3 = (f32[128,256]{1,0:T(8,128)S(1)}, f32[128,256]{1,0:T(8,128)S(1)}, u32[]{:S(2)}, u32[]{:S(2)}) collective-permute-start(f32[128,256]{1,0:T(8,128)S(1)} %collective-permute-done.1.far), channel_id=1, source_target_pairs={{0,32},{32,0},{64,96},{96,64},{128,160},{160,128},{192,224},{224,1... | collective-permute-start | bytes 393224 | tf_op jit(solution)/shard_map/ppermute | solution.py:30
  18.3 1.2 %collective-permute-done.3.far_sibling = f32[128,256]{1,0:T(8,128)S(1)} collective-permute-done((f32[128,256]{1,0:T(8,128)S(1)}, f32[128,256]{1,0:T(8,128)S(1)}, u32[]{:S(2)}, u32[]{:S(2)}) %collective-permute-start.3) | collective-permute-done | bytes 131104 | tf_op jit(solution)/shard_map/ppermute | solution.py:30
  19.5 0.0 collective-permute-done.2.near_sibling
  19.5 1.0 %quad.1 = (f32[4,256,256]{2,1,0:T(8,128)S(1)}, f32[256,256]{1,0:T(8,128)S(1)}) custom-call(f32[256,256]{1,0:T(8,128)S(1)} %get-tuple-element.25.kernel_ref, f32[256,256]{1,0:T(8,128)S(1)} %collective-permute-done.near, f32[256,256]{1,0:T(8,128)S(1)} %collective-permute-done.2.near_sibling, f32[128,256]{1,0:T(8,128)S(1)} %collective-permute-done.1.far, ...), custom_call_target="tpu_custom_call" | custom-call | tf_op jit(solution)/shard_map/quad/pallas_call | solution.py:333
  20.5 0.2 collective-permute-start.5
  20.7 1.3 %collective-permute-start.4 = (f32[256,256]{1,0:T(8,128)S(1)}, f32[256,256]{1,0:T(8,128)S(1)}, u32[]{:S(2)}, u32[]{:S(2)}) collective-permute-start(f32[256,256]{1,0:T(8,128)S(1)} %get-tuple-element.33.product_ref), channel_id=1, source_target_pairs={{0,6},{1,7},{2,4},{3,5},{4,2},{5,3},{6,0},{7,1},{8,14},{9,15},{10,... | collective-permute-start | bytes 786440 | tf_op jit(solution)/shard_map/ppermute | solution.py:337
  22.0 0.1 collective-permute-done.5.sibling_ref
  22.2 2.8 %collective-permute-start.6 = (f32[128,256]{1,0:T(8,128)S(1)}, f32[128,256]{1,0:T(8,128)S(1)}, u32[]{:S(2)}, u32[]{:S(2)}) collective-permute-start(f32[128,256]{1,0:T(8,128)S(1)} %get-tuple-element.35), channel_id=1, source_target_pairs={{0,128},{1,129},{2,130},{3,131},{4,132},{5,133},{6,134},{7,135},{8... | collective-permute-start | bytes 393224 | tf_op jit(solution)/shard_map/ppermute | solution.py:303
  25.0 0.9 %collective-permute-start.9 = (f32[256,256]{1,0:T(8,128)S(1)}, f32[256,256]{1,0:T(8,128)S(1)}, u32[]{:S(2)}, u32[]{:S(2)}) collective-permute-start(f32[256,256]{1,0:T(8,128)S(1)} %get-tuple-element.37.chip_ref), channel_id=1, source_target_pairs={{0,64},{1,65},{2,66},{3,67},{4,68},{5,69},{6,70},{7,71},{8,72},{9,... | collective-permute-start | bytes 786440 | tf_op jit(solution)/shard_map/ppermute | solution.py:302
  25.9 0.1 collective-permute-done.4.whole_ref.near
  26.0 1.9 %collective-permute-done.6.far_ref = f32[128,256]{1,0:T(8,128)S(1)} collective-permute-done((f32[128,256]{1,0:T(8,128)S(1)}, f32[128,256]{1,0:T(8,128)S(1)}, u32[]{:S(2)}, u32[]{:S(2)}) %collective-permute-start.6) | collective-permute-done | bytes 131104 | tf_op jit(solution)/shard_map/ppermute | solution.py:303
  27.9 3.6 %collective-permute-start.8 = (f32[256,256]{1,0:T(8,128)S(1)}, f32[256,256]{1,0:T(8,128)S(1)}, u32[]{:S(2)}, u32[]{:S(2)}) collective-permute-start(f32[256,256]{1,0:T(8,128)S(1)} %collective-permute-done.4.whole_ref.near), channel_id=1, source_target_pairs={{0,32},{32,0},{64,96},{96,64},{128,160},{160,128},{192,224},{224,1... | collective-permute-start | bytes 786440 | tf_op jit(solution)/shard_map/ppermute | solution.py:30
  31.5 4.4 %collective-permute-start.7 = (f32[128,256]{1,0:T(8,128)S(1)}, f32[128,256]{1,0:T(8,128)S(1)}, u32[]{:S(2)}, u32[]{:S(2)}) collective-permute-start(f32[128,256]{1,0:T(8,128)S(1)} %relay.1), channel_id=1, source_target_pairs={{0,8},{1,9},{2,10},{3,11},{4,12},{5,13},{6,14},{7,15},{8,0},{9,1},... | collective-permute-start | bytes 393224 | tf_op jit(solution)/shard_map/ppermute | solution.py:354
  35.9 2.7 %collective-permute-done.7.far = f32[128,256]{1,0:T(8,128)S(1)} collective-permute-done((f32[128,256]{1,0:T(8,128)S(1)}, f32[128,256]{1,0:T(8,128)S(1)}, u32[]{:S(2)}, u32[]{:S(2)}) %collective-permute-start.7) | collective-permute-done | bytes 131104 | tf_op jit(solution)/shard_map/ppermute | solution.py:354
  38.5 0.0 collective-permute-done.9.near_ref
  38.5 0.0 collective-permute-done.8.near_sibling
  38.6 0.1 collective-permute-start.12
  38.7 0.5 %collective-permute-start.10 = (f32[128,256]{1,0:T(8,128)S(1)}, f32[128,256]{1,0:T(8,128)S(1)}, u32[]{:S(2)}, u32[]{:S(2)}) collective-permute-start(f32[128,256]{1,0:T(8,128)S(1)} %collective-permute-done.7.far), channel_id=1, source_target_pairs={{0,32},{32,0},{64,96},{96,64},{128,160},{160,128},{192,224},{224,1... | collective-permute-start | bytes 393224 | tf_op jit(solution)/shard_map/ppermute | solution.py:30
  39.2 1.2 %collective-permute-done.10.far_sibling = f32[128,256]{1,0:T(8,128)S(1)} collective-permute-done((f32[128,256]{1,0:T(8,128)S(1)}, f32[128,256]{1,0:T(8,128)S(1)}, u32[]{:S(2)}, u32[]{:S(2)}) %collective-permute-start.10) | collective-permute-done | bytes 131104 | tf_op jit(solution)/shard_map/ppermute | solution.py:30
  40.4 0.6 %block.1 = (f32[4,256,256]{2,1,0:T(8,128)S(1)}, f32[8,256]{1,0:T(8,128)S(1)}) custom-call(f32[256,256]{1,0:T(8,128)S(1)} %get-tuple-element.33.product_ref, f32[256,256]{1,0:T(8,128)S(1)} %collective-permute-done.4.whole_ref.near, f32[256,256]{1,0:T(8,128)S(1)} %collective-permute-done.8.near_sibling, f32[128,256]{1,0:T(8,128)S(1)} %collective-permute-done.7.far, ...), custom_call_target="tpu_custom_call" | custom-call | tf_op jit(solution)/shard_map/block/pallas_call | solution.py:362
  41.0 3.0 %collective-permute-start.11 = (f32[8,256]{1,0:T(8,128)S(1)}, f32[8,256]{1,0:T(8,128)S(1)}, u32[]{:S(2)}, u32[]{:S(2)}) collective-permute-start(f32[8,256]{1,0:T(8,128)S(1)} %get-tuple-element.43), channel_id=1, source_target_pairs={{0,16},{1,17},{2,18},{3,19},{4,20},{5,21},{6,22},{7,23},{8,24},{9,... | collective-permute-start | bytes 24584 | tf_op jit(solution)/shard_map/ppermute | solution.py:366
  44.0 2.5 %sides.1 = (f32[256,256]{1,0:T(8,128)S(1)}, f32[8,256]{1,0:T(8,128)S(1)}) custom-call(f32[4,256,256]{2,1,0:T(8,128)S(1)} %get-tuple-element.32.quad_ref, f32[4,256,256]{2,1,0:T(8,128)S(1)} %get-tuple-element.40.block_ref), custom_call_target="tpu_custom_call" | custom-call | tf_op jit(solution)/shard_map/sides/pallas_call | solution.py:367
  46.5 0.0 collective-permute-done.11.message_ref
  46.5 0.0 collective-permute-done.12.sibling_join_ref
  46.5 0.0 copy-done
  46.5 0.0 copy-done.1
  46.5 1.2 %final.1 = (f32[256,256]{1,0:T(8,128)}, f32[256,256]{1,0:T(8,128)}) custom-call(f32[256,256]{1,0:T(8,128)S(1)} %bitcast.5, f32[256,256]{1,0:T(8,128)S(1)} %bitcast.6, f32[256,256]{1,0:T(8,128)S(1)} %get-tuple-element.25.kernel_ref, f32[256,256]{1,0:T(8,128)S(1)} %get-tuple-element.41.path_ref, f32[8,256]{1,0:T(8,128)S(1)} %get-tuple-element.42.known_ref, ...), custom_call_target="tpu_custom_call" | custom-call | tf_op jit(solution)/shard_map/final/pallas_call | solution.py:369
  (3 shorter events, 0.1 us)
Async XLA Ops:
  1.7 16.1 %collective-permute-start = (f32[256,256]{1,0:T(8,128)S(1)}, f32[256,256]{1,0:T(8,128)S(1)}, u32[]{:S(2)}, u32[]{:S(2)}) collective-permute-start(f32[256,256]{1,0:T(8,128)S(1)} %get-tuple-element.25.kernel_ref), channel_id=1, source_target_pairs={{0,1},{1,0},{2,3},{3,2},{4,5},{5,4},{6,7},{7,6},{8,9},{9,8},{10,11... | collective-permute-start | bytes 786440 | tf_op jit(solution)/shard_map/ppermute | solution.py:302
  7.0 10.8 %collective-permute-start.1 = (f32[128,256]{1,0:T(8,128)S(1)}, f32[128,256]{1,0:T(8,128)S(1)}, u32[]{:S(2)}, u32[]{:S(2)}) collective-permute-start(f32[128,256]{1,0:T(8,128)S(1)} %get-tuple-element.26), channel_id=1, source_target_pairs={{0,2},{1,3},{2,0},{3,1},{4,6},{5,7},{6,4},{7,5},{8,10},{9,11},{10,... | collective-permute-start | bytes 393224 | tf_op jit(solution)/shard_map/ppermute | solution.py:303
  7.0 39.5 %copy-start = (f32[1,256,256]{2,1,0:T(8,128)S(1)}, f32[1,256,256]{2,1,0:T(8,128)}, u32[]{:S(2)}) copy-start(f32[1,256,256]{2,1,0:T(8,128)} %param.6) | copy-start | bytes 786436
  7.0 39.5 %copy-start.1 = (f32[1,256,256]{2,1,0:T(8,128)S(1)}, f32[1,256,256]{2,1,0:T(8,128)}, u32[]{:S(2)}) copy-start(f32[1,256,256]{2,1,0:T(8,128)} %param.7) | copy-start | bytes 786436
  17.8 1.7 %collective-permute-start.2 = (f32[256,256]{1,0:T(8,128)S(1)}, f32[256,256]{1,0:T(8,128)S(1)}, u32[]{:S(2)}, u32[]{:S(2)}) collective-permute-start(f32[256,256]{1,0:T(8,128)S(1)} %collective-permute-done.near), channel_id=1, source_target_pairs={{0,32},{32,0},{64,96},{96,64},{128,160},{160,128},{192,224},{224,1... | collective-permute-start | bytes 786440 | tf_op jit(solution)/shard_map/ppermute | solution.py:30
  17.8 1.7 %collective-permute-start.3 = (f32[128,256]{1,0:T(8,128)S(1)}, f32[128,256]{1,0:T(8,128)S(1)}, u32[]{:S(2)}, u32[]{:S(2)}) collective-permute-start(f32[128,256]{1,0:T(8,128)S(1)} %collective-permute-done.1.far), channel_id=1, source_target_pairs={{0,32},{32,0},{64,96},{96,64},{128,160},{160,128},{192,224},{224,1... | collective-permute-start | bytes 393224 | tf_op jit(solution)/shard_map/ppermute | solution.py:30
  20.5 1.6 %collective-permute-start.5 = (f32[256,256]{1,0:T(8,128)S(1)}, f32[256,256]{1,0:T(8,128)S(1)}, u32[]{:S(2)}, u32[]{:S(2)}) collective-permute-start(f32[256,256]{1,0:T(8,128)S(1)} %counts.1.own_ref), channel_id=1, source_target_pairs={{0,32},{32,0},{64,96},{96,64},{128,160},{160,128},{192,224},{224,1... | collective-permute-start | bytes 786440 | tf_op jit(solution)/shard_map/ppermute | solution.py:30
  20.7 5.2 %collective-permute-start.4 = (f32[256,256]{1,0:T(8,128)S(1)}, f32[256,256]{1,0:T(8,128)S(1)}, u32[]{:S(2)}, u32[]{:S(2)}) collective-permute-start(f32[256,256]{1,0:T(8,128)S(1)} %get-tuple-element.33.product_ref), channel_id=1, source_target_pairs={{0,6},{1,7},{2,4},{3,5},{4,2},{5,3},{6,0},{7,1},{8,14},{9,15},{10,... | collective-permute-start | bytes 786440 | tf_op jit(solution)/shard_map/ppermute | solution.py:337
  22.2 5.7 %collective-permute-start.6 = (f32[128,256]{1,0:T(8,128)S(1)}, f32[128,256]{1,0:T(8,128)S(1)}, u32[]{:S(2)}, u32[]{:S(2)}) collective-permute-start(f32[128,256]{1,0:T(8,128)S(1)} %get-tuple-element.35), channel_id=1, source_target_pairs={{0,128},{1,129},{2,130},{3,131},{4,132},{5,133},{6,134},{7,135},{8... | collective-permute-start | bytes 393224 | tf_op jit(solution)/shard_map/ppermute | solution.py:303
  25.0 13.5 %collective-permute-start.9 = (f32[256,256]{1,0:T(8,128)S(1)}, f32[256,256]{1,0:T(8,128)S(1)}, u32[]{:S(2)}, u32[]{:S(2)}) collective-permute-start(f32[256,256]{1,0:T(8,128)S(1)} %get-tuple-element.37.chip_ref), channel_id=1, source_target_pairs={{0,64},{1,65},{2,66},{3,67},{4,68},{5,69},{6,70},{7,71},{8,72},{9,... | collective-permute-start | bytes 786440 | tf_op jit(solution)/shard_map/ppermute | solution.py:302
  27.9 10.6 %collective-permute-start.8 = (f32[256,256]{1,0:T(8,128)S(1)}, f32[256,256]{1,0:T(8,128)S(1)}, u32[]{:S(2)}, u32[]{:S(2)}) collective-permute-start(f32[256,256]{1,0:T(8,128)S(1)} %collective-permute-done.4.whole_ref.near), channel_id=1, source_target_pairs={{0,32},{32,0},{64,96},{96,64},{128,160},{160,128},{192,224},{224,1... | collective-permute-start | bytes 786440 | tf_op jit(solution)/shard_map/ppermute | solution.py:30
  31.5 7.0 %collective-permute-start.7 = (f32[128,256]{1,0:T(8,128)S(1)}, f32[128,256]{1,0:T(8,128)S(1)}, u32[]{:S(2)}, u32[]{:S(2)}) collective-permute-start(f32[128,256]{1,0:T(8,128)S(1)} %relay.1), channel_id=1, source_target_pairs={{0,8},{1,9},{2,10},{3,11},{4,12},{5,13},{6,14},{7,15},{8,0},{9,1},... | collective-permute-start | bytes 393224 | tf_op jit(solution)/shard_map/ppermute | solution.py:354
  38.6 7.9 %collective-permute-start.12 = (f32[256,256]{1,0:T(8,128)S(1)}, f32[256,256]{1,0:T(8,128)S(1)}, u32[]{:S(2)}, u32[]{:S(2)}) collective-permute-start(f32[256,256]{1,0:T(8,128)S(1)} %join.1.join_ref), channel_id=1, source_target_pairs={{0,32},{32,0},{64,96},{96,64},{128,160},{160,128},{192,224},{224,1... | collective-permute-start | bytes 786440 | tf_op jit(solution)/shard_map/ppermute | solution.py:30
  38.7 1.7 %collective-permute-start.10 = (f32[128,256]{1,0:T(8,128)S(1)}, f32[128,256]{1,0:T(8,128)S(1)}, u32[]{:S(2)}, u32[]{:S(2)}) collective-permute-start(f32[128,256]{1,0:T(8,128)S(1)} %collective-permute-done.7.far), channel_id=1, source_target_pairs={{0,32},{32,0},{64,96},{96,64},{128,160},{160,128},{192,224},{224,1... | collective-permute-start | bytes 393224 | tf_op jit(solution)/shard_map/ppermute | solution.py:30
  41.0 5.5 %collective-permute-start.11 = (f32[8,256]{1,0:T(8,128)S(1)}, f32[8,256]{1,0:T(8,128)S(1)}, u32[]{:S(2)}, u32[]{:S(2)}) collective-permute-start(f32[8,256]{1,0:T(8,128)S(1)} %get-tuple-element.43), channel_id=1, source_target_pairs={{0,16},{1,17},{2,18},{3,19},{4,20},{5,21},{6,22},{7,23},{8,24},{9,... | collective-permute-start | bytes 24584 | tf_op jit(solution)/shard_map/ppermute | solution.py:366

commit v11 on v10

--- a/solution.py
+++ b/solution.py
@@ -349,15 +349,14 @@
         lambda x, c, y, z: (x ^ (1 + 2 * c), y, z),
         lambda x, y, z: (x ^ 2, y, z),
     )
-    near, far_counts = lax.optimization_barrier((near, far_counts))
     half_near = call(relay_kernel, out_shape=half, name="relay")(near)
     far = lax.ppermute(
         half_near,
         axes,
         everywhere(lambda x, c, y, z: (x, y, z ^ 6) if c else (x, y ^ 1, z)),
     )
-    near_sibling = other_core(near)
-    far, near_sibling, near_counts = lax.optimization_barrier((far, near_sibling, near_counts))
+    held, near_counts, far_counts = lax.optimization_barrier((near, near_counts, far_counts))
+    near_sibling = other_core(held)
     far_sibling = other_core(far)
     block, message = call(
         block_kernel, out_shape=(shape(4, size, size), shape(8, size)), name="block"

time: 47.8 us -> 46.4 us (0.971)
  the two profiles are of different devices: /device:TPU:1 before, /device:TPU:33 now
where the time goes in v11:
time: 46.4 us; the launch traced here: 46.3 us
  starting transfers between devices  26.1 us (56%)
  Pallas kernels  15 us (32%)
  waiting for transfers between devices  4.42 us (10%)
  between operations  0.73 us (2%)
    ppermute x6, starting transfers between devices, other_core(): return lax.ppermute(value, 'dp', along_dp(lambda x, c: (x, 1 - c)))  9.35 us
    pallas_call x1, Pallas kernels, count_pairs(): pl.pallas_call(functools.partial(count_kernel, part), out_shape=shape(siz...  8.87 us
    ppermute x1, starting transfers between devices, per_device(): lax.ppermute(half_near, axes, everywhere(lambda x, c, y, z: (x, y, z ^ 6)...  6.22 us
    ppermute x2, starting transfers between devices, exchange(): lax.ppermute(whole, axes, everywhere(near_step))  4.29 us
    ppermute x1, starting transfers between devices, per_device(): lax.ppermute(message, 'clique', along_clique(lambda y, z: (y ^ 2, z)))  3.02 us
    ppermute x6, waiting for transfers between devices, other_core(): return lax.ppermute(value, 'dp', along_dp(lambda x, c: (x, 1 - c)))  2.31 us
    pallas_call x1, Pallas kernels, per_device(): call(sides_kernel, out_shape=(whole, shape(8, size)), name='sides')  2.2 us
    ppermute x2, starting transfers between devices, exchange(): lax.ppermute(half, axes, everywhere(lambda x, c, y, z: far_step(x, y, z)))  1.97 us
  transfers between devices with their start and end apart: 13, of which 5 were waited for; matrix products, arithmetic and copies ran while one was open for 0% of the time, Pallas kernels for 25%

profile of v11, /device:TPU:33, one launch (start us, length us, event | category | flops | bytes accessed | tf_op | source)
XLA Modules:
  0.0 46.3 jit_solution(1017681346363531964)
XLA Ops:
  0.6 1.1 %read.1 = (s32[33]{0:T(128)S(1)}, f32[256,256]{1,0:T(8,128)S(1)}, f32[128,256]{1,0:T(8,128)S(1)}) custom-call(s32[33]{0:T(128)} %order_hbm.1, f32[256,256]{1,0:T(8,128)} %bitcast.4), custom_call_target="tpu_custom_call" | custom-call | tf_op jit(solution)/shard_map/read/pallas_call | solution.py:314
  1.7 1.7 %collective-permute-start = (f32[256,256]{1,0:T(8,128)S(1)}, f32[256,256]{1,0:T(8,128)S(1)}, u32[]{:S(2)}, u32[]{:S(2)}) collective-permute-start(f32[256,256]{1,0:T(8,128)S(1)} %get-tuple-element.23.kernel_ref), channel_id=1, source_target_pairs={{0,1},{1,0},{2,3},{3,2},{4,5},{5,4},{6,7},{7,6},{8,9},{9,8},{10,11... | collective-permute-start | bytes 786440 | tf_op jit(solution)/shard_map/ppermute | solution.py:302
  3.4 1.5 %collective-permute-start.1 = (f32[128,256]{1,0:T(8,128)S(1)}, f32[128,256]{1,0:T(8,128)S(1)}, u32[]{:S(2)}, u32[]{:S(2)}) collective-permute-start(f32[128,256]{1,0:T(8,128)S(1)} %get-tuple-element.24), channel_id=1, source_target_pairs={{0,2},{1,3},{2,0},{3,1},{4,6},{5,7},{6,4},{7,5},{8,10},{9,11},{10,... | collective-permute-start | bytes 393224 | tf_op jit(solution)/shard_map/ppermute | solution.py:303
  4.9 0.0 copy-start
  4.9 0.0 copy-start.1
  4.9 8.9 %counts.1.own_ref = f32[256,256]{1,0:T(8,128)S(1)} custom-call(s32[33]{0:T(128)S(1)} %get-tuple-element.25.order_ref, s32[33,65536]{1,0:T(8,128)} %right_ref.1, s32[33,65536]{1,0:T(8,128)} %right_ref.1), custom_call_target="tpu_custom_call" | custom-call | tf_op jit(solution)/shard_map/counts/pallas_call | solution.py:273
  13.8 1.4 %collective-permute-done.1.far = f32[128,256]{1,0:T(8,128)S(1)} collective-permute-done((f32[128,256]{1,0:T(8,128)S(1)}, f32[128,256]{1,0:T(8,128)S(1)}, u32[]{:S(2)}, u32[]{:S(2)}) %collective-permute-start.1) | collective-permute-done | bytes 131104 | tf_op jit(solution)/shard_map/ppermute | solution.py:303
  15.2 0.0 collective-permute-done.near
  15.2 0.1 collective-permute-start.2
  15.3 0.4 collective-permute-start.3
  15.7 1.2 %collective-permute-done.3.far_sibling = f32[128,256]{1,0:T(8,128)S(1)} collective-permute-done((f32[128,256]{1,0:T(8,128)S(1)}, f32[128,256]{1,0:T(8,128)S(1)}, u32[]{:S(2)}, u32[]{:S(2)}) %collective-permute-start.3) | collective-permute-done | bytes 131104 | tf_op jit(solution)/shard_map/ppermute | solution.py:30
  16.9 0.0 collective-permute-done.2.near_sibling
  16.9 1.0 %quad.1 = (f32[4,256,256]{2,1,0:T(8,128)S(1)}, f32[256,256]{1,0:T(8,128)S(1)}) custom-call(f32[256,256]{1,0:T(8,128)S(1)} %get-tuple-element.23.kernel_ref, f32[256,256]{1,0:T(8,128)S(1)} %collective-permute-done.near, f32[256,256]{1,0:T(8,128)S(1)} %collective-permute-done.2.near_sibling, f32[128,256]{1,0:T(8,128)S(1)} %collective-permute-done.1.far, ...), custom_call_target="tpu_custom_call" | custom-call | tf_op jit(solution)/shard_map/quad/pallas_call | solution.py:333
  17.9 0.2 collective-permute-start.5
  18.1 1.3 %collective-permute-start.4 = (f32[256,256]{1,0:T(8,128)S(1)}, f32[256,256]{1,0:T(8,128)S(1)}, u32[]{:S(2)}, u32[]{:S(2)}) collective-permute-start(f32[256,256]{1,0:T(8,128)S(1)} %get-tuple-element.31.product_ref), channel_id=1, source_target_pairs={{0,6},{1,7},{2,4},{3,5},{4,2},{5,3},{6,0},{7,1},{8,14},{9,15},{10,... | collective-permute-start | bytes 786440 | tf_op jit(solution)/shard_map/ppermute | solution.py:337
  19.4 0.1 collective-permute-done.5.sibling_ref
  19.6 2.6 %collective-permute-start.6 = (f32[256,256]{1,0:T(8,128)S(1)}, f32[256,256]{1,0:T(8,128)S(1)}, u32[]{:S(2)}, u32[]{:S(2)}) collective-permute-start(f32[256,256]{1,0:T(8,128)S(1)} %get-tuple-element.33.chip_ref), channel_id=1, source_target_pairs={{0,64},{1,65},{2,66},{3,67},{4,68},{5,69},{6,70},{7,71},{8,72},{9,... | collective-permute-start | bytes 786440 | tf_op jit(solution)/shard_map/ppermute | solution.py:302
  22.1 0.5 %collective-permute-start.7 = (f32[128,256]{1,0:T(8,128)S(1)}, f32[128,256]{1,0:T(8,128)S(1)}, u32[]{:S(2)}, u32[]{:S(2)}) collective-permute-start(f32[128,256]{1,0:T(8,128)S(1)} %get-tuple-element.34), channel_id=1, source_target_pairs={{0,128},{1,129},{2,130},{3,131},{4,132},{5,133},{6,134},{7,135},{8... | collective-permute-start | bytes 393224 | tf_op jit(solution)/shard_map/ppermute | solution.py:303
  22.6 0.7 %collective-permute-done.4.whole_ref.near = f32[256,256]{1,0:T(8,128)S(1)} collective-permute-done((f32[256,256]{1,0:T(8,128)S(1)}, f32[256,256]{1,0:T(8,128)S(1)}, u32[]{:S(2)}, u32[]{:S(2)}) %collective-permute-start.4) | collective-permute-done | bytes 262176 | tf_op jit(solution)/shard_map/ppermute | solution.py:337
  23.3 6.2 %collective-permute-start.9 = (f32[128,256]{1,0:T(8,128)S(1)}, f32[128,256]{1,0:T(8,128)S(1)}, u32[]{:S(2)}, u32[]{:S(2)}) collective-permute-start(f32[128,256]{1,0:T(8,128)S(1)} %relay.1), channel_id=1, source_target_pairs={{0,8},{1,9},{2,10},{3,11},{4,12},{5,13},{6,14},{7,15},{8,0},{9,1},... | collective-permute-start | bytes 393224 | tf_op jit(solution)/shard_map/ppermute | solution.py:353
  29.6 0.0 collective-permute-done.7.far_ref
  29.6 0.0 collective-permute-done.6.near_ref
  29.6 5.3 %collective-permute-start.8 = (f32[256,256]{1,0:T(8,128)S(1)}, f32[256,256]{1,0:T(8,128)S(1)}, u32[]{:S(2)}, u32[]{:S(2)}) collective-permute-start(f32[256,256]{1,0:T(8,128)S(1)} %collective-permute-done.4.whole_ref.near), channel_id=1, source_target_pairs={{0,32},{32,0},{64,96},{96,64},{128,160},{160,128},{192,224},{224,1... | collective-permute-start | bytes 786440 | tf_op jit(solution)/shard_map/ppermute | solution.py:30
  34.9 0.1 collective-permute-start.12
  35.0 0.0 collective-permute-done.9.far
  35.0 3.2 %collective-permute-start.10 = (f32[128,256]{1,0:T(8,128)S(1)}, f32[128,256]{1,0:T(8,128)S(1)}, u32[]{:S(2)}, u32[]{:S(2)}) collective-permute-start(f32[128,256]{1,0:T(8,128)S(1)} %collective-permute-done.9.far), channel_id=1, source_target_pairs={{0,32},{32,0},{64,96},{96,64},{128,160},{160,128},{192,224},{224,1... | collective-permute-start | bytes 393224 | tf_op jit(solution)/shard_map/ppermute | solution.py:30
  38.2 1.0 %collective-permute-done.10.far_sibling = f32[128,256]{1,0:T(8,128)S(1)} collective-permute-done((f32[128,256]{1,0:T(8,128)S(1)}, f32[128,256]{1,0:T(8,128)S(1)}, u32[]{:S(2)}, u32[]{:S(2)}) %collective-permute-start.10) | collective-permute-done | bytes 131104 | tf_op jit(solution)/shard_map/ppermute | solution.py:30
  39.2 0.0 collective-permute-done.8.near_sibling
  39.2 0.6 %block.1 = (f32[4,256,256]{2,1,0:T(8,128)S(1)}, f32[8,256]{1,0:T(8,128)S(1)}) custom-call(f32[256,256]{1,0:T(8,128)S(1)} %get-tuple-element.31.product_ref, f32[256,256]{1,0:T(8,128)S(1)} %collective-permute-done.4.whole_ref.near, f32[256,256]{1,0:T(8,128)S(1)} %collective-permute-done.8.near_sibling, f32[128,256]{1,0:T(8,128)S(1)} %collective-permute-done.9.far, ...), custom_call_target="tpu_custom_call" | custom-call | tf_op jit(solution)/shard_map/block/pallas_call | solution.py:361
  39.8 3.0 %collective-permute-start.11 = (f32[8,256]{1,0:T(8,128)S(1)}, f32[8,256]{1,0:T(8,128)S(1)}, u32[]{:S(2)}, u32[]{:S(2)}) collective-permute-start(f32[8,256]{1,0:T(8,128)S(1)} %get-tuple-element.39), channel_id=1, source_target_pairs={{0,16},{1,17},{2,18},{3,19},{4,20},{5,21},{6,22},{7,23},{8,24},{9,... | collective-permute-start | bytes 24584 | tf_op jit(solution)/shard_map/ppermute | solution.py:365
  42.8 2.2 %sides.1 = (f32[256,256]{1,0:T(8,128)S(1)}, f32[8,256]{1,0:T(8,128)S(1)}) custom-call(f32[4,256,256]{2,1,0:T(8,128)S(1)} %get-tuple-element.30.quad_ref, f32[4,256,256]{2,1,0:T(8,128)S(1)} %get-tuple-element.36.block_ref), custom_call_target="tpu_custom_call" | custom-call | tf_op jit(solution)/shard_map/sides/pallas_call | solution.py:366
  45.0 0.0 collective-permute-done.12.sibling_join_ref
  45.0 0.0 collective-permute-done.11.message_ref
  45.1 0.0 copy-done
  45.1 0.0 copy-done.1
  45.1 1.2 %final.1 = (f32[256,256]{1,0:T(8,128)}, f32[256,256]{1,0:T(8,128)}) custom-call(f32[256,256]{1,0:T(8,128)S(1)} %bitcast.5, f32[256,256]{1,0:T(8,128)S(1)} %bitcast.6, f32[256,256]{1,0:T(8,128)S(1)} %get-tuple-element.23.kernel_ref, f32[256,256]{1,0:T(8,128)S(1)} %get-tuple-element.37.path_ref, f32[8,256]{1,0:T(8,128)S(1)} %get-tuple-element.38.known_ref, ...), custom_call_target="tpu_custom_call" | custom-call | tf_op jit(solution)/shard_map/final/pallas_call | solution.py:368
  (3 shorter events, 0.1 us)
Async XLA Ops:
  1.7 13.5 %collective-permute-start = (f32[256,256]{1,0:T(8,128)S(1)}, f32[256,256]{1,0:T(8,128)S(1)}, u32[]{:S(2)}, u32[]{:S(2)}) collective-permute-start(f32[256,256]{1,0:T(8,128)S(1)} %get-tuple-element.23.kernel_ref), channel_id=1, source_target_pairs={{0,1},{1,0},{2,3},{3,2},{4,5},{5,4},{6,7},{7,6},{8,9},{9,8},{10,11... | collective-permute-start | bytes 786440 | tf_op jit(solution)/shard_map/ppermute | solution.py:302
  3.4 11.7 %collective-permute-start.1 = (f32[128,256]{1,0:T(8,128)S(1)}, f32[128,256]{1,0:T(8,128)S(1)}, u32[]{:S(2)}, u32[]{:S(2)}) collective-permute-start(f32[128,256]{1,0:T(8,128)S(1)} %get-tuple-element.24), channel_id=1, source_target_pairs={{0,2},{1,3},{2,0},{3,1},{4,6},{5,7},{6,4},{7,5},{8,10},{9,11},{10,... | collective-permute-start | bytes 393224 | tf_op jit(solution)/shard_map/ppermute | solution.py:303
  4.9 40.2 %copy-start = (f32[1,256,256]{2,1,0:T(8,128)S(1)}, f32[1,256,256]{2,1,0:T(8,128)}, u32[]{:S(2)}) copy-start(f32[1,256,256]{2,1,0:T(8,128)} %param.6) | copy-start | bytes 786436
  4.9 40.2 %copy-start.1 = (f32[1,256,256]{2,1,0:T(8,128)S(1)}, f32[1,256,256]{2,1,0:T(8,128)}, u32[]{:S(2)}) copy-start(f32[1,256,256]{2,1,0:T(8,128)} %param.7) | copy-start | bytes 786436
  15.2 1.7 %collective-permute-start.2 = (f32[256,256]{1,0:T(8,128)S(1)}, f32[256,256]{1,0:T(8,128)S(1)}, u32[]{:S(2)}, u32[]{:S(2)}) collective-permute-start(f32[256,256]{1,0:T(8,128)S(1)} %collective-permute-done.near), channel_id=1, source_target_pairs={{0,32},{32,0},{64,96},{96,64},{128,160},{160,128},{192,224},{224,1... | collective-permute-start | bytes 786440 | tf_op jit(solution)/shard_map/ppermute | solution.py:30
  15.3 1.6 %collective-permute-start.3 = (f32[128,256]{1,0:T(8,128)S(1)}, f32[128,256]{1,0:T(8,128)S(1)}, u32[]{:S(2)}, u32[]{:S(2)}) collective-permute-start(f32[128,256]{1,0:T(8,128)S(1)} %collective-permute-done.1.far), channel_id=1, source_target_pairs={{0,32},{32,0},{64,96},{96,64},{128,160},{160,128},{192,224},{224,1... | collective-permute-start | bytes 393224 | tf_op jit(solution)/shard_map/ppermute | solution.py:30
  17.9 1.6 %collective-permute-start.5 = (f32[256,256]{1,0:T(8,128)S(1)}, f32[256,256]{1,0:T(8,128)S(1)}, u32[]{:S(2)}, u32[]{:S(2)}) collective-permute-start(f32[256,256]{1,0:T(8,128)S(1)} %counts.1.own_ref), channel_id=1, source_target_pairs={{0,32},{32,0},{64,96},{96,64},{128,160},{160,128},{192,224},{224,1... | collective-permute-start | bytes 786440 | tf_op jit(solution)/shard_map/ppermute | solution.py:30
  18.1 5.2 %collective-permute-start.4 = (f32[256,256]{1,0:T(8,128)S(1)}, f32[256,256]{1,0:T(8,128)S(1)}, u32[]{:S(2)}, u32[]{:S(2)}) collective-permute-start(f32[256,256]{1,0:T(8,128)S(1)} %get-tuple-element.31.product_ref), channel_id=1, source_target_pairs={{0,6},{1,7},{2,4},{3,5},{4,2},{5,3},{6,0},{7,1},{8,14},{9,15},{10,... | collective-permute-start | bytes 786440 | tf_op jit(solution)/shard_map/ppermute | solution.py:337
  19.6 10.0 %collective-permute-start.6 = (f32[256,256]{1,0:T(8,128)S(1)}, f32[256,256]{1,0:T(8,128)S(1)}, u32[]{:S(2)}, u32[]{:S(2)}) collective-permute-start(f32[256,256]{1,0:T(8,128)S(1)} %get-tuple-element.33.chip_ref), channel_id=1, source_target_pairs={{0,64},{1,65},{2,66},{3,67},{4,68},{5,69},{6,70},{7,71},{8,72},{9,... | collective-permute-start | bytes 786440 | tf_op jit(solution)/shard_map/ppermute | solution.py:302
  22.1 7.4 %collective-permute-start.7 = (f32[128,256]{1,0:T(8,128)S(1)}, f32[128,256]{1,0:T(8,128)S(1)}, u32[]{:S(2)}, u32[]{:S(2)}) collective-permute-start(f32[128,256]{1,0:T(8,128)S(1)} %get-tuple-element.34), channel_id=1, source_target_pairs={{0,128},{1,129},{2,130},{3,131},{4,132},{5,133},{6,134},{7,135},{8... | collective-permute-start | bytes 393224 | tf_op jit(solution)/shard_map/ppermute | solution.py:303
  23.3 11.6 %collective-permute-start.9 = (f32[128,256]{1,0:T(8,128)S(1)}, f32[128,256]{1,0:T(8,128)S(1)}, u32[]{:S(2)}, u32[]{:S(2)}) collective-permute-start(f32[128,256]{1,0:T(8,128)S(1)} %relay.1), channel_id=1, source_target_pairs={{0,8},{1,9},{2,10},{3,11},{4,12},{5,13},{6,14},{7,15},{8,0},{9,1},... | collective-permute-start | bytes 393224 | tf_op jit(solution)/shard_map/ppermute | solution.py:353
  29.6 9.7 %collective-permute-start.8 = (f32[256,256]{1,0:T(8,128)S(1)}, f32[256,256]{1,0:T(8,128)S(1)}, u32[]{:S(2)}, u32[]{:S(2)}) collective-permute-start(f32[256,256]{1,0:T(8,128)S(1)} %collective-permute-done.4.whole_ref.near), channel_id=1, source_target_pairs={{0,32},{32,0},{64,96},{96,64},{128,160},{160,128},{192,224},{224,1... | collective-permute-start | bytes 786440 | tf_op jit(solution)/shard_map/ppermute | solution.py:30
  34.9 10.1 %collective-permute-start.12 = (f32[256,256]{1,0:T(8,128)S(1)}, f32[256,256]{1,0:T(8,128)S(1)}, u32[]{:S(2)}, u32[]{:S(2)}) collective-permute-start(f32[256,256]{1,0:T(8,128)S(1)} %join.1.join_ref), channel_id=1, source_target_pairs={{0,32},{32,0},{64,96},{96,64},{128,160},{160,128},{192,224},{224,1... | collective-permute-start | bytes 786440 | tf_op jit(solution)/shard_map/ppermute | solution.py:30
  35.0 4.2 %collective-permute-start.10 = (f32[128,256]{1,0:T(8,128)S(1)}, f32[128,256]{1,0:T(8,128)S(1)}, u32[]{:S(2)}, u32[]{:S(2)}) collective-permute-start(f32[128,256]{1,0:T(8,128)S(1)} %collective-permute-done.9.far), channel_id=1, source_target_pairs={{0,32},{32,0},{64,96},{96,64},{128,160},{160,128},{192,224},{224,1... | collective-permute-start | bytes 393224 | tf_op jit(solution)/shard_map/ppermute | solution.py:30
  39.8 5.2 %collective-permute-start.11 = (f32[8,256]{1,0:T(8,128)S(1)}, f32[8,256]{1,0:T(8,128)S(1)}, u32[]{:S(2)}, u32[]{:S(2)}) collective-permute-start(f32[8,256]{1,0:T(8,128)S(1)} %get-tuple-element.39), channel_id=1, source_target_pairs={{0,16},{1,17},{2,18},{3,19},{4,20},{5,21},{6,22},{7,23},{8,24},{9,... | collective-permute-start | bytes 24584 | tf_op jit(solution)/shard_map/ppermute | solution.py:365

commit v12 on v9

--- a/solution.py
+++ b/solution.py
@@ -114,14 +114,18 @@
     return (core, y, 2 * lax.rem(y, 2) + lax.div(z, QUAD), lax.rem(z, QUAD))
 
 
-def block_kernel(product_ref, near, near_sibling, far, far_sibling, block_ref, message_ref):
+def put_halves(stack_ref, slot, own, sibling, core):
+    half = own.shape[0]
+    stack_ref[slot, pl.ds(core * half, half), :] = own[...]
+    stack_ref[slot, pl.ds((1 - core) * half, half), :] = sibling[...]
+
+
+def block_kernel(product_ref, a1, a2, a3, b1, b2, b3, block_ref, message_ref):
     core, y, mine, _ = spots()
-    size, half = (product_ref.shape[0], far.shape[0])
+    size = product_ref.shape[0]
     block_ref[mine] = product_ref[...]
-    block_ref[mine ^ (1 + core)] = near[...]
-    block_ref[mine ^ (2 - core)] = near_sibling[...]
-    block_ref[mine ^ 3, pl.ds(core * half, half), :] = far[...]
-    block_ref[mine ^ 3, pl.ds((1 - core) * half, half), :] = far_sibling[...]
+    for flip, (own, sibling) in enumerate(((a1, b1), (a2, b2), (a3, b3)), 1):
+        put_halves(block_ref, mine ^ flip, own, sibling, core)
     eye = diagonal(size)
     ones = jnp.ones((1, size), jnp.float32)
 
@@ -328,12 +332,8 @@
     quad, quad_product, half_product = call(
         quad_kernel, out_shape=(shape(QUAD, size, size), whole, half), name="quad"
     )(kernel, near, other_core(near), far, other_core(far))
-    near, far = exchange(
-        quad_product,
-        half_product,
-        lambda x, c, y, z: (x, y ^ 1, z) if c else (x, y, z ^ 6),
-        lambda x, y, z: (x, y ^ 1, z ^ 6),
-    )
+    across = lax.ppermute(half_product, "clique", along_clique(lambda y, z: (y, z ^ 6)))
+    beside = lax.ppermute(half_product, "clique", along_clique(lambda y, z: (y ^ 1, z)))
     counts, quad = lax.optimization_barrier((counts, quad))
     chip_counts, half_counts = call(chip_kernel, out_shape=(whole, half), name="chip")(
         counts, other_core(counts)
@@ -344,14 +344,14 @@
         lambda x, c, y, z: (x ^ (1 + 2 * c), y, z),
         lambda x, y, z: (x ^ 2, y, z),
     )
-    near, far, far_counts = lax.optimization_barrier((near, far, far_counts))
-    near_sibling, far_sibling = (other_core(near), other_core(far))
-    near_sibling, far_sibling, near_counts = lax.optimization_barrier(
-        (near_sibling, far_sibling, near_counts)
-    )
+    relayed = lax.ppermute(across, "clique", along_clique(lambda y, z: (y ^ 1, z)))
+    held, beside, far_counts = lax.optimization_barrier((across, beside, far_counts))
+    relayed, near_counts = lax.optimization_barrier((relayed, near_counts))
+    arrived = (held, beside, relayed)
     block, message = call(
         block_kernel, out_shape=(shape(4, size, size), shape(8, size)), name="block"
-    )(quad_product, near, near_sibling, far, far_sibling)
+    )(quad_product, *arrived, *[other_core(value) for value in arrived])
+    message, near_counts = lax.optimization_barrier((message, near_counts))
     joined = call(join_kernel, out_shape=whole, name="join")(near_counts, far_counts)
     arrived = lax.ppermute(message, "clique", along_clique(lambda y, z: (y ^ 2, z)))
     path, known = call(sides_kernel, out_shape=(whole, shape(8, size)), name="sides")(quad, block)

time: 46.5 us -> 45.6 us (0.981)
  starting transfers between devices: 20.9 us -> 18.9 us
  waiting for transfers between devices: 9.73 us -> 10.9 us
    ppermute x3 -> x2, starting transfers between devices: 6.31 us -> 0.52 us  [exchange(): lax.ppermute(half, axes, everywhere(lambda x, c, y, z: far_step(x, y, z)))]
    ppermute x0 -> x3, starting transfers between devices: none -> 5.06 us  [the longest x1 3.59 us: per_device(): lax.ppermute(half_product, 'clique', along_clique(lambda y, z: (y, z ^ 6)))]
    ppermute x0 -> x3, waiting for transfers between devices: none -> 3.33 us  [the longest x1 3.33 us: per_device(): lax.ppermute(half_product, 'clique', along_clique(lambda y, z: (y ^ 1, z)))]
    ppermute x3 -> x2, waiting for transfers between devices: 7.24 us -> 5.31 us  [exchange(): lax.ppermute(half, axes, everywhere(lambda x, c, y, z: far_step(x, y, z)))]
    ppermute x6 -> x7, starting transfers between devices: 4.11 us -> 2.6 us  [other_core(): return lax.ppermute(value, 'dp', along_dp(lambda x, c: (x, 1 - c)))]
    ppermute x3 -> x2, starting transfers between devices: 7.42 us -> 7.83 us  [exchange(): lax.ppermute(whole, axes, everywhere(near_step))]
    ppermute x6 -> x7, waiting for transfers between devices: 2.48 us -> 2.24 us  [other_core(): return lax.ppermute(value, 'dp', along_dp(lambda x, c: (x, 1 - c)))]
  transfers between devices with their start and end apart: 13 -> 15, of which waited for: 4 -> 7; matrix products, arithmetic and copies ran while one was open for 0% -> 0% of each run, Pallas kernels for 25% -> 24%
where the time goes in v12:
time: 45.6 us; the launch traced here: 45.5 us
  starting transfers between devices  18.9 us (41%)
  Pallas kernels  14.9 us (33%)
  waiting for transfers between devices  10.9 us (24%)
  between operations  0.73 us (2%)
    pallas_call x1, Pallas kernels, count_pairs(): pl.pallas_call(functools.partial(count_kernel, part), out_shape=shape(siz...  8.57 us
    ppermute x2, starting transfers between devices, exchange(): lax.ppermute(whole, axes, everywhere(near_step))  7.83 us
    ppermute x2, waiting for transfers between devices, exchange(): lax.ppermute(half, axes, everywhere(lambda x, c, y, z: far_step(x, y, z)))  5.31 us
    ppermute x1, starting transfers between devices, per_device(): lax.ppermute(half_product, 'clique', along_clique(lambda y, z: (y, z ^ 6)))  3.59 us
    ppermute x1, waiting for transfers between devices, per_device(): lax.ppermute(half_product, 'clique', along_clique(lambda y, z: (y ^ 1, z)))  3.33 us
    ppermute x1, starting transfers between devices, per_device(): lax.ppermute(message, 'clique', along_clique(lambda y, z: (y ^ 2, z)))  2.93 us
    ppermute x7, starting transfers between devices, other_core(): return lax.ppermute(value, 'dp', along_dp(lambda x, c: (x, 1 - c)))  2.6 us
    pallas_call x1, Pallas kernels, per_device(): call(sides_kernel, out_shape=(whole, shape(8, size)), name='sides')  2.48 us
  transfers between devices with their start and end apart: 15, of which 7 were waited for; matrix products, arithmetic and copies ran while one was open for 0% of the time, Pallas kernels for 24%

profile of v12, /device:TPU:1, one launch (start us, length us, event | category | flops | bytes accessed | tf_op | source)
XLA Modules:
  0.0 45.5 jit_solution(9981547532357656856)
XLA Ops:
  0.6 1.1 %read.1 = (s32[33]{0:T(128)S(1)}, f32[256,256]{1,0:T(8,128)S(1)}, f32[128,256]{1,0:T(8,128)S(1)}) custom-call(s32[33]{0:T(128)} %order_hbm.1, f32[256,256]{1,0:T(8,128)} %bitcast.4), custom_call_target="tpu_custom_call" | custom-call | tf_op jit(solution)/shard_map/read/pallas_call | solution.py:313
  1.7 5.3 %collective-permute-start = (f32[256,256]{1,0:T(8,128)S(1)}, f32[256,256]{1,0:T(8,128)S(1)}, u32[]{:S(2)}, u32[]{:S(2)}) collective-permute-start(f32[256,256]{1,0:T(8,128)S(1)} %get-tuple-element.28.kernel_ref), channel_id=1, source_target_pairs={{0,1},{1,0},{2,3},{3,2},{4,5},{5,4},{6,7},{7,6},{8,9},{9,8},{10,11... | collective-permute-start | bytes 786440 | tf_op jit(solution)/shard_map/ppermute | solution.py:301
  7.0 0.0 collective-permute-start.1
  7.0 0.0 copy-start
  7.0 0.0 copy-start.1
  7.0 8.6 %counts.1.own_ref = f32[256,256]{1,0:T(8,128)S(1)} custom-call(s32[33]{0:T(128)S(1)} %get-tuple-element.30.order_ref, s32[33,65536]{1,0:T(8,128)} %right_ref.1, s32[33,65536]{1,0:T(8,128)} %right_ref.1), custom_call_target="tpu_custom_call" | custom-call | tf_op jit(solution)/shard_map/counts/pallas_call | solution.py:272
  15.5 2.2 %collective-permute-done.1.far = f32[128,256]{1,0:T(8,128)S(1)} collective-permute-done((f32[128,256]{1,0:T(8,128)S(1)}, f32[128,256]{1,0:T(8,128)S(1)}, u32[]{:S(2)}, u32[]{:S(2)}) %collective-permute-start.1) | collective-permute-done | bytes 131104 | tf_op jit(solution)/shard_map/ppermute | solution.py:302
  17.8 0.0 collective-permute-done.near
  17.8 0.0 collective-permute-start.2
  17.8 0.5 %collective-permute-start.3 = (f32[128,256]{1,0:T(8,128)S(1)}, f32[128,256]{1,0:T(8,128)S(1)}, u32[]{:S(2)}, u32[]{:S(2)}) collective-permute-start(f32[128,256]{1,0:T(8,128)S(1)} %collective-permute-done.1.far), channel_id=1, source_target_pairs={{0,32},{32,0},{64,96},{96,64},{128,160},{160,128},{192,224},{224,1... | collective-permute-start | bytes 393224 | tf_op jit(solution)/shard_map/ppermute | solution.py:30
  18.3 1.2 %collective-permute-done.3.far_sibling = f32[128,256]{1,0:T(8,128)S(1)} collective-permute-done((f32[128,256]{1,0:T(8,128)S(1)}, f32[128,256]{1,0:T(8,128)S(1)}, u32[]{:S(2)}, u32[]{:S(2)}) %collective-permute-start.3) | collective-permute-done | bytes 131104 | tf_op jit(solution)/shard_map/ppermute | solution.py:30
  19.5 0.0 collective-permute-done.2.near_sibling
  19.5 1.0 %quad.1 = (f32[4,256,256]{2,1,0:T(8,128)S(1)}, f32[256,256]{1,0:T(8,128)S(1)}, f32[128,256]{1,0:T(8,128)S(1)}) custom-call(f32[256,256]{1,0:T(8,128)S(1)} %get-tuple-element.28.kernel_ref, f32[256,256]{1,0:T(8,128)S(1)} %collective-permute-done.near, f32[256,256]{1,0:T(8,128)S(1)} %collective-permute-done.2.near_sibling, ...), custom_call_target="tpu_custom_call" | custom-call | tf_op jit(solution)/shard_map/quad/pallas_call | solution.py:332
  20.5 0.2 collective-permute-start.6
  20.7 3.6 %collective-permute-start.4 = (f32[128,256]{1,0:T(8,128)S(1)}, f32[128,256]{1,0:T(8,128)S(1)}, u32[]{:S(2)}, u32[]{:S(2)}) collective-permute-start(f32[128,256]{1,0:T(8,128)S(1)} %get-tuple-element.37), channel_id=1, source_target_pairs={{0,6},{1,7},{2,4},{3,5},{4,2},{5,3},{6,0},{7,1},{8,14},{9,15},{10,... | collective-permute-start | bytes 393224 | tf_op jit(solution)/shard_map/ppermute | solution.py:335
  24.3 0.0 collective-permute-done.6.sibling_ref
  24.4 2.6 %collective-permute-start.9 = (f32[256,256]{1,0:T(8,128)S(1)}, f32[256,256]{1,0:T(8,128)S(1)}, u32[]{:S(2)}, u32[]{:S(2)}) collective-permute-start(f32[256,256]{1,0:T(8,128)S(1)} %get-tuple-element.42.chip_ref), channel_id=1, source_target_pairs={{0,64},{1,65},{2,66},{3,67},{4,68},{5,69},{6,70},{7,71},{8,72},{9,... | collective-permute-start | bytes 786440 | tf_op jit(solution)/shard_map/ppermute | solution.py:301
  27.0 1.3 %collective-permute-start.5 = (f32[128,256]{1,0:T(8,128)S(1)}, f32[128,256]{1,0:T(8,128)S(1)}, u32[]{:S(2)}, u32[]{:S(2)}) collective-permute-start(f32[128,256]{1,0:T(8,128)S(1)} %get-tuple-element.37), channel_id=1, source_target_pairs={{0,8},{1,9},{2,10},{3,11},{4,12},{5,13},{6,14},{7,15},{8,0},{9,1},... | collective-permute-start | bytes 393224 | tf_op jit(solution)/shard_map/ppermute | solution.py:336
  28.3 0.5 %collective-permute-start.7 = (f32[128,256]{1,0:T(8,128)S(1)}, f32[128,256]{1,0:T(8,128)S(1)}, u32[]{:S(2)}, u32[]{:S(2)}) collective-permute-start(f32[128,256]{1,0:T(8,128)S(1)} %get-tuple-element.39), channel_id=1, source_target_pairs={{0,128},{1,129},{2,130},{3,131},{4,132},{5,133},{6,134},{7,135},{8... | collective-permute-start | bytes 393224 | tf_op jit(solution)/shard_map/ppermute | solution.py:302
  28.8 0.0 collective-permute-done.4.a1
  28.8 0.2 collective-permute-start.8
  28.9 3.3 %collective-permute-done.5.a2 = f32[128,256]{1,0:T(8,128)S(1)} collective-permute-done((f32[128,256]{1,0:T(8,128)S(1)}, f32[128,256]{1,0:T(8,128)S(1)}, u32[]{:S(2)}, u32[]{:S(2)}) %collective-permute-start.5) | collective-permute-done | bytes 131104 | tf_op jit(solution)/shard_map/ppermute | solution.py:336
  32.3 3.1 %collective-permute-done.7.far_ref = f32[128,256]{1,0:T(8,128)S(1)} collective-permute-done((f32[128,256]{1,0:T(8,128)S(1)}, f32[128,256]{1,0:T(8,128)S(1)}, u32[]{:S(2)}, u32[]{:S(2)}) %collective-permute-start.7) | collective-permute-done | bytes 131104 | tf_op jit(solution)/shard_map/ppermute | solution.py:302
  35.3 0.9 %collective-permute-start.10 = (f32[128,256]{1,0:T(8,128)S(1)}, f32[128,256]{1,0:T(8,128)S(1)}, u32[]{:S(2)}, u32[]{:S(2)}) collective-permute-start(f32[128,256]{1,0:T(8,128)S(1)} %collective-permute-done.4.a1), channel_id=1, source_target_pairs={{0,32},{32,0},{64,96},{96,64},{128,160},{160,128},{192,224},{224,1... | collective-permute-start | bytes 393224 | tf_op jit(solution)/shard_map/ppermute | solution.py:30
  36.3 0.0 collective-permute-start.11
  36.3 0.0 collective-permute-done.8.a3
  36.3 0.0 collective-permute-done.9.near_ref
  36.3 0.5 %collective-permute-start.12 = (f32[128,256]{1,0:T(8,128)S(1)}, f32[128,256]{1,0:T(8,128)S(1)}, u32[]{:S(2)}, u32[]{:S(2)}) collective-permute-start(f32[128,256]{1,0:T(8,128)S(1)} %collective-permute-done.8.a3), channel_id=1, source_target_pairs={{0,32},{32,0},{64,96},{96,64},{128,160},{160,128},{192,224},{224,1... | collective-permute-start | bytes 393224 | tf_op jit(solution)/shard_map/ppermute | solution.py:30
  36.8 0.5 %collective-permute-done.10.b1 = f32[128,256]{1,0:T(8,128)S(1)} collective-permute-done((f32[128,256]{1,0:T(8,128)S(1)}, f32[128,256]{1,0:T(8,128)S(1)}, u32[]{:S(2)}, u32[]{:S(2)}) %collective-permute-start.10) | collective-permute-done | bytes 131104 | tf_op jit(solution)/shard_map/ppermute | solution.py:30
  37.3 0.4 collective-permute-done.11.b2
  37.6 0.2 collective-permute-done.12.b3
  37.8 0.6 %block.1 = (f32[4,256,256]{2,1,0:T(8,128)S(1)}, f32[8,256]{1,0:T(8,128)S(1)}) custom-call(f32[256,256]{1,0:T(8,128)S(1)} %get-tuple-element.36.product_ref, f32[128,256]{1,0:T(8,128)S(1)} %collective-permute-done.4.a1, f32[128,256]{1,0:T(8,128)S(1)} %collective-permute-done.5.a2, f32[128,256]{1,0:T(8,128)S(1)} %collective-permute-done.8.a3, ...), custom_call_target="tpu_custom_call" | custom-call | tf_op jit(solution)/shard_map/block/pallas_call | solution.py:351
  38.4 0.4 collective-permute-start.14
  38.9 2.9 %collective-permute-start.13 = (f32[8,256]{1,0:T(8,128)S(1)}, f32[8,256]{1,0:T(8,128)S(1)}, u32[]{:S(2)}, u32[]{:S(2)}) collective-permute-start(f32[8,256]{1,0:T(8,128)S(1)} %get-tuple-element.49), channel_id=1, source_target_pairs={{0,16},{1,17},{2,18},{3,19},{4,20},{5,21},{6,22},{7,23},{8,24},{9,... | collective-permute-start | bytes 24584 | tf_op jit(solution)/shard_map/ppermute | solution.py:356
  41.8 2.5 %sides.1 = (f32[256,256]{1,0:T(8,128)S(1)}, f32[8,256]{1,0:T(8,128)S(1)}) custom-call(f32[4,256,256]{2,1,0:T(8,128)S(1)} %get-tuple-element.35.quad_ref, f32[4,256,256]{2,1,0:T(8,128)S(1)} %get-tuple-element.44.block_ref), custom_call_target="tpu_custom_call" | custom-call | tf_op jit(solution)/shard_map/sides/pallas_call | solution.py:357
  44.3 0.0 collective-permute-done.13.message_ref
  44.3 0.0 collective-permute-done.14.sibling_join_ref
  44.3 0.0 copy-done
  44.3 0.0 copy-done.1
  44.3 1.2 %final.1 = (f32[256,256]{1,0:T(8,128)}, f32[256,256]{1,0:T(8,128)}) custom-call(f32[256,256]{1,0:T(8,128)S(1)} %bitcast.5, f32[256,256]{1,0:T(8,128)S(1)} %bitcast.6, f32[256,256]{1,0:T(8,128)S(1)} %get-tuple-element.28.kernel_ref, f32[256,256]{1,0:T(8,128)S(1)} %get-tuple-element.45.path_ref, f32[8,256]{1,0:T(8,128)S(1)} %get-tuple-element.46.known_ref, ...), custom_call_target="tpu_custom_call" | custom-call | tf_op jit(solution)/shard_map/final/pallas_call | solution.py:359
  (2 shorter events, 0.1 us)
Async XLA Ops:
  1.7 16.1 %collective-permute-start = (f32[256,256]{1,0:T(8,128)S(1)}, f32[256,256]{1,0:T(8,128)S(1)}, u32[]{:S(2)}, u32[]{:S(2)}) collective-permute-start(f32[256,256]{1,0:T(8,128)S(1)} %get-tuple-element.28.kernel_ref), channel_id=1, source_target_pairs={{0,1},{1,0},{2,3},{3,2},{4,5},{5,4},{6,7},{7,6},{8,9},{9,8},{10,11... | collective-permute-start | bytes 786440 | tf_op jit(solution)/shard_map/ppermute | solution.py:301
  7.0 10.8 %collective-permute-start.1 = (f32[128,256]{1,0:T(8,128)S(1)}, f32[128,256]{1,0:T(8,128)S(1)}, u32[]{:S(2)}, u32[]{:S(2)}) collective-permute-start(f32[128,256]{1,0:T(8,128)S(1)} %get-tuple-element.29), channel_id=1, source_target_pairs={{0,2},{1,3},{2,0},{3,1},{4,6},{5,7},{6,4},{7,5},{8,10},{9,11},{10,... | collective-permute-start | bytes 393224 | tf_op jit(solution)/shard_map/ppermute | solution.py:302
  7.0 37.3 %copy-start = (f32[1,256,256]{2,1,0:T(8,128)S(1)}, f32[1,256,256]{2,1,0:T(8,128)}, u32[]{:S(2)}) copy-start(f32[1,256,256]{2,1,0:T(8,128)} %param.6) | copy-start | bytes 786436
  7.0 37.3 %copy-start.1 = (f32[1,256,256]{2,1,0:T(8,128)S(1)}, f32[1,256,256]{2,1,0:T(8,128)}, u32[]{:S(2)}) copy-start(f32[1,256,256]{2,1,0:T(8,128)} %param.7) | copy-start | bytes 786436
  17.8 1.7 %collective-permute-start.2 = (f32[256,256]{1,0:T(8,128)S(1)}, f32[256,256]{1,0:T(8,128)S(1)}, u32[]{:S(2)}, u32[]{:S(2)}) collective-permute-start(f32[256,256]{1,0:T(8,128)S(1)} %collective-permute-done.near), channel_id=1, source_target_pairs={{0,32},{32,0},{64,96},{96,64},{128,160},{160,128},{192,224},{224,1... | collective-permute-start | bytes 786440 | tf_op jit(solution)/shard_map/ppermute | solution.py:30
  17.8 1.7 %collective-permute-start.3 = (f32[128,256]{1,0:T(8,128)S(1)}, f32[128,256]{1,0:T(8,128)S(1)}, u32[]{:S(2)}, u32[]{:S(2)}) collective-permute-start(f32[128,256]{1,0:T(8,128)S(1)} %collective-permute-done.1.far), channel_id=1, source_target_pairs={{0,32},{32,0},{64,96},{96,64},{128,160},{160,128},{192,224},{224,1... | collective-permute-start | bytes 393224 | tf_op jit(solution)/shard_map/ppermute | solution.py:30
  20.5 3.8 %collective-permute-start.6 = (f32[256,256]{1,0:T(8,128)S(1)}, f32[256,256]{1,0:T(8,128)S(1)}, u32[]{:S(2)}, u32[]{:S(2)}) collective-permute-start(f32[256,256]{1,0:T(8,128)S(1)} %counts.1.own_ref), channel_id=1, source_target_pairs={{0,32},{32,0},{64,96},{96,64},{128,160},{160,128},{192,224},{224,1... | collective-permute-start | bytes 786440 | tf_op jit(solution)/shard_map/ppermute | solution.py:30
  20.7 8.0 %collective-permute-start.4 = (f32[128,256]{1,0:T(8,128)S(1)}, f32[128,256]{1,0:T(8,128)S(1)}, u32[]{:S(2)}, u32[]{:S(2)}) collective-permute-start(f32[128,256]{1,0:T(8,128)S(1)} %get-tuple-element.37), channel_id=1, source_target_pairs={{0,6},{1,7},{2,4},{3,5},{4,2},{5,3},{6,0},{7,1},{8,14},{9,15},{10,... | collective-permute-start | bytes 393224 | tf_op jit(solution)/shard_map/ppermute | solution.py:335
  24.4 11.9 %collective-permute-start.9 = (f32[256,256]{1,0:T(8,128)S(1)}, f32[256,256]{1,0:T(8,128)S(1)}, u32[]{:S(2)}, u32[]{:S(2)}) collective-permute-start(f32[256,256]{1,0:T(8,128)S(1)} %get-tuple-element.42.chip_ref), channel_id=1, source_target_pairs={{0,64},{1,65},{2,66},{3,67},{4,68},{5,69},{6,70},{7,71},{8,72},{9,... | collective-permute-start | bytes 786440 | tf_op jit(solution)/shard_map/ppermute | solution.py:301
  27.0 5.3 %collective-permute-start.5 = (f32[128,256]{1,0:T(8,128)S(1)}, f32[128,256]{1,0:T(8,128)S(1)}, u32[]{:S(2)}, u32[]{:S(2)}) collective-permute-start(f32[128,256]{1,0:T(8,128)S(1)} %get-tuple-element.37), channel_id=1, source_target_pairs={{0,8},{1,9},{2,10},{3,11},{4,12},{5,13},{6,14},{7,15},{8,0},{9,1},... | collective-permute-start | bytes 393224 | tf_op jit(solution)/shard_map/ppermute | solution.py:336
  28.3 7.1 %collective-permute-start.7 = (f32[128,256]{1,0:T(8,128)S(1)}, f32[128,256]{1,0:T(8,128)S(1)}, u32[]{:S(2)}, u32[]{:S(2)}) collective-permute-start(f32[128,256]{1,0:T(8,128)S(1)} %get-tuple-element.39), channel_id=1, source_target_pairs={{0,128},{1,129},{2,130},{3,131},{4,132},{5,133},{6,134},{7,135},{8... | collective-permute-start | bytes 393224 | tf_op jit(solution)/shard_map/ppermute | solution.py:302
  28.8 7.5 %collective-permute-start.8 = (f32[128,256]{1,0:T(8,128)S(1)}, f32[128,256]{1,0:T(8,128)S(1)}, u32[]{:S(2)}, u32[]{:S(2)}) collective-permute-start(f32[128,256]{1,0:T(8,128)S(1)} %collective-permute-done.4.a1), channel_id=1, source_target_pairs={{0,8},{1,9},{2,10},{3,11},{4,12},{5,13},{6,14},{7,15},{8,0},{9,1},... | collective-permute-start | bytes 393224 | tf_op jit(solution)/shard_map/ppermute | solution.py:347
  35.3 1.9 %collective-permute-start.10 = (f32[128,256]{1,0:T(8,128)S(1)}, f32[128,256]{1,0:T(8,128)S(1)}, u32[]{:S(2)}, u32[]{:S(2)}) collective-permute-start(f32[128,256]{1,0:T(8,128)S(1)} %collective-permute-done.4.a1), channel_id=1, source_target_pairs={{0,32},{32,0},{64,96},{96,64},{128,160},{160,128},{192,224},{224,1... | collective-permute-start | bytes 393224 | tf_op jit(solution)/shard_map/ppermute | solution.py:30
  36.3 1.3 %collective-permute-start.11 = (f32[128,256]{1,0:T(8,128)S(1)}, f32[128,256]{1,0:T(8,128)S(1)}, u32[]{:S(2)}, u32[]{:S(2)}) collective-permute-start(f32[128,256]{1,0:T(8,128)S(1)} %collective-permute-done.5.a2), channel_id=1, source_target_pairs={{0,32},{32,0},{64,96},{96,64},{128,160},{160,128},{192,224},{224,1... | collective-permute-start | bytes 393224 | tf_op jit(solution)/shard_map/ppermute | solution.py:30
  36.3 1.5 %collective-permute-start.12 = (f32[128,256]{1,0:T(8,128)S(1)}, f32[128,256]{1,0:T(8,128)S(1)}, u32[]{:S(2)}, u32[]{:S(2)}) collective-permute-start(f32[128,256]{1,0:T(8,128)S(1)} %collective-permute-done.8.a3), channel_id=1, source_target_pairs={{0,32},{32,0},{64,96},{96,64},{128,160},{160,128},{192,224},{224,1... | collective-permute-start | bytes 393224 | tf_op jit(solution)/shard_map/ppermute | solution.py:30
  38.4 5.8 %collective-permute-start.14 = (f32[256,256]{1,0:T(8,128)S(1)}, f32[256,256]{1,0:T(8,128)S(1)}, u32[]{:S(2)}, u32[]{:S(2)}) collective-permute-start(f32[256,256]{1,0:T(8,128)S(1)} %join.1.join_ref), channel_id=1, source_target_pairs={{0,32},{32,0},{64,96},{96,64},{128,160},{160,128},{192,224},{224,1... | collective-permute-start | bytes 786440 | tf_op jit(solution)/shard_map/ppermute | solution.py:30
  38.9 5.4 %collective-permute-start.13 = (f32[8,256]{1,0:T(8,128)S(1)}, f32[8,256]{1,0:T(8,128)S(1)}, u32[]{:S(2)}, u32[]{:S(2)}) collective-permute-start(f32[8,256]{1,0:T(8,128)S(1)} %get-tuple-element.49), channel_id=1, source_target_pairs={{0,16},{1,17},{2,18},{3,19},{4,20},{5,21},{6,22},{7,23},{8,24},{9,... | collective-permute-start | bytes 24584 | tf_op jit(solution)/shard_map/ppermute | solution.py:356

commit v13 on v12

--- a/solution.py
+++ b/solution.py
@@ -329,14 +329,15 @@
     )
     counts = count_pairs(order, table_rows, size)
     near, far, counts = lax.optimization_barrier((near, far, counts))
+    sibling_counts = other_core(counts)
     quad, quad_product, half_product = call(
         quad_kernel, out_shape=(shape(QUAD, size, size), whole, half), name="quad"
     )(kernel, near, other_core(near), far, other_core(far))
     across = lax.ppermute(half_product, "clique", along_clique(lambda y, z: (y, z ^ 6)))
     beside = lax.ppermute(half_product, "clique", along_clique(lambda y, z: (y ^ 1, z)))
-    counts, quad = lax.optimization_barrier((counts, quad))
+    counts, sibling_counts, quad = lax.optimization_barrier((counts, sibling_counts, quad))
     chip_counts, half_counts = call(chip_kernel, out_shape=(whole, half), name="chip")(
-        counts, other_core(counts)
+        counts, sibling_counts
     )
     near_counts, far_counts = exchange(
         chip_counts,

time: 45.6 us -> 45.8 us (level)
  transfers between devices with their start and end apart: 15 -> 15, of which waited for: 7 -> 7; matrix products, arithmetic and copies ran while one was open for 0% -> 0% of each run, Pallas kernels for 24% -> 26%
where the time goes in v13:
time: 45.8 us; the launch traced here: 45.7 us
  starting transfers between devices  19.2 us (42%)
  Pallas kernels  14.9 us (33%)
  waiting for transfers between devices  10.8 us (24%)
  between operations  0.74 us (2%)
    pallas_call x1, Pallas kernels, count_pairs(): pl.pallas_call(functools.partial(count_kernel, part), out_shape=shape(siz...  8.57 us
    ppermute x2, starting transfers between devices, exchange(): lax.ppermute(whole, axes, everywhere(near_step))  7.83 us
    ppermute x2, waiting for transfers between devices, exchange(): lax.ppermute(half, axes, everywhere(lambda x, c, y, z: far_step(x, y, z)))  5.24 us
    ppermute x1, starting transfers between devices, per_device(): lax.ppermute(half_product, 'clique', along_clique(lambda y, z: (y, z ^ 6)))  3.43 us
    ppermute x1, waiting for transfers between devices, per_device(): lax.ppermute(half_product, 'clique', along_clique(lambda y, z: (y ^ 1, z)))  2.98 us
    ppermute x1, starting transfers between devices, per_device(): lax.ppermute(message, 'clique', along_clique(lambda y, z: (y ^ 2, z)))  2.93 us
    ppermute x7, starting transfers between devices, other_core(): return lax.ppermute(value, 'dp', along_dp(lambda x, c: (x, 1 - c)))  2.62 us
    ppermute x7, waiting for transfers between devices, other_core(): return lax.ppermute(value, 'dp', along_dp(lambda x, c: (x, 1 - c)))  2.61 us
  transfers between devices with their start and end apart: 15, of which 7 were waited for; matrix products, arithmetic and copies ran while one was open for 0% of the time, Pallas kernels for 26%

profile of v13, /device:TPU:1, one launch (start us, length us, event | category | flops | bytes accessed | tf_op | source)
XLA Modules:
  0.0 45.7 jit_solution(11287509976111708602)
XLA Ops:
  0.6 1.1 %read.1 = (s32[33]{0:T(128)S(1)}, f32[256,256]{1,0:T(8,128)S(1)}, f32[128,256]{1,0:T(8,128)S(1)}) custom-call(s32[33]{0:T(128)} %order_hbm.1, f32[256,256]{1,0:T(8,128)} %bitcast.4), custom_call_target="tpu_custom_call" | custom-call | tf_op jit(solution)/shard_map/read/pallas_call | solution.py:313
  1.7 5.3 %collective-permute-start = (f32[256,256]{1,0:T(8,128)S(1)}, f32[256,256]{1,0:T(8,128)S(1)}, u32[]{:S(2)}, u32[]{:S(2)}) collective-permute-start(f32[256,256]{1,0:T(8,128)S(1)} %get-tuple-element.29.kernel_ref), channel_id=1, source_target_pairs={{0,1},{1,0},{2,3},{3,2},{4,5},{5,4},{6,7},{7,6},{8,9},{9,8},{10,11... | collective-permute-start | bytes 786440 | tf_op jit(solution)/shard_map/ppermute | solution.py:301
  7.0 0.0 collective-permute-start.1
  7.0 0.0 copy-start
  7.0 0.0 copy-start.1
  7.0 8.6 %counts.1.own_ref = f32[256,256]{1,0:T(8,128)S(1)} custom-call(s32[33]{0:T(128)S(1)} %get-tuple-element.31.order_ref, s32[33,65536]{1,0:T(8,128)} %right_ref.1, s32[33,65536]{1,0:T(8,128)} %right_ref.1), custom_call_target="tpu_custom_call" | custom-call | tf_op jit(solution)/shard_map/counts/pallas_call | solution.py:272
  15.5 2.2 %collective-permute-done.1.far = f32[128,256]{1,0:T(8,128)S(1)} collective-permute-done((f32[128,256]{1,0:T(8,128)S(1)}, f32[128,256]{1,0:T(8,128)S(1)}, u32[]{:S(2)}, u32[]{:S(2)}) %collective-permute-start.1) | collective-permute-done | bytes 131104 | tf_op jit(solution)/shard_map/ppermute | solution.py:302
  17.8 0.0 collective-permute-done.near
  17.8 0.0 collective-permute-start.3
  17.8 0.5 %collective-permute-start.2 = (f32[256,256]{1,0:T(8,128)S(1)}, f32[256,256]{1,0:T(8,128)S(1)}, u32[]{:S(2)}, u32[]{:S(2)}) collective-permute-start(f32[256,256]{1,0:T(8,128)S(1)} %counts.1.own_ref), channel_id=1, source_target_pairs={{0,32},{32,0},{64,96},{96,64},{128,160},{160,128},{192,224},{224,1... | collective-permute-start | bytes 786440 | tf_op jit(solution)/shard_map/ppermute | solution.py:30
  18.3 0.0 collective-permute-start.4
  18.3 1.6 %collective-permute-done.4.far_sibling = f32[128,256]{1,0:T(8,128)S(1)} collective-permute-done((f32[128,256]{1,0:T(8,128)S(1)}, f32[128,256]{1,0:T(8,128)S(1)}, u32[]{:S(2)}, u32[]{:S(2)}) %collective-permute-start.4) | collective-permute-done | bytes 131104 | tf_op jit(solution)/shard_map/ppermute | solution.py:30
  19.9 0.0 collective-permute-done.3.near_sibling
  19.9 1.0 %quad.1 = (f32[4,256,256]{2,1,0:T(8,128)S(1)}, f32[256,256]{1,0:T(8,128)S(1)}, f32[128,256]{1,0:T(8,128)S(1)}) custom-call(f32[256,256]{1,0:T(8,128)S(1)} %get-tuple-element.29.kernel_ref, f32[256,256]{1,0:T(8,128)S(1)} %collective-permute-done.near, f32[256,256]{1,0:T(8,128)S(1)} %collective-permute-done.3.near_sibling, ...), custom_call_target="tpu_custom_call" | custom-call | tf_op jit(solution)/shard_map/quad/pallas_call | solution.py:333
  20.9 0.0 collective-permute-done.2.sibling_ref
  20.9 3.4 %collective-permute-start.5 = (f32[128,256]{1,0:T(8,128)S(1)}, f32[128,256]{1,0:T(8,128)S(1)}, u32[]{:S(2)}, u32[]{:S(2)}) collective-permute-start(f32[128,256]{1,0:T(8,128)S(1)} %get-tuple-element.38), channel_id=1, source_target_pairs={{0,6},{1,7},{2,4},{3,5},{4,2},{5,3},{6,0},{7,1},{8,14},{9,15},{10,... | collective-permute-start | bytes 393224 | tf_op jit(solution)/shard_map/ppermute | solution.py:336
  24.4 2.6 %collective-permute-start.9 = (f32[256,256]{1,0:T(8,128)S(1)}, f32[256,256]{1,0:T(8,128)S(1)}, u32[]{:S(2)}, u32[]{:S(2)}) collective-permute-start(f32[256,256]{1,0:T(8,128)S(1)} %get-tuple-element.44.chip_ref), channel_id=1, source_target_pairs={{0,64},{1,65},{2,66},{3,67},{4,68},{5,69},{6,70},{7,71},{8,72},{9,... | collective-permute-start | bytes 786440 | tf_op jit(solution)/shard_map/ppermute | solution.py:301
  27.0 1.3 %collective-permute-start.6 = (f32[128,256]{1,0:T(8,128)S(1)}, f32[128,256]{1,0:T(8,128)S(1)}, u32[]{:S(2)}, u32[]{:S(2)}) collective-permute-start(f32[128,256]{1,0:T(8,128)S(1)} %get-tuple-element.38), channel_id=1, source_target_pairs={{0,8},{1,9},{2,10},{3,11},{4,12},{5,13},{6,14},{7,15},{8,0},{9,1},... | collective-permute-start | bytes 393224 | tf_op jit(solution)/shard_map/ppermute | solution.py:337
  28.3 0.5 %collective-permute-start.7 = (f32[128,256]{1,0:T(8,128)S(1)}, f32[128,256]{1,0:T(8,128)S(1)}, u32[]{:S(2)}, u32[]{:S(2)}) collective-permute-start(f32[128,256]{1,0:T(8,128)S(1)} %get-tuple-element.41), channel_id=1, source_target_pairs={{0,128},{1,129},{2,130},{3,131},{4,132},{5,133},{6,134},{7,135},{8... | collective-permute-start | bytes 393224 | tf_op jit(solution)/shard_map/ppermute | solution.py:302
  28.8 0.0 collective-permute-done.5.a1
  28.8 0.6 %collective-permute-start.8 = (f32[128,256]{1,0:T(8,128)S(1)}, f32[128,256]{1,0:T(8,128)S(1)}, u32[]{:S(2)}, u32[]{:S(2)}) collective-permute-start(f32[128,256]{1,0:T(8,128)S(1)} %collective-permute-done.5.a1), channel_id=1, source_target_pairs={{0,8},{1,9},{2,10},{3,11},{4,12},{5,13},{6,14},{7,15},{8,0},{9,1},... | collective-permute-start | bytes 393224 | tf_op jit(solution)/shard_map/ppermute | solution.py:348
  29.4 3.0 %collective-permute-done.6.a2 = f32[128,256]{1,0:T(8,128)S(1)} collective-permute-done((f32[128,256]{1,0:T(8,128)S(1)}, f32[128,256]{1,0:T(8,128)S(1)}, u32[]{:S(2)}, u32[]{:S(2)}) %collective-permute-start.6) | collective-permute-done | bytes 131104 | tf_op jit(solution)/shard_map/ppermute | solution.py:337
  32.3 3.0 %collective-permute-done.7.far_ref = f32[128,256]{1,0:T(8,128)S(1)} collective-permute-done((f32[128,256]{1,0:T(8,128)S(1)}, f32[128,256]{1,0:T(8,128)S(1)}, u32[]{:S(2)}, u32[]{:S(2)}) %collective-permute-start.7) | collective-permute-done | bytes 131104 | tf_op jit(solution)/shard_map/ppermute | solution.py:302
  35.3 1.2 %collective-permute-start.10 = (f32[128,256]{1,0:T(8,128)S(1)}, f32[128,256]{1,0:T(8,128)S(1)}, u32[]{:S(2)}, u32[]{:S(2)}) collective-permute-start(f32[128,256]{1,0:T(8,128)S(1)} %collective-permute-done.5.a1), channel_id=1, source_target_pairs={{0,32},{32,0},{64,96},{96,64},{128,160},{160,128},{192,224},{224,1... | collective-permute-start | bytes 393224 | tf_op jit(solution)/shard_map/ppermute | solution.py:30
  36.5 0.0 collective-permute-start.11
  36.5 0.0 collective-permute-done.9.near_ref
  36.5 0.0 collective-permute-done.8.a3
  36.5 0.5 %collective-permute-start.12 = (f32[128,256]{1,0:T(8,128)S(1)}, f32[128,256]{1,0:T(8,128)S(1)}, u32[]{:S(2)}, u32[]{:S(2)}) collective-permute-start(f32[128,256]{1,0:T(8,128)S(1)} %collective-permute-done.8.a3), channel_id=1, source_target_pairs={{0,32},{32,0},{64,96},{96,64},{128,160},{160,128},{192,224},{224,1... | collective-permute-start | bytes 393224 | tf_op jit(solution)/shard_map/ppermute | solution.py:30
  37.0 0.5 %collective-permute-done.10.b1 = f32[128,256]{1,0:T(8,128)S(1)} collective-permute-done((f32[128,256]{1,0:T(8,128)S(1)}, f32[128,256]{1,0:T(8,128)S(1)}, u32[]{:S(2)}, u32[]{:S(2)}) %collective-permute-start.10) | collective-permute-done | bytes 131104 | tf_op jit(solution)/shard_map/ppermute | solution.py:30
  37.5 0.4 collective-permute-done.11.b2
  37.9 0.2 collective-permute-done.12.b3
  38.1 0.6 %block.1 = (f32[4,256,256]{2,1,0:T(8,128)S(1)}, f32[8,256]{1,0:T(8,128)S(1)}) custom-call(f32[256,256]{1,0:T(8,128)S(1)} %get-tuple-element.37.product_ref, f32[128,256]{1,0:T(8,128)S(1)} %collective-permute-done.5.a1, f32[128,256]{1,0:T(8,128)S(1)} %collective-permute-done.6.a2, f32[128,256]{1,0:T(8,128)S(1)} %collective-permute-done.8.a3, ...), custom_call_target="tpu_custom_call" | custom-call | tf_op jit(solution)/shard_map/block/pallas_call | solution.py:352
  38.7 0.4 collective-permute-start.14
  39.1 2.9 %collective-permute-start.13 = (f32[8,256]{1,0:T(8,128)S(1)}, f32[8,256]{1,0:T(8,128)S(1)}, u32[]{:S(2)}, u32[]{:S(2)}) collective-permute-start(f32[8,256]{1,0:T(8,128)S(1)} %get-tuple-element.51), channel_id=1, source_target_pairs={{0,16},{1,17},{2,18},{3,19},{4,20},{5,21},{6,22},{7,23},{8,24},{9,... | collective-permute-start | bytes 24584 | tf_op jit(solution)/shard_map/ppermute | solution.py:357
  42.0 2.5 %sides.1 = (f32[256,256]{1,0:T(8,128)S(1)}, f32[8,256]{1,0:T(8,128)S(1)}) custom-call(f32[4,256,256]{2,1,0:T(8,128)S(1)} %get-tuple-element.36.quad_ref, f32[4,256,256]{2,1,0:T(8,128)S(1)} %get-tuple-element.46.block_ref), custom_call_target="tpu_custom_call" | custom-call | tf_op jit(solution)/shard_map/sides/pallas_call | solution.py:358
  44.5 0.0 collective-permute-done.13.message_ref
  44.5 0.0 collective-permute-done.14.sibling_join_ref
  44.5 0.0 copy-done
  44.5 0.0 copy-done.1
  44.5 1.2 %final.1 = (f32[256,256]{1,0:T(8,128)}, f32[256,256]{1,0:T(8,128)}) custom-call(f32[256,256]{1,0:T(8,128)S(1)} %bitcast.5, f32[256,256]{1,0:T(8,128)S(1)} %bitcast.6, f32[256,256]{1,0:T(8,128)S(1)} %get-tuple-element.29.kernel_ref, f32[256,256]{1,0:T(8,128)S(1)} %get-tuple-element.47.path_ref, f32[8,256]{1,0:T(8,128)S(1)} %get-tuple-element.48.known_ref, ...), custom_call_target="tpu_custom_call" | custom-call | tf_op jit(solution)/shard_map/final/pallas_call | solution.py:360
  (2 shorter events, 0.1 us)
Async XLA Ops:
  1.7 16.1 %collective-permute-start = (f32[256,256]{1,0:T(8,128)S(1)}, f32[256,256]{1,0:T(8,128)S(1)}, u32[]{:S(2)}, u32[]{:S(2)}) collective-permute-start(f32[256,256]{1,0:T(8,128)S(1)} %get-tuple-element.29.kernel_ref), channel_id=1, source_target_pairs={{0,1},{1,0},{2,3},{3,2},{4,5},{5,4},{6,7},{7,6},{8,9},{9,8},{10,11... | collective-permute-start | bytes 786440 | tf_op jit(solution)/shard_map/ppermute | solution.py:301
  7.0 10.8 %collective-permute-start.1 = (f32[128,256]{1,0:T(8,128)S(1)}, f32[128,256]{1,0:T(8,128)S(1)}, u32[]{:S(2)}, u32[]{:S(2)}) collective-permute-start(f32[128,256]{1,0:T(8,128)S(1)} %get-tuple-element.30), channel_id=1, source_target_pairs={{0,2},{1,3},{2,0},{3,1},{4,6},{5,7},{6,4},{7,5},{8,10},{9,11},{10,... | collective-permute-start | bytes 393224 | tf_op jit(solution)/shard_map/ppermute | solution.py:302
  7.0 37.6 %copy-start = (f32[1,256,256]{2,1,0:T(8,128)S(1)}, f32[1,256,256]{2,1,0:T(8,128)}, u32[]{:S(2)}) copy-start(f32[1,256,256]{2,1,0:T(8,128)} %param.6) | copy-start | bytes 786436
  7.0 37.6 %copy-start.1 = (f32[1,256,256]{2,1,0:T(8,128)S(1)}, f32[1,256,256]{2,1,0:T(8,128)}, u32[]{:S(2)}) copy-start(f32[1,256,256]{2,1,0:T(8,128)} %param.7) | copy-start | bytes 786436
  17.8 2.1 %collective-permute-start.3 = (f32[256,256]{1,0:T(8,128)S(1)}, f32[256,256]{1,0:T(8,128)S(1)}, u32[]{:S(2)}, u32[]{:S(2)}) collective-permute-start(f32[256,256]{1,0:T(8,128)S(1)} %collective-permute-done.near), channel_id=1, source_target_pairs={{0,32},{32,0},{64,96},{96,64},{128,160},{160,128},{192,224},{224,1... | collective-permute-start | bytes 786440 | tf_op jit(solution)/shard_map/ppermute | solution.py:30
  17.8 3.1 %collective-permute-start.2 = (f32[256,256]{1,0:T(8,128)S(1)}, f32[256,256]{1,0:T(8,128)S(1)}, u32[]{:S(2)}, u32[]{:S(2)}) collective-permute-start(f32[256,256]{1,0:T(8,128)S(1)} %counts.1.own_ref), channel_id=1, source_target_pairs={{0,32},{32,0},{64,96},{96,64},{128,160},{160,128},{192,224},{224,1... | collective-permute-start | bytes 786440 | tf_op jit(solution)/shard_map/ppermute | solution.py:30
  18.3 1.6 %collective-permute-start.4 = (f32[128,256]{1,0:T(8,128)S(1)}, f32[128,256]{1,0:T(8,128)S(1)}, u32[]{:S(2)}, u32[]{:S(2)}) collective-permute-start(f32[128,256]{1,0:T(8,128)S(1)} %collective-permute-done.1.far), channel_id=1, source_target_pairs={{0,32},{32,0},{64,96},{96,64},{128,160},{160,128},{192,224},{224,1... | collective-permute-start | bytes 393224 | tf_op jit(solution)/shard_map/ppermute | solution.py:30
  20.9 7.9 %collective-permute-start.5 = (f32[128,256]{1,0:T(8,128)S(1)}, f32[128,256]{1,0:T(8,128)S(1)}, u32[]{:S(2)}, u32[]{:S(2)}) collective-permute-start(f32[128,256]{1,0:T(8,128)S(1)} %get-tuple-element.38), channel_id=1, source_target_pairs={{0,6},{1,7},{2,4},{3,5},{4,2},{5,3},{6,0},{7,1},{8,14},{9,15},{10,... | collective-permute-start | bytes 393224 | tf_op jit(solution)/shard_map/ppermute | solution.py:336
  24.4 12.1 %collective-permute-start.9 = (f32[256,256]{1,0:T(8,128)S(1)}, f32[256,256]{1,0:T(8,128)S(1)}, u32[]{:S(2)}, u32[]{:S(2)}) collective-permute-start(f32[256,256]{1,0:T(8,128)S(1)} %get-tuple-element.44.chip_ref), channel_id=1, source_target_pairs={{0,64},{1,65},{2,66},{3,67},{4,68},{5,69},{6,70},{7,71},{8,72},{9,... | collective-permute-start | bytes 786440 | tf_op jit(solution)/shard_map/ppermute | solution.py:301
  27.0 5.4 %collective-permute-start.6 = (f32[128,256]{1,0:T(8,128)S(1)}, f32[128,256]{1,0:T(8,128)S(1)}, u32[]{:S(2)}, u32[]{:S(2)}) collective-permute-start(f32[128,256]{1,0:T(8,128)S(1)} %get-tuple-element.38), channel_id=1, source_target_pairs={{0,8},{1,9},{2,10},{3,11},{4,12},{5,13},{6,14},{7,15},{8,0},{9,1},... | collective-permute-start | bytes 393224 | tf_op jit(solution)/shard_map/ppermute | solution.py:337
  28.3 7.1 %collective-permute-start.7 = (f32[128,256]{1,0:T(8,128)S(1)}, f32[128,256]{1,0:T(8,128)S(1)}, u32[]{:S(2)}, u32[]{:S(2)}) collective-permute-start(f32[128,256]{1,0:T(8,128)S(1)} %get-tuple-element.41), channel_id=1, source_target_pairs={{0,128},{1,129},{2,130},{3,131},{4,132},{5,133},{6,134},{7,135},{8... | collective-permute-start | bytes 393224 | tf_op jit(solution)/shard_map/ppermute | solution.py:302
  28.8 7.7 %collective-permute-start.8 = (f32[128,256]{1,0:T(8,128)S(1)}, f32[128,256]{1,0:T(8,128)S(1)}, u32[]{:S(2)}, u32[]{:S(2)}) collective-permute-start(f32[128,256]{1,0:T(8,128)S(1)} %collective-permute-done.5.a1), channel_id=1, source_target_pairs={{0,8},{1,9},{2,10},{3,11},{4,12},{5,13},{6,14},{7,15},{8,0},{9,1},... | collective-permute-start | bytes 393224 | tf_op jit(solution)/shard_map/ppermute | solution.py:348
  35.3 2.2 %collective-permute-start.10 = (f32[128,256]{1,0:T(8,128)S(1)}, f32[128,256]{1,0:T(8,128)S(1)}, u32[]{:S(2)}, u32[]{:S(2)}) collective-permute-start(f32[128,256]{1,0:T(8,128)S(1)} %collective-permute-done.5.a1), channel_id=1, source_target_pairs={{0,32},{32,0},{64,96},{96,64},{128,160},{160,128},{192,224},{224,1... | collective-permute-start | bytes 393224 | tf_op jit(solution)/shard_map/ppermute | solution.py:30
  36.5 1.3 %collective-permute-start.11 = (f32[128,256]{1,0:T(8,128)S(1)}, f32[128,256]{1,0:T(8,128)S(1)}, u32[]{:S(2)}, u32[]{:S(2)}) collective-permute-start(f32[128,256]{1,0:T(8,128)S(1)} %collective-permute-done.6.a2), channel_id=1, source_target_pairs={{0,32},{32,0},{64,96},{96,64},{128,160},{160,128},{192,224},{224,1... | collective-permute-start | bytes 393224 | tf_op jit(solution)/shard_map/ppermute | solution.py:30
  36.5 1.5 %collective-permute-start.12 = (f32[128,256]{1,0:T(8,128)S(1)}, f32[128,256]{1,0:T(8,128)S(1)}, u32[]{:S(2)}, u32[]{:S(2)}) collective-permute-start(f32[128,256]{1,0:T(8,128)S(1)} %collective-permute-done.8.a3), channel_id=1, source_target_pairs={{0,32},{32,0},{64,96},{96,64},{128,160},{160,128},{192,224},{224,1... | collective-permute-start | bytes 393224 | tf_op jit(solution)/shard_map/ppermute | solution.py:30
  38.7 5.8 %collective-permute-start.14 = (f32[256,256]{1,0:T(8,128)S(1)}, f32[256,256]{1,0:T(8,128)S(1)}, u32[]{:S(2)}, u32[]{:S(2)}) collective-permute-start(f32[256,256]{1,0:T(8,128)S(1)} %join.1.join_ref), channel_id=1, source_target_pairs={{0,32},{32,0},{64,96},{96,64},{128,160},{160,128},{192,224},{224,1... | collective-permute-start | bytes 786440 | tf_op jit(solution)/shard_map/ppermute | solution.py:30
  39.1 5.4 %collective-permute-start.13 = (f32[8,256]{1,0:T(8,128)S(1)}, f32[8,256]{1,0:T(8,128)S(1)}, u32[]{:S(2)}, u32[]{:S(2)}) collective-permute-start(f32[8,256]{1,0:T(8,128)S(1)} %get-tuple-element.51), channel_id=1, source_target_pairs={{0,16},{1,17},{2,18},{3,19},{4,20},{5,21},{6,22},{7,23},{8,24},{9,... | collective-permute-start | bytes 24584 | tf_op jit(solution)/shard_map/ppermute | solution.py:357

commit v14 on v12

--- a/solution.py
+++ b/solution.py
@@ -72,10 +72,16 @@
 
 def read_kernel(order_hbm, potential_hbm, order_ref, kernel_ref, half_ref, copied_ref, semaphores):
     core, _, _ = place()
-    copies = (
-        pltpu.make_async_copy(order_hbm, order_ref, semaphores.at[0]),
-        pltpu.make_async_copy(potential_hbm, copied_ref, semaphores.at[1]),
-    )
+    pieces = semaphores.shape[0] - 1
+    part = copied_ref.shape[0] // pieces
+    copies = [pltpu.make_async_copy(order_hbm, order_ref, semaphores.at[pieces])]
+    for piece in range(pieces):
+        rows = pl.ds(piece * part, part)
+        copies.append(
+            pltpu.make_async_copy(
+                potential_hbm.at[rows, :], copied_ref.at[rows, :], semaphores.at[piece]
+            )
+        )
     for copy in copies:
         copy.start()
     for copy in copies:
@@ -315,7 +321,7 @@
         in_specs=[hbm, hbm],
         out_specs=(vmem, vmem, vmem),
         out_shape=(jax.ShapeDtypeStruct(attribute_order.shape, jnp.int32), whole, half),
-        scratch_shapes=[pltpu.VMEM((size, size), jnp.float32), pltpu.SemaphoreType.DMA((2,))],
+        scratch_shapes=[pltpu.VMEM((size, size), jnp.float32), pltpu.SemaphoreType.DMA((5,))],
         name="read",
     )(
         pltpu.with_memory_space_constraint(attribute_order, pltpu.HBM),
@@ -345,8 +351,8 @@
         lambda x, y, z: (x ^ 2, y, z),
     )
     relayed = lax.ppermute(across, "clique", along_clique(lambda y, z: (y ^ 1, z)))
-    held, beside, far_counts = lax.optimization_barrier((across, beside, far_counts))
-    relayed, near_counts = lax.optimization_barrier((relayed, near_counts))
+    held, beside = lax.optimization_barrier((across, beside))
+    relayed, far_counts, near_counts = lax.optimization_barrier((relayed, far_counts, near_counts))
     arrived = (held, beside, relayed)
     block, message = call(
         block_kernel, out_shape=(shape(4, size, size), shape(8, size)), name="block"

time: 45.6 us -> 47.5 us (1.042)
  starting transfers between devices: 18.9 us -> 25.1 us
  waiting for transfers between devices: 10.9 us -> 6.29 us
    ppermute x7, starting transfers between devices: 2.6 us -> 7.83 us  [other_core(): return lax.ppermute(value, 'dp', along_dp(lambda x, c: (x, 1 - c)))]
    ppermute x2, waiting for transfers between devices: 5.31 us -> 1.92 us  [exchange(): lax.ppermute(half, axes, everywhere(lambda x, c, y, z: far_step(x, y, z)))]
    ppermute x1, waiting for transfers between devices: 3.33 us -> 0.63 us  [per_device(): lax.ppermute(half_product, 'clique', along_clique(lambda y, z: (y ^ 1, z)))]
    ppermute x1, waiting for transfers between devices: 0.01 us -> 1.52 us  [per_device(): lax.ppermute(half_product, 'clique', along_clique(lambda y, z: (y, z ^ 6)))]
    ppermute x2, starting transfers between devices: 0.52 us -> 1.87 us  [exchange(): lax.ppermute(half, axes, everywhere(lambda x, c, y, z: far_step(x, y, z)))]
  transfers between devices with their start and end apart: 15 -> 15, of which waited for: 7 -> 5; matrix products, arithmetic and copies ran while one was open for 0% -> 0% of each run, Pallas kernels for 24% -> 24%
where the time goes in v14:
time: 47.5 us; the launch traced here: 47.4 us
  starting transfers between devices  25.1 us (53%)
  Pallas kernels  15.3 us (32%)
  waiting for transfers between devices  6.29 us (13%)
  between operations  0.74 us (2%)
    pallas_call x1, Pallas kernels, count_pairs(): pl.pallas_call(functools.partial(count_kernel, part), out_shape=shape(siz...  8.9 us
    ppermute x7, starting transfers between devices, other_core(): return lax.ppermute(value, 'dp', along_dp(lambda x, c: (x, 1 - c)))  7.83 us
    ppermute x2, starting transfers between devices, exchange(): lax.ppermute(whole, axes, everywhere(near_step))  7.82 us
    ppermute x1, starting transfers between devices, per_device(): lax.ppermute(half_product, 'clique', along_clique(lambda y, z: (y, z ^ 6)))  3.59 us
    ppermute x1, starting transfers between devices, per_device(): lax.ppermute(message, 'clique', along_clique(lambda y, z: (y ^ 2, z)))  2.64 us
    pallas_call x1, Pallas kernels, per_device(): call(sides_kernel, out_shape=(whole, shape(8, size)), name='sides')  2.48 us
    ppermute x7, waiting for transfers between devices, other_core(): return lax.ppermute(value, 'dp', along_dp(lambda x, c: (x, 1 - c)))  2.21 us
    ppermute x2, waiting for transfers between devices, exchange(): lax.ppermute(half, axes, everywhere(lambda x, c, y, z: far_step(x, y, z)))  1.92 us
  transfers between devices with their start and end apart: 15, of which 5 were waited for; matrix products, arithmetic and copies ran while one was open for 0% of the time, Pallas kernels for 24%

profile of v14, /device:TPU:1, one launch (start us, length us, event | category | flops | bytes accessed | tf_op | source)
XLA Modules:
  0.0 47.4 jit_solution(8928172281419603115)
XLA Ops:
  0.6 1.1 %read.1 = (s32[33]{0:T(128)S(1)}, f32[256,256]{1,0:T(8,128)S(1)}, f32[128,256]{1,0:T(8,128)S(1)}) custom-call(s32[33]{0:T(128)} %order_hbm.1, f32[256,256]{1,0:T(8,128)} %bitcast.4), custom_call_target="tpu_custom_call" | custom-call | tf_op jit(solution)/shard_map/read/pallas_call | solution.py:319
  1.7 5.3 %collective-permute-start = (f32[256,256]{1,0:T(8,128)S(1)}, f32[256,256]{1,0:T(8,128)S(1)}, u32[]{:S(2)}, u32[]{:S(2)}) collective-permute-start(f32[256,256]{1,0:T(8,128)S(1)} %get-tuple-element.28.kernel_ref), channel_id=1, source_target_pairs={{0,1},{1,0},{2,3},{3,2},{4,5},{5,4},{6,7},{7,6},{8,9},{9,8},{10,11... | collective-permute-start | bytes 786440 | tf_op jit(solution)/shard_map/ppermute | solution.py:307
  7.0 0.0 collective-permute-start.1
  7.0 0.0 copy-start
  7.0 0.0 copy-start.1
  7.0 8.9 %counts.1.own_ref = f32[256,256]{1,0:T(8,128)S(1)} custom-call(s32[33]{0:T(128)S(1)} %get-tuple-element.30.order_ref, s32[33,65536]{1,0:T(8,128)} %right_ref.1, s32[33,65536]{1,0:T(8,128)} %right_ref.1), custom_call_target="tpu_custom_call" | custom-call | tf_op jit(solution)/shard_map/counts/pallas_call | solution.py:278
  15.9 1.9 %collective-permute-done.1.far = f32[128,256]{1,0:T(8,128)S(1)} collective-permute-done((f32[128,256]{1,0:T(8,128)S(1)}, f32[128,256]{1,0:T(8,128)S(1)}, u32[]{:S(2)}, u32[]{:S(2)}) %collective-permute-start.1) | collective-permute-done | bytes 131104 | tf_op jit(solution)/shard_map/ppermute | solution.py:308
  17.8 0.0 collective-permute-done.near
  17.8 0.0 collective-permute-start.2
  17.8 0.5 %collective-permute-start.3 = (f32[128,256]{1,0:T(8,128)S(1)}, f32[128,256]{1,0:T(8,128)S(1)}, u32[]{:S(2)}, u32[]{:S(2)}) collective-permute-start(f32[128,256]{1,0:T(8,128)S(1)} %collective-permute-done.1.far), channel_id=1, source_target_pairs={{0,32},{32,0},{64,96},{96,64},{128,160},{160,128},{192,224},{224,1... | collective-permute-start | bytes 393224 | tf_op jit(solution)/shard_map/ppermute | solution.py:30
  18.3 1.2 %collective-permute-done.3.far_sibling = f32[128,256]{1,0:T(8,128)S(1)} collective-permute-done((f32[128,256]{1,0:T(8,128)S(1)}, f32[128,256]{1,0:T(8,128)S(1)}, u32[]{:S(2)}, u32[]{:S(2)}) %collective-permute-start.3) | collective-permute-done | bytes 131104 | tf_op jit(solution)/shard_map/ppermute | solution.py:30
  19.5 0.0 collective-permute-done.2.near_sibling
  19.5 1.0 %quad.1 = (f32[4,256,256]{2,1,0:T(8,128)S(1)}, f32[256,256]{1,0:T(8,128)S(1)}, f32[128,256]{1,0:T(8,128)S(1)}) custom-call(f32[256,256]{1,0:T(8,128)S(1)} %get-tuple-element.28.kernel_ref, f32[256,256]{1,0:T(8,128)S(1)} %collective-permute-done.near, f32[256,256]{1,0:T(8,128)S(1)} %collective-permute-done.2.near_sibling, ...), custom_call_target="tpu_custom_call" | custom-call | tf_op jit(solution)/shard_map/quad/pallas_call | solution.py:338
  20.5 0.2 collective-permute-start.7
  20.8 3.6 %collective-permute-start.4 = (f32[128,256]{1,0:T(8,128)S(1)}, f32[128,256]{1,0:T(8,128)S(1)}, u32[]{:S(2)}, u32[]{:S(2)}) collective-permute-start(f32[128,256]{1,0:T(8,128)S(1)} %get-tuple-element.37), channel_id=1, source_target_pairs={{0,6},{1,7},{2,4},{3,5},{4,2},{5,3},{6,0},{7,1},{8,14},{9,15},{10,... | collective-permute-start | bytes 393224 | tf_op jit(solution)/shard_map/ppermute | solution.py:341
  24.4 0.0 collective-permute-done.7.sibling_ref
  24.4 2.6 %collective-permute-start.9 = (f32[256,256]{1,0:T(8,128)S(1)}, f32[256,256]{1,0:T(8,128)S(1)}, u32[]{:S(2)}, u32[]{:S(2)}) collective-permute-start(f32[256,256]{1,0:T(8,128)S(1)} %get-tuple-element.42.chip_ref), channel_id=1, source_target_pairs={{0,64},{1,65},{2,66},{3,67},{4,68},{5,69},{6,70},{7,71},{8,72},{9,... | collective-permute-start | bytes 786440 | tf_op jit(solution)/shard_map/ppermute | solution.py:307
  27.0 1.3 %collective-permute-start.5 = (f32[128,256]{1,0:T(8,128)S(1)}, f32[128,256]{1,0:T(8,128)S(1)}, u32[]{:S(2)}, u32[]{:S(2)}) collective-permute-start(f32[128,256]{1,0:T(8,128)S(1)} %get-tuple-element.37), channel_id=1, source_target_pairs={{0,8},{1,9},{2,10},{3,11},{4,12},{5,13},{6,14},{7,15},{8,0},{9,1},... | collective-permute-start | bytes 393224 | tf_op jit(solution)/shard_map/ppermute | solution.py:342
  28.3 1.5 %collective-permute-done.4.a1 = f32[128,256]{1,0:T(8,128)S(1)} collective-permute-done((f32[128,256]{1,0:T(8,128)S(1)}, f32[128,256]{1,0:T(8,128)S(1)}, u32[]{:S(2)}, u32[]{:S(2)}) %collective-permute-start.4) | collective-permute-done | bytes 131104 | tf_op jit(solution)/shard_map/ppermute | solution.py:341
  29.8 0.0 collective-permute-start.6
  29.8 1.9 %collective-permute-start.8 = (f32[128,256]{1,0:T(8,128)S(1)}, f32[128,256]{1,0:T(8,128)S(1)}, u32[]{:S(2)}, u32[]{:S(2)}) collective-permute-start(f32[128,256]{1,0:T(8,128)S(1)} %get-tuple-element.41), channel_id=1, source_target_pairs={{0,128},{1,129},{2,130},{3,131},{4,132},{5,133},{6,134},{7,135},{8... | collective-permute-start | bytes 393224 | tf_op jit(solution)/shard_map/ppermute | solution.py:308
  31.7 0.6 %collective-permute-done.5.a2 = f32[128,256]{1,0:T(8,128)S(1)} collective-permute-done((f32[128,256]{1,0:T(8,128)S(1)}, f32[128,256]{1,0:T(8,128)S(1)}, u32[]{:S(2)}, u32[]{:S(2)}) %collective-permute-start.5) | collective-permute-done | bytes 131104 | tf_op jit(solution)/shard_map/ppermute | solution.py:342
  32.3 3.2 %collective-permute-start.10 = (f32[128,256]{1,0:T(8,128)S(1)}, f32[128,256]{1,0:T(8,128)S(1)}, u32[]{:S(2)}, u32[]{:S(2)}) collective-permute-start(f32[128,256]{1,0:T(8,128)S(1)} %collective-permute-done.4.a1), channel_id=1, source_target_pairs={{0,32},{32,0},{64,96},{96,64},{128,160},{160,128},{192,224},{224,1... | collective-permute-start | bytes 393224 | tf_op jit(solution)/shard_map/ppermute | solution.py:30
  35.5 0.0 collective-permute-start.11
  35.5 0.0 collective-permute-done.6.a3
  35.5 0.0 collective-permute-done.8.far_ref
  35.5 0.0 collective-permute-done.9.near_ref
  35.5 3.4 %collective-permute-start.12 = (f32[128,256]{1,0:T(8,128)S(1)}, f32[128,256]{1,0:T(8,128)S(1)}, u32[]{:S(2)}, u32[]{:S(2)}) collective-permute-start(f32[128,256]{1,0:T(8,128)S(1)} %collective-permute-done.6.a3), channel_id=1, source_target_pairs={{0,32},{32,0},{64,96},{96,64},{128,160},{160,128},{192,224},{224,1... | collective-permute-start | bytes 393224 | tf_op jit(solution)/shard_map/ppermute | solution.py:30
  39.0 0.0 collective-permute-done.10.b1
  39.0 0.0 collective-permute-done.11.b2
  39.0 1.0 %collective-permute-done.12.b3 = f32[128,256]{1,0:T(8,128)S(1)} collective-permute-done((f32[128,256]{1,0:T(8,128)S(1)}, f32[128,256]{1,0:T(8,128)S(1)}, u32[]{:S(2)}, u32[]{:S(2)}) %collective-permute-start.12) | collective-permute-done | bytes 131104 | tf_op jit(solution)/shard_map/ppermute | solution.py:30
  39.9 0.6 %block.1 = (f32[4,256,256]{2,1,0:T(8,128)S(1)}, f32[8,256]{1,0:T(8,128)S(1)}) custom-call(f32[256,256]{1,0:T(8,128)S(1)} %get-tuple-element.36.product_ref, f32[128,256]{1,0:T(8,128)S(1)} %collective-permute-done.4.a1, f32[128,256]{1,0:T(8,128)S(1)} %collective-permute-done.5.a2, f32[128,256]{1,0:T(8,128)S(1)} %collective-permute-done.6.a3, ...), custom_call_target="tpu_custom_call" | custom-call | tf_op jit(solution)/shard_map/block/pallas_call | solution.py:357
  40.6 0.4 collective-permute-start.14
  41.0 2.6 %collective-permute-start.13 = (f32[8,256]{1,0:T(8,128)S(1)}, f32[8,256]{1,0:T(8,128)S(1)}, u32[]{:S(2)}, u32[]{:S(2)}) collective-permute-start(f32[8,256]{1,0:T(8,128)S(1)} %get-tuple-element.49), channel_id=1, source_target_pairs={{0,16},{1,17},{2,18},{3,19},{4,20},{5,21},{6,22},{7,23},{8,24},{9,... | collective-permute-start | bytes 24584 | tf_op jit(solution)/shard_map/ppermute | solution.py:362
  43.6 2.5 %sides.1 = (f32[256,256]{1,0:T(8,128)S(1)}, f32[8,256]{1,0:T(8,128)S(1)}) custom-call(f32[4,256,256]{2,1,0:T(8,128)S(1)} %get-tuple-element.35.quad_ref, f32[4,256,256]{2,1,0:T(8,128)S(1)} %get-tuple-element.44.block_ref), custom_call_target="tpu_custom_call" | custom-call | tf_op jit(solution)/shard_map/sides/pallas_call | solution.py:363
  46.1 0.0 collective-permute-done.13.message_ref
  46.1 0.0 collective-permute-done.14.sibling_join_ref
  46.2 0.0 copy-done
  46.2 0.0 copy-done.1
  46.2 1.2 %final.1 = (f32[256,256]{1,0:T(8,128)}, f32[256,256]{1,0:T(8,128)}) custom-call(f32[256,256]{1,0:T(8,128)S(1)} %bitcast.5, f32[256,256]{1,0:T(8,128)S(1)} %bitcast.6, f32[256,256]{1,0:T(8,128)S(1)} %get-tuple-element.28.kernel_ref, f32[256,256]{1,0:T(8,128)S(1)} %get-tuple-element.45.path_ref, f32[8,256]{1,0:T(8,128)S(1)} %get-tuple-element.46.known_ref, ...), custom_call_target="tpu_custom_call" | custom-call | tf_op jit(solution)/shard_map/final/pallas_call | solution.py:365
  (2 shorter events, 0.1 us)
Async XLA Ops:
  1.7 16.1 %collective-permute-start = (f32[256,256]{1,0:T(8,128)S(1)}, f32[256,256]{1,0:T(8,128)S(1)}, u32[]{:S(2)}, u32[]{:S(2)}) collective-permute-start(f32[256,256]{1,0:T(8,128)S(1)} %get-tuple-element.28.kernel_ref), channel_id=1, source_target_pairs={{0,1},{1,0},{2,3},{3,2},{4,5},{5,4},{6,7},{7,6},{8,9},{9,8},{10,11... | collective-permute-start | bytes 786440 | tf_op jit(solution)/shard_map/ppermute | solution.py:307
  7.0 10.8 %collective-permute-start.1 = (f32[128,256]{1,0:T(8,128)S(1)}, f32[128,256]{1,0:T(8,128)S(1)}, u32[]{:S(2)}, u32[]{:S(2)}) collective-permute-start(f32[128,256]{1,0:T(8,128)S(1)} %get-tuple-element.29), channel_id=1, source_target_pairs={{0,2},{1,3},{2,0},{3,1},{4,6},{5,7},{6,4},{7,5},{8,10},{9,11},{10,... | collective-permute-start | bytes 393224 | tf_op jit(solution)/shard_map/ppermute | solution.py:308
  7.0 39.2 %copy-start = (f32[1,256,256]{2,1,0:T(8,128)S(1)}, f32[1,256,256]{2,1,0:T(8,128)}, u32[]{:S(2)}) copy-start(f32[1,256,256]{2,1,0:T(8,128)} %param.6) | copy-start | bytes 786436
  7.0 39.2 %copy-start.1 = (f32[1,256,256]{2,1,0:T(8,128)S(1)}, f32[1,256,256]{2,1,0:T(8,128)}, u32[]{:S(2)}) copy-start(f32[1,256,256]{2,1,0:T(8,128)} %param.7) | copy-start | bytes 786436
  17.8 1.7 %collective-permute-start.2 = (f32[256,256]{1,0:T(8,128)S(1)}, f32[256,256]{1,0:T(8,128)S(1)}, u32[]{:S(2)}, u32[]{:S(2)}) collective-permute-start(f32[256,256]{1,0:T(8,128)S(1)} %collective-permute-done.near), channel_id=1, source_target_pairs={{0,32},{32,0},{64,96},{96,64},{128,160},{160,128},{192,224},{224,1... | collective-permute-start | bytes 786440 | tf_op jit(solution)/shard_map/ppermute | solution.py:30
  17.8 1.7 %collective-permute-start.3 = (f32[128,256]{1,0:T(8,128)S(1)}, f32[128,256]{1,0:T(8,128)S(1)}, u32[]{:S(2)}, u32[]{:S(2)}) collective-permute-start(f32[128,256]{1,0:T(8,128)S(1)} %collective-permute-done.1.far), channel_id=1, source_target_pairs={{0,32},{32,0},{64,96},{96,64},{128,160},{160,128},{192,224},{224,1... | collective-permute-start | bytes 393224 | tf_op jit(solution)/shard_map/ppermute | solution.py:30
  20.5 3.8 %collective-permute-start.7 = (f32[256,256]{1,0:T(8,128)S(1)}, f32[256,256]{1,0:T(8,128)S(1)}, u32[]{:S(2)}, u32[]{:S(2)}) collective-permute-start(f32[256,256]{1,0:T(8,128)S(1)} %counts.1.own_ref), channel_id=1, source_target_pairs={{0,32},{32,0},{64,96},{96,64},{128,160},{160,128},{192,224},{224,1... | collective-permute-start | bytes 786440 | tf_op jit(solution)/shard_map/ppermute | solution.py:30
  20.8 9.0 %collective-permute-start.4 = (f32[128,256]{1,0:T(8,128)S(1)}, f32[128,256]{1,0:T(8,128)S(1)}, u32[]{:S(2)}, u32[]{:S(2)}) collective-permute-start(f32[128,256]{1,0:T(8,128)S(1)} %get-tuple-element.37), channel_id=1, source_target_pairs={{0,6},{1,7},{2,4},{3,5},{4,2},{5,3},{6,0},{7,1},{8,14},{9,15},{10,... | collective-permute-start | bytes 393224 | tf_op jit(solution)/shard_map/ppermute | solution.py:341
  24.4 11.1 %collective-permute-start.9 = (f32[256,256]{1,0:T(8,128)S(1)}, f32[256,256]{1,0:T(8,128)S(1)}, u32[]{:S(2)}, u32[]{:S(2)}) collective-permute-start(f32[256,256]{1,0:T(8,128)S(1)} %get-tuple-element.42.chip_ref), channel_id=1, source_target_pairs={{0,64},{1,65},{2,66},{3,67},{4,68},{5,69},{6,70},{7,71},{8,72},{9,... | collective-permute-start | bytes 786440 | tf_op jit(solution)/shard_map/ppermute | solution.py:307
  27.0 5.3 %collective-permute-start.5 = (f32[128,256]{1,0:T(8,128)S(1)}, f32[128,256]{1,0:T(8,128)S(1)}, u32[]{:S(2)}, u32[]{:S(2)}) collective-permute-start(f32[128,256]{1,0:T(8,128)S(1)} %get-tuple-element.37), channel_id=1, source_target_pairs={{0,8},{1,9},{2,10},{3,11},{4,12},{5,13},{6,14},{7,15},{8,0},{9,1},... | collective-permute-start | bytes 393224 | tf_op jit(solution)/shard_map/ppermute | solution.py:342
  29.8 5.7 %collective-permute-start.6 = (f32[128,256]{1,0:T(8,128)S(1)}, f32[128,256]{1,0:T(8,128)S(1)}, u32[]{:S(2)}, u32[]{:S(2)}) collective-permute-start(f32[128,256]{1,0:T(8,128)S(1)} %collective-permute-done.4.a1), channel_id=1, source_target_pairs={{0,8},{1,9},{2,10},{3,11},{4,12},{5,13},{6,14},{7,15},{8,0},{9,1},... | collective-permute-start | bytes 393224 | tf_op jit(solution)/shard_map/ppermute | solution.py:353
  29.8 5.7 %collective-permute-start.8 = (f32[128,256]{1,0:T(8,128)S(1)}, f32[128,256]{1,0:T(8,128)S(1)}, u32[]{:S(2)}, u32[]{:S(2)}) collective-permute-start(f32[128,256]{1,0:T(8,128)S(1)} %get-tuple-element.41), channel_id=1, source_target_pairs={{0,128},{1,129},{2,130},{3,131},{4,132},{5,133},{6,134},{7,135},{8... | collective-permute-start | bytes 393224 | tf_op jit(solution)/shard_map/ppermute | solution.py:308
  32.3 6.7 %collective-permute-start.10 = (f32[128,256]{1,0:T(8,128)S(1)}, f32[128,256]{1,0:T(8,128)S(1)}, u32[]{:S(2)}, u32[]{:S(2)}) collective-permute-start(f32[128,256]{1,0:T(8,128)S(1)} %collective-permute-done.4.a1), channel_id=1, source_target_pairs={{0,32},{32,0},{64,96},{96,64},{128,160},{160,128},{192,224},{224,1... | collective-permute-start | bytes 393224 | tf_op jit(solution)/shard_map/ppermute | solution.py:30
  35.5 3.5 %collective-permute-start.11 = (f32[128,256]{1,0:T(8,128)S(1)}, f32[128,256]{1,0:T(8,128)S(1)}, u32[]{:S(2)}, u32[]{:S(2)}) collective-permute-start(f32[128,256]{1,0:T(8,128)S(1)} %collective-permute-done.5.a2), channel_id=1, source_target_pairs={{0,32},{32,0},{64,96},{96,64},{128,160},{160,128},{192,224},{224,1... | collective-permute-start | bytes 393224 | tf_op jit(solution)/shard_map/ppermute | solution.py:30
  35.5 4.4 %collective-permute-start.12 = (f32[128,256]{1,0:T(8,128)S(1)}, f32[128,256]{1,0:T(8,128)S(1)}, u32[]{:S(2)}, u32[]{:S(2)}) collective-permute-start(f32[128,256]{1,0:T(8,128)S(1)} %collective-permute-done.6.a3), channel_id=1, source_target_pairs={{0,32},{32,0},{64,96},{96,64},{128,160},{160,128},{192,224},{224,1... | collective-permute-start | bytes 393224 | tf_op jit(solution)/shard_map/ppermute | solution.py:30
  40.6 5.6 %collective-permute-start.14 = (f32[256,256]{1,0:T(8,128)S(1)}, f32[256,256]{1,0:T(8,128)S(1)}, u32[]{:S(2)}, u32[]{:S(2)}) collective-permute-start(f32[256,256]{1,0:T(8,128)S(1)} %join.1.join_ref), channel_id=1, source_target_pairs={{0,32},{32,0},{64,96},{96,64},{128,160},{160,128},{192,224},{224,1... | collective-permute-start | bytes 786440 | tf_op jit(solution)/shard_map/ppermute | solution.py:30
  41.0 5.1 %collective-permute-start.13 = (f32[8,256]{1,0:T(8,128)S(1)}, f32[8,256]{1,0:T(8,128)S(1)}, u32[]{:S(2)}, u32[]{:S(2)}) collective-permute-start(f32[8,256]{1,0:T(8,128)S(1)} %get-tuple-element.49), channel_id=1, source_target_pairs={{0,16},{1,17},{2,18},{3,19},{4,20},{5,21},{6,22},{7,23},{8,24},{9,... | collective-permute-start | bytes 24584 | tf_op jit(solution)/shard_map/ppermute | solution.py:362

commit v15 on v12

--- a/solution.py
+++ b/solution.py
@@ -353,7 +353,7 @@
     )(quad_product, *arrived, *[other_core(value) for value in arrived])
     message, near_counts = lax.optimization_barrier((message, near_counts))
     joined = call(join_kernel, out_shape=whole, name="join")(near_counts, far_counts)
-    arrived = lax.ppermute(message, "clique", along_clique(lambda y, z: (y ^ 2, z)))
+    arrived = lax.ppermute(message, "clique", along_clique(lambda y, z: (y ^ 3, z)))
     path, known = call(sides_kernel, out_shape=(whole, shape(8, size)), name="sides")(quad, block)
     total_rows = table_rows.shape[1] * lax.axis_size("dp")
     updated, beliefs = call(

time: 45.6 us -> 45.4 us (level)
  no operation moved by 1% of the time
where the time goes in v15:
time: 45.4 us; the launch traced here: 45.3 us
  starting transfers between devices  18.8 us (41%)
  Pallas kernels  14.9 us (33%)
  waiting for transfers between devices  10.9 us (24%)
  between operations  0.73 us (2%)
    pallas_call x1, Pallas kernels, count_pairs(): pl.pallas_call(functools.partial(count_kernel, part), out_shape=shape(siz...  8.57 us
    ppermute x2, starting transfers between devices, exchange(): lax.ppermute(whole, axes, everywhere(near_step))  7.83 us
    ppermute x2, waiting for transfers between devices, exchange(): lax.ppermute(half, axes, everywhere(lambda x, c, y, z: far_step(x, y, z)))  5.31 us
    ppermute x1, starting transfers between devices, per_device(): lax.ppermute(half_product, 'clique', along_clique(lambda y, z: (y, z ^ 6)))  3.59 us
    ppermute x1, waiting for transfers between devices, per_device(): lax.ppermute(half_product, 'clique', along_clique(lambda y, z: (y ^ 1, z)))  3.33 us
    ppermute x1, starting transfers between devices, per_device(): lax.ppermute(message, 'clique', along_clique(lambda y, z: (y ^ 3, z)))  2.75 us
    ppermute x7, starting transfers between devices, other_core(): return lax.ppermute(value, 'dp', along_dp(lambda x, c: (x, 1 - c)))  2.6 us
    pallas_call x1, Pallas kernels, per_device(): call(sides_kernel, out_shape=(whole, shape(8, size)), name='sides')  2.48 us
  transfers between devices with their start and end apart: 15, of which 7 were waited for; matrix products, arithmetic and copies ran while one was open for 0% of the time, Pallas kernels for 24%

profile of v15, /device:TPU:1, one launch (start us, length us, event | category | flops | bytes accessed | tf_op | source)
XLA Modules:
  0.0 45.3 jit_solution(4606465897314193717)
XLA Ops:
  0.6 1.1 %read.1 = (s32[33]{0:T(128)S(1)}, f32[256,256]{1,0:T(8,128)S(1)}, f32[128,256]{1,0:T(8,128)S(1)}) custom-call(s32[33]{0:T(128)} %order_hbm.1, f32[256,256]{1,0:T(8,128)} %bitcast.4), custom_call_target="tpu_custom_call" | custom-call | tf_op jit(solution)/shard_map/read/pallas_call | solution.py:313
  1.7 5.3 %collective-permute-start = (f32[256,256]{1,0:T(8,128)S(1)}, f32[256,256]{1,0:T(8,128)S(1)}, u32[]{:S(2)}, u32[]{:S(2)}) collective-permute-start(f32[256,256]{1,0:T(8,128)S(1)} %get-tuple-element.28.kernel_ref), channel_id=1, source_target_pairs={{0,1},{1,0},{2,3},{3,2},{4,5},{5,4},{6,7},{7,6},{8,9},{9,8},{10,11... | collective-permute-start | bytes 786440 | tf_op jit(solution)/shard_map/ppermute | solution.py:301
  7.0 0.0 collective-permute-start.1
  7.0 0.0 copy-start
  7.0 0.0 copy-start.1
  7.0 8.6 %counts.1.own_ref = f32[256,256]{1,0:T(8,128)S(1)} custom-call(s32[33]{0:T(128)S(1)} %get-tuple-element.30.order_ref, s32[33,65536]{1,0:T(8,128)} %right_ref.1, s32[33,65536]{1,0:T(8,128)} %right_ref.1), custom_call_target="tpu_custom_call" | custom-call | tf_op jit(solution)/shard_map/counts/pallas_call | solution.py:272
  15.5 2.2 %collective-permute-done.1.far = f32[128,256]{1,0:T(8,128)S(1)} collective-permute-done((f32[128,256]{1,0:T(8,128)S(1)}, f32[128,256]{1,0:T(8,128)S(1)}, u32[]{:S(2)}, u32[]{:S(2)}) %collective-permute-start.1) | collective-permute-done | bytes 131104 | tf_op jit(solution)/shard_map/ppermute | solution.py:302
  17.8 0.0 collective-permute-done.near
  17.8 0.0 collective-permute-start.2
  17.8 0.5 %collective-permute-start.3 = (f32[128,256]{1,0:T(8,128)S(1)}, f32[128,256]{1,0:T(8,128)S(1)}, u32[]{:S(2)}, u32[]{:S(2)}) collective-permute-start(f32[128,256]{1,0:T(8,128)S(1)} %collective-permute-done.1.far), channel_id=1, source_target_pairs={{0,32},{32,0},{64,96},{96,64},{128,160},{160,128},{192,224},{224,1... | collective-permute-start | bytes 393224 | tf_op jit(solution)/shard_map/ppermute | solution.py:30
  18.3 1.2 %collective-permute-done.3.far_sibling = f32[128,256]{1,0:T(8,128)S(1)} collective-permute-done((f32[128,256]{1,0:T(8,128)S(1)}, f32[128,256]{1,0:T(8,128)S(1)}, u32[]{:S(2)}, u32[]{:S(2)}) %collective-permute-start.3) | collective-permute-done | bytes 131104 | tf_op jit(solution)/shard_map/ppermute | solution.py:30
  19.5 0.0 collective-permute-done.2.near_sibling
  19.5 1.0 %quad.1 = (f32[4,256,256]{2,1,0:T(8,128)S(1)}, f32[256,256]{1,0:T(8,128)S(1)}, f32[128,256]{1,0:T(8,128)S(1)}) custom-call(f32[256,256]{1,0:T(8,128)S(1)} %get-tuple-element.28.kernel_ref, f32[256,256]{1,0:T(8,128)S(1)} %collective-permute-done.near, f32[256,256]{1,0:T(8,128)S(1)} %collective-permute-done.2.near_sibling, ...), custom_call_target="tpu_custom_call" | custom-call | tf_op jit(solution)/shard_map/quad/pallas_call | solution.py:332
  20.5 0.2 collective-permute-start.6
  20.7 3.6 %collective-permute-start.4 = (f32[128,256]{1,0:T(8,128)S(1)}, f32[128,256]{1,0:T(8,128)S(1)}, u32[]{:S(2)}, u32[]{:S(2)}) collective-permute-start(f32[128,256]{1,0:T(8,128)S(1)} %get-tuple-element.37), channel_id=1, source_target_pairs={{0,6},{1,7},{2,4},{3,5},{4,2},{5,3},{6,0},{7,1},{8,14},{9,15},{10,... | collective-permute-start | bytes 393224 | tf_op jit(solution)/shard_map/ppermute | solution.py:335
  24.3 0.0 collective-permute-done.6.sibling_ref
  24.4 2.6 %collective-permute-start.9 = (f32[256,256]{1,0:T(8,128)S(1)}, f32[256,256]{1,0:T(8,128)S(1)}, u32[]{:S(2)}, u32[]{:S(2)}) collective-permute-start(f32[256,256]{1,0:T(8,128)S(1)} %get-tuple-element.42.chip_ref), channel_id=1, source_target_pairs={{0,64},{1,65},{2,66},{3,67},{4,68},{5,69},{6,70},{7,71},{8,72},{9,... | collective-permute-start | bytes 786440 | tf_op jit(solution)/shard_map/ppermute | solution.py:301
  27.0 1.3 %collective-permute-start.5 = (f32[128,256]{1,0:T(8,128)S(1)}, f32[128,256]{1,0:T(8,128)S(1)}, u32[]{:S(2)}, u32[]{:S(2)}) collective-permute-start(f32[128,256]{1,0:T(8,128)S(1)} %get-tuple-element.37), channel_id=1, source_target_pairs={{0,8},{1,9},{2,10},{3,11},{4,12},{5,13},{6,14},{7,15},{8,0},{9,1},... | collective-permute-start | bytes 393224 | tf_op jit(solution)/shard_map/ppermute | solution.py:336
  28.3 0.5 %collective-permute-start.7 = (f32[128,256]{1,0:T(8,128)S(1)}, f32[128,256]{1,0:T(8,128)S(1)}, u32[]{:S(2)}, u32[]{:S(2)}) collective-permute-start(f32[128,256]{1,0:T(8,128)S(1)} %get-tuple-element.39), channel_id=1, source_target_pairs={{0,128},{1,129},{2,130},{3,131},{4,132},{5,133},{6,134},{7,135},{8... | collective-permute-start | bytes 393224 | tf_op jit(solution)/shard_map/ppermute | solution.py:302
  28.8 0.0 collective-permute-done.4.a1
  28.8 0.2 collective-permute-start.8
  28.9 3.3 %collective-permute-done.5.a2 = f32[128,256]{1,0:T(8,128)S(1)} collective-permute-done((f32[128,256]{1,0:T(8,128)S(1)}, f32[128,256]{1,0:T(8,128)S(1)}, u32[]{:S(2)}, u32[]{:S(2)}) %collective-permute-start.5) | collective-permute-done | bytes 131104 | tf_op jit(solution)/shard_map/ppermute | solution.py:336
  32.3 3.1 %collective-permute-done.7.far_ref = f32[128,256]{1,0:T(8,128)S(1)} collective-permute-done((f32[128,256]{1,0:T(8,128)S(1)}, f32[128,256]{1,0:T(8,128)S(1)}, u32[]{:S(2)}, u32[]{:S(2)}) %collective-permute-start.7) | collective-permute-done | bytes 131104 | tf_op jit(solution)/shard_map/ppermute | solution.py:302
  35.3 0.9 %collective-permute-start.10 = (f32[128,256]{1,0:T(8,128)S(1)}, f32[128,256]{1,0:T(8,128)S(1)}, u32[]{:S(2)}, u32[]{:S(2)}) collective-permute-start(f32[128,256]{1,0:T(8,128)S(1)} %collective-permute-done.4.a1), channel_id=1, source_target_pairs={{0,32},{32,0},{64,96},{96,64},{128,160},{160,128},{192,224},{224,1... | collective-permute-start | bytes 393224 | tf_op jit(solution)/shard_map/ppermute | solution.py:30
  36.3 0.0 collective-permute-start.11
  36.3 0.0 collective-permute-done.8.a3
  36.3 0.0 collective-permute-done.9.near_ref
  36.3 0.5 %collective-permute-start.12 = (f32[128,256]{1,0:T(8,128)S(1)}, f32[128,256]{1,0:T(8,128)S(1)}, u32[]{:S(2)}, u32[]{:S(2)}) collective-permute-start(f32[128,256]{1,0:T(8,128)S(1)} %collective-permute-done.8.a3), channel_id=1, source_target_pairs={{0,32},{32,0},{64,96},{96,64},{128,160},{160,128},{192,224},{224,1... | collective-permute-start | bytes 393224 | tf_op jit(solution)/shard_map/ppermute | solution.py:30
  36.8 0.5 %collective-permute-done.10.b1 = f32[128,256]{1,0:T(8,128)S(1)} collective-permute-done((f32[128,256]{1,0:T(8,128)S(1)}, f32[128,256]{1,0:T(8,128)S(1)}, u32[]{:S(2)}, u32[]{:S(2)}) %collective-permute-start.10) | collective-permute-done | bytes 131104 | tf_op jit(solution)/shard_map/ppermute | solution.py:30
  37.3 0.4 collective-permute-done.11.b2
  37.6 0.2 collective-permute-done.12.b3
  37.8 0.6 %block.1 = (f32[4,256,256]{2,1,0:T(8,128)S(1)}, f32[8,256]{1,0:T(8,128)S(1)}) custom-call(f32[256,256]{1,0:T(8,128)S(1)} %get-tuple-element.36.product_ref, f32[128,256]{1,0:T(8,128)S(1)} %collective-permute-done.4.a1, f32[128,256]{1,0:T(8,128)S(1)} %collective-permute-done.5.a2, f32[128,256]{1,0:T(8,128)S(1)} %collective-permute-done.8.a3, ...), custom_call_target="tpu_custom_call" | custom-call | tf_op jit(solution)/shard_map/block/pallas_call | solution.py:351
  38.4 0.4 collective-permute-start.14
  38.9 2.8 %collective-permute-start.13 = (f32[8,256]{1,0:T(8,128)S(1)}, f32[8,256]{1,0:T(8,128)S(1)}, u32[]{:S(2)}, u32[]{:S(2)}) collective-permute-start(f32[8,256]{1,0:T(8,128)S(1)} %get-tuple-element.49), channel_id=1, source_target_pairs={{0,24},{1,25},{2,26},{3,27},{4,28},{5,29},{6,30},{7,31},{8,16},{9,... | collective-permute-start | bytes 24584 | tf_op jit(solution)/shard_map/ppermute | solution.py:356
  41.6 2.5 %sides.1 = (f32[256,256]{1,0:T(8,128)S(1)}, f32[8,256]{1,0:T(8,128)S(1)}) custom-call(f32[4,256,256]{2,1,0:T(8,128)S(1)} %get-tuple-element.35.quad_ref, f32[4,256,256]{2,1,0:T(8,128)S(1)} %get-tuple-element.44.block_ref), custom_call_target="tpu_custom_call" | custom-call | tf_op jit(solution)/shard_map/sides/pallas_call | solution.py:357
  44.1 0.0 collective-permute-done.13.message_ref
  44.1 0.0 collective-permute-done.14.sibling_join_ref
  44.1 0.0 copy-done
  44.1 0.0 copy-done.1
  44.1 1.2 %final.1 = (f32[256,256]{1,0:T(8,128)}, f32[256,256]{1,0:T(8,128)}) custom-call(f32[256,256]{1,0:T(8,128)S(1)} %bitcast.5, f32[256,256]{1,0:T(8,128)S(1)} %bitcast.6, f32[256,256]{1,0:T(8,128)S(1)} %get-tuple-element.28.kernel_ref, f32[256,256]{1,0:T(8,128)S(1)} %get-tuple-element.45.path_ref, f32[8,256]{1,0:T(8,128)S(1)} %get-tuple-element.46.known_ref, ...), custom_call_target="tpu_custom_call" | custom-call | tf_op jit(solution)/shard_map/final/pallas_call | solution.py:359
  (2 shorter events, 0.1 us)
Async XLA Ops:
  1.7 16.1 %collective-permute-start = (f32[256,256]{1,0:T(8,128)S(1)}, f32[256,256]{1,0:T(8,128)S(1)}, u32[]{:S(2)}, u32[]{:S(2)}) collective-permute-start(f32[256,256]{1,0:T(8,128)S(1)} %get-tuple-element.28.kernel_ref), channel_id=1, source_target_pairs={{0,1},{1,0},{2,3},{3,2},{4,5},{5,4},{6,7},{7,6},{8,9},{9,8},{10,11... | collective-permute-start | bytes 786440 | tf_op jit(solution)/shard_map/ppermute | solution.py:301
  7.0 10.8 %collective-permute-start.1 = (f32[128,256]{1,0:T(8,128)S(1)}, f32[128,256]{1,0:T(8,128)S(1)}, u32[]{:S(2)}, u32[]{:S(2)}) collective-permute-start(f32[128,256]{1,0:T(8,128)S(1)} %get-tuple-element.29), channel_id=1, source_target_pairs={{0,2},{1,3},{2,0},{3,1},{4,6},{5,7},{6,4},{7,5},{8,10},{9,11},{10,... | collective-permute-start | bytes 393224 | tf_op jit(solution)/shard_map/ppermute | solution.py:302
  7.0 37.2 %copy-start = (f32[1,256,256]{2,1,0:T(8,128)S(1)}, f32[1,256,256]{2,1,0:T(8,128)}, u32[]{:S(2)}) copy-start(f32[1,256,256]{2,1,0:T(8,128)} %param.6) | copy-start | bytes 786436
  7.0 37.2 %copy-start.1 = (f32[1,256,256]{2,1,0:T(8,128)S(1)}, f32[1,256,256]{2,1,0:T(8,128)}, u32[]{:S(2)}) copy-start(f32[1,256,256]{2,1,0:T(8,128)} %param.7) | copy-start | bytes 786436
  17.8 1.7 %collective-permute-start.2 = (f32[256,256]{1,0:T(8,128)S(1)}, f32[256,256]{1,0:T(8,128)S(1)}, u32[]{:S(2)}, u32[]{:S(2)}) collective-permute-start(f32[256,256]{1,0:T(8,128)S(1)} %collective-permute-done.near), channel_id=1, source_target_pairs={{0,32},{32,0},{64,96},{96,64},{128,160},{160,128},{192,224},{224,1... | collective-permute-start | bytes 786440 | tf_op jit(solution)/shard_map/ppermute | solution.py:30
  17.8 1.7 %collective-permute-start.3 = (f32[128,256]{1,0:T(8,128)S(1)}, f32[128,256]{1,0:T(8,128)S(1)}, u32[]{:S(2)}, u32[]{:S(2)}) collective-permute-start(f32[128,256]{1,0:T(8,128)S(1)} %collective-permute-done.1.far), channel_id=1, source_target_pairs={{0,32},{32,0},{64,96},{96,64},{128,160},{160,128},{192,224},{224,1... | collective-permute-start | bytes 393224 | tf_op jit(solution)/shard_map/ppermute | solution.py:30
  20.5 3.8 %collective-permute-start.6 = (f32[256,256]{1,0:T(8,128)S(1)}, f32[256,256]{1,0:T(8,128)S(1)}, u32[]{:S(2)}, u32[]{:S(2)}) collective-permute-start(f32[256,256]{1,0:T(8,128)S(1)} %counts.1.own_ref), channel_id=1, source_target_pairs={{0,32},{32,0},{64,96},{96,64},{128,160},{160,128},{192,224},{224,1... | collective-permute-start | bytes 786440 | tf_op jit(solution)/shard_map/ppermute | solution.py:30
  20.7 8.0 %collective-permute-start.4 = (f32[128,256]{1,0:T(8,128)S(1)}, f32[128,256]{1,0:T(8,128)S(1)}, u32[]{:S(2)}, u32[]{:S(2)}) collective-permute-start(f32[128,256]{1,0:T(8,128)S(1)} %get-tuple-element.37), channel_id=1, source_target_pairs={{0,6},{1,7},{2,4},{3,5},{4,2},{5,3},{6,0},{7,1},{8,14},{9,15},{10,... | collective-permute-start | bytes 393224 | tf_op jit(solution)/shard_map/ppermute | solution.py:335
  24.4 11.9 %collective-permute-start.9 = (f32[256,256]{1,0:T(8,128)S(1)}, f32[256,256]{1,0:T(8,128)S(1)}, u32[]{:S(2)}, u32[]{:S(2)}) collective-permute-start(f32[256,256]{1,0:T(8,128)S(1)} %get-tuple-element.42.chip_ref), channel_id=1, source_target_pairs={{0,64},{1,65},{2,66},{3,67},{4,68},{5,69},{6,70},{7,71},{8,72},{9,... | collective-permute-start | bytes 786440 | tf_op jit(solution)/shard_map/ppermute | solution.py:301
  27.0 5.3 %collective-permute-start.5 = (f32[128,256]{1,0:T(8,128)S(1)}, f32[128,256]{1,0:T(8,128)S(1)}, u32[]{:S(2)}, u32[]{:S(2)}) collective-permute-start(f32[128,256]{1,0:T(8,128)S(1)} %get-tuple-element.37), channel_id=1, source_target_pairs={{0,8},{1,9},{2,10},{3,11},{4,12},{5,13},{6,14},{7,15},{8,0},{9,1},... | collective-permute-start | bytes 393224 | tf_op jit(solution)/shard_map/ppermute | solution.py:336
  28.3 7.1 %collective-permute-start.7 = (f32[128,256]{1,0:T(8,128)S(1)}, f32[128,256]{1,0:T(8,128)S(1)}, u32[]{:S(2)}, u32[]{:S(2)}) collective-permute-start(f32[128,256]{1,0:T(8,128)S(1)} %get-tuple-element.39), channel_id=1, source_target_pairs={{0,128},{1,129},{2,130},{3,131},{4,132},{5,133},{6,134},{7,135},{8... | collective-permute-start | bytes 393224 | tf_op jit(solution)/shard_map/ppermute | solution.py:302
  28.8 7.5 %collective-permute-start.8 = (f32[128,256]{1,0:T(8,128)S(1)}, f32[128,256]{1,0:T(8,128)S(1)}, u32[]{:S(2)}, u32[]{:S(2)}) collective-permute-start(f32[128,256]{1,0:T(8,128)S(1)} %collective-permute-done.4.a1), channel_id=1, source_target_pairs={{0,8},{1,9},{2,10},{3,11},{4,12},{5,13},{6,14},{7,15},{8,0},{9,1},... | collective-permute-start | bytes 393224 | tf_op jit(solution)/shard_map/ppermute | solution.py:347
  35.3 1.9 %collective-permute-start.10 = (f32[128,256]{1,0:T(8,128)S(1)}, f32[128,256]{1,0:T(8,128)S(1)}, u32[]{:S(2)}, u32[]{:S(2)}) collective-permute-start(f32[128,256]{1,0:T(8,128)S(1)} %collective-permute-done.4.a1), channel_id=1, source_target_pairs={{0,32},{32,0},{64,96},{96,64},{128,160},{160,128},{192,224},{224,1... | collective-permute-start | bytes 393224 | tf_op jit(solution)/shard_map/ppermute | solution.py:30
  36.3 1.3 %collective-permute-start.11 = (f32[128,256]{1,0:T(8,128)S(1)}, f32[128,256]{1,0:T(8,128)S(1)}, u32[]{:S(2)}, u32[]{:S(2)}) collective-permute-start(f32[128,256]{1,0:T(8,128)S(1)} %collective-permute-done.5.a2), channel_id=1, source_target_pairs={{0,32},{32,0},{64,96},{96,64},{128,160},{160,128},{192,224},{224,1... | collective-permute-start | bytes 393224 | tf_op jit(solution)/shard_map/ppermute | solution.py:30
  36.3 1.5 %collective-permute-start.12 = (f32[128,256]{1,0:T(8,128)S(1)}, f32[128,256]{1,0:T(8,128)S(1)}, u32[]{:S(2)}, u32[]{:S(2)}) collective-permute-start(f32[128,256]{1,0:T(8,128)S(1)} %collective-permute-done.8.a3), channel_id=1, source_target_pairs={{0,32},{32,0},{64,96},{96,64},{128,160},{160,128},{192,224},{224,1... | collective-permute-start | bytes 393224 | tf_op jit(solution)/shard_map/ppermute | solution.py:30
  38.4 5.7 %collective-permute-start.14 = (f32[256,256]{1,0:T(8,128)S(1)}, f32[256,256]{1,0:T(8,128)S(1)}, u32[]{:S(2)}, u32[]{:S(2)}) collective-permute-start(f32[256,256]{1,0:T(8,128)S(1)} %join.1.join_ref), channel_id=1, source_target_pairs={{0,32},{32,0},{64,96},{96,64},{128,160},{160,128},{192,224},{224,1... | collective-permute-start | bytes 786440 | tf_op jit(solution)/shard_map/ppermute | solution.py:30
  38.9 5.2 %collective-permute-start.13 = (f32[8,256]{1,0:T(8,128)S(1)}, f32[8,256]{1,0:T(8,128)S(1)}, u32[]{:S(2)}, u32[]{:S(2)}) collective-permute-start(f32[8,256]{1,0:T(8,128)S(1)} %get-tuple-element.49), channel_id=1, source_target_pairs={{0,24},{1,25},{2,26},{3,27},{4,28},{5,29},{6,30},{7,31},{8,16},{9,... | collective-permute-start | bytes 24584 | tf_op jit(solution)/shard_map/ppermute | solution.py:356

commit v16 on v15

--- a/solution.py
+++ b/solution.py
@@ -85,21 +85,13 @@
     half_ref[...] = kernel_ref[pl.ds(core * half, half), :]
 
 
-def put_others(stack_ref, mine, near, near_sibling, far, far_sibling, core):
-    half = far.shape[0]
-    across = mine ^ 2
-    stack_ref[mine ^ (1 + 2 * core)] = near[...]
-    stack_ref[mine ^ (3 - 2 * core)] = near_sibling[...]
-    stack_ref[across, pl.ds(core * half, half), :] = far[...]
-    stack_ref[across, pl.ds((1 - core) * half, half), :] = far_sibling[...]
-
-
-def quad_kernel(kernel_ref, near, near_sibling, far, far_sibling, quad_ref, product_ref, half_ref):
+def quad_kernel(kernel_ref, a1, a2, a3, b1, b2, b3, quad_ref, product_ref, half_ref):
     core, _, z = place()
     mine = lax.rem(z, QUAD)
     half, size = half_ref.shape
     quad_ref[mine] = kernel_ref[...]
-    put_others(quad_ref, mine, near, near_sibling, far, far_sibling, core)
+    for flip, (own, sibling) in enumerate(((a1, b1), (a2, b2), (a3, b3)), 1):
+        put_halves(quad_ref, mine ^ flip, own, sibling, core)
     scale = 1.0 / size
     left = product(quad_ref[0], quad_ref[1]) * scale
     right = product(quad_ref[2], quad_ref[3]) * scale
@@ -321,17 +313,15 @@
         pltpu.with_memory_space_constraint(attribute_order, pltpu.HBM),
         pltpu.with_memory_space_constraint(potential, pltpu.HBM),
     )
-    near, far = exchange(
-        kernel,
-        half_of_kernel,
-        lambda x, c, y, z: (x, y, z ^ (1 + 2 * c)),
-        lambda x, y, z: (x, y, z ^ 2),
-    )
+    quads = [
+        lax.ppermute(half_of_kernel, "clique", along_clique(lambda y, z, f=f: (y, z ^ f)))
+        for f in (1, 2, 3)
+    ]
     counts = count_pairs(order, table_rows, size)
-    near, far, counts = lax.optimization_barrier((near, far, counts))
+    quads, counts = lax.optimization_barrier((quads, counts))
     quad, quad_product, half_product = call(
         quad_kernel, out_shape=(shape(QUAD, size, size), whole, half), name="quad"
-    )(kernel, near, other_core(near), far, other_core(far))
+    )(kernel, *quads, *[other_core(value) for value in quads])
     across = lax.ppermute(half_product, "clique", along_clique(lambda y, z: (y, z ^ 6)))
     beside = lax.ppermute(half_product, "clique", along_clique(lambda y, z: (y ^ 1, z)))
     counts, quad = lax.optimization_barrier((counts, quad))

time: 45.4 us -> 45.7 us (level)
  starting transfers between devices: 18.8 us -> 20.9 us
  waiting for transfers between devices: 10.9 us -> 8.94 us
    ppermute x0 -> x3, starting transfers between devices: none -> 5.64 us  [per_device(): lax.ppermute(half_of_kernel, 'clique', along_clique(lambda y, z, f=f: (y,...]
    ppermute x2 -> x1, starting transfers between devices: 7.83 us -> 2.56 us  [exchange(): lax.ppermute(whole, axes, everywhere(near_step))]
    ppermute x2 -> x1, waiting for transfers between devices: 5.31 us -> 2.99 us  [exchange(): lax.ppermute(half, axes, everywhere(lambda x, c, y, z: far_step(x, y, z)))]
    ppermute x7 -> x8, starting transfers between devices: 2.6 us -> 4.17 us  [other_core(): return lax.ppermute(value, 'dp', along_dp(lambda x, c: (x, 1 - c)))]
    ppermute x0 -> x3, waiting for transfers between devices: none -> 1.21 us  [per_device(): lax.ppermute(half_of_kernel, 'clique', along_clique(lambda y, z, f=f: (y,...]
    ppermute x1, starting transfers between devices: 0.17 us -> 0.88 us  [per_device(): lax.ppermute(across, 'clique', along_clique(lambda y, z: (y ^ 1, z)))]
    ppermute x1, waiting for transfers between devices: 3.33 us -> 2.69 us  [per_device(): lax.ppermute(half_product, 'clique', along_clique(lambda y, z: (y ^ 1, z)))]
    ppermute x1, starting transfers between devices: 3.59 us -> 3.02 us  [per_device(): lax.ppermute(half_product, 'clique', along_clique(lambda y, z: (y, z ^ 6)))]
  transfers between devices with their start and end apart: 15 -> 17, of which waited for: 7 -> 9; matrix products, arithmetic and copies ran while one was open for 0% -> 0% of each run, Pallas kernels for 24% -> 24%
where the time goes in v16:
time: 45.7 us; the launch traced here: 45.5 us
  starting transfers between devices  20.9 us (46%)
  Pallas kernels  14.9 us (33%)
  waiting for transfers between devices  8.94 us (20%)
  between operations  0.74 us (2%)
    pallas_call x1, Pallas kernels, count_pairs(): pl.pallas_call(functools.partial(count_kernel, part), out_shape=shape(siz...  8.57 us
    ppermute x3, starting transfers between devices, per_device(): lax.ppermute(half_of_kernel, 'clique', along_clique(lambda y, z, f=f: (y,...  5.64 us
    ppermute x8, starting transfers between devices, other_core(): return lax.ppermute(value, 'dp', along_dp(lambda x, c: (x, 1 - c)))  4.17 us
    ppermute x1, starting transfers between devices, per_device(): lax.ppermute(half_product, 'clique', along_clique(lambda y, z: (y, z ^ 6)))  3.02 us
    ppermute x1, waiting for transfers between devices, exchange(): lax.ppermute(half, axes, everywhere(lambda x, c, y, z: far_step(x, y, z)))  2.99 us
    ppermute x1, starting transfers between devices, per_device(): lax.ppermute(message, 'clique', along_clique(lambda y, z: (y ^ 3, z)))  2.76 us
    ppermute x1, waiting for transfers between devices, per_device(): lax.ppermute(half_product, 'clique', along_clique(lambda y, z: (y ^ 1, z)))  2.69 us
    ppermute x1, starting transfers between devices, exchange(): lax.ppermute(whole, axes, everywhere(near_step))  2.56 us
  transfers between devices with their start and end apart: 17, of which 9 were waited for; matrix products, arithmetic and copies ran while one was open for 0% of the time, Pallas kernels for 24%

profile of v16, /device:TPU:1, one launch (start us, length us, event | category | flops | bytes accessed | tf_op | source)
XLA Modules:
  0.0 45.5 jit_solution(17647232171551913471)
XLA Ops:
  0.6 1.1 %read.1 = (s32[33]{0:T(128)S(1)}, f32[256,256]{1,0:T(8,128)S(1)}, f32[128,256]{1,0:T(8,128)S(1)}) custom-call(s32[33]{0:T(128)} %order_hbm.1, f32[256,256]{1,0:T(8,128)} %bitcast.4), custom_call_target="tpu_custom_call" | custom-call | tf_op jit(solution)/shard_map/read/pallas_call | solution.py:305
  1.7 5.3 %collective-permute-start.2 = (f32[128,256]{1,0:T(8,128)S(1)}, f32[128,256]{1,0:T(8,128)S(1)}, u32[]{:S(2)}, u32[]{:S(2)}) collective-permute-start(f32[128,256]{1,0:T(8,128)S(1)} %get-tuple-element.30), channel_id=1, source_target_pairs={{0,3},{1,2},{2,1},{3,0},{4,7},{5,6},{6,5},{7,4},{8,11},{9,10},{10,... | collective-permute-start | bytes 393224 | tf_op jit(solution)/shard_map/ppermute | solution.py:317
  7.0 0.0 collective-permute-start.1
  7.0 0.4 collective-permute-start
  7.3 0.0 copy-start
  7.3 0.0 copy-start.1
  7.3 8.6 %counts.1.own_ref = f32[256,256]{1,0:T(8,128)S(1)} custom-call(s32[33]{0:T(128)S(1)} %get-tuple-element.31.order_ref, s32[33,65536]{1,0:T(8,128)} %right_ref.1, s32[33,65536]{1,0:T(8,128)} %right_ref.1), custom_call_target="tpu_custom_call" | custom-call | tf_op jit(solution)/shard_map/counts/pallas_call | solution.py:264
  15.9 0.0 collective-permute-done.2.a3
  15.9 1.2 %collective-permute-done.1.a2 = f32[128,256]{1,0:T(8,128)S(1)} collective-permute-done((f32[128,256]{1,0:T(8,128)S(1)}, f32[128,256]{1,0:T(8,128)S(1)}, u32[]{:S(2)}, u32[]{:S(2)}) %collective-permute-start.1) | collective-permute-done | bytes 131104 | tf_op jit(solution)/shard_map/ppermute | solution.py:317
  17.1 0.0 collective-permute-done.a1
  17.1 1.3 %collective-permute-start.3 = (f32[128,256]{1,0:T(8,128)S(1)}, f32[128,256]{1,0:T(8,128)S(1)}, u32[]{:S(2)}, u32[]{:S(2)}) collective-permute-start(f32[128,256]{1,0:T(8,128)S(1)} %collective-permute-done.a1), channel_id=1, source_target_pairs={{0,32},{32,0},{64,96},{96,64},{128,160},{160,128},{192,224},{224,1... | collective-permute-start | bytes 393224 | tf_op jit(solution)/shard_map/ppermute | solution.py:30
  18.5 0.0 collective-permute-start.4
  18.5 0.5 %collective-permute-start.5 = (f32[128,256]{1,0:T(8,128)S(1)}, f32[128,256]{1,0:T(8,128)S(1)}, u32[]{:S(2)}, u32[]{:S(2)}) collective-permute-start(f32[128,256]{1,0:T(8,128)S(1)} %collective-permute-done.2.a3), channel_id=1, source_target_pairs={{0,32},{32,0},{64,96},{96,64},{128,160},{160,128},{192,224},{224,1... | collective-permute-start | bytes 393224 | tf_op jit(solution)/shard_map/ppermute | solution.py:30
  19.0 0.5 %collective-permute-done.3.b1 = f32[128,256]{1,0:T(8,128)S(1)} collective-permute-done((f32[128,256]{1,0:T(8,128)S(1)}, f32[128,256]{1,0:T(8,128)S(1)}, u32[]{:S(2)}, u32[]{:S(2)}) %collective-permute-start.3) | collective-permute-done | bytes 131104 | tf_op jit(solution)/shard_map/ppermute | solution.py:30
  19.5 0.4 collective-permute-done.4.b2
  19.8 0.2 collective-permute-done.5.b3
  20.0 1.0 %quad.1 = (f32[4,256,256]{2,1,0:T(8,128)S(1)}, f32[256,256]{1,0:T(8,128)S(1)}, f32[128,256]{1,0:T(8,128)S(1)}) custom-call(f32[256,256]{1,0:T(8,128)S(1)} %get-tuple-element.29.kernel_ref, f32[128,256]{1,0:T(8,128)S(1)} %collective-permute-done.a1, f32[128,256]{1,0:T(8,128)S(1)} %collective-permute-done.1.a2, f32[128,256]{1,0:T(8,128)S(1)} %collective-permute-done.2.a3, ...), custom_call_target="tpu_custom_call" | custom-call | tf_op jit(solution)/shard_map/quad/pallas_call | solution.py:322
  21.0 0.4 collective-permute-start.8
  21.4 3.0 %collective-permute-start.6 = (f32[128,256]{1,0:T(8,128)S(1)}, f32[128,256]{1,0:T(8,128)S(1)}, u32[]{:S(2)}, u32[]{:S(2)}) collective-permute-start(f32[128,256]{1,0:T(8,128)S(1)} %get-tuple-element.39), channel_id=1, source_target_pairs={{0,6},{1,7},{2,4},{3,5},{4,2},{5,3},{6,0},{7,1},{8,14},{9,15},{10,... | collective-permute-start | bytes 393224 | tf_op jit(solution)/shard_map/ppermute | solution.py:325
  24.5 0.0 collective-permute-done.8.sibling_ref
  24.5 2.6 %collective-permute-start.11 = (f32[256,256]{1,0:T(8,128)S(1)}, f32[256,256]{1,0:T(8,128)S(1)}, u32[]{:S(2)}, u32[]{:S(2)}) collective-permute-start(f32[256,256]{1,0:T(8,128)S(1)} %get-tuple-element.44.chip_ref), channel_id=1, source_target_pairs={{0,64},{1,65},{2,66},{3,67},{4,68},{5,69},{6,70},{7,71},{8,72},{9,... | collective-permute-start | bytes 786440 | tf_op jit(solution)/shard_map/ppermute | solution.py:293
  27.1 1.3 %collective-permute-start.7 = (f32[128,256]{1,0:T(8,128)S(1)}, f32[128,256]{1,0:T(8,128)S(1)}, u32[]{:S(2)}, u32[]{:S(2)}) collective-permute-start(f32[128,256]{1,0:T(8,128)S(1)} %get-tuple-element.39), channel_id=1, source_target_pairs={{0,8},{1,9},{2,10},{3,11},{4,12},{5,13},{6,14},{7,15},{8,0},{9,1},... | collective-permute-start | bytes 393224 | tf_op jit(solution)/shard_map/ppermute | solution.py:326
  28.4 0.5 %collective-permute-start.9 = (f32[128,256]{1,0:T(8,128)S(1)}, f32[128,256]{1,0:T(8,128)S(1)}, u32[]{:S(2)}, u32[]{:S(2)}) collective-permute-start(f32[128,256]{1,0:T(8,128)S(1)} %get-tuple-element.41), channel_id=1, source_target_pairs={{0,128},{1,129},{2,130},{3,131},{4,132},{5,133},{6,134},{7,135},{8... | collective-permute-start | bytes 393224 | tf_op jit(solution)/shard_map/ppermute | solution.py:294
  28.9 0.0 collective-permute-done.6.a1
  28.9 0.9 %collective-permute-start.10 = (f32[128,256]{1,0:T(8,128)S(1)}, f32[128,256]{1,0:T(8,128)S(1)}, u32[]{:S(2)}, u32[]{:S(2)}) collective-permute-start(f32[128,256]{1,0:T(8,128)S(1)} %collective-permute-done.6.a1), channel_id=1, source_target_pairs={{0,8},{1,9},{2,10},{3,11},{4,12},{5,13},{6,14},{7,15},{8,0},{9,1},... | collective-permute-start | bytes 393224 | tf_op jit(solution)/shard_map/ppermute | solution.py:337
  29.8 2.7 %collective-permute-done.7.a2 = f32[128,256]{1,0:T(8,128)S(1)} collective-permute-done((f32[128,256]{1,0:T(8,128)S(1)}, f32[128,256]{1,0:T(8,128)S(1)}, u32[]{:S(2)}, u32[]{:S(2)}) %collective-permute-start.7) | collective-permute-done | bytes 131104 | tf_op jit(solution)/shard_map/ppermute | solution.py:326
  32.5 3.0 %collective-permute-done.9.far_ref = f32[128,256]{1,0:T(8,128)S(1)} collective-permute-done((f32[128,256]{1,0:T(8,128)S(1)}, f32[128,256]{1,0:T(8,128)S(1)}, u32[]{:S(2)}, u32[]{:S(2)}) %collective-permute-start.9) | collective-permute-done | bytes 131104 | tf_op jit(solution)/shard_map/ppermute | solution.py:294
  35.4 1.0 %collective-permute-start.12 = (f32[128,256]{1,0:T(8,128)S(1)}, f32[128,256]{1,0:T(8,128)S(1)}, u32[]{:S(2)}, u32[]{:S(2)}) collective-permute-start(f32[128,256]{1,0:T(8,128)S(1)} %collective-permute-done.6.a1), channel_id=1, source_target_pairs={{0,32},{32,0},{64,96},{96,64},{128,160},{160,128},{192,224},{224,1... | collective-permute-start | bytes 393224 | tf_op jit(solution)/shard_map/ppermute | solution.py:30
  36.4 0.0 collective-permute-start.13
  36.4 0.0 collective-permute-done.10.a3
  36.4 0.0 collective-permute-done.11.near_ref
  36.4 0.5 %collective-permute-start.14 = (f32[128,256]{1,0:T(8,128)S(1)}, f32[128,256]{1,0:T(8,128)S(1)}, u32[]{:S(2)}, u32[]{:S(2)}) collective-permute-start(f32[128,256]{1,0:T(8,128)S(1)} %collective-permute-done.10.a3), channel_id=1, source_target_pairs={{0,32},{32,0},{64,96},{96,64},{128,160},{160,128},{192,224},{224,1... | collective-permute-start | bytes 393224 | tf_op jit(solution)/shard_map/ppermute | solution.py:30
  36.9 0.5 %collective-permute-done.12.b1 = f32[128,256]{1,0:T(8,128)S(1)} collective-permute-done((f32[128,256]{1,0:T(8,128)S(1)}, f32[128,256]{1,0:T(8,128)S(1)}, u32[]{:S(2)}, u32[]{:S(2)}) %collective-permute-start.12) | collective-permute-done | bytes 131104 | tf_op jit(solution)/shard_map/ppermute | solution.py:30
  37.4 0.4 collective-permute-done.13.b2
  37.8 0.2 collective-permute-done.14.b3
  38.0 0.6 %block.1 = (f32[4,256,256]{2,1,0:T(8,128)S(1)}, f32[8,256]{1,0:T(8,128)S(1)}) custom-call(f32[256,256]{1,0:T(8,128)S(1)} %get-tuple-element.38.product_ref, f32[128,256]{1,0:T(8,128)S(1)} %collective-permute-done.6.a1, f32[128,256]{1,0:T(8,128)S(1)} %collective-permute-done.7.a2, f32[128,256]{1,0:T(8,128)S(1)} %collective-permute-done.10.a3, ...), custom_call_target="tpu_custom_call" | custom-call | tf_op jit(solution)/shard_map/block/pallas_call | solution.py:341
  38.6 0.4 collective-permute-start.16
  39.0 2.8 %collective-permute-start.15 = (f32[8,256]{1,0:T(8,128)S(1)}, f32[8,256]{1,0:T(8,128)S(1)}, u32[]{:S(2)}, u32[]{:S(2)}) collective-permute-start(f32[8,256]{1,0:T(8,128)S(1)} %get-tuple-element.51), channel_id=1, source_target_pairs={{0,24},{1,25},{2,26},{3,27},{4,28},{5,29},{6,30},{7,31},{8,16},{9,... | collective-permute-start | bytes 24584 | tf_op jit(solution)/shard_map/ppermute | solution.py:346
  41.8 2.5 %sides.1 = (f32[256,256]{1,0:T(8,128)S(1)}, f32[8,256]{1,0:T(8,128)S(1)}) custom-call(f32[4,256,256]{2,1,0:T(8,128)S(1)} %get-tuple-element.37.quad_ref, f32[4,256,256]{2,1,0:T(8,128)S(1)} %get-tuple-element.46.block_ref), custom_call_target="tpu_custom_call" | custom-call | tf_op jit(solution)/shard_map/sides/pallas_call | solution.py:347
  44.2 0.0 collective-permute-done.15.message_ref
  44.3 0.0 collective-permute-done.16.sibling_join_ref
  44.3 0.0 copy-done
  44.3 0.0 copy-done.1
  44.3 1.2 %final.1 = (f32[256,256]{1,0:T(8,128)}, f32[256,256]{1,0:T(8,128)}) custom-call(f32[256,256]{1,0:T(8,128)S(1)} %bitcast.5, f32[256,256]{1,0:T(8,128)S(1)} %bitcast.6, f32[256,256]{1,0:T(8,128)S(1)} %get-tuple-element.29.kernel_ref, f32[256,256]{1,0:T(8,128)S(1)} %get-tuple-element.47.path_ref, f32[8,256]{1,0:T(8,128)S(1)} %get-tuple-element.48.known_ref, ...), custom_call_target="tpu_custom_call" | custom-call | tf_op jit(solution)/shard_map/final/pallas_call | solution.py:349
  (2 shorter events, 0.1 us)
Async XLA Ops:
  1.7 14.2 %collective-permute-start.2 = (f32[128,256]{1,0:T(8,128)S(1)}, f32[128,256]{1,0:T(8,128)S(1)}, u32[]{:S(2)}, u32[]{:S(2)}) collective-permute-start(f32[128,256]{1,0:T(8,128)S(1)} %get-tuple-element.30), channel_id=1, source_target_pairs={{0,3},{1,2},{2,1},{3,0},{4,7},{5,6},{6,5},{7,4},{8,11},{9,10},{10,... | collective-permute-start | bytes 393224 | tf_op jit(solution)/shard_map/ppermute | solution.py:317
  7.0 10.2 %collective-permute-start.1 = (f32[128,256]{1,0:T(8,128)S(1)}, f32[128,256]{1,0:T(8,128)S(1)}, u32[]{:S(2)}, u32[]{:S(2)}) collective-permute-start(f32[128,256]{1,0:T(8,128)S(1)} %get-tuple-element.30), channel_id=1, source_target_pairs={{0,2},{1,3},{2,0},{3,1},{4,6},{5,7},{6,4},{7,5},{8,10},{9,11},{10,... | collective-permute-start | bytes 393224 | tf_op jit(solution)/shard_map/ppermute | solution.py:317
  7.0 10.2 %collective-permute-start = (f32[128,256]{1,0:T(8,128)S(1)}, f32[128,256]{1,0:T(8,128)S(1)}, u32[]{:S(2)}, u32[]{:S(2)}) collective-permute-start(f32[128,256]{1,0:T(8,128)S(1)} %get-tuple-element.30), channel_id=1, source_target_pairs={{0,1},{1,0},{2,3},{3,2},{4,5},{5,4},{6,7},{7,6},{8,9},{9,8},{10,11... | collective-permute-start | bytes 393224 | tf_op jit(solution)/shard_map/ppermute | solution.py:317
  7.3 36.9 %copy-start = (f32[1,256,256]{2,1,0:T(8,128)S(1)}, f32[1,256,256]{2,1,0:T(8,128)}, u32[]{:S(2)}) copy-start(f32[1,256,256]{2,1,0:T(8,128)} %param.6) | copy-start | bytes 786436
  7.3 36.9 %copy-start.1 = (f32[1,256,256]{2,1,0:T(8,128)S(1)}, f32[1,256,256]{2,1,0:T(8,128)}, u32[]{:S(2)}) copy-start(f32[1,256,256]{2,1,0:T(8,128)} %param.7) | copy-start | bytes 786436
  17.1 2.3 %collective-permute-start.3 = (f32[128,256]{1,0:T(8,128)S(1)}, f32[128,256]{1,0:T(8,128)S(1)}, u32[]{:S(2)}, u32[]{:S(2)}) collective-permute-start(f32[128,256]{1,0:T(8,128)S(1)} %collective-permute-done.a1), channel_id=1, source_target_pairs={{0,32},{32,0},{64,96},{96,64},{128,160},{160,128},{192,224},{224,1... | collective-permute-start | bytes 393224 | tf_op jit(solution)/shard_map/ppermute | solution.py:30
  18.5 1.3 %collective-permute-start.4 = (f32[128,256]{1,0:T(8,128)S(1)}, f32[128,256]{1,0:T(8,128)S(1)}, u32[]{:S(2)}, u32[]{:S(2)}) collective-permute-start(f32[128,256]{1,0:T(8,128)S(1)} %collective-permute-done.1.a2), channel_id=1, source_target_pairs={{0,32},{32,0},{64,96},{96,64},{128,160},{160,128},{192,224},{224,1... | collective-permute-start | bytes 393224 | tf_op jit(solution)/shard_map/ppermute | solution.py:30
  18.5 1.5 %collective-permute-start.5 = (f32[128,256]{1,0:T(8,128)S(1)}, f32[128,256]{1,0:T(8,128)S(1)}, u32[]{:S(2)}, u32[]{:S(2)}) collective-permute-start(f32[128,256]{1,0:T(8,128)S(1)} %collective-permute-done.2.a3), channel_id=1, source_target_pairs={{0,32},{32,0},{64,96},{96,64},{128,160},{160,128},{192,224},{224,1... | collective-permute-start | bytes 393224 | tf_op jit(solution)/shard_map/ppermute | solution.py:30
  21.0 3.4 %collective-permute-start.8 = (f32[256,256]{1,0:T(8,128)S(1)}, f32[256,256]{1,0:T(8,128)S(1)}, u32[]{:S(2)}, u32[]{:S(2)}) collective-permute-start(f32[256,256]{1,0:T(8,128)S(1)} %counts.1.own_ref), channel_id=1, source_target_pairs={{0,32},{32,0},{64,96},{96,64},{128,160},{160,128},{192,224},{224,1... | collective-permute-start | bytes 786440 | tf_op jit(solution)/shard_map/ppermute | solution.py:30
  21.4 7.4 %collective-permute-start.6 = (f32[128,256]{1,0:T(8,128)S(1)}, f32[128,256]{1,0:T(8,128)S(1)}, u32[]{:S(2)}, u32[]{:S(2)}) collective-permute-start(f32[128,256]{1,0:T(8,128)S(1)} %get-tuple-element.39), channel_id=1, source_target_pairs={{0,6},{1,7},{2,4},{3,5},{4,2},{5,3},{6,0},{7,1},{8,14},{9,15},{10,... | collective-permute-start | bytes 393224 | tf_op jit(solution)/shard_map/ppermute | solution.py:325
  24.5 11.9 %collective-permute-start.11 = (f32[256,256]{1,0:T(8,128)S(1)}, f32[256,256]{1,0:T(8,128)S(1)}, u32[]{:S(2)}, u32[]{:S(2)}) collective-permute-start(f32[256,256]{1,0:T(8,128)S(1)} %get-tuple-element.44.chip_ref), channel_id=1, source_target_pairs={{0,64},{1,65},{2,66},{3,67},{4,68},{5,69},{6,70},{7,71},{8,72},{9,... | collective-permute-start | bytes 786440 | tf_op jit(solution)/shard_map/ppermute | solution.py:293
  27.1 5.4 %collective-permute-start.7 = (f32[128,256]{1,0:T(8,128)S(1)}, f32[128,256]{1,0:T(8,128)S(1)}, u32[]{:S(2)}, u32[]{:S(2)}) collective-permute-start(f32[128,256]{1,0:T(8,128)S(1)} %get-tuple-element.39), channel_id=1, source_target_pairs={{0,8},{1,9},{2,10},{3,11},{4,12},{5,13},{6,14},{7,15},{8,0},{9,1},... | collective-permute-start | bytes 393224 | tf_op jit(solution)/shard_map/ppermute | solution.py:326
  28.4 7.1 %collective-permute-start.9 = (f32[128,256]{1,0:T(8,128)S(1)}, f32[128,256]{1,0:T(8,128)S(1)}, u32[]{:S(2)}, u32[]{:S(2)}) collective-permute-start(f32[128,256]{1,0:T(8,128)S(1)} %get-tuple-element.41), channel_id=1, source_target_pairs={{0,128},{1,129},{2,130},{3,131},{4,132},{5,133},{6,134},{7,135},{8... | collective-permute-start | bytes 393224 | tf_op jit(solution)/shard_map/ppermute | solution.py:294
  28.9 7.5 %collective-permute-start.10 = (f32[128,256]{1,0:T(8,128)S(1)}, f32[128,256]{1,0:T(8,128)S(1)}, u32[]{:S(2)}, u32[]{:S(2)}) collective-permute-start(f32[128,256]{1,0:T(8,128)S(1)} %collective-permute-done.6.a1), channel_id=1, source_target_pairs={{0,8},{1,9},{2,10},{3,11},{4,12},{5,13},{6,14},{7,15},{8,0},{9,1},... | collective-permute-start | bytes 393224 | tf_op jit(solution)/shard_map/ppermute | solution.py:337
  35.4 2.0 %collective-permute-start.12 = (f32[128,256]{1,0:T(8,128)S(1)}, f32[128,256]{1,0:T(8,128)S(1)}, u32[]{:S(2)}, u32[]{:S(2)}) collective-permute-start(f32[128,256]{1,0:T(8,128)S(1)} %collective-permute-done.6.a1), channel_id=1, source_target_pairs={{0,32},{32,0},{64,96},{96,64},{128,160},{160,128},{192,224},{224,1... | collective-permute-start | bytes 393224 | tf_op jit(solution)/shard_map/ppermute | solution.py:30
  36.4 1.3 %collective-permute-start.13 = (f32[128,256]{1,0:T(8,128)S(1)}, f32[128,256]{1,0:T(8,128)S(1)}, u32[]{:S(2)}, u32[]{:S(2)}) collective-permute-start(f32[128,256]{1,0:T(8,128)S(1)} %collective-permute-done.7.a2), channel_id=1, source_target_pairs={{0,32},{32,0},{64,96},{96,64},{128,160},{160,128},{192,224},{224,1... | collective-permute-start | bytes 393224 | tf_op jit(solution)/shard_map/ppermute | solution.py:30
  36.4 1.5 %collective-permute-start.14 = (f32[128,256]{1,0:T(8,128)S(1)}, f32[128,256]{1,0:T(8,128)S(1)}, u32[]{:S(2)}, u32[]{:S(2)}) collective-permute-start(f32[128,256]{1,0:T(8,128)S(1)} %collective-permute-done.10.a3), channel_id=1, source_target_pairs={{0,32},{32,0},{64,96},{96,64},{128,160},{160,128},{192,224},{224,1... | collective-permute-start | bytes 393224 | tf_op jit(solution)/shard_map/ppermute | solution.py:30
  38.6 5.7 %collective-permute-start.16 = (f32[256,256]{1,0:T(8,128)S(1)}, f32[256,256]{1,0:T(8,128)S(1)}, u32[]{:S(2)}, u32[]{:S(2)}) collective-permute-start(f32[256,256]{1,0:T(8,128)S(1)} %join.1.join_ref), channel_id=1, source_target_pairs={{0,32},{32,0},{64,96},{96,64},{128,160},{160,128},{192,224},{224,1... | collective-permute-start | bytes 786440 | tf_op jit(solution)/shard_map/ppermute | solution.py:30
  39.0 5.2 %collective-permute-start.15 = (f32[8,256]{1,0:T(8,128)S(1)}, f32[8,256]{1,0:T(8,128)S(1)}, u32[]{:S(2)}, u32[]{:S(2)}) collective-permute-start(f32[8,256]{1,0:T(8,128)S(1)} %get-tuple-element.51), channel_id=1, source_target_pairs={{0,24},{1,25},{2,26},{3,27},{4,28},{5,29},{6,30},{7,31},{8,16},{9,... | collective-permute-start | bytes 24584 | tf_op jit(solution)/shard_map/ppermute | solution.py:346
